TPU v7x, 32 devices: a whole 2x2x4 slice. The times are simulated.
32 devices in a mesh: dp: 4 (over z), mp: 8 (over y, x, core).
Axes of the slice: x: 2, y: 2, z: 4, core: 2. Of those that a mesh axis runs over, the one named last changes fastest.
Arguments:
- block_input: bfloat16 [8192, 2048], P(('dp', 'mp')), may hold values from -6 to 6
- out_cotangent: bfloat16 [8192, 2048], P(('dp', 'mp')), may hold values from -6 to 6
- objective: int32 [16], P('dp'), may hold values from 0 to 1, as said below
- prefix_len: int32 [16], P('dp'), may hold values from 64 to 511
- target_mask: int32 [8192], P(('dp', 'mp')), may hold values from 0 to 1, as said below
- qkv_weight: float32 [2048, 3, 2048], P('dp', None, 'mp'), may hold values from -0.125 to 0.125
- out_weight: float32 [2048, 2048], P('mp', 'dp'), may hold values from -3 to 3
- gateup_weight: float32 [2048, 2, 5472], P('dp', None, 'mp'), may hold values from -0.125 to 0.125
- down_weight: float32 [5472, 2048], P('mp', 'dp'), may hold values from -0.625 to 0.625
- norm_params: float32 [4, 2048], replicated, as said below
- qkv_first: float32 [2048, 3, 2048], P('dp', None, 'mp'), may hold values from -0.125 to 0.125
- out_first: float32 [2048, 2048], P('mp', 'dp'), may hold values from -0.005859375 to 0.005859375
- gateup_first: float32 [2048, 2, 5472], P('dp', None, 'mp'), may hold values from -0.09375 to 0.09375
- down_first: float32 [5472, 2048], P('mp', 'dp'), may hold values from -0.013671875 to 0.013671875
- norm_first: float32 [4, 2048], replicated, may hold values from -0.21875 to 0.21875
- qkv_second: float32 [2048, 3, 2048], P('dp', None, 'mp'), may hold values from 3.0517578e-05 to 0.00048828125
- out_second: float32 [2048, 2048], P('mp', 'dp'), may hold values from 7.080078e-08 to 1.1230469e-06
- gateup_second: float32 [2048, 2, 5472], P('dp', None, 'mp'), may hold values from 1.953125e-05 to 0.0003125
- down_second: float32 [5472, 2048], P('mp', 'dp'), may hold values from 4.3945312e-07 to 7.080078e-06
- norm_second: float32 [4, 2048], replicated, may hold values from 0.00012207031 to 0.001953125
Outputs:
- block_output: bfloat16 [8192, 2048], P(('dp', 'mp'))
- input_grad: float32 [8192, 2048], P(('dp', 'mp'))
- qkv_new: float32 [2048, 3, 2048], P('dp', None, 'mp')
- qkv_first_new: float32 [2048, 3, 2048], P('dp', None, 'mp')
- qkv_second_new: float32 [2048, 3, 2048], P('dp', None, 'mp')
- out_new: float32 [2048, 2048], P('mp', 'dp')
- out_first_new: float32 [2048, 2048], P('mp', 'dp')
- out_second_new: float32 [2048, 2048], P('mp', 'dp')
- gateup_new: float32 [2048, 2, 5472], P('dp', None, 'mp')
- gateup_first_new: float32 [2048, 2, 5472], P('dp', None, 'mp')
- gateup_second_new: float32 [2048, 2, 5472], P('dp', None, 'mp')
- down_new: float32 [5472, 2048], P('mp', 'dp')
- down_first_new: float32 [5472, 2048], P('mp', 'dp')
- down_second_new: float32 [5472, 2048], P('mp', 'dp')
- norm_new: float32 [4, 2048], replicated
- norm_first_new: float32 [4, 2048], replicated
- norm_second_new: float32 [4, 2048], replicated
Inputs may be any that keep to these rules, and one draw needn't show every extreme that they name: `objective`: at least one sequence of each kind. `target_mask`: the last residue of every sequence is a target. `norm_params`: rows 0 and 2 are the gains of the first and second norm, rows 1 and 3 their biases.
All inputs are finite; a program needn't handle non-finite values.
Results may differ from a plain program's by a relative error of at most 0.024.
Values may be sent and summed in bfloat16 or wider, within the bound.
No kernel may reach another device: no remote copies, remote signals or barrier semaphores. Data moves between devices by JAX's collectives and lax.ppermute only.
A program may use at most 256 MiB of HBM per device.

v0:
```python
import jax
import jax.numpy as jnp
from jax import lax
from jax.sharding import PartitionSpec as P

D = 2048
HD = 128
FF = 5461
FF_PAD = 5472
STEP = 5


deep_alpha = 48.0**0.5
norm_eps = 1e-05
masked_score = -1e30
rope_base = 10000.0
beta_one = 0.5
beta_two = 0.5
adam_eps = 1e-08
decay_rate = 0.1


def rope_tables(seq_len, head_dim):
    position = jnp.arange(seq_len, dtype=jnp.float32)
    freqs = rope_base ** (-jnp.arange(0, head_dim, 2, dtype=jnp.float32) / head_dim)
    angles = position[:, None] * freqs[None, :]
    return (jnp.cos(angles), jnp.sin(angles))


def rotate(values, cosine, sine_table):
    half_dim = values.shape[-1] // 2
    first_half = values[..., :half_dim]
    second_half = values[..., half_dim:]
    cos_b = cosine[:, None, :]
    sin_b = sine_table[:, None, :]
    return jnp.concatenate(
        [first_half * cos_b - second_half * sin_b, second_half * cos_b + first_half * sin_b], -1
    )


def norm_forward(hidden, norm_gain, norm_bias):
    row_mean = jnp.mean(hidden, -1, keepdims=True)
    centred = hidden - row_mean
    variance = jnp.mean(centred * centred, -1, keepdims=True)
    inv_std = lax.rsqrt(variance + norm_eps)
    normed = centred * inv_std
    return (normed * norm_gain + norm_bias, normed, inv_std)


def norm_backward(grad_rows, normed, inv_std, norm_gain):
    grad_normed = grad_rows * norm_gain
    mean_grad = jnp.mean(grad_normed, -1, keepdims=True)
    mean_proj = jnp.mean(grad_normed * normed, -1, keepdims=True)
    grad_in = inv_std * (grad_normed - mean_grad - normed * mean_proj)
    return (grad_in, jnp.sum(grad_rows * normed, 0), jnp.sum(grad_rows, 0))


def adamw(weight, gradient, first_moment, second, step_rate):
    first_new = beta_one * first_moment + (1.0 - beta_one) * gradient
    second_new = beta_two * second + (1.0 - beta_two) * gradient * gradient
    first_hat = first_new / (1.0 - beta_one**STEP)
    second_hat = second_new / (1.0 - beta_two**STEP)
    weight_new = weight - step_rate * (
        first_hat / (jnp.sqrt(second_hat) + adam_eps) + decay_rate * weight
    )
    return (weight_new, first_new, second_new)


def local(
    block_input,
    out_cotangent,
    objective,
    prefix_len,
    target_mask,
    qkv_weight,
    out_weight,
    gateup_weight,
    down_weight,
    norm_params,
    qkv_first,
    out_first,
    gateup_first,
    down_first,
    norm_first,
    qkv_second,
    out_second,
    gateup_second,
    down_second,
    norm_second,
):
    mp_count = lax.axis_size("mp")
    mp_index = lax.axis_index("mp")
    own_rows = block_input.shape[0]
    seq_count = objective.shape[0]
    group_rows = own_rows * mp_count
    seq_len = group_rows // seq_count
    local_dim = qkv_weight.shape[2]
    local_heads = local_dim // HD
    local_units = gateup_weight.shape[2]
    score_scale = HD ** (-0.5)
    row_start = mp_index * own_rows
    qkv_full, out_full, gateup_full, down_full = (
        lax.all_gather(qkv_weight.astype(jnp.bfloat16), "dp", axis=0, tiled=True),
        lax.all_gather(out_weight.astype(jnp.bfloat16), "dp", axis=1, tiled=True),
        lax.all_gather(gateup_weight.astype(jnp.bfloat16), "dp", axis=0, tiled=True),
        lax.all_gather(down_weight.astype(jnp.bfloat16), "dp", axis=1, tiled=True),
    )
    input_all = lax.all_gather(block_input, "mp", axis=0, tiled=True)
    projected = jnp.einsum("td,dce->tce", input_all, qkv_full, preferred_element_type=jnp.float32)
    shaped = projected.reshape(seq_count, seq_len, 3, local_heads, HD)
    cosine, sine_table = rope_tables(seq_len, HD)
    query_rows = rotate(shaped[:, :, 0], cosine, sine_table).astype(jnp.bfloat16)
    key_rows = rotate(shaped[:, :, 1], cosine, sine_table).astype(jnp.bfloat16)
    value_rows = shaped[:, :, 2].astype(jnp.bfloat16)
    row_index = jnp.arange(seq_len)[:, None]
    col_index = jnp.arange(seq_len)[None, :]
    visible = (
        (objective[:, None, None] > 0)
        | (col_index[None] < prefix_len[:, None, None])
        | (col_index <= row_index)[None]
    )
    scores = (
        jnp.einsum("sihe,sjhe->shij", query_rows, key_rows, preferred_element_type=jnp.float32)
        * score_scale
    )
    scores = jnp.where(visible[:, None], scores, masked_score)
    row_max = jnp.max(scores, -1, keepdims=True)
    exp_scores = jnp.exp(scores - row_max)
    row_total = jnp.sum(exp_scores, -1, keepdims=True)
    soft_weights = exp_scores / row_total
    log_total = row_max + jnp.log(row_total)
    attended = jnp.einsum(
        "shij,sjhe->sihe",
        soft_weights.astype(jnp.bfloat16),
        value_rows,
        preferred_element_type=jnp.float32,
    )
    attended_low = attended.reshape(group_rows, local_dim).astype(jnp.bfloat16)
    attn_part = jnp.dot(attended_low, out_full, preferred_element_type=jnp.float32)
    attn_total = lax.psum(attn_part, "mp")
    hidden_all = deep_alpha * input_all.astype(jnp.float32) + attn_total
    middle_all, _, _ = norm_forward(hidden_all, norm_params[0], norm_params[1])
    middle_low = middle_all.astype(jnp.bfloat16)
    hidden_one = lax.dynamic_slice_in_dim(hidden_all, row_start, own_rows, 0)
    middle = lax.dynamic_slice_in_dim(middle_all, row_start, own_rows, 0)
    live_units = (mp_index * local_units + jnp.arange(local_units) < FF).astype(jnp.float32)
    gate_up = jnp.einsum("td,dcf->tcf", middle_low, gateup_full, preferred_element_type=jnp.float32)
    hidden_low = (jax.nn.gelu(gate_up[:, 0]) * gate_up[:, 1] * live_units).astype(jnp.bfloat16)
    ffn_part = jnp.dot(hidden_low, down_full, preferred_element_type=jnp.float32)
    ffn_total = lax.psum(ffn_part.astype(jnp.bfloat16), "mp").astype(jnp.float32)
    ffn_own = lax.dynamic_slice_in_dim(ffn_total, row_start, own_rows, 0)
    hidden_two = deep_alpha * middle + ffn_own
    output_rows, normed_two, inv_two = norm_forward(hidden_two, norm_params[2], norm_params[3])
    mask_f32 = target_mask.astype(jnp.float32)
    grad_rows = out_cotangent.astype(jnp.float32) * mask_f32[:, None]
    grad_two, gain_two, bias_two = norm_backward(grad_rows, normed_two, inv_two, norm_params[2])
    ffn_back = lax.all_gather(grad_two.astype(jnp.bfloat16), "mp", axis=0, tiled=True)
    gate_again = jnp.einsum(
        "td,dcf->tcf", middle_low, gateup_full, preferred_element_type=jnp.float32
    )
    gate_act, gelu_pull = jax.vjp(jax.nn.gelu, gate_again[:, 0])
    up_part = gate_again[:, 1]
    hidden_again = (gate_act * up_part * live_units).astype(jnp.bfloat16)
    grad_hidden = (
        jnp.einsum("td,fd->tf", ffn_back, down_full, preferred_element_type=jnp.float32)
        * live_units
    )
    down_grad = jnp.einsum("tf,td->fd", hidden_again, ffn_back, preferred_element_type=jnp.float32)
    grad_gate = gelu_pull(grad_hidden * up_part)[0]
    grad_up = grad_hidden * gate_act
    grad_gateup = jnp.stack([grad_gate, grad_up], 1).astype(jnp.bfloat16)
    middle_part = jnp.einsum(
        "tcf,dcf->td", grad_gateup, gateup_full, preferred_element_type=jnp.float32
    )
    gateup_grad = jnp.einsum(
        "td,tcf->dcf", middle_low, grad_gateup, preferred_element_type=jnp.float32
    )
    grad_middle = (
        lax.psum_scatter(
            middle_part.astype(jnp.bfloat16), "mp", scatter_dimension=0, tiled=True
        ).astype(jnp.float32)
        + deep_alpha * grad_two
    )
    _, normed_one, inv_one = norm_forward(hidden_one, norm_params[0], norm_params[1])
    grad_one, gain_one, bias_one = norm_backward(grad_middle, normed_one, inv_one, norm_params[0])
    attn_back = lax.all_gather(grad_one.astype(jnp.bfloat16), "mp", axis=0, tiled=True)
    grad_attended = jnp.einsum(
        "td,ed->te", attn_back, out_full, preferred_element_type=jnp.float32
    ).astype(jnp.bfloat16)
    grad_attended = grad_attended.reshape(seq_count, seq_len, local_heads, HD)
    out_grad = jnp.einsum("te,td->ed", attended_low, attn_back, preferred_element_type=jnp.float32)
    scores_again = (
        jnp.einsum("sihe,sjhe->shij", query_rows, key_rows, preferred_element_type=jnp.float32)
        * score_scale
    )
    scores_again = jnp.where(visible[:, None], scores_again, masked_score)
    soft_again = jnp.exp(scores_again - log_total)
    grad_soft = jnp.einsum(
        "sihe,sjhe->shij", grad_attended, value_rows, preferred_element_type=jnp.float32
    )
    value_grad = jnp.einsum(
        "shij,sihe->sjhe",
        soft_again.astype(jnp.bfloat16),
        grad_attended,
        preferred_element_type=jnp.float32,
    )
    row_dot = jnp.sum(soft_again * grad_soft, -1, keepdims=True)
    grad_scores = (soft_again * (grad_soft - row_dot)).astype(jnp.bfloat16)
    query_grad = (
        jnp.einsum("shij,sjhe->sihe", grad_scores, key_rows, preferred_element_type=jnp.float32)
        * score_scale
    )
    key_grad = (
        jnp.einsum("shij,sihe->sjhe", grad_scores, query_rows, preferred_element_type=jnp.float32)
        * score_scale
    )
    query_lin = rotate(query_grad, cosine, -sine_table)
    key_lin = rotate(key_grad, cosine, -sine_table)
    grad_proj = (
        jnp.stack([query_lin, key_lin, value_grad], 2)
        .astype(jnp.bfloat16)
        .reshape(group_rows, 3, local_dim)
    )
    input_part = jnp.einsum("tce,dce->td", grad_proj, qkv_full, preferred_element_type=jnp.float32)
    qkv_grad = jnp.einsum("td,tce->dce", input_all, grad_proj, preferred_element_type=jnp.float32)
    input_raw = (
        lax.psum_scatter(
            input_part.astype(jnp.bfloat16), "mp", scatter_dimension=0, tiled=True
        ).astype(jnp.float32)
        + deep_alpha * grad_one
    )
    qkv_grad, out_grad, gateup_grad, down_grad = (
        lax.psum_scatter(
            qkv_grad.astype(jnp.bfloat16), "dp", scatter_dimension=0, tiled=True
        ).astype(jnp.float32),
        lax.psum_scatter(
            out_grad.astype(jnp.bfloat16), "dp", scatter_dimension=1, tiled=True
        ).astype(jnp.float32),
        lax.psum_scatter(
            gateup_grad.astype(jnp.bfloat16), "dp", scatter_dimension=0, tiled=True
        ).astype(jnp.float32),
        lax.psum_scatter(
            down_grad.astype(jnp.bfloat16), "dp", scatter_dimension=1, tiled=True
        ).astype(jnp.float32),
    )
    norm_grad = jnp.stack([gain_one, bias_one, gain_two, bias_two], 0)
    norm_grad, target_count = lax.psum((norm_grad, jnp.sum(mask_f32)), ("dp", "mp"))
    rate_list = (D ** (-0.5), 0.5, D ** (-0.5), (FF_PAD // 64) ** (-0.5), 0.4)
    qkv_res = adamw(qkv_weight, qkv_grad / target_count, qkv_first, qkv_second, rate_list[0])
    out_res = adamw(out_weight, out_grad / target_count, out_first, out_second, rate_list[1])
    gateup_res = adamw(
        gateup_weight, gateup_grad / target_count, gateup_first, gateup_second, rate_list[2]
    )
    down_res = adamw(down_weight, down_grad / target_count, down_first, down_second, rate_list[3])
    norm_res = adamw(norm_params, norm_grad / target_count, norm_first, norm_second, rate_list[4])
    return (
        output_rows.astype(jnp.bfloat16),
        input_raw / target_count,
        qkv_res[0],
        qkv_res[1],
        qkv_res[2],
        out_res[0],
        out_res[1],
        out_res[2],
        gateup_res[0],
        gateup_res[1],
        gateup_res[2],
        down_res[0],
        down_res[1],
        down_res[2],
        norm_res[0],
        norm_res[1],
        norm_res[2],
    )


def solution(mesh):
    return jax.shard_map(
        local,
        mesh=mesh,
        in_specs=(
            P(("dp", "mp"), None),
            P(("dp", "mp"), None),
            P("dp"),
            P("dp"),
            P(("dp", "mp")),
            P("dp", None, "mp"),
            P("mp", "dp"),
            P("dp", None, "mp"),
            P("mp", "dp"),
            P(),
            P("dp", None, "mp"),
            P("mp", "dp"),
            P("dp", None, "mp"),
            P("mp", "dp"),
            P(),
            P("dp", None, "mp"),
            P("mp", "dp"),
            P("dp", None, "mp"),
            P("mp", "dp"),
            P(),
        ),
        out_specs=(
            P(("dp", "mp"), None),
            P(("dp", "mp"), None),
            P("dp", None, "mp"),
            P("dp", None, "mp"),
            P("dp", None, "mp"),
            P("mp", "dp"),
            P("mp", "dp"),
            P("mp", "dp"),
            P("dp", None, "mp"),
            P("dp", None, "mp"),
            P("dp", None, "mp"),
            P("mp", "dp"),
            P("mp", "dp"),
            P("mp", "dp"),
            P(),
            P(),
            P(),
        ),
        check_vma=False,
    )
```

profile of v0, /device:TPU:0, one launch (start us, length us, event | category | flops | bytes accessed | tf_op | source)
XLA Modules:
  0.0 1280.0 jit_solution(2433256142239264889)
XLA Ops:
  14.7 61.7 %all-gather.10.cloned.1.call-done = bf16[2048,3,256]{2,0,1:T(8,128)(2,1)} async-done(((bf16[512,3,256]{2,0,1:T(8,128)(2,1)}), bf16[2048,3,256]{2,0,1:T(8,128)(2,1)}) %all-gather.10.cloned.1.call-update) | async-done | bytes 3145744 | tf_op jit(solution)/shard_map/all_gather | solution.py:103
  76.4 54.8 %all-gather.8.cloned.1.call-done = bf16[2048,2048]{1,0:T(8,128)(2,1)} async-done(((bf16[256,2048]{1,0:T(8,128)(2,1)}), bf16[2048,2048]{1,0:T(8,128)(2,1)}) %all-gather.8.cloned.1.call-update) | async-done | bytes 8388624 | tf_op jit(solution)/shard_map/all_gather | solution.py:108
  131.2 11.6 fusion.6
  142.8 8.3 reshape.239
  151.1 3.9 fusion.82
  155.0 3.3 slice.73
  174.5 9.7 fusion.51
  190.5 211.6 %all-reduce.4.cloned.1.call-done = f32[2048,2048]{1,0:T(8,128)} async-done(((f32[2048,2048]{1,0:T(8,128)}), f32[2048,2048]{1,0:T(8,128)}) %all-reduce.4.cloned.1.call-update) | async-done | bytes 16777232 | tf_op jit(solution)/shard_map/psum | solution.py:140
  402.1 16.0 %fusion.81 = (f32[2048]{0:T(1024)S(1)}, f32[2048,2048]{1,0:T(8,128)}) fusion(f32[2048,2048]{1,0:T(8,128)} %all-reduce.4.cloned.1.call-done, bf16[2048,2048]{1,0:T(8,128)(2,1)} %all-gather.8.cloned.1.call-done), kind=kLoop, calls=%fused_computation.166 | loop fusion | flops 16775168 | bytes 41951232 | tf_op jit(solution)/shard_map/reduce_sum | solution.py:42
  418.2 7.7 multiply_reduce_fusion
  425.9 12.2 multiply_add_fusion
  438.1 69.6 %all-gather.14.cloned.1.call-done = bf16[2048,2,684]{0,1,2:T(2,128)(2,1)} async-done(((bf16[512,2,684]{0,1,2:T(2,128)(2,1)}), bf16[2048,2,684]{0,1,2:T(2,128)(2,1)}) %all-gather.14.cloned.1.call-update) | async-done | bytes 5603344 | tf_op jit(solution)/shard_map/all_gather | solution.py:105
  507.7 22.2 %fusion.2 = f32[2048,2,684]{0,2,1:T(8,128)} fusion(bf16[2048,2,684]{0,1,2:T(2,128)(2,1)} %all-gather.14.cloned.1.call-done, f32[2048,2048]{1,0:T(8,128)} %multiply_add_fusion), kind=kOutput, calls=%fused_computation.7 | convolution fusion | flops 11479810048 | bytes 33587200 | tf_op jit(solution)/shard_map/td,dcf->tcf/dot_general | solution.py:147
  529.9 5.5 multiply_convert_fusion.2
  535.5 30.5 %all-gather.16.cloned.1.call-done = bf16[684,2048]{1,0:T(8,128)(2,1)} async-done(((bf16[684,512]{1,0:T(8,128)(2,1)}), bf16[684,2048]{1,0:T(8,128)(2,1)}) %all-gather.16.cloned.1.call-update) | async-done | bytes 2801680 | tf_op jit(solution)/shard_map/all_gather | solution.py:106
  566.0 22.7 %convolution_convert_fusion = bf16[2048,2048]{1,0:T(8,128)(2,1)} fusion(bf16[2048,684]{0,1:T(8,128)(2,1)S(1)} %multiply_convert_fusion.2, bf16[684,2048]{1,0:T(8,128)(2,1)} %all-gather.16.cloned.1.call-done), kind=kOutput, calls=%fused_computation.21 | convolution fusion | flops 5742002176 | bytes 13991936 | tf_op jit(solution)/shard_map/dot_general | solution.py:149
  589.4 124.4 %all-reduce.6.cloned.1.call-done = bf16[2048,2048]{1,0:T(8,128)(2,1)} async-done(((bf16[2048,2048]{1,0:T(8,128)(2,1)}), bf16[2048,2048]{1,0:T(8,128)(2,1)}) %all-reduce.6.cloned.1.call-update) | async-done | bytes 8388624 | tf_op jit(solution)/shard_map/psum | solution.py:150
  720.4 54.5 %all-gather.18.cloned.1.call-done = bf16[2048,2048]{1,0:T(8,128)(2,1)} async-done(((bf16[256,2048]{1,0:T(8,128)(2,1)}), bf16[2048,2048]{1,0:T(8,128)(2,1)}) %all-gather.18.cloned.1.call-update) | async-done | bytes 8388624 | tf_op jit(solution)/shard_map/all_gather | solution.py:157
  774.9 15.4 %fusion.36 = (bf16[2048,1,684]{0,2,1:T(8,128)(2,1)S(1)}, bf16[2048,1,684]{0,2,1:T(8,128)(2,1)S(1)}) fusion(f32[2048,2,684]{0,2,1:T(8,128)} %fusion.2, f32[684]{0:T(1024)S(1)} %fusion.66, bf16[2048,2048]{1,0:T(8,128)(2,1)} %all-gather.18.cloned.1.call-done, bf16[684,2048]{1,0:T(8,128)(2,1)} %all-gather.16.cloned.1.call-done), kind=kOutput, calls=%fused_computation.56 | convolution fusion | flops 5772828672 | bytes 28002992 | tf_op jit(solution)/shard_map/td,fd->tf/dot_general | solution.py:165
  792.8 17.9 %bitcast_convert_fusion.1 = bf16[2048,2048]{1,0:T(8,128)(2,1)} fusion(bf16[2048,2,684]{0,1,2:T(2,128)(2,1)} %all-gather.14.cloned.1.call-done, bf16[2048,1,684]{0,2,1:T(8,128)(2,1)S(1)} %get-tuple-element.102, bf16[2048,1,684]{0,2,1:T(8,128)(2,1)S(1)} %get-tuple-element.101), kind=kOutput, calls=%fused_computation.1 | convolution fusion | flops 11482611712 | bytes 19595264 | tf_op jit(solution)/shard_map/tcf,dcf->td/dot_general | solution.py:172
  814.9 67.4 %reduce-scatter.7.cloned.1.call-done = bf16[256,2048]{1,0:T(8,128)(2,1)} async-done(((bf16[2048,2048]{1,0:T(8,128)(2,1)}), bf16[256,2048]{1,0:T(8,128)(2,1)}) %reduce-scatter.7.cloned.1.call-update) | async-done | bytes 1048592 | tf_op jit(solution)/shard_map/reduce_scatter | solution.py:179
  885.4 4.1 fusion.78
  889.6 18.6 %fusion.19 = bf16[2048,2,684]{0,2,1:T(8,128)(2,1)} fusion(f32[2048,2048]{1,0:T(8,128)} %multiply_add_fusion, bf16[2048,1,684]{0,2,1:T(8,128)(2,1)} %copy-done.49, bf16[2048,1,684]{0,2,1:T(8,128)(2,1)} %copy-done.48), kind=kOutput, calls=%fused_computation.39 | convolution fusion | flops 11493818368 | bytes 27983872 | tf_op jit(solution)/shard_map/td,tcf->dcf/dot_general | solution.py:175
  910.0 10.6 convolution_convert_fusion.1
  921.4 22.6 %all-gather.20.cloned.1.call-done = bf16[2048,2048]{1,0:T(8,128)(2,1)} async-done(((bf16[256,2048]{1,0:T(8,128)(2,1)}), bf16[2048,2048]{1,0:T(8,128)(2,1)}) %all-gather.20.cloned.1.call-update) | async-done | bytes 8388624 | tf_op jit(solution)/shard_map/all_gather | solution.py:186
  944.0 5.8 convolution_convert_fusion.3
  950.8 6.0 fusion.46
  960.6 4.5 multiply_reduce_fusion.1
  965.2 4.8 multiply_convert_fusion
  985.7 6.8 convolution_convert_fusion.2
  994.7 12.0 fusion.31
  1008.6 10.8 bitcast_convert_fusion
  1022.4 3.2 copy.121
  1029.3 41.8 %all-reduce = (f32[]{:T(128)}, f32[4,2048]{1,0:T(4,128)S(1)}) all-reduce(f32[]{:T(128)} %convert_reduce_fusion, f32[4,2048]{1,0:T(4,128)S(1)} %pad_maximum_fusion.11), channel_id=1, replica_groups=mesh['dp'=4,'mp'=8] {'dp','mp'}, use_global_device_ids=true, to_apply=%region_18.19 | all-reduce | flops 8193 | bytes 65544 | tf_op jit(solution)/shard_map/psum | solution.py:247
  1071.1 5.2 multiply_subtract_fusion
  1076.3 3.7 copy.133
  1080.0 3.7 copy.134
  1083.7 3.7 copy.135
  1088.8 15.8 %reduce-scatter.17.cloned.1.call-done = bf16[684,512]{1,0:T(8,128)(2,1)} async-done(((bf16[684,2048]{1,0:T(8,128)(2,1)}), bf16[684,512]{1,0:T(8,128)(2,1)}) %reduce-scatter.17.cloned.1.call-update) | async-done | bytes 700432 | tf_op jit(solution)/shard_map/reduce_scatter | solution.py:242
  1104.6 5.1 multiply_subtract_fusion.2
  1109.7 24.2 %reduce-scatter.13.cloned.1.call-done = bf16[256,512]{1,0:T(8,128)(2,1)} async-done(((bf16[256,2048]{1,0:T(8,128)(2,1)}), bf16[256,512]{1,0:T(8,128)(2,1)}) %reduce-scatter.13.cloned.1.call-update) | async-done | bytes 262160 | tf_op jit(solution)/shard_map/reduce_scatter | solution.py:236
  1133.9 3.6 multiply_subtract_fusion.3
  1137.5 57.5 %reduce-scatter.11.cloned.1.call-done = bf16[512,3,256]{0,2,1:T(8,128)(2,1)} async-done(((bf16[2048,3,256]{0,2,1:T(8,128)(2,1)}), bf16[512,3,256]{0,2,1:T(8,128)(2,1)}) %reduce-scatter.11.cloned.1.call-update) | async-done | bytes 786448 | tf_op jit(solution)/shard_map/reduce_scatter | solution.py:233
  1195.0 5.5 multiply_subtract_fusion.1
  1203.5 3.2 copy.131
  1206.8 3.3 copy.132
  1210.1 59.7 %reduce-scatter.9.cloned.1.call-done = bf16[256,2048]{1,0:T(8,128)(2,1)} async-done(((bf16[2048,2048]{1,0:T(8,128)(2,1)}), bf16[256,2048]{1,0:T(8,128)(2,1)}) %reduce-scatter.9.cloned.1.call-update) | async-done | bytes 1048592 | tf_op jit(solution)/shard_map/reduce_scatter | solution.py:227
  1269.7 3.5 add_divide_fusion
  (192 shorter events, 84.9 us)
Async XLA Ops:
  7.2 3.3 copy-start.28
  7.2 6.0 copy-start.47
  7.2 6.0 copy-start.46
  7.2 69.1 %all-gather.10.cloned.1.call-start = ((), (), s32[]{:S(2)}) async-start(), calls=%async_computation.7 | async-start | bytes 3932160 | tf_op jit(solution)/shard_map/all_gather | solution.py:103
  9.7 121.5 %all-gather.8.cloned.1.call-start = ((), (), s32[]{:S(2)}) async-start(), calls=%async_computation.6 | async-start | bytes 9437184 | tf_op jit(solution)/shard_map/all_gather | solution.py:108
  10.5 164.0 %all-gather.12.cloned.1.call-start = ((), (), s32[]{:S(2)}) async-start(), calls=%async_computation.8 | async-start | bytes 1310720 | tf_op jit(solution)/shard_map/all_gather | solution.py:104
  11.3 390.9 %all-reduce.4.cloned.1.call-start = ((), (), s32[]{:S(2)}) async-start(), calls=%async_computation.9 | async-start | bytes 33554432 | tf_op jit(solution)/shard_map/psum | solution.py:140
  13.2 150.0 %copy-start.26 = (f32[512,64]{1,0:T(8,128)}, f32[512,64]{1,0:T(8,128)S(1)}, u32[]{:S(2)}) copy-start(f32[512,64]{1,0:T(8,128)S(1)} %get-tuple-element.124) | copy-start | bytes 393220
  160.7 8.2 copy-start.14
  164.7 3.0 copy-start.5
  164.7 3.0 copy-start.7
  164.7 3.0 copy-start.9
  164.7 3.0 copy-start.11
  167.7 3.3 copy-start
  167.7 3.4 copy-start.34
  174.5 9.7 copy-start.1
  184.2 323.5 %all-gather.14.cloned.1.call-start = ((), (), s32[]{:S(2)}) async-start(), calls=%async_computation.10 | async-start | bytes 7004160 | tf_op jit(solution)/shard_map/all_gather | solution.py:105
  188.0 377.9 %all-gather.16.cloned.1.call-start = ((), (), s32[]{:S(2)}) async-start(), calls=%async_computation.11 | async-start | bytes 3522560 | tf_op jit(solution)/shard_map/all_gather | solution.py:106
  190.4 523.4 %all-reduce.6.cloned.1.call-start = ((), (), s32[]{:S(2)}) async-start(), calls=%async_computation.12 | async-start | bytes 16777216 | tf_op jit(solution)/shard_map/psum | solution.py:150
  535.4 53.3 %copy-start.24 = (bf16[2048,684]{0,1:T(8,128)(2,1)}, bf16[2048,684]{0,1:T(8,128)(2,1)S(1)}, u32[]{:S(2)}) copy-start(bf16[2048,684]{0,1:T(8,128)(2,1)S(1)} %multiply_convert_fusion.2) | copy-start | bytes 8404996
  588.7 186.2 %all-gather.18.cloned.1.call-start = ((), (), s32[]{:S(2)}) async-start(), calls=%async_computation.13 | async-start | bytes 9437184 | tf_op jit(solution)/shard_map/all_gather | solution.py:157
  589.4 127.0 %copy-start.20 = (bf16[256,2048]{1,0:T(8,128)(2,1)S(1)}, bf16[256,2048]{1,0:T(8,128)(2,1)}, u32[]{:S(2)}) copy-start(bf16[256,2048]{1,0:T(8,128)(2,1)} %param.21) | copy-start | bytes 3145732
  720.4 162.0 %reduce-scatter.7.cloned.1.call-start = ((), (), s32[]{:S(2)}) async-start(), calls=%async_computation.14 | async-start | bytes 9437184 | tf_op jit(solution)/shard_map/reduce_scatter | solution.py:179
  810.7 133.2 %all-gather.20.cloned.1.call-start = ((), (), s32[]{:S(2)}) async-start(), calls=%async_computation.15 | async-start | bytes 9437184 | tf_op jit(solution)/shard_map/all_gather | solution.py:186
  882.4 3.0 copy-start.21
  889.6 181.5 %reduce-scatter.15.cloned.1.call-start = ((), (), s32[]{:S(2)}) async-start(), calls=%async_computation.19 | async-start | bytes 7045120 | tf_op jit(solution)/shard_map/reduce_scatter | solution.py:239
  908.2 196.3 %reduce-scatter.17.cloned.1.call-start = ((), (), s32[]{:S(2)}) async-start(), calls=%async_computation.20 | async-start | bytes 3522560 | tf_op jit(solution)/shard_map/reduce_scatter | solution.py:242
  920.7 23.3 %copy-start.30 = (bf16[256,2048]{1,0:T(8,128)(2,1)S(1)}, bf16[256,2048]{1,0:T(8,128)(2,1)}, u32[]{:S(2)}) copy-start(bf16[256,2048]{1,0:T(8,128)(2,1)} %all-gather.12.cloned.1.call-done) | copy-start | bytes 3145732
  920.7 213.2 %reduce-scatter.13.cloned.1.call-start = ((), (), s32[]{:S(2)}) async-start(), calls=%async_computation.18 | async-start | bytes 1310720 | tf_op jit(solution)/shard_map/reduce_scatter | solution.py:236
  956.8 3.8 copy-start.15
  965.1 4.8 copy-start.10
  965.2 4.8 copy-start.12
  980.8 4.9 copy-start.2
  985.7 6.9 copy-start.22
  992.6 202.4 %reduce-scatter.11.cloned.1.call-start = ((), (), s32[]{:S(2)}) async-start(), calls=%async_computation.17 | async-start | bytes 3932160 | tf_op jit(solution)/shard_map/reduce_scatter | solution.py:233
  1006.7 263.0 %reduce-scatter.9.cloned.1.call-start = ((), (), s32[]{:S(2)}) async-start(), calls=%async_computation.16 | async-start | bytes 9437184 | tf_op jit(solution)/shard_map/reduce_scatter | solution.py:227
  1020.8 4.8 copy-start.45
  1020.8 5.4 copy-start.40
  1020.8 5.4 copy-start.41
  1022.4 48.6 %copy-start.4 = (f32[512,2,684]{0,1,2:T(2,128)S(1)}, f32[512,2,684]{0,1,2:T(2,128)}, u32[]{:S(2)}) copy-start(f32[512,2,684]{0,1,2:T(2,128)} %param.27) | copy-start | bytes 8404996
  1083.7 3.7 copy-start.37
  1083.7 3.7 copy-start.42
  1083.7 3.7 copy-start.43
  1083.7 20.9 %copy-start.19 = (f32[684,512]{1,0:T(8,128)S(1)}, f32[684,512]{1,0:T(8,128)}, u32[]{:S(2)}) copy-start(f32[684,512]{1,0:T(8,128)} %param.28) | copy-start | bytes 4202500
  1083.7 20.9 %copy-start.29 = (f32[684,512]{1,0:T(8,128)S(1)}, f32[684,512]{1,0:T(8,128)}, u32[]{:S(2)}) copy-start(f32[684,512]{1,0:T(8,128)} %param.33) | copy-start | bytes 4202500
  1109.7 85.3 %copy-start.17 = (f32[512,3,256]{0,2,1:T(8,128)S(1)}, f32[512,3,256]{0,2,1:T(8,128)}, u32[]{:S(2)}) copy-start(f32[512,3,256]{0,2,1:T(8,128)} %copy.125) | copy-start | bytes 4718596
  1109.7 85.3 %copy-start.18 = (f32[512,3,256]{0,2,1:T(8,128)S(1)}, f32[512,3,256]{0,2,1:T(8,128)}, u32[]{:S(2)}) copy-start(f32[512,3,256]{0,2,1:T(8,128)} %copy.121) | copy-start | bytes 4718596
  1203.5 66.2 %copy-start.13 = (f32[256,2048]{1,0:T(8,128)S(1)}, f32[256,2048]{1,0:T(8,128)}, u32[]{:S(2)}) copy-start(f32[256,2048]{1,0:T(8,128)} %get-tuple-element.94) | copy-start | bytes 6291460
  (17 other events, 26.7 us)
Sparse Core Ops, SparseCore 0:
  10.2 66.1 all-gather.9
  78.3 52.8 all-gather.7
  133.3 27.9 all-gather.11
  184.3 217.7 all-reduce.3
  404.1 103.5 all-gather.13
  509.7 56.2 all-gather.15
  588.9 124.8 all-reduce.5
  720.5 54.3 all-gather.17
  810.9 71.4 reduce-scatter.6
  889.7 54.2 all-gather.19
  946.3 100.1 reduce-scatter.14
  1048.6 55.8 reduce-scatter.16
  1106.9 26.9 reduce-scatter.12
  1136.0 58.9 reduce-scatter.10
  1198.3 71.3 reduce-scatter.8
where the time goes:
time: 1290 us; the launch traced here: 1280 us
  waiting for transfers between devices  855 us (66%)
  matrix products  182 us (14%)
  other arithmetic  105 us (8%)
  local copies, waits for them, and re-layouts  79.8 us (6%)
  blocking collectives  41.8 us (3%)
  between operations  14.8 us (1%)
    psum x1, waiting for transfers between devices, local(): attn_total = lax.psum(attn_part, 'mp')  212 us
    psum x1, waiting for transfers between devices, local(): lax.psum(ffn_part.astype(jnp.bfloat16), 'mp').astype(jnp.float32)  124 us
    all_gather x1, waiting for transfers between devices, local(): lax.all_gather(gateup_weight.astype(jnp.bfloat16), 'dp', axis=0, tiled=True)  69.6 us
    reduce_scatter x1, waiting for transfers between devices, local(): lax.psum_scatter(middle_part.astype(jnp.bfloat16), 'mp', scatter_dimensio...  67.4 us
    all_gather x1, waiting for transfers between devices, local(): lax.all_gather(qkv_weight.astype(jnp.bfloat16), 'dp', axis=0, tiled=True)  61.7 us
    reduce_scatter x1, waiting for transfers between devices, local(): lax.psum_scatter(input_part.astype(jnp.bfloat16), 'mp', scatter_dimension...  59.7 us
    reduce_scatter x1, waiting for transfers between devices, local(): lax.psum_scatter(qkv_grad.astype(jnp.bfloat16), 'dp', scatter_dimension=0...  57.5 us
    all_gather x1, waiting for transfers between devices, local(): input_all = lax.all_gather(block_input, 'mp', axis=0, tiled=True)  54.8 us
  transfers between devices with their start and end apart: 15, of which 13 were waited for; matrix products, arithmetic and copies ran while one was open for 21% of the time, Pallas kernels for 0%

commit v1 on v0

v1 whole, which is shorter than its diff:
```python
import functools

import jax
import jax.numpy as jnp
from jax import lax
from jax.experimental import pallas as pl
from jax.experimental.pallas import tpu as pltpu
from jax.sharding import PartitionSpec as P

D = 2048
HD = 128
FF = 5461
FF_PAD = 5472
STEP = 5


deep_alpha = 48.0**0.5
norm_eps = 1e-05
masked_score = -1e30
rope_base = 10000.0
beta_one = 0.5
beta_two = 0.5
adam_eps = 1e-08
decay_rate = 0.1


def rope_tables(position, head_dim):
    freqs = rope_base ** (-jnp.arange(0, head_dim, 2, dtype=jnp.float32) / head_dim)
    angles = position.astype(jnp.float32)[:, None] * freqs[None, :]
    cosine, sine = jnp.cos(angles), jnp.sin(angles)
    return (jnp.concatenate([cosine, cosine], -1), jnp.concatenate([-sine, sine], -1))


def turn(values, cosine, sine):
    return values * cosine + pltpu.roll(values, HD // 2, 1) * sine


def dot_nt(left, right):
    return lax.dot_general(
        left, right, (((1,), (1,)), ((), ())), preferred_element_type=jnp.float32
    )


def dot_nn(left, right):
    return lax.dot_general(
        left, right, (((1,), (0,)), ((), ())), preferred_element_type=jnp.float32
    )


def dot_tn(left, right):
    return lax.dot_general(
        left, right, (((0,), (0,)), ((), ())), preferred_element_type=jnp.float32
    )


def soft_rows(info_ref, query, key):
    seq_len = query.shape[0]
    flip = info_ref[2]
    row_at = lax.broadcasted_iota(jnp.int32, (seq_len, seq_len), 0) ^ flip
    col_at = lax.broadcasted_iota(jnp.int32, (seq_len, seq_len), 1) ^ flip
    bound = jnp.where(info_ref[0] > 0, seq_len, info_ref[1])
    visible = (col_at < bound) | (col_at <= row_at)
    scores = jnp.where(visible, dot_nt(query, key) * HD ** (-0.5), masked_score)
    exp_scores = jnp.exp(scores - jnp.max(scores, -1, keepdims=True))
    return exp_scores / jnp.sum(exp_scores, -1, keepdims=True)


def attend_kernel(info_ref, proj_ref, cos_ref, sin_ref, query_ref, key_ref, value_ref, out_ref):
    local_dim = out_ref.shape[1]
    cosine, sine = cos_ref[...], sin_ref[...]
    for start in range(0, local_dim, HD):
        cols = slice(start, start + HD)
        query = turn(proj_ref[:, start : start + HD], cosine, sine).astype(jnp.bfloat16)
        key_at = local_dim + start
        key = turn(proj_ref[:, key_at : key_at + HD], cosine, sine).astype(jnp.bfloat16)
        value_at = 2 * local_dim + start
        value = proj_ref[:, value_at : value_at + HD].astype(jnp.bfloat16)
        soft = soft_rows(info_ref, query, key).astype(jnp.bfloat16)
        query_ref[:, cols] = query
        key_ref[:, cols] = key
        value_ref[:, cols] = value
        out_ref[:, cols] = dot_nn(soft, value).astype(jnp.bfloat16)


def attend_back_kernel(
    info_ref, query_ref, key_ref, value_ref, grad_ref, cos_ref, sin_ref, out_ref
):
    local_dim = grad_ref.shape[1]
    cosine, sine = cos_ref[...], sin_ref[...]
    scale = HD ** (-0.5)
    for start in range(0, local_dim, HD):
        cols = slice(start, start + HD)
        query, key, value = query_ref[:, cols], key_ref[:, cols], value_ref[:, cols]
        grad = grad_ref[:, cols]
        soft = soft_rows(info_ref, query, key)
        grad_soft = dot_nt(grad, value)
        row_dot = jnp.sum(soft * grad_soft, -1, keepdims=True)
        grad_scores = (soft * (grad_soft - row_dot)).astype(jnp.bfloat16)
        value_grad = dot_tn(soft.astype(jnp.bfloat16), grad)
        query_grad = turn(dot_nn(grad_scores, key) * scale, cosine, -sine)
        key_grad = turn(dot_tn(grad_scores, query) * scale, cosine, -sine)
        for index, rows in enumerate((query_grad, key_grad, value_grad)):
            at = index * local_dim + start
            out_ref[:, at : at + HD] = rows.astype(jnp.bfloat16)


def attend_forward(info, proj, cosine, sine):
    seq_len, width = proj.shape
    low = jax.ShapeDtypeStruct((seq_len, width // 3), jnp.bfloat16)
    vmem = pl.BlockSpec(memory_space=pltpu.VMEM)
    return pl.pallas_call(
        attend_kernel,
        out_shape=(low, low, low, low),
        in_specs=[pl.BlockSpec(memory_space=pltpu.SMEM), vmem, vmem, vmem],
        out_specs=(vmem, vmem, vmem, vmem),
        name="attend_forward",
    )(info, proj, cosine, sine)


def attend_backward(info, query, key, value, grad, cosine, sine):
    seq_len, local_dim = query.shape
    vmem = pl.BlockSpec(memory_space=pltpu.VMEM)
    return pl.pallas_call(
        attend_back_kernel,
        out_shape=jax.ShapeDtypeStruct((seq_len, 3 * local_dim), jnp.bfloat16),
        in_specs=[pl.BlockSpec(memory_space=pltpu.SMEM)] + [vmem] * 6,
        out_specs=vmem,
        name="attend_backward",
    )(info, query, key, value, grad, cosine, sine)


def norm_forward(hidden, norm_gain, norm_bias):
    row_mean = jnp.mean(hidden, -1, keepdims=True)
    centred = hidden - row_mean
    variance = jnp.mean(centred * centred, -1, keepdims=True)
    inv_std = lax.rsqrt(variance + norm_eps)
    normed = centred * inv_std
    return (normed * norm_gain + norm_bias, normed, inv_std)


def norm_backward(grad_rows, normed, inv_std, norm_gain):
    grad_normed = grad_rows * norm_gain
    mean_grad = jnp.mean(grad_normed, -1, keepdims=True)
    mean_proj = jnp.mean(grad_normed * normed, -1, keepdims=True)
    grad_in = inv_std * (grad_normed - mean_grad - normed * mean_proj)
    return (grad_in, jnp.sum(grad_rows * normed, 0), jnp.sum(grad_rows, 0))


def adamw(weight, gradient, first_moment, second, step_rate):
    first_new = beta_one * first_moment + (1.0 - beta_one) * gradient
    second_new = beta_two * second + (1.0 - beta_two) * gradient * gradient
    first_hat = first_new / (1.0 - beta_one**STEP)
    second_hat = second_new / (1.0 - beta_two**STEP)
    weight_new = weight - step_rate * (
        first_hat / (jnp.sqrt(second_hat) + adam_eps) + decay_rate * weight
    )
    return (weight_new, first_new, second_new)


def swap(values, axis, bit):
    size = lax.axis_size(axis)
    return lax.ppermute(values, axis, [(at, at ^ bit) for at in range(size)])


def sum_everywhere(values):
    for axis in ("mp", "dp"):
        bit = 1
        while bit < lax.axis_size(axis):
            values = values + swap(values, axis, bit)
            bit *= 2
    return values


def gather_near(rows):
    half = rows.shape[0] // 2
    near_x, near_y = swap(rows, "mp", 2), swap(rows, "mp", 4)
    far_low, far_high = swap(near_x[:half], "mp", 4), swap(near_y[half:], "mp", 2)
    mates = [swap(part, "mp", 1) for part in (rows, near_x, near_y, far_low, far_high)]
    return [
        jnp.concatenate(parts, 0)
        for parts in (
            (rows, mates[0]),
            (near_x, mates[1]),
            (near_y, mates[2]),
            (far_low, far_high, mates[3], mates[4]),
        )
    ]


def scatter_near(parts):
    own_rows = parts[0].shape[0] // 2
    half = own_rows // 2
    sums = [
        part[:own_rows].astype(jnp.float32)
        + swap(part[own_rows:].astype(jnp.bfloat16), "mp", 1).astype(jnp.float32)
        for part in parts
    ]
    far = sums[3].astype(jnp.bfloat16)
    far_low, far_high = swap(far[:half], "mp", 4), swap(far[half:], "mp", 2)
    x_low = (sums[1][:half] + far_low.astype(jnp.float32)).astype(jnp.bfloat16)
    y_high = (sums[2][half:] + far_high.astype(jnp.float32)).astype(jnp.bfloat16)
    x_high, y_low = sums[1][half:].astype(jnp.bfloat16), sums[2][:half].astype(jnp.bfloat16)
    x_low, x_high = swap(x_low, "mp", 2), swap(x_high, "mp", 2)
    y_low, y_high = swap(y_low, "mp", 4), swap(y_high, "mp", 4)
    across_x = jnp.concatenate([x_low, x_high], 0).astype(jnp.float32)
    across_y = jnp.concatenate([y_low, y_high], 0).astype(jnp.float32)
    return sums[0] + across_x + across_y


def gather_all(rows, seq_count):
    whole = lax.all_gather(rows, "mp", axis=0, tiled=True)
    return jnp.split(whole, seq_count, 0)


def scatter_all(parts):
    whole = jnp.concatenate(parts, 0).astype(jnp.bfloat16)
    return lax.psum_scatter(whole, "mp", scatter_dimension=0, tiled=True).astype(jnp.float32)


def local(
    block_input,
    out_cotangent,
    objective,
    prefix_len,
    target_mask,
    qkv_weight,
    out_weight,
    gateup_weight,
    down_weight,
    norm_params,
    qkv_first,
    out_first,
    gateup_first,
    down_first,
    norm_first,
    qkv_second,
    out_second,
    gateup_second,
    down_second,
    norm_second,
):
    mp_index = lax.axis_index("mp")
    own_rows = block_input.shape[0]
    seq_count = objective.shape[0]
    seq_len = own_rows * lax.axis_size("mp") // seq_count
    shard_rows, _, local_dim = qkv_weight.shape
    local_units = gateup_weight.shape[2]
    seqs = range(seq_count)
    near = lax.axis_size("mp") == 8 and seq_count == 4 and own_rows % 32 == 0
    if near:
        gather_rows, scatter_rows = gather_near, scatter_near
        flip = (mp_index % 2) * own_rows
        seq_at = [(mp_index // 2) ^ seq for seq in seqs]
    else:
        gather_rows = functools.partial(gather_all, seq_count=seq_count)
        scatter_rows = scatter_all
        flip = jnp.zeros((), jnp.int32)
        seq_at = list(seqs)
    infos = [
        jnp.stack([objective[at], prefix_len[at], flip.astype(jnp.int32)]) for at in seq_at
    ]
    cosine, sine = rope_tables(jnp.arange(seq_len, dtype=jnp.int32) ^ flip, HD)

    qkv_low = qkv_weight.astype(jnp.bfloat16).reshape(shard_rows, 3 * local_dim)
    qkv_full = lax.all_gather(qkv_low, "dp", axis=0, tiled=True)
    out_full = lax.all_gather(out_weight.astype(jnp.bfloat16), "dp", axis=1, tiled=True)
    gateup_full = lax.all_gather(gateup_weight.astype(jnp.bfloat16), "dp", axis=0, tiled=True)
    down_full = lax.all_gather(down_weight.astype(jnp.bfloat16), "dp", axis=1, tiled=True)

    mask_f32 = target_mask.astype(jnp.float32)
    target_count = sum_everywhere(jnp.full((8, 128), jnp.sum(mask_f32)))[0, 0]

    inputs = gather_rows(block_input)
    attended, kept = [], []
    for seq in seqs:
        proj = jnp.dot(inputs[seq], qkv_full, preferred_element_type=jnp.float32)
        query, key, value, out = attend_forward(infos[seq], proj, cosine, sine)
        kept.append((query, key, value))
        attended.append(out)
    attn_own = scatter_rows(
        [jnp.dot(rows, out_full, preferred_element_type=jnp.bfloat16) for rows in attended]
    )
    hidden_one = deep_alpha * block_input.astype(jnp.float32) + attn_own
    middle, normed_one, inv_one = norm_forward(hidden_one, norm_params[0], norm_params[1])
    middles = gather_rows(middle.astype(jnp.bfloat16))

    live_units = (mp_index * local_units + jnp.arange(local_units) < FF).astype(jnp.float32)
    gate_ups = [
        jnp.einsum("td,dcf->tcf", rows, gateup_full, preferred_element_type=jnp.float32)
        for rows in middles
    ]
    hiddens = [
        (jax.nn.gelu(gate_up[:, 0]) * gate_up[:, 1] * live_units).astype(jnp.bfloat16)
        for gate_up in gate_ups
    ]
    ffn_own = scatter_rows(
        [jnp.dot(rows, down_full, preferred_element_type=jnp.bfloat16) for rows in hiddens]
    )
    hidden_two = deep_alpha * middle + ffn_own
    output_rows, normed_two, inv_two = norm_forward(hidden_two, norm_params[2], norm_params[3])
    grad_rows = out_cotangent.astype(jnp.float32) * mask_f32[:, None]
    grad_two, gain_two, bias_two = norm_backward(grad_rows, normed_two, inv_two, norm_params[2])

    ffn_backs = gather_rows(grad_two.astype(jnp.bfloat16))
    grad_gateups, middle_parts = [], []
    for seq in seqs:
        gate_act, gelu_pull = jax.vjp(jax.nn.gelu, gate_ups[seq][:, 0])
        grad_hidden = (
            jnp.einsum("td,fd->tf", ffn_backs[seq], down_full, preferred_element_type=jnp.float32)
            * live_units
        )
        grad_gate = gelu_pull(grad_hidden * gate_ups[seq][:, 1])[0]
        grad_up = grad_hidden * gate_act
        grad_gateup = jnp.stack([grad_gate, grad_up], 1).astype(jnp.bfloat16)
        grad_gateups.append(grad_gateup)
        middle_parts.append(
            jnp.einsum(
                "tcf,dcf->td", grad_gateup, gateup_full, preferred_element_type=jnp.bfloat16
            )
        )
    ffn_back_all = jnp.concatenate(ffn_backs, 0)
    down_grad = jnp.einsum(
        "tf,td->fd", jnp.concatenate(hiddens, 0), ffn_back_all, preferred_element_type=jnp.bfloat16
    )
    gateup_grad = jnp.einsum(
        "td,tcf->dcf",
        jnp.concatenate(middles, 0),
        jnp.concatenate(grad_gateups, 0),
        preferred_element_type=jnp.bfloat16,
    )
    grad_middle = scatter_rows(middle_parts) + deep_alpha * grad_two
    grad_one, gain_one, bias_one = norm_backward(grad_middle, normed_one, inv_one, norm_params[0])

    attn_backs = gather_rows(grad_one.astype(jnp.bfloat16))
    grad_projs = []
    for seq in seqs:
        grad_attended = jnp.einsum(
            "td,ed->te", attn_backs[seq], out_full, preferred_element_type=jnp.float32
        ).astype(jnp.bfloat16)
        grad_projs.append(attend_backward(infos[seq], *kept[seq], grad_attended, cosine, sine))
    out_grad = jnp.einsum(
        "te,td->ed",
        jnp.concatenate(attended, 0),
        jnp.concatenate(attn_backs, 0),
        preferred_element_type=jnp.bfloat16,
    )
    qkv_grad = jnp.einsum(
        "td,te->de",
        jnp.concatenate(inputs, 0),
        jnp.concatenate(grad_projs, 0),
        preferred_element_type=jnp.bfloat16,
    )
    input_raw = (
        scatter_rows(
            [
                jnp.einsum("te,de->td", rows, qkv_full, preferred_element_type=jnp.bfloat16)
                for rows in grad_projs
            ]
        )
        + deep_alpha * grad_one
    )
    qkv_grad, out_grad, gateup_grad, down_grad = (
        lax.psum_scatter(qkv_grad, "dp", scatter_dimension=0, tiled=True)
        .astype(jnp.float32)
        .reshape(qkv_weight.shape),
        lax.psum_scatter(out_grad, "dp", scatter_dimension=1, tiled=True).astype(jnp.float32),
        lax.psum_scatter(gateup_grad, "dp", scatter_dimension=0, tiled=True).astype(jnp.float32),
        lax.psum_scatter(down_grad, "dp", scatter_dimension=1, tiled=True).astype(jnp.float32),
    )
    norm_grad = sum_everywhere(jnp.stack([gain_one, bias_one, gain_two, bias_two], 0))
    rate_list = (D ** (-0.5), 0.5, D ** (-0.5), (FF_PAD // 64) ** (-0.5), 0.4)
    qkv_res = adamw(qkv_weight, qkv_grad / target_count, qkv_first, qkv_second, rate_list[0])
    out_res = adamw(out_weight, out_grad / target_count, out_first, out_second, rate_list[1])
    gateup_res = adamw(
        gateup_weight, gateup_grad / target_count, gateup_first, gateup_second, rate_list[2]
    )
    down_res = adamw(down_weight, down_grad / target_count, down_first, down_second, rate_list[3])
    norm_res = adamw(norm_params, norm_grad / target_count, norm_first, norm_second, rate_list[4])
    return (
        output_rows.astype(jnp.bfloat16),
        input_raw / target_count,
        qkv_res[0],
        qkv_res[1],
        qkv_res[2],
        out_res[0],
        out_res[1],
        out_res[2],
        gateup_res[0],
        gateup_res[1],
        gateup_res[2],
        down_res[0],
        down_res[1],
        down_res[2],
        norm_res[0],
        norm_res[1],
        norm_res[2],
    )


def solution(mesh):
    return jax.shard_map(
        local,
        mesh=mesh,
        in_specs=(
            P(("dp", "mp"), None),
            P(("dp", "mp"), None),
            P("dp"),
            P("dp"),
            P(("dp", "mp")),
            P("dp", None, "mp"),
            P("mp", "dp"),
            P("dp", None, "mp"),
            P("mp", "dp"),
            P(),
            P("dp", None, "mp"),
            P("mp", "dp"),
            P("dp", None, "mp"),
            P("mp", "dp"),
            P(),
            P("dp", None, "mp"),
            P("mp", "dp"),
            P("dp", None, "mp"),
            P("mp", "dp"),
            P(),
        ),
        out_specs=(
            P(("dp", "mp"), None),
            P(("dp", "mp"), None),
            P("dp", None, "mp"),
            P("dp", None, "mp"),
            P("dp", None, "mp"),
            P("mp", "dp"),
            P("mp", "dp"),
            P("mp", "dp"),
            P("dp", None, "mp"),
            P("dp", None, "mp"),
            P("dp", None, "mp"),
            P("mp", "dp"),
            P("mp", "dp"),
            P("mp", "dp"),
            P(),
            P(),
            P(),
        ),
        check_vma=False,
    )
```

time: 1290 us -> 755 us (0.59)
  waiting for transfers between devices: 855 us -> 276 us
  starting transfers between devices: 1.2 us -> 66.4 us
  blocking collectives: 41.8 us -> 0 us
  Pallas kernels: 0 us -> 37.9 us
  local copies, waits for them, and re-layouts: 79.8 us -> 111 us
  other arithmetic: 105 us -> 78.5 us
  matrix products: 182 us -> 156 us
    psum x2 -> x0, waiting for transfers between devices: 336 us -> none  [the longest x1 212 us: local(): attn_total = lax.psum(attn_part, 'mp')]
    reduce_scatter x6 -> x4, waiting for transfers between devices: 225 us -> 13.4 us  [the longest x1 13.4 us: local(): lax.psum_scatter(gateup_grad, 'dp', scatter_dimension=0, tiled=True)]
    ppermute x0 -> x86, waiting for transfers between devices: none -> 206 us  [swap(): return lax.ppermute(values, axis, [(at, at ^ bit) for at in range(size)])]
    all_gather x4 -> x1, waiting for transfers between devices: 194 us -> 23.1 us  [local(): qkv_full = lax.all_gather(qkv_low, 'dp', axis=0, tiled=True)]
    all_gather x1, waiting for transfers between devices: 69.6 us -> 0.01 us  [local(): lax.all_gather(gateup_weight.astype(jnp.bfloat16), 'dp', axis=0, tiled=True)]
    ppermute x0 -> x86, starting transfers between devices: none -> 65.7 us  [swap(): return lax.ppermute(values, axis, [(at, at ^ bit) for at in range(size)])]
    psum x1 -> x0, blocking collectives: 41.8 us -> none  [local(): lax.psum((norm_grad, jnp.sum(mask_f32)), ('dp', 'mp'))]
    unnamed x112 -> x218, local copies, waits for them, and re-layouts: 47.4 us -> 86.3 us
  transfers between devices with their start and end apart: 15 -> 94, of which waited for: 13 -> 40; matrix products, arithmetic and copies ran while one was open for 21% -> 41% of each run, Pallas kernels for 0% -> 5%
where the time goes in v1:
time: 755 us; the launch traced here: 743 us
  waiting for transfers between devices  276 us (37%)
  matrix products  156 us (21%)
  local copies, waits for them, and re-layouts  111 us (15%)
  other arithmetic  78.5 us (10%)
  starting transfers between devices  66.4 us (9%)
  Pallas kernels  37.9 us (5%)
  between operations  16.3 us (2%)
    ppermute x86, waiting for transfers between devices, swap(): return lax.ppermute(values, axis, [(at, at ^ bit) for at in range(size)])  206 us
    unnamed x218, local copies, waits for them, and re-layouts  86.3 us
    ppermute x86, starting transfers between devices, swap(): return lax.ppermute(values, axis, [(at, at ^ bit) for at in range(size)])  65.7 us
    dot_general x4, matrix products, local(): jnp.einsum('td,dcf->tcf', rows, gateup_full, preferred_element_type=jnp.f...  28 us
    all_gather x1, waiting for transfers between devices, local(): qkv_full = lax.all_gather(qkv_low, 'dp', axis=0, tiled=True)  23.1 us
    sub x5, other arithmetic, adamw(): weight - step_rate * (first_hat / (jnp.sqrt(second_hat) + adam_eps) + dec...  21.5 us
    pallas_call x4, Pallas kernels, attend_backward(): pl.pallas_call(attend_back_kernel, out_shape=jax.ShapeDtypeStruct((seq_le...  20.7 us
    all_gather x1, waiting for transfers between devices, local(): lax.all_gather(out_weight.astype(jnp.bfloat16), 'dp', axis=1, tiled=True)  19.5 us
  transfers between devices with their start and end apart: 94, of which 40 were waited for; matrix products, arithmetic and copies ran while one was open for 41% of the time, Pallas kernels for 5%

profile of v1, /device:TPU:0, one launch (start us, length us, event | category | flops | bytes accessed | tf_op | source)
XLA Modules:
  0.0 742.6 jit_solution(15993183401262082844)
XLA Ops:
  21.6 16.0 %collective-permute-done.2 = bf16[256,2048]{1,0:T(8,128)(2,1)S(1)} collective-permute-done((bf16[256,2048]{1,0:T(8,128)(2,1)S(1)}, bf16[256,2048]{1,0:T(8,128)(2,1)S(1)}, u32[]{:S(2)}, u32[]{:S(2)}) %collective-permute-start.2) | collective-permute-done | bytes 1048608 | tf_op jit(solution)/shard_map/ppermute | solution.py:162
  53.4 23.1 %all-gather.5.cloned.1.call-done = bf16[2048,768]{0,1:T(8,128)(2,1)} async-done(((bf16[512,768]{0,1:T(8,128)(2,1)}), bf16[2048,768]{0,1:T(8,128)(2,1)}) %all-gather.5.cloned.1.call-update) | async-done | bytes 3145744 | tf_op jit(solution)/shard_map/all_gather | solution.py:265
  76.5 5.2 fusion.34.proj_ref
  85.8 19.5 %all-gather.7.cloned.1.call-done = bf16[256,2048]{1,0:T(8,128)(2,1)} async-done(((bf16[256,512]{1,0:T(8,128)(2,1)}), bf16[256,2048]{1,0:T(8,128)(2,1)}) %all-gather.7.cloned.1.call-update) | async-done | bytes 1048592 | tf_op jit(solution)/shard_map/all_gather | solution.py:266
  112.9 4.4 attend_forward.5
  122.1 4.5 fusion.42.proj_ref
  126.6 4.5 attend_forward.6
  134.0 4.5 fusion.50.proj_ref
  138.5 4.1 attend_forward.7
  153.2 11.7 %collective-permute-done.11 = bf16[128,2048]{1,0:T(8,128)(2,1)S(1)} collective-permute-done((bf16[128,2048]{1,0:T(8,128)(2,1)S(1)}, bf16[128,2048]{1,0:T(8,128)(2,1)S(1)}, u32[]{:S(2)}, u32[]{:S(2)}) %collective-permute-start.11) | collective-permute-done | bytes 524320 | tf_op jit(solution)/shard_map/ppermute | solution.py:162
  165.7 7.2 collective-permute-done.17
  175.8 7.3 collective-permute-done.12
  192.4 21.8 %collective-permute-done.25 = bf16[256,2048]{1,0:T(8,128)(2,1)S(1)} collective-permute-done((bf16[256,2048]{1,0:T(8,128)(2,1)}, bf16[256,2048]{1,0:T(8,128)(2,1)S(1)}, u32[]{:S(2)}, u32[]{:S(2)}) %collective-permute-start.25) | collective-permute-done | bytes 1048608 | tf_op jit(solution)/shard_map/ppermute | solution.py:162
  220.8 6.9 collective-permute-done.26
  229.6 9.1 %fusion.54 = f32[512,2,684]{0,2,1:T(8,128)S(1)} fusion(bf16[256,2048]{1,0:T(8,128)(2,1)} %collective-permute-done.19, bf16[256,2048]{1,0:T(8,128)(2,1)} %get-tuple-element.120, bf16[2048,2,684]{0,1,2:T(2,128)(2,1)} %all-gather.9.cloned.1.call-done), kind=kOutput, calls=%fused_computation.67 | convolution fusion | flops 2873098240 | bytes 10502144 | tf_op jit(solution)/shard_map/td,dcf->tcf/dot_general | solution.py:289
  238.8 6.2 fusion.67
  245.0 6.0 fusion.57
  251.0 6.8 fusion.60
  262.9 14.5 %all-gather.11.cloned.1.call-done = bf16[684,2048]{1,0:T(8,128)(2,1)} async-done(((bf16[684,512]{1,0:T(8,128)(2,1)}), bf16[684,2048]{1,0:T(8,128)(2,1)}) %all-gather.11.cloned.1.call-update) | async-done | bytes 2801680 | tf_op jit(solution)/shard_map/all_gather | solution.py:268
  296.2 11.7 %collective-permute-done.30 = bf16[128,2048]{1,0:T(8,128)(2,1)S(1)} collective-permute-done((bf16[128,2048]{1,0:T(8,128)(2,1)S(1)}, bf16[128,2048]{1,0:T(8,128)(2,1)S(1)}, u32[]{:S(2)}, u32[]{:S(2)}) %collective-permute-start.30) | collective-permute-done | bytes 524320 | tf_op jit(solution)/shard_map/ppermute | solution.py:162
  308.6 8.5 %collective-permute-done.36 = bf16[128,2048]{1,0:T(8,128)(2,1)S(1)} collective-permute-done((bf16[128,2048]{1,0:T(8,128)(2,1)S(1)}, bf16[128,2048]{1,0:T(8,128)(2,1)S(1)}, u32[]{:S(2)}, u32[]{:S(2)}) %collective-permute-start.36) | collective-permute-done | bytes 524320 | tf_op jit(solution)/shard_map/ppermute | solution.py:162
  318.7 9.1 %collective-permute-done.31 = bf16[128,2048]{1,0:T(8,128)(2,1)S(1)} collective-permute-done((bf16[128,2048]{1,0:T(8,128)(2,1)S(1)}, bf16[128,2048]{1,0:T(8,128)(2,1)S(1)}, u32[]{:S(2)}, u32[]{:S(2)}) %collective-permute-start.31) | collective-permute-done | bytes 524320 | tf_op jit(solution)/shard_map/ppermute | solution.py:162
  344.0 16.0 %collective-permute-done.44 = bf16[256,2048]{1,0:T(8,128)(2,1)S(1)} collective-permute-done((bf16[256,2048]{1,0:T(8,128)(2,1)S(1)}, bf16[256,2048]{1,0:T(8,128)(2,1)S(1)}, u32[]{:S(2)}, u32[]{:S(2)}) %collective-permute-start.44) | collective-permute-done | bytes 1048608 | tf_op jit(solution)/shard_map/ppermute | solution.py:162
  365.8 6.6 collective-permute-done.45
  373.0 4.7 convolution_bitcast_fusion.3
  384.3 4.9 convolution_bitcast_fusion.1
  391.9 4.7 convolution_bitcast_fusion
  396.8 4.5 fusion.210
  401.3 4.7 convolution_bitcast_fusion.2
  417.2 10.1 %collective-permute-done.49 = bf16[128,2048]{1,0:T(8,128)(2,1)S(1)} collective-permute-done((bf16[128,2048]{1,0:T(8,128)(2,1)S(1)}, bf16[128,2048]{1,0:T(8,128)(2,1)S(1)}, u32[]{:S(2)}, u32[]{:S(2)}) %collective-permute-start.49) | collective-permute-done | bytes 524320 | tf_op jit(solution)/shard_map/ppermute | solution.py:162
  429.7 6.7 collective-permute-done.55
  438.7 7.7 %fusion.26 = bf16[684,2048]{1,0:T(8,128)(2,1)} fusion(bf16[2048,2048]{1,0:T(8,128)(2,1)S(1)} %constant_dynamic-update-slice_fusion.30, bf16[512,684]{0,1:T(8,128)(2,1)S(1)} %copy-done.48, bf16[512,684]{0,1:T(8,128)(2,1)S(1)} %copy-done.49, bf16[512,684]{0,1:T(8,128)(2,1)S(1)} %copy-done.47, bf16[512,684]{0,1:T(8,128)(2,1)S(1)} %copy-done.46), kind=kOutput, calls=%fused_computation.28 | convolution fusion | flops 5749014528 | bytes 13991936 | tf_op jit(solution)/shard_map/tf,td->fd/dot_general | solution.py:322
  450.4 5.1 multiply_reduce_fusion.1
  469.7 11.3 %collective-permute-done.59 = bf16[256,2048]{1,0:T(8,128)(2,1)S(1)} collective-permute-done((bf16[256,2048]{1,0:T(8,128)(2,1)S(1)}, bf16[256,2048]{1,0:T(8,128)(2,1)S(1)}, u32[]{:S(2)}, u32[]{:S(2)}) %collective-permute-start.59) | collective-permute-done | bytes 1048608 | tf_op jit(solution)/shard_map/ppermute | solution.py:162
  490.7 5.1 attend_backward.4
  513.8 6.7 fusion.196
  526.7 5.1 attend_backward.7
  531.9 5.1 attend_backward.6
  539.7 5.3 attend_backward.5
  545.0 10.8 %fusion.17 = bf16[2048,768]{1,0:T(8,128)(2,1)} fusion(bf16[2048,2048]{1,0:T(8,128)(2,1)} %constant_dynamic-update-slice_fusion, bf16[512,768]{1,0:T(8,128)(2,1)S(1)} %copy-done.43, bf16[512,768]{1,0:T(8,128)(2,1)S(1)} %copy-done.41, bf16[512,768]{1,0:T(8,128)(2,1)} %attend_backward.5, bf16[512,768]{1,0:T(8,128)(2,1)S(1)} %copy-done.40), kind=kOutput, calls=%fused_computation.19 | convolution fusion | flops 6455033856 | bytes 14680064 | tf_op jit(solution)/shard_map/td,te->de/dot_general | solution.py:347
  573.4 17.4 %fusion = bf16[2048,2,684]{0,2,1:T(8,128)(2,1)} fusion(bf16[2048,2048]{1,0:T(8,128)(2,1)} %constant_dynamic-update-slice_fusion.20, bf16[512,1,684]{0,2,1:T(8,128)(2,1)S(1)} %copy-done.77, bf16[512,1,684]{0,2,1:T(8,128)(2,1)S(1)} %copy-done.75, bf16[512,1,684]{0,2,1:T(8,128)(2,1)S(1)} %copy-done.81, bf16[512,1,684]{0,2,1:T(8,128)(2,1)S(1)} %copy-done.79, ...), kind=kOutput, calls=%fused_computation | convolution fusion | flops 11520442368 | bytes 19595264 | tf_op jit(solution)/shard_map/td,tcf->dcf/dot_general | solution.py:325
  623.7 4.6 fusion.275
  644.5 19.5 %collective-permute-done.74 = bf16[128,2048]{1,0:T(8,128)(2,1)S(1)} collective-permute-done((bf16[128,2048]{1,0:T(8,128)(2,1)S(1)}, bf16[128,2048]{1,0:T(8,128)(2,1)S(1)}, u32[]{:S(2)}, u32[]{:S(2)}) %collective-permute-start.74) | collective-permute-done | bytes 524320 | tf_op jit(solution)/shard_map/ppermute | solution.py:162
  669.0 5.6 multiply_subtract_fusion.2
  680.7 5.0 add_divide_fusion
  691.9 5.4 multiply_subtract_fusion.1
  705.1 13.4 %reduce-scatter.9.cloned.1.call-done = bf16[512,2,684]{0,2,1:T(8,128)(2,1)} async-done(((bf16[2048,2,684]{0,2,1:T(8,128)(2,1)}), bf16[512,2,684]{0,2,1:T(8,128)(2,1)}) %reduce-scatter.9.cloned.1.call-update) | async-done | bytes 1400848 | tf_op jit(solution)/shard_map/reduce_scatter | solution.py:367
  718.5 5.7 multiply_subtract_fusion
  (526 shorter events, 311.8 us)
Async XLA Ops:
  7.2 69.3 %all-gather.5.cloned.1.call-start = ((), (), s32[]{:S(2)}) async-start(), calls=%async_computation.4 | async-start | bytes 3932160 | tf_op jit(solution)/shard_map/all_gather | solution.py:265
  10.2 95.1 %all-gather.7.cloned.1.call-start = ((), (), s32[]{:S(2)}) async-start(), calls=%async_computation.5 | async-start | bytes 1310720 | tf_op jit(solution)/shard_map/all_gather | solution.py:266
  11.3 218.3 %all-gather.9.cloned.1.call-start = ((), (), s32[]{:S(2)}) async-start(), calls=%async_computation.6 | async-start | bytes 7004160 | tf_op jit(solution)/shard_map/all_gather | solution.py:267
  11.4 26.2 %collective-permute-start.2 = (bf16[256,2048]{1,0:T(8,128)(2,1)S(1)}, bf16[256,2048]{1,0:T(8,128)(2,1)S(1)}, u32[]{:S(2)}, u32[]{:S(2)}) collective-permute-start(bf16[256,2048]{1,0:T(8,128)(2,1)S(1)} %copy-done.13), channel_id=1, source_target_pairs={{0,2},{1,3},{2,0},{3,1},{4,6},{5,7},{6,4},{7,5},{8,10},{9,11},{10,... | collective-permute-start | bytes 3145736 | tf_op jit(solution)/shard_map/ppermute | solution.py:162
  14.4 25.0 %collective-permute-start.6 = (bf16[256,2048]{1,0:T(8,128)(2,1)S(1)}, bf16[256,2048]{1,0:T(8,128)(2,1)}, u32[]{:S(2)}, u32[]{:S(2)}) collective-permute-start(bf16[256,2048]{1,0:T(8,128)(2,1)S(1)} %copy-done.13), channel_id=1, source_target_pairs={{0,4},{1,5},{2,6},{3,7},{4,0},{5,1},{6,2},{7,3},{8,12},{9,13},{10,... | collective-permute-start | bytes 3145736 | tf_op jit(solution)/shard_map/ppermute | solution.py:162
  16.0 37.4 %collective-permute-start = (bf16[256,2048]{1,0:T(8,128)(2,1)S(1)}, bf16[256,2048]{1,0:T(8,128)(2,1)}, u32[]{:S(2)}, u32[]{:S(2)}) collective-permute-start(bf16[256,2048]{1,0:T(8,128)(2,1)S(1)} %copy-done.13), channel_id=1, source_target_pairs={{0,1},{1,0},{2,3},{3,2},{4,5},{5,4},{6,7},{7,6},{8,9},{9,8},{10,11... | collective-permute-start | bytes 3145736 | tf_op jit(solution)/shard_map/ppermute | solution.py:162
  19.8 257.6 %all-gather.11.cloned.1.call-start = ((), (), s32[]{:S(2)}) async-start(), calls=%async_computation.7 | async-start | bytes 3522560 | tf_op jit(solution)/shard_map/all_gather | solution.py:268
  46.0 63.9 %collective-permute-start.3 = (bf16[256,2048]{1,0:T(8,128)(2,1)S(1)}, bf16[256,2048]{1,0:T(8,128)(2,1)S(1)}, u32[]{:S(2)}, u32[]{:S(2)}) collective-permute-start(bf16[256,2048]{1,0:T(8,128)(2,1)S(1)} %collective-permute-done.2), channel_id=1, source_target_pairs={{0,1},{1,0},{2,3},{3,2},{4,5},{5,4},{6,7},{7,6},{8,9},{9,8},{10,11... | collective-permute-start | bytes 3145736 | tf_op jit(solution)/shard_map/ppermute | solution.py:162
  50.7 83.2 %collective-permute-start.14 = (bf16[256,2048]{1,0:T(8,128)(2,1)}, bf16[256,2048]{1,0:T(8,128)(2,1)}, u32[]{:S(2)}, u32[]{:S(2)}) collective-permute-start(bf16[256,2048]{1,0:T(8,128)(2,1)} %collective-permute-done.6), channel_id=1, source_target_pairs={{0,1},{1,0},{2,3},{3,2},{4,5},{5,4},{6,7},{7,6},{8,9},{9,8},{10,11... | collective-permute-start | bytes 3145736 | tf_op jit(solution)/shard_map/ppermute | solution.py:162
  51.3 70.8 %collective-permute-start.8 = (bf16[128,2048]{1,0:T(8,128)(2,1)}, bf16[128,2048]{1,0:T(8,128)(2,1)}, u32[]{:S(2)}, u32[]{:S(2)}) collective-permute-start(bf16[128,2048]{1,0:T(8,128)(2,1)} %collective-permute-done.5), channel_id=1, source_target_pairs={{0,1},{1,0},{2,3},{3,2},{4,5},{5,4},{6,7},{7,6},{8,9},{9,8},{10,11... | collective-permute-start | bytes 1572872 | tf_op jit(solution)/shard_map/ppermute | solution.py:162
  53.4 68.7 %collective-permute-start.9 = (bf16[128,2048]{1,0:T(8,128)(2,1)}, bf16[128,2048]{1,0:T(8,128)(2,1)}, u32[]{:S(2)}, u32[]{:S(2)}) collective-permute-start(bf16[128,2048]{1,0:T(8,128)(2,1)} %collective-permute-done.7), channel_id=1, source_target_pairs={{0,1},{1,0},{2,3},{3,2},{4,5},{5,4},{6,7},{7,6},{8,9},{9,8},{10,11... | collective-permute-start | bytes 1572872 | tf_op jit(solution)/shard_map/ppermute | solution.py:162
  109.9 64.7 %collective-permute-start.1 = (bf16[256,2048]{1,0:T(8,128)(2,1)}, bf16[256,2048]{1,0:T(8,128)(2,1)}, u32[]{:S(2)}, u32[]{:S(2)}) collective-permute-start(bf16[256,2048]{1,0:T(8,128)(2,1)} %slice.327), channel_id=1, source_target_pairs={{0,1},{1,0},{2,3},{3,2},{4,5},{5,4},{6,7},{7,6},{8,9},{9,8},{10,11... | collective-permute-start | bytes 3145736 | tf_op jit(solution)/shard_map/ppermute | solution.py:162
  121.5 23.6 %collective-permute-start.4 = (bf16[256,2048]{1,0:T(8,128)(2,1)}, bf16[256,2048]{1,0:T(8,128)(2,1)}, u32[]{:S(2)}, u32[]{:S(2)}) collective-permute-start(bf16[256,2048]{1,0:T(8,128)(2,1)} %slice.329), channel_id=1, source_target_pairs={{0,1},{1,0},{2,3},{3,2},{4,5},{5,4},{6,7},{7,6},{8,9},{9,8},{10,11... | collective-permute-start | bytes 3145736 | tf_op jit(solution)/shard_map/ppermute | solution.py:162
  146.8 27.8 %collective-permute-start.13 = (bf16[128,2048]{1,0:T(8,128)(2,1)S(1)}, bf16[128,2048]{1,0:T(8,128)(2,1)S(1)}, u32[]{:S(2)}, u32[]{:S(2)}) collective-permute-start(bf16[128,2048]{1,0:T(8,128)(2,1)S(1)} %slice.549), channel_id=1, source_target_pairs={{0,2},{1,3},{2,0},{3,1},{4,6},{5,7},{6,4},{7,5},{8,10},{9,11},{10,... | collective-permute-start | bytes 1572872 | tf_op jit(solution)/shard_map/ppermute | solution.py:162
  151.6 21.3 %collective-permute-start.17 = (bf16[128,2048]{1,0:T(8,128)(2,1)S(1)}, bf16[128,2048]{1,0:T(8,128)(2,1)S(1)}, u32[]{:S(2)}, u32[]{:S(2)}) collective-permute-start(bf16[128,2048]{1,0:T(8,128)(2,1)S(1)} %get-tuple-element.151), channel_id=1, source_target_pairs={{0,2},{1,3},{2,0},{3,1},{4,6},{5,7},{6,4},{7,5},{8,10},{9,11},{10,... | collective-permute-start | bytes 1572872 | tf_op jit(solution)/shard_map/ppermute | solution.py:162
  152.6 23.2 %collective-permute-start.16 = (bf16[128,2048]{1,0:T(8,128)(2,1)S(1)}, bf16[128,2048]{1,0:T(8,128)(2,1)S(1)}, u32[]{:S(2)}, u32[]{:S(2)}) collective-permute-start(bf16[128,2048]{1,0:T(8,128)(2,1)S(1)} %slice.548), channel_id=1, source_target_pairs={{0,4},{1,5},{2,6},{3,7},{4,0},{5,1},{6,2},{7,3},{8,12},{9,13},{10,... | collective-permute-start | bytes 1572872 | tf_op jit(solution)/shard_map/ppermute | solution.py:162
  190.4 23.8 %collective-permute-start.25 = (bf16[256,2048]{1,0:T(8,128)(2,1)}, bf16[256,2048]{1,0:T(8,128)(2,1)S(1)}, u32[]{:S(2)}, u32[]{:S(2)}) collective-permute-start(bf16[256,2048]{1,0:T(8,128)(2,1)} %get-tuple-element.120), channel_id=1, source_target_pairs={{0,4},{1,5},{2,6},{3,7},{4,0},{5,1},{6,2},{7,3},{8,12},{9,13},{10,... | collective-permute-start | bytes 3145736 | tf_op jit(solution)/shard_map/ppermute | solution.py:162
  191.9 24.1 %collective-permute-start.21 = (bf16[256,2048]{1,0:T(8,128)(2,1)}, bf16[256,2048]{1,0:T(8,128)(2,1)S(1)}, u32[]{:S(2)}, u32[]{:S(2)}) collective-permute-start(bf16[256,2048]{1,0:T(8,128)(2,1)} %get-tuple-element.120), channel_id=1, source_target_pairs={{0,2},{1,3},{2,0},{3,1},{4,6},{5,7},{6,4},{7,5},{8,10},{9,11},{10,... | collective-permute-start | bytes 3145736 | tf_op jit(solution)/shard_map/ppermute | solution.py:162
  192.4 37.2 %collective-permute-start.19 = (bf16[256,2048]{1,0:T(8,128)(2,1)}, bf16[256,2048]{1,0:T(8,128)(2,1)}, u32[]{:S(2)}, u32[]{:S(2)}) collective-permute-start(bf16[256,2048]{1,0:T(8,128)(2,1)} %get-tuple-element.120), channel_id=1, source_target_pairs={{0,1},{1,0},{2,3},{3,2},{4,5},{5,4},{6,7},{7,6},{8,9},{9,8},{10,11... | collective-permute-start | bytes 3145736 | tf_op jit(solution)/shard_map/ppermute | solution.py:162
  220.2 448.8 %reduce-scatter.11.cloned.1.call-start = ((), (), s32[]{:S(2)}) async-start(), calls=%async_computation.11 | async-start | bytes 3522560 | tf_op jit(solution)/shard_map/reduce_scatter | solution.py:368
  220.4 24.6 %collective-permute-start.22 = (bf16[256,2048]{1,0:T(8,128)(2,1)}, bf16[256,2048]{1,0:T(8,128)(2,1)}, u32[]{:S(2)}, u32[]{:S(2)}) collective-permute-start(bf16[256,2048]{1,0:T(8,128)(2,1)} %copy-done.27), channel_id=1, source_target_pairs={{0,1},{1,0},{2,3},{3,2},{4,5},{5,4},{6,7},{7,6},{8,9},{9,8},{10,11... | collective-permute-start | bytes 3145736 | tf_op jit(solution)/shard_map/ppermute | solution.py:162
  227.8 23.2 %collective-permute-start.28 = (bf16[128,2048]{1,0:T(8,128)(2,1)}, bf16[128,2048]{1,0:T(8,128)(2,1)}, u32[]{:S(2)}, u32[]{:S(2)}) collective-permute-start(bf16[128,2048]{1,0:T(8,128)(2,1)} %collective-permute-done.26), channel_id=1, source_target_pairs={{0,1},{1,0},{2,3},{3,2},{4,5},{5,4},{6,7},{7,6},{8,9},{9,8},{10,11... | collective-permute-start | bytes 1572872 | tf_op jit(solution)/shard_map/ppermute | solution.py:162
  229.6 21.4 %collective-permute-start.27 = (bf16[128,2048]{1,0:T(8,128)(2,1)}, bf16[128,2048]{1,0:T(8,128)(2,1)}, u32[]{:S(2)}, u32[]{:S(2)}) collective-permute-start(bf16[128,2048]{1,0:T(8,128)(2,1)} %collective-permute-done.24), channel_id=1, source_target_pairs={{0,1},{1,0},{2,3},{3,2},{4,5},{5,4},{6,7},{7,6},{8,9},{9,8},{10,11... | collective-permute-start | bytes 1572872 | tf_op jit(solution)/shard_map/ppermute | solution.py:162
  287.5 31.2 %collective-permute-start.20 = (bf16[256,2048]{1,0:T(8,128)(2,1)S(1)}, bf16[256,2048]{1,0:T(8,128)(2,1)S(1)}, u32[]{:S(2)}, u32[]{:S(2)}) collective-permute-start(bf16[256,2048]{1,0:T(8,128)(2,1)S(1)} %slice.345), channel_id=1, source_target_pairs={{0,1},{1,0},{2,3},{3,2},{4,5},{5,4},{6,7},{7,6},{8,9},{9,8},{10,11... | collective-permute-start | bytes 3145736 | tf_op jit(solution)/shard_map/ppermute | solution.py:162
  290.9 27.8 %collective-permute-start.32 = (bf16[128,2048]{1,0:T(8,128)(2,1)S(1)}, bf16[128,2048]{1,0:T(8,128)(2,1)S(1)}, u32[]{:S(2)}, u32[]{:S(2)}) collective-permute-start(bf16[128,2048]{1,0:T(8,128)(2,1)S(1)} %slice.547), channel_id=1, source_target_pairs={{0,2},{1,3},{2,0},{3,1},{4,6},{5,7},{6,4},{7,5},{8,10},{9,11},{10,... | collective-permute-start | bytes 1572872 | tf_op jit(solution)/shard_map/ppermute | solution.py:162
  294.5 22.5 %collective-permute-start.36 = (bf16[128,2048]{1,0:T(8,128)(2,1)S(1)}, bf16[128,2048]{1,0:T(8,128)(2,1)S(1)}, u32[]{:S(2)}, u32[]{:S(2)}) collective-permute-start(bf16[128,2048]{1,0:T(8,128)(2,1)S(1)} %get-tuple-element.149), channel_id=1, source_target_pairs={{0,2},{1,3},{2,0},{3,1},{4,6},{5,7},{6,4},{7,5},{8,10},{9,11},{10,... | collective-permute-start | bytes 1572872 | tf_op jit(solution)/shard_map/ppermute | solution.py:162
  295.5 23.2 %collective-permute-start.35 = (bf16[128,2048]{1,0:T(8,128)(2,1)S(1)}, bf16[128,2048]{1,0:T(8,128)(2,1)S(1)}, u32[]{:S(2)}, u32[]{:S(2)}) collective-permute-start(bf16[128,2048]{1,0:T(8,128)(2,1)S(1)} %slice.546), channel_id=1, source_target_pairs={{0,4},{1,5},{2,6},{3,7},{4,0},{5,1},{6,2},{7,3},{8,12},{9,13},{10,... | collective-permute-start | bytes 1572872 | tf_op jit(solution)/shard_map/ppermute | solution.py:162
  308.0 19.8 %collective-permute-start.31 = (bf16[128,2048]{1,0:T(8,128)(2,1)S(1)}, bf16[128,2048]{1,0:T(8,128)(2,1)S(1)}, u32[]{:S(2)}, u32[]{:S(2)}) collective-permute-start(bf16[128,2048]{1,0:T(8,128)(2,1)S(1)} %fusion.193), channel_id=1, source_target_pairs={{0,2},{1,3},{2,0},{3,1},{4,6},{5,7},{6,4},{7,5},{8,10},{9,11},{10,... | collective-permute-start | bytes 1572872 | tf_op jit(solution)/shard_map/ppermute | solution.py:162
  336.6 23.4 %collective-permute-start.44 = (bf16[256,2048]{1,0:T(8,128)(2,1)S(1)}, bf16[256,2048]{1,0:T(8,128)(2,1)S(1)}, u32[]{:S(2)}, u32[]{:S(2)}) collective-permute-start(bf16[256,2048]{1,0:T(8,128)(2,1)S(1)} %get-tuple-element.115), channel_id=1, source_target_pairs={{0,4},{1,5},{2,6},{3,7},{4,0},{5,1},{6,2},{7,3},{8,12},{9,13},{10,... | collective-permute-start | bytes 3145736 | tf_op jit(solution)/shard_map/ppermute | solution.py:162
  338.1 24.1 %collective-permute-start.40 = (bf16[256,2048]{1,0:T(8,128)(2,1)S(1)}, bf16[256,2048]{1,0:T(8,128)(2,1)S(1)}, u32[]{:S(2)}, u32[]{:S(2)}) collective-permute-start(bf16[256,2048]{1,0:T(8,128)(2,1)S(1)} %get-tuple-element.115), channel_id=1, source_target_pairs={{0,2},{1,3},{2,0},{3,1},{4,6},{5,7},{6,4},{7,5},{8,10},{9,11},{10,... | collective-permute-start | bytes 3145736 | tf_op jit(solution)/shard_map/ppermute | solution.py:162
  339.6 23.6 %collective-permute-start.38 = (bf16[256,2048]{1,0:T(8,128)(2,1)S(1)}, bf16[256,2048]{1,0:T(8,128)(2,1)S(1)}, u32[]{:S(2)}, u32[]{:S(2)}) collective-permute-start(bf16[256,2048]{1,0:T(8,128)(2,1)S(1)} %get-tuple-element.115), channel_id=1, source_target_pairs={{0,1},{1,0},{2,3},{3,2},{4,5},{5,4},{6,7},{7,6},{8,9},{9,8},{10,11... | collective-permute-start | bytes 3145736 | tf_op jit(solution)/shard_map/ppermute | solution.py:162
  378.8 67.8 %collective-permute-start.39 = (bf16[256,2048]{1,0:T(8,128)(2,1)}, bf16[256,2048]{1,0:T(8,128)(2,1)}, u32[]{:S(2)}, u32[]{:S(2)}) collective-permute-start(bf16[256,2048]{1,0:T(8,128)(2,1)} %slice.367), channel_id=1, source_target_pairs={{0,1},{1,0},{2,3},{3,2},{4,5},{5,4},{6,7},{7,6},{8,9},{9,8},{10,11... | collective-permute-start | bytes 3145736 | tf_op jit(solution)/shard_map/ppermute | solution.py:162
  410.1 36.4 %collective-permute-start.51 = (bf16[128,2048]{1,0:T(8,128)(2,1)}, bf16[128,2048]{1,0:T(8,128)(2,1)}, u32[]{:S(2)}, u32[]{:S(2)}) collective-permute-start(bf16[128,2048]{1,0:T(8,128)(2,1)} %slice.545), channel_id=1, source_target_pairs={{0,2},{1,3},{2,0},{3,1},{4,6},{5,7},{6,4},{7,5},{8,10},{9,11},{10,... | collective-permute-start | bytes 1572872 | tf_op jit(solution)/shard_map/ppermute | solution.py:162
  413.9 22.5 %collective-permute-start.55 = (bf16[128,2048]{1,0:T(8,128)(2,1)S(1)}, bf16[128,2048]{1,0:T(8,128)(2,1)S(1)}, u32[]{:S(2)}, u32[]{:S(2)}) collective-permute-start(bf16[128,2048]{1,0:T(8,128)(2,1)S(1)} %get-tuple-element.147), channel_id=1, source_target_pairs={{0,2},{1,3},{2,0},{3,1},{4,6},{5,7},{6,4},{7,5},{8,10},{9,11},{10,... | collective-permute-start | bytes 1572872 | tf_op jit(solution)/shard_map/ppermute | solution.py:162
  415.8 30.8 %collective-permute-start.54 = (bf16[128,2048]{1,0:T(8,128)(2,1)}, bf16[128,2048]{1,0:T(8,128)(2,1)}, u32[]{:S(2)}, u32[]{:S(2)}) collective-permute-start(bf16[128,2048]{1,0:T(8,128)(2,1)} %slice.544), channel_id=1, source_target_pairs={{0,4},{1,5},{2,6},{3,7},{4,0},{5,1},{6,2},{7,3},{8,12},{9,13},{10,... | collective-permute-start | bytes 1572872 | tf_op jit(solution)/shard_map/ppermute | solution.py:162
  428.2 18.9 %collective-permute-start.50 = (bf16[128,2048]{1,0:T(8,128)(2,1)}, bf16[128,2048]{1,0:T(8,128)(2,1)}, u32[]{:S(2)}, u32[]{:S(2)}) collective-permute-start(bf16[128,2048]{1,0:T(8,128)(2,1)} %fusion.191), channel_id=1, source_target_pairs={{0,2},{1,3},{2,0},{3,1},{4,6},{5,7},{6,4},{7,5},{8,10},{9,11},{10,... | collective-permute-start | bytes 1572872 | tf_op jit(solution)/shard_map/ppermute | solution.py:162
  446.5 228.2 %reduce-scatter.7.cloned.1.call-start = ((), (), s32[]{:S(2)}) async-start(), calls=%async_computation.9 | async-start | bytes 1310720 | tf_op jit(solution)/shard_map/reduce_scatter | solution.py:366
  457.8 23.2 %collective-permute-start.59 = (bf16[256,2048]{1,0:T(8,128)(2,1)S(1)}, bf16[256,2048]{1,0:T(8,128)(2,1)S(1)}, u32[]{:S(2)}, u32[]{:S(2)}) collective-permute-start(bf16[256,2048]{1,0:T(8,128)(2,1)S(1)} %get-tuple-element.125), channel_id=1, source_target_pairs={{0,2},{1,3},{2,0},{3,1},{4,6},{5,7},{6,4},{7,5},{8,10},{9,11},{10,... | collective-permute-start | bytes 3145736 | tf_op jit(solution)/shard_map/ppermute | solution.py:162
  462.7 22.2 %collective-permute-start.63 = (bf16[256,2048]{1,0:T(8,128)(2,1)S(1)}, bf16[256,2048]{1,0:T(8,128)(2,1)S(1)}, u32[]{:S(2)}, u32[]{:S(2)}) collective-permute-start(bf16[256,2048]{1,0:T(8,128)(2,1)S(1)} %get-tuple-element.125), channel_id=1, source_target_pairs={{0,4},{1,5},{2,6},{3,7},{4,0},{5,1},{6,2},{7,3},{8,12},{9,13},{10,... | collective-permute-start | bytes 3145736 | tf_op jit(solution)/shard_map/ppermute | solution.py:162
  463.5 25.7 %collective-permute-start.57 = (bf16[256,2048]{1,0:T(8,128)(2,1)S(1)}, bf16[256,2048]{1,0:T(8,128)(2,1)S(1)}, u32[]{:S(2)}, u32[]{:S(2)}) collective-permute-start(bf16[256,2048]{1,0:T(8,128)(2,1)S(1)} %get-tuple-element.125), channel_id=1, source_target_pairs={{0,1},{1,0},{2,3},{3,2},{4,5},{5,4},{6,7},{7,6},{8,9},{9,8},{10,11... | collective-permute-start | bytes 3145736 | tf_op jit(solution)/shard_map/ppermute | solution.py:162
  481.0 20.6 %collective-permute-start.60 = (bf16[256,2048]{1,0:T(8,128)(2,1)S(1)}, bf16[256,2048]{1,0:T(8,128)(2,1)}, u32[]{:S(2)}, u32[]{:S(2)}) collective-permute-start(bf16[256,2048]{1,0:T(8,128)(2,1)S(1)} %collective-permute-done.59), channel_id=1, source_target_pairs={{0,1},{1,0},{2,3},{3,2},{4,5},{5,4},{6,7},{7,6},{8,9},{9,8},{10,11... | collective-permute-start | bytes 3145736 | tf_op jit(solution)/shard_map/ppermute | solution.py:162
  520.5 165.2 %reduce-scatter.5.cloned.1.call-start = ((), (), s32[]{:S(2)}) async-start(), calls=%async_computation.8 | async-start | bytes 3932160 | tf_op jit(solution)/shard_map/reduce_scatter | solution.py:363
  555.8 162.7 %reduce-scatter.9.cloned.1.call-start = ((), (), s32[]{:S(2)}) async-start(), calls=%async_computation.10 | async-start | bytes 7045120 | tf_op jit(solution)/shard_map/reduce_scatter | solution.py:367
  634.3 43.9 %collective-permute-start.58 = (bf16[256,2048]{1,0:T(8,128)(2,1)}, bf16[256,2048]{1,0:T(8,128)(2,1)}, u32[]{:S(2)}, u32[]{:S(2)}) collective-permute-start(bf16[256,2048]{1,0:T(8,128)(2,1)} %slice.383), channel_id=1, source_target_pairs={{0,1},{1,0},{2,3},{3,2},{4,5},{5,4},{6,7},{7,6},{8,9},{9,8},{10,11... | collective-permute-start | bytes 3145736 | tf_op jit(solution)/shard_map/ppermute | solution.py:162
  638.7 39.5 %collective-permute-start.70 = (bf16[128,2048]{1,0:T(8,128)(2,1)}, bf16[128,2048]{1,0:T(8,128)(2,1)}, u32[]{:S(2)}, u32[]{:S(2)}) collective-permute-start(bf16[128,2048]{1,0:T(8,128)(2,1)} %slice.543), channel_id=1, source_target_pairs={{0,2},{1,3},{2,0},{3,1},{4,6},{5,7},{6,4},{7,5},{8,10},{9,11},{10,... | collective-permute-start | bytes 1572872 | tf_op jit(solution)/shard_map/ppermute | solution.py:162
  640.8 23.2 %collective-permute-start.74 = (bf16[128,2048]{1,0:T(8,128)(2,1)S(1)}, bf16[128,2048]{1,0:T(8,128)(2,1)S(1)}, u32[]{:S(2)}, u32[]{:S(2)}) collective-permute-start(bf16[128,2048]{1,0:T(8,128)(2,1)S(1)} %get-tuple-element.144), channel_id=1, source_target_pairs={{0,2},{1,3},{2,0},{3,1},{4,6},{5,7},{6,4},{7,5},{8,10},{9,11},{10,... | collective-permute-start | bytes 1572872 | tf_op jit(solution)/shard_map/ppermute | solution.py:162
  641.3 25.4 %collective-permute-start.68 = (bf16[128,2048]{1,0:T(8,128)(2,1)S(1)}, bf16[128,2048]{1,0:T(8,128)(2,1)S(1)}, u32[]{:S(2)}, u32[]{:S(2)}) collective-permute-start(bf16[128,2048]{1,0:T(8,128)(2,1)S(1)} %get-tuple-element.145), channel_id=1, source_target_pairs={{0,4},{1,5},{2,6},{3,7},{4,0},{5,1},{6,2},{7,3},{8,12},{9,13},{10,... | collective-permute-start | bytes 1572872 | tf_op jit(solution)/shard_map/ppermute | solution.py:162
  644.2 34.0 %collective-permute-start.73 = (bf16[128,2048]{1,0:T(8,128)(2,1)}, bf16[128,2048]{1,0:T(8,128)(2,1)S(1)}, u32[]{:S(2)}, u32[]{:S(2)}) collective-permute-start(bf16[128,2048]{1,0:T(8,128)(2,1)} %slice.542), channel_id=1, source_target_pairs={{0,4},{1,5},{2,6},{3,7},{4,0},{5,1},{6,2},{7,3},{8,12},{9,13},{10,... | collective-permute-start | bytes 1572872 | tf_op jit(solution)/shard_map/ppermute | solution.py:162
  (134 other events, 1173.6 us)
Sparse Core Ops, SparseCore 0:
  10.3 66.1 all-gather.4
  78.6 26.6 all-gather.6
  107.4 102.9 all-gather.8
  220.3 57.0 all-gather.10
  446.6 53.0 reduce-scatter.10
  520.7 25.6 reduce-scatter.6
  556.0 60.0 reduce-scatter.4
  618.3 100.1 reduce-scatter.8

commit v2 on v1

--- a/solution.py
+++ b/solution.py
@@ -171,6 +171,40 @@
     return values
 
 
+def assemble_kernel(order_ref, *refs):
+    *parts, out_ref, done = refs
+    width = parts[0].shape[1]
+    copies = []
+    for index, part in enumerate(parts):
+        at = pl.multiple_of(order_ref[index] * width, width)
+        copies.append(
+            pltpu.make_async_copy(part, out_ref.at[:, pl.ds(at, width)], done.at[index])
+        )
+    for copy in copies:
+        copy.start()
+    for copy in copies:
+        copy.wait()
+
+
+def gather_columns(part):
+    count = lax.axis_size("dp")
+    parts = [part] + [
+        lax.ppermute(part, "dp", [(at, (at + far) % count) for at in range(count)])
+        for far in range(1, count)
+    ]
+    order = (lax.axis_index("dp") - jnp.arange(count, dtype=jnp.int32)) % count
+    anywhere = pl.BlockSpec(memory_space=pl.ANY)
+    rows, width = part.shape
+    return pl.pallas_call(
+        assemble_kernel,
+        out_shape=jax.ShapeDtypeStruct((rows, width * count), part.dtype),
+        in_specs=[pl.BlockSpec(memory_space=pltpu.SMEM)] + [anywhere] * count,
+        out_specs=anywhere,
+        scratch_shapes=[pltpu.SemaphoreType.DMA((count,))],
+        name="assemble",
+    )(order, *parts)
+
+
 def gather_near(rows):
     half = rows.shape[0] // 2
     near_x, near_y = swap(rows, "mp", 2), swap(rows, "mp", 4)
@@ -215,6 +249,14 @@
 def scatter_all(parts):
     whole = jnp.concatenate(parts, 0).astype(jnp.bfloat16)
     return lax.psum_scatter(whole, "mp", scatter_dimension=0, tiled=True).astype(jnp.float32)
+
+
+def adamw_as(order, weight, gradient, first_moment, second, step_rate, scale):
+    turned = [jnp.transpose(rows, order) for rows in (weight, first_moment, second)]
+    gradient = gradient.astype(jnp.float32) * scale
+    news = adamw(turned[0], gradient, turned[1], turned[2], step_rate)
+    back = [order.index(dim) for dim in range(len(order))]
+    return tuple(jnp.transpose(rows, back) for rows in news)
 
 
 def local(
@@ -263,8 +305,9 @@
 
     qkv_low = qkv_weight.astype(jnp.bfloat16).reshape(shard_rows, 3 * local_dim)
     qkv_full = lax.all_gather(qkv_low, "dp", axis=0, tiled=True)
-    out_full = lax.all_gather(out_weight.astype(jnp.bfloat16), "dp", axis=1, tiled=True)
-    gateup_full = lax.all_gather(gateup_weight.astype(jnp.bfloat16), "dp", axis=0, tiled=True)
+    out_full = gather_columns(out_weight.astype(jnp.bfloat16))
+    gateup_low = jnp.transpose(gateup_weight, (1, 2, 0)).astype(jnp.bfloat16)
+    gateup_full = lax.all_gather(gateup_low, "dp", axis=2, tiled=True)
     down_full = lax.all_gather(down_weight.astype(jnp.bfloat16), "dp", axis=1, tiled=True)
 
     mask_f32 = target_mask.astype(jnp.float32)
@@ -277,6 +320,7 @@
         query, key, value, out = attend_forward(infos[seq], proj, cosine, sine)
         kept.append((query, key, value))
         attended.append(out)
+    attended, out_full = lax.optimization_barrier((attended, out_full))
     attn_own = scatter_rows(
         [jnp.dot(rows, out_full, preferred_element_type=jnp.bfloat16) for rows in attended]
     )
@@ -286,11 +330,11 @@
 
     live_units = (mp_index * local_units + jnp.arange(local_units) < FF).astype(jnp.float32)
     gate_ups = [
-        jnp.einsum("td,dcf->tcf", rows, gateup_full, preferred_element_type=jnp.float32)
+        jnp.einsum("td,cfd->ctf", rows, gateup_full, preferred_element_type=jnp.float32)
         for rows in middles
     ]
     hiddens = [
-        (jax.nn.gelu(gate_up[:, 0]) * gate_up[:, 1] * live_units).astype(jnp.bfloat16)
+        (jax.nn.gelu(gate_up[0]) * gate_up[1] * live_units).astype(jnp.bfloat16)
         for gate_up in gate_ups
     ]
     ffn_own = scatter_rows(
@@ -302,54 +346,63 @@
     grad_two, gain_two, bias_two = norm_backward(grad_rows, normed_two, inv_two, norm_params[2])
 
     ffn_backs = gather_rows(grad_two.astype(jnp.bfloat16))
+    down_grad = jnp.einsum(
+        "tf,td->fd",
+        jnp.concatenate(hiddens, 0),
+        jnp.concatenate(ffn_backs, 0),
+        preferred_element_type=jnp.bfloat16,
+    )
+    ffn_backs[-1], down_grad = lax.optimization_barrier((ffn_backs[-1], down_grad))
+    down_grad = lax.psum_scatter(down_grad, "dp", scatter_dimension=1, tiled=True)
     grad_gateups, middle_parts = [], []
     for seq in seqs:
-        gate_act, gelu_pull = jax.vjp(jax.nn.gelu, gate_ups[seq][:, 0])
+        gate_act, gelu_pull = jax.vjp(jax.nn.gelu, gate_ups[seq][0])
         grad_hidden = (
             jnp.einsum("td,fd->tf", ffn_backs[seq], down_full, preferred_element_type=jnp.float32)
             * live_units
         )
-        grad_gate = gelu_pull(grad_hidden * gate_ups[seq][:, 1])[0]
+        grad_gate = gelu_pull(grad_hidden * gate_ups[seq][1])[0]
         grad_up = grad_hidden * gate_act
-        grad_gateup = jnp.stack([grad_gate, grad_up], 1).astype(jnp.bfloat16)
+        grad_gateup = jnp.stack([grad_gate, grad_up], 0).astype(jnp.bfloat16)
         grad_gateups.append(grad_gateup)
         middle_parts.append(
             jnp.einsum(
-                "tcf,dcf->td", grad_gateup, gateup_full, preferred_element_type=jnp.bfloat16
+                "ctf,cfd->td", grad_gateup, gateup_full, preferred_element_type=jnp.bfloat16
             )
         )
-    ffn_back_all = jnp.concatenate(ffn_backs, 0)
-    down_grad = jnp.einsum(
-        "tf,td->fd", jnp.concatenate(hiddens, 0), ffn_back_all, preferred_element_type=jnp.bfloat16
-    )
     gateup_grad = jnp.einsum(
-        "td,tcf->dcf",
+        "ctf,td->cfd",
+        jnp.concatenate(grad_gateups, 1),
         jnp.concatenate(middles, 0),
-        jnp.concatenate(grad_gateups, 0),
         preferred_element_type=jnp.bfloat16,
     )
     grad_middle = scatter_rows(middle_parts) + deep_alpha * grad_two
     grad_one, gain_one, bias_one = norm_backward(grad_middle, normed_one, inv_one, norm_params[0])
 
-    attn_backs = gather_rows(grad_one.astype(jnp.bfloat16))
+    grad_one_low, gateup_grad = lax.optimization_barrier(
+        (grad_one.astype(jnp.bfloat16), gateup_grad)
+    )
+    gateup_grad, down_grad = lax.optimization_barrier((gateup_grad, down_grad))
+    gateup_grad = lax.psum_scatter(gateup_grad, "dp", scatter_dimension=2, tiled=True)
+    attn_backs = gather_rows(grad_one_low)
     grad_projs = []
     for seq in seqs:
         grad_attended = jnp.einsum(
             "td,ed->te", attn_backs[seq], out_full, preferred_element_type=jnp.float32
         ).astype(jnp.bfloat16)
         grad_projs.append(attend_backward(infos[seq], *kept[seq], grad_attended, cosine, sine))
-    out_grad = jnp.einsum(
-        "te,td->ed",
-        jnp.concatenate(attended, 0),
-        jnp.concatenate(attn_backs, 0),
-        preferred_element_type=jnp.bfloat16,
-    )
-    qkv_grad = jnp.einsum(
-        "td,te->de",
-        jnp.concatenate(inputs, 0),
-        jnp.concatenate(grad_projs, 0),
-        preferred_element_type=jnp.bfloat16,
-    )
+    attended, grad_projs = lax.optimization_barrier((attended, grad_projs))
+    attend_grad = jnp.concatenate(
+        [
+            jnp.einsum("te,td->ed", jnp.concatenate(left, 0), jnp.concatenate(right, 0),
+                       preferred_element_type=jnp.bfloat16)
+            for left, right in ((attended, attn_backs), (grad_projs, inputs))
+        ],
+        0,
+    )
+    grad_projs, attend_grad = lax.optimization_barrier((grad_projs, attend_grad))
+    attend_grad, gateup_grad = lax.optimization_barrier((attend_grad, gateup_grad))
+    attend_grad = lax.psum_scatter(attend_grad, "dp", scatter_dimension=1, tiled=True)
     input_raw = (
         scatter_rows(
             [
@@ -359,26 +412,33 @@
         )
         + deep_alpha * grad_one
     )
-    qkv_grad, out_grad, gateup_grad, down_grad = (
-        lax.psum_scatter(qkv_grad, "dp", scatter_dimension=0, tiled=True)
-        .astype(jnp.float32)
-        .reshape(qkv_weight.shape),
-        lax.psum_scatter(out_grad, "dp", scatter_dimension=1, tiled=True).astype(jnp.float32),
-        lax.psum_scatter(gateup_grad, "dp", scatter_dimension=0, tiled=True).astype(jnp.float32),
-        lax.psum_scatter(down_grad, "dp", scatter_dimension=1, tiled=True).astype(jnp.float32),
-    )
-    norm_grad = sum_everywhere(jnp.stack([gain_one, bias_one, gain_two, bias_two], 0))
+    out_grad = attend_grad[:local_dim]
+    qkv_grad = attend_grad[local_dim:].reshape(3, local_dim, shard_rows)
+    norm_grad = jnp.stack([gain_one, bias_one, gain_two, bias_two], 0)
+    norm_grad, input_raw = lax.optimization_barrier((norm_grad, input_raw))
+    norm_grad = sum_everywhere(norm_grad)
     rate_list = (D ** (-0.5), 0.5, D ** (-0.5), (FF_PAD // 64) ** (-0.5), 0.4)
-    qkv_res = adamw(qkv_weight, qkv_grad / target_count, qkv_first, qkv_second, rate_list[0])
-    out_res = adamw(out_weight, out_grad / target_count, out_first, out_second, rate_list[1])
-    gateup_res = adamw(
-        gateup_weight, gateup_grad / target_count, gateup_first, gateup_second, rate_list[2]
-    )
-    down_res = adamw(down_weight, down_grad / target_count, down_first, down_second, rate_list[3])
-    norm_res = adamw(norm_params, norm_grad / target_count, norm_first, norm_second, rate_list[4])
+    scale = 1.0 / target_count
+    qkv_res = adamw_as(
+        (1, 0, 2), qkv_weight, qkv_grad.transpose(0, 2, 1), qkv_first, qkv_second, rate_list[0], scale
+    )
+    out_res = adamw_as((0, 1), out_weight, out_grad, out_first, out_second, rate_list[1], scale)
+    gateup_res = adamw_as(
+        (2, 1, 0),
+        gateup_weight,
+        gateup_grad.transpose(1, 0, 2),
+        gateup_first,
+        gateup_second,
+        rate_list[2],
+        scale,
+    )
+    down_res = adamw_as(
+        (0, 1), down_weight, down_grad, down_first, down_second, rate_list[3], scale
+    )
+    norm_res = adamw(norm_params, norm_grad * scale, norm_first, norm_second, rate_list[4])
     return (
         output_rows.astype(jnp.bfloat16),
-        input_raw / target_count,
+        input_raw * scale,
         qkv_res[0],
         qkv_res[1],
         qkv_res[2],

time: 755 us -> 719 us (0.952)
  Pallas kernels: 37.9 us -> 71.1 us
  waiting for transfers between devices: 276 us -> 248 us
  local copies, waits for them, and re-layouts: 111 us -> 93.4 us
  other arithmetic: 78.5 us -> 68.4 us
    pallas_call x0 -> x1, Pallas kernels: none -> 33.6 us  [gather_columns(): pl.pallas_call(assemble_kernel, out_shape=jax.ShapeDtypeStruct((rows, wid...]
    all_gather x1, waiting for transfers between devices: 23.1 us -> 0.02 us  [local(): qkv_full = lax.all_gather(qkv_low, 'dp', axis=0, tiled=True)]
    all_gather x2 -> x1, waiting for transfers between devices: 19.5 us -> 0.01 us  [local(): gateup_full = lax.all_gather(gateup_low, 'dp', axis=2, tiled=True)]
    unnamed x218 -> x260, local copies, waits for them, and re-layouts: 86.3 us -> 69.4 us
    reduce_scatter x3 -> x2, waiting for transfers between devices: 13.4 us -> 0.01 us  [the longest x1 0.01 us: local(): lax.psum_scatter(gateup_grad, 'dp', scatter_dimension=2, tiled=True)]
    ppermute x86, starting transfers between devices: 65.7 us -> 54 us  [swap(): return lax.ppermute(values, axis, [(at, at ^ bit) for at in range(size)])]
    ppermute x86, waiting for transfers between devices: 206 us -> 216 us  [swap(): return lax.ppermute(values, axis, [(at, at ^ bit) for at in range(size)])]
    sub x5 -> x4, other arithmetic: 21.5 us -> 11.8 us  [adamw(): weight - step_rate * (first_hat / (jnp.sqrt(second_hat) + adam_eps) + dec...]
  transfers between devices with their start and end apart: 94 -> 95, of which waited for: 40 -> 37; matrix products, arithmetic and copies ran while one was open for 41% -> 39% of each run, Pallas kernels for 5% -> 10%
where the time goes in v2:
time: 719 us; the launch traced here: 714 us
  waiting for transfers between devices  248 us (34%)
  matrix products  153 us (21%)
  local copies, waits for them, and re-layouts  93.4 us (13%)
  Pallas kernels  71.1 us (10%)
  other arithmetic  68.4 us (10%)
  starting transfers between devices  63.4 us (9%)
  between operations  17.1 us (2%)
    ppermute x86, waiting for transfers between devices, swap(): return lax.ppermute(values, axis, [(at, at ^ bit) for at in range(size)])  216 us
    unnamed x260, local copies, waits for them, and re-layouts  69.4 us
    ppermute x86, starting transfers between devices, swap(): return lax.ppermute(values, axis, [(at, at ^ bit) for at in range(size)])  54 us
    pallas_call x1, Pallas kernels, gather_columns(): pl.pallas_call(assemble_kernel, out_shape=jax.ShapeDtypeStruct((rows, wid...  33.6 us
    dot_general x4, matrix products, local(): jnp.einsum('td,cfd->ctf', rows, gateup_full, preferred_element_type=jnp.f...  28.3 us
    all_gather x1, waiting for transfers between devices, local(): lax.all_gather(down_weight.astype(jnp.bfloat16), 'dp', axis=1, tiled=True)  21.8 us
    pallas_call x4, Pallas kernels, attend_backward(): pl.pallas_call(attend_back_kernel, out_shape=jax.ShapeDtypeStruct((seq_le...  20.5 us
    dot_general x4, matrix products, local(): proj = jnp.dot(inputs[seq], qkv_full, preferred_element_type=jnp.float32)  20 us
  transfers between devices with their start and end apart: 95, of which 37 were waited for; matrix products, arithmetic and copies ran while one was open for 39% of the time, Pallas kernels for 10%

profile of v2, /device:TPU:0, one launch (start us, length us, event | category | flops | bytes accessed | tf_op | source)
XLA Modules:
  0.0 713.8 jit_solution(2305383532159524046)
XLA Ops:
  21.4 15.2 %collective-permute-done.3 = bf16[256,2048]{1,0:T(8,128)(2,1)} collective-permute-done((bf16[256,2048]{1,0:T(8,128)(2,1)}, bf16[256,2048]{1,0:T(8,128)(2,1)}, u32[]{:S(2)}, u32[]{:S(2)}) %collective-permute-start.3) | collective-permute-done | bytes 1048608 | tf_op jit(solution)/shard_map/ppermute | solution.py:162
  49.6 4.6 collective-permute-start.9
  59.6 9.5 %collective-permute-done.9.refs_1_ = bf16[256,512]{1,0:T(8,128)(2,1)} collective-permute-done((bf16[256,512]{1,0:T(8,128)(2,1)}, bf16[256,512]{1,0:T(8,128)(2,1)}, u32[]{:S(2)}, u32[]{:S(2)}) %collective-permute-start.9) | collective-permute-done | bytes 262176 | tf_op jit(solution)/shard_map/ppermute | solution.py:192
  69.0 33.6 %assemble.1 = bf16[256,2048]{1,0:T(8,128)(2,1)} custom-call(s32[4]{0:T(128)} %and_select_fusion.order_ref, bf16[256,512]{1,0:T(8,128)(2,1)} %convert_element_type.290.refs_0_, bf16[256,512]{1,0:T(8,128)(2,1)} %collective-permute-done.9.refs_1_, bf16[256,512]{1,0:T(8,128)(2,1)} %copy-done.64, bf16[256,512]{1,0:T(8,128)(2,1)} %collective-permute-done.11.refs_3_), custom_call_target="tpu_custom_call" | custom-call | tf_op jit(solution)/shard_map/assemble/pallas_call | solution.py:198
  102.7 5.7 fusion.48.proj_ref
  108.4 4.5 fusion.52.proj_ref
  112.9 4.6 fusion.44.proj_ref
  121.6 4.2 attend_forward.6
  125.7 4.1 attend_forward.5
  129.9 5.2 fusion.40.proj_ref
  135.1 4.6 attend_forward.4
  150.0 9.8 %collective-permute-done.15 = bf16[128,2048]{1,0:T(8,128)(2,1)S(1)} collective-permute-done((bf16[128,2048]{1,0:T(8,128)(2,1)S(1)}, bf16[128,2048]{1,0:T(8,128)(2,1)S(1)}, u32[]{:S(2)}, u32[]{:S(2)}) %collective-permute-start.15) | collective-permute-done | bytes 524320 | tf_op jit(solution)/shard_map/ppermute | solution.py:162
  160.5 12.4 %collective-permute-done.20 = bf16[128,2048]{1,0:T(8,128)(2,1)S(1)} collective-permute-done((bf16[128,2048]{1,0:T(8,128)(2,1)S(1)}, bf16[128,2048]{1,0:T(8,128)(2,1)S(1)}, u32[]{:S(2)}, u32[]{:S(2)}) %collective-permute-start.20) | collective-permute-done | bytes 524320 | tf_op jit(solution)/shard_map/ppermute | solution.py:162
  173.8 9.8 %collective-permute-done.16 = bf16[128,2048]{1,0:T(8,128)(2,1)S(1)} collective-permute-done((bf16[128,2048]{1,0:T(8,128)(2,1)S(1)}, bf16[128,2048]{1,0:T(8,128)(2,1)S(1)}, u32[]{:S(2)}, u32[]{:S(2)}) %collective-permute-start.16) | collective-permute-done | bytes 524320 | tf_op jit(solution)/shard_map/ppermute | solution.py:162
  190.4 22.3 %collective-permute-done.24 = bf16[256,2048]{1,0:T(8,128)(2,1)S(1)} collective-permute-done((bf16[256,2048]{1,0:T(8,128)(2,1)}, bf16[256,2048]{1,0:T(8,128)(2,1)S(1)}, u32[]{:S(2)}, u32[]{:S(2)}) %collective-permute-start.24) | collective-permute-done | bytes 1048608 | tf_op jit(solution)/shard_map/ppermute | solution.py:162
  219.6 5.5 collective-permute-done.27
  226.2 9.1 %fusion.115 = f32[2,512,684]{1,2,0:T(8,128)S(1)} fusion(bf16[256,2048]{1,0:T(8,128)(2,1)} %collective-permute-done.22, bf16[256,2048]{1,0:T(8,128)(2,1)} %get-tuple-element.176, bf16[2,684,2048]{2,0,1:T(2,128)(2,1)} %all-gather.6.cloned.1.call-done), kind=kOutput, calls=%fused_computation.172 | convolution fusion | flops 2873098240 | bytes 10502144 | tf_op jit(solution)/shard_map/td,cfd->ctf/dot_general | solution.py:333
  235.4 6.2 fusion.112
  241.6 6.0 fusion.114
  247.7 7.0 fusion.113
  259.7 21.8 %all-gather.8.cloned.1.call-done = bf16[684,2048]{1,0:T(8,128)(2,1)} async-done(((bf16[684,512]{1,0:T(8,128)(2,1)}), bf16[684,2048]{1,0:T(8,128)(2,1)}) %all-gather.8.cloned.1.call-update) | async-done | bytes 2801680 | tf_op jit(solution)/shard_map/all_gather | solution.py:311
  300.3 9.7 %collective-permute-done.33 = bf16[128,2048]{1,0:T(8,128)(2,1)S(1)} collective-permute-done((bf16[128,2048]{1,0:T(8,128)(2,1)S(1)}, bf16[128,2048]{1,0:T(8,128)(2,1)S(1)}, u32[]{:S(2)}, u32[]{:S(2)}) %collective-permute-start.33) | collective-permute-done | bytes 524320 | tf_op jit(solution)/shard_map/ppermute | solution.py:162
  311.6 11.6 %collective-permute-done.39 = bf16[128,2048]{1,0:T(8,128)(2,1)S(1)} collective-permute-done((bf16[128,2048]{1,0:T(8,128)(2,1)S(1)}, bf16[128,2048]{1,0:T(8,128)(2,1)S(1)}, u32[]{:S(2)}, u32[]{:S(2)}) %collective-permute-start.39) | collective-permute-done | bytes 524320 | tf_op jit(solution)/shard_map/ppermute | solution.py:162
  328.4 5.3 collective-permute-done.34
  354.7 13.4 %collective-permute-done.43 = bf16[256,2048]{1,0:T(8,128)(2,1)S(1)} collective-permute-done((bf16[256,2048]{1,0:T(8,128)(2,1)S(1)}, bf16[256,2048]{1,0:T(8,128)(2,1)S(1)}, u32[]{:S(2)}, u32[]{:S(2)}) %collective-permute-start.43) | collective-permute-done | bytes 1048608 | tf_op jit(solution)/shard_map/ppermute | solution.py:162
  373.6 4.7 convolution_bitcast_fusion.3
  386.2 7.5 %fusion.31 = bf16[684,2048]{1,0:T(8,128)(2,1)} fusion(bf16[2048,2048]{1,0:T(8,128)(2,1)S(1)} %constant_dynamic-update-slice_fusion, bf16[512,684]{0,1:T(8,128)(2,1)S(1)} %copy-done.60, bf16[512,684]{0,1:T(8,128)(2,1)S(1)} %copy-done.61, bf16[512,684]{0,1:T(8,128)(2,1)S(1)} %copy-done.59, bf16[512,684]{0,1:T(8,128)(2,1)S(1)} %copy-done.58), kind=kOutput, calls=%fused_computation.34 | convolution fusion | flops 5749014528 | bytes 13991936 | tf_op jit(solution)/shard_map/tf,td->fd/dot_general | solution.py:349
  396.4 5.0 fusion.215
  401.5 5.0 convolution_bitcast_fusion.2
  410.7 4.7 convolution_bitcast_fusion.1
  420.7 4.7 convolution_bitcast_fusion
  439.8 5.7 collective-permute-done.53
  447.4 13.2 %collective-permute-done.58 = bf16[128,2048]{1,0:T(8,128)(2,1)S(1)} collective-permute-done((bf16[128,2048]{1,0:T(8,128)(2,1)S(1)}, bf16[128,2048]{1,0:T(8,128)(2,1)S(1)}, u32[]{:S(2)}, u32[]{:S(2)}) %collective-permute-start.58) | collective-permute-done | bytes 524320 | tf_op jit(solution)/shard_map/ppermute | solution.py:162
  462.4 17.2 %fusion = bf16[2,684,2048]{2,1,0:T(8,128)(2,1)} fusion(bf16[2048,2048]{1,0:T(8,128)(2,1)} %constant_dynamic-update-slice_fusion.10, bf16[1,512,684]{1,2,0:T(8,128)(2,1)S(1)} %copy-done.100, bf16[1,512,684]{1,2,0:T(8,128)(2,1)S(1)} %copy-done.98, bf16[1,512,684]{1,2,0:T(8,128)(2,1)S(1)} %copy-done.104, bf16[1,512,684]{1,2,0:T(8,128)(2,1)S(1)} %copy-done.102, ...), kind=kOutput, calls=%fused_computation | convolution fusion | flops 11520442368 | bytes 19595264 | tf_op jit(solution)/shard_map/ctf,td->cfd/dot_general | solution.py:373
  479.6 4.9 multiply_reduce_fusion
  497.1 17.1 %collective-permute-done.61 = bf16[256,2048]{1,0:T(8,128)(2,1)} collective-permute-done((bf16[256,2048]{1,0:T(8,128)(2,1)S(1)}, bf16[256,2048]{1,0:T(8,128)(2,1)}, u32[]{:S(2)}, u32[]{:S(2)}) %collective-permute-start.61) | collective-permute-done | bytes 1048608 | tf_op jit(solution)/shard_map/ppermute | solution.py:162
  521.9 4.8 collective-permute-done.65
  530.2 5.1 attend_backward.4
  540.7 5.1 attend_backward.7
  548.5 5.1 attend_backward.6
  556.9 5.1 attend_backward.5
  575.6 6.0 fusion.201
  581.7 7.7 %fusion.17 = bf16[768,2048]{1,0:T(8,128)(2,1)S(1)} fusion(bf16[2048,2048]{1,0:T(8,128)(2,1)S(1)} %bitcast.235, bf16[512,768]{1,0:T(8,128)(2,1)S(1)} %copy-done.54, bf16[512,768]{1,0:T(8,128)(2,1)S(1)} %copy-done.53, bf16[512,768]{1,0:T(8,128)(2,1)S(1)} %copy-done.55, bf16[512,768]{1,0:T(8,128)(2,1)S(1)} %copy-done.51), kind=kOutput, calls=%fused_computation.20 | convolution fusion | flops 6455033856 | bytes 14680064 | tf_op jit(solution)/shard_map/te,td->ed/dot_general | solution.py:397
  613.1 9.7 %collective-permute-done.77 = bf16[128,2048]{1,0:T(8,128)(2,1)S(1)} collective-permute-done((bf16[128,2048]{1,0:T(8,128)(2,1)S(1)}, bf16[128,2048]{1,0:T(8,128)(2,1)S(1)}, u32[]{:S(2)}, u32[]{:S(2)}) %collective-permute-start.77) | collective-permute-done | bytes 524320 | tf_op jit(solution)/shard_map/ppermute | solution.py:162
  623.8 12.3 %collective-permute-done.72 = bf16[128,2048]{1,0:T(8,128)(2,1)S(1)} collective-permute-done((bf16[128,2048]{1,0:T(8,128)(2,1)S(1)}, bf16[128,2048]{1,0:T(8,128)(2,1)S(1)}, u32[]{:S(2)}, u32[]{:S(2)}) %collective-permute-start.72) | collective-permute-done | bytes 524320 | tf_op jit(solution)/shard_map/ppermute | solution.py:162
  636.9 9.6 %collective-permute-done.78 = bf16[128,2048]{1,0:T(8,128)(2,1)S(1)} collective-permute-done((bf16[128,2048]{1,0:T(8,128)(2,1)S(1)}, bf16[128,2048]{1,0:T(8,128)(2,1)S(1)}, u32[]{:S(2)}, u32[]{:S(2)}) %collective-permute-start.78) | collective-permute-done | bytes 524320 | tf_op jit(solution)/shard_map/ppermute | solution.py:162
  665.6 5.1 collective-permute-done.83
  698.6 5.8 fusion.120
  (574 shorter events, 279.9 us)
Async XLA Ops:
  7.2 95.4 %all-gather.4.cloned.1.call-start = ((), (), s32[]{:S(2)}) async-start(), calls=%async_computation.3 | async-start | bytes 3932160 | tf_op jit(solution)/shard_map/all_gather | solution.py:307
  10.0 216.2 %all-gather.6.cloned.1.call-start = ((), (), s32[]{:S(2)}) async-start(), calls=%async_computation.4 | async-start | bytes 7004160 | tf_op jit(solution)/shard_map/all_gather | solution.py:310
  10.0 26.5 %collective-permute-start.3 = (bf16[256,2048]{1,0:T(8,128)(2,1)}, bf16[256,2048]{1,0:T(8,128)(2,1)}, u32[]{:S(2)}, u32[]{:S(2)}) collective-permute-start(bf16[256,2048]{1,0:T(8,128)(2,1)} %param.20), channel_id=1, source_target_pairs={{0,4},{1,5},{2,6},{3,7},{4,0},{5,1},{6,2},{7,3},{8,12},{9,13},{10,... | collective-permute-start | bytes 3145736 | tf_op jit(solution)/shard_map/ppermute | solution.py:162
  13.1 24.9 %collective-permute-start.1 = (bf16[256,2048]{1,0:T(8,128)(2,1)}, bf16[256,2048]{1,0:T(8,128)(2,1)}, u32[]{:S(2)}, u32[]{:S(2)}) collective-permute-start(bf16[256,2048]{1,0:T(8,128)(2,1)} %param.20), channel_id=1, source_target_pairs={{0,2},{1,3},{2,0},{3,1},{4,6},{5,7},{6,4},{7,5},{8,10},{9,11},{10,... | collective-permute-start | bytes 3145736 | tf_op jit(solution)/shard_map/ppermute | solution.py:162
  15.3 34.3 %collective-permute-start.10 = (bf16[256,512]{1,0:T(8,128)(2,1)}, bf16[256,512]{1,0:T(8,128)(2,1)S(1)}, u32[]{:S(2)}, u32[]{:S(2)}) collective-permute-start(bf16[256,512]{1,0:T(8,128)(2,1)} %convert_element_type.290.refs_0_), channel_id=1, source_target_pairs={{0,16},{8,24},{16,0},{24,8},{1,17},{9,25},{17,1},{25,9},{2,18},{10... | collective-permute-start | bytes 786440 | tf_op jit(solution)/shard_map/ppermute | solution.py:192
  17.9 39.2 %collective-permute-start.11 = (bf16[256,512]{1,0:T(8,128)(2,1)}, bf16[256,512]{1,0:T(8,128)(2,1)}, u32[]{:S(2)}, u32[]{:S(2)}) collective-permute-start(bf16[256,512]{1,0:T(8,128)(2,1)} %convert_element_type.290.refs_0_), channel_id=1, source_target_pairs={{0,24},{8,0},{16,8},{24,16},{1,25},{9,1},{17,9},{25,17},{2,26},{10... | collective-permute-start | bytes 786440 | tf_op jit(solution)/shard_map/ppermute | solution.py:192
  21.4 260.2 %all-gather.8.cloned.1.call-start = ((), (), s32[]{:S(2)}) async-start(), calls=%async_computation.5 | async-start | bytes 3522560 | tf_op jit(solution)/shard_map/all_gather | solution.py:311
  36.6 66.0 %collective-permute-start.4 = (bf16[256,2048]{1,0:T(8,128)(2,1)}, bf16[256,2048]{1,0:T(8,128)(2,1)S(1)}, u32[]{:S(2)}, u32[]{:S(2)}) collective-permute-start(bf16[256,2048]{1,0:T(8,128)(2,1)} %collective-permute-done.3), channel_id=1, source_target_pairs={{0,1},{1,0},{2,3},{3,2},{4,5},{5,4},{6,7},{7,6},{8,9},{9,8},{10,11... | collective-permute-start | bytes 3145736 | tf_op jit(solution)/shard_map/ppermute | solution.py:162
  57.1 55.8 %collective-permute-start.2 = (bf16[256,2048]{1,0:T(8,128)(2,1)}, bf16[256,2048]{1,0:T(8,128)(2,1)S(1)}, u32[]{:S(2)}, u32[]{:S(2)}) collective-permute-start(bf16[256,2048]{1,0:T(8,128)(2,1)} %collective-permute-done.1), channel_id=1, source_target_pairs={{0,1},{1,0},{2,3},{3,2},{4,5},{5,4},{6,7},{7,6},{8,9},{9,8},{10,11... | collective-permute-start | bytes 3145736 | tf_op jit(solution)/shard_map/ppermute | solution.py:162
  57.1 51.2 %collective-permute-start.7 = (bf16[128,2048]{1,0:T(8,128)(2,1)}, bf16[128,2048]{1,0:T(8,128)(2,1)}, u32[]{:S(2)}, u32[]{:S(2)}) collective-permute-start(bf16[128,2048]{1,0:T(8,128)(2,1)} %collective-permute-done.5), channel_id=1, source_target_pairs={{0,1},{1,0},{2,3},{3,2},{4,5},{5,4},{6,7},{7,6},{8,9},{9,8},{10,11... | collective-permute-start | bytes 1572872 | tf_op jit(solution)/shard_map/ppermute | solution.py:162
  57.6 50.7 %collective-permute-start.8 = (bf16[128,2048]{1,0:T(8,128)(2,1)}, bf16[128,2048]{1,0:T(8,128)(2,1)}, u32[]{:S(2)}, u32[]{:S(2)}) collective-permute-start(bf16[128,2048]{1,0:T(8,128)(2,1)} %collective-permute-done.6), channel_id=1, source_target_pairs={{0,1},{1,0},{2,3},{3,2},{4,5},{5,4},{6,7},{7,6},{8,9},{9,8},{10,11... | collective-permute-start | bytes 1572872 | tf_op jit(solution)/shard_map/ppermute | solution.py:162
  69.0 60.9 %collective-permute-start = (bf16[256,2048]{1,0:T(8,128)(2,1)S(1)}, bf16[256,2048]{1,0:T(8,128)(2,1)}, u32[]{:S(2)}, u32[]{:S(2)}) collective-permute-start(bf16[256,2048]{1,0:T(8,128)(2,1)S(1)} %copy-done.10), channel_id=1, source_target_pairs={{0,1},{1,0},{2,3},{3,2},{4,5},{5,4},{6,7},{7,6},{8,9},{9,8},{10,11... | collective-permute-start | bytes 3145736 | tf_op jit(solution)/shard_map/ppermute | solution.py:162
  142.0 31.8 %collective-permute-start.12 = (bf16[256,2048]{1,0:T(8,128)(2,1)S(1)}, bf16[256,2048]{1,0:T(8,128)(2,1)S(1)}, u32[]{:S(2)}, u32[]{:S(2)}) collective-permute-start(bf16[256,2048]{1,0:T(8,128)(2,1)S(1)} %slice.337), channel_id=1, source_target_pairs={{0,1},{1,0},{2,3},{3,2},{4,5},{5,4},{6,7},{7,6},{8,9},{9,8},{10,11... | collective-permute-start | bytes 3145736 | tf_op jit(solution)/shard_map/ppermute | solution.py:162
  146.8 26.9 %collective-permute-start.17 = (bf16[128,2048]{1,0:T(8,128)(2,1)S(1)}, bf16[128,2048]{1,0:T(8,128)(2,1)S(1)}, u32[]{:S(2)}, u32[]{:S(2)}) collective-permute-start(bf16[128,2048]{1,0:T(8,128)(2,1)S(1)} %slice.562), channel_id=1, source_target_pairs={{0,2},{1,3},{2,0},{3,1},{4,6},{5,7},{6,4},{7,5},{8,10},{9,11},{10,... | collective-permute-start | bytes 1572872 | tf_op jit(solution)/shard_map/ppermute | solution.py:162
  147.4 25.5 %collective-permute-start.20 = (bf16[128,2048]{1,0:T(8,128)(2,1)S(1)}, bf16[128,2048]{1,0:T(8,128)(2,1)S(1)}, u32[]{:S(2)}, u32[]{:S(2)}) collective-permute-start(bf16[128,2048]{1,0:T(8,128)(2,1)S(1)} %get-tuple-element.206), channel_id=1, source_target_pairs={{0,2},{1,3},{2,0},{3,1},{4,6},{5,7},{6,4},{7,5},{8,10},{9,11},{10,... | collective-permute-start | bytes 1572872 | tf_op jit(solution)/shard_map/ppermute | solution.py:162
  149.3 24.4 %collective-permute-start.19 = (bf16[128,2048]{1,0:T(8,128)(2,1)S(1)}, bf16[128,2048]{1,0:T(8,128)(2,1)S(1)}, u32[]{:S(2)}, u32[]{:S(2)}) collective-permute-start(bf16[128,2048]{1,0:T(8,128)(2,1)S(1)} %slice.561), channel_id=1, source_target_pairs={{0,4},{1,5},{2,6},{3,7},{4,0},{5,1},{6,2},{7,3},{8,12},{9,13},{10,... | collective-permute-start | bytes 1572872 | tf_op jit(solution)/shard_map/ppermute | solution.py:162
  159.9 23.7 %collective-permute-start.16 = (bf16[128,2048]{1,0:T(8,128)(2,1)S(1)}, bf16[128,2048]{1,0:T(8,128)(2,1)S(1)}, u32[]{:S(2)}, u32[]{:S(2)}) collective-permute-start(bf16[128,2048]{1,0:T(8,128)(2,1)S(1)} %fusion.200), channel_id=1, source_target_pairs={{0,2},{1,3},{2,0},{3,1},{4,6},{5,7},{6,4},{7,5},{8,10},{9,11},{10,... | collective-permute-start | bytes 1572872 | tf_op jit(solution)/shard_map/ppermute | solution.py:162
  189.1 23.6 %collective-permute-start.24 = (bf16[256,2048]{1,0:T(8,128)(2,1)}, bf16[256,2048]{1,0:T(8,128)(2,1)S(1)}, u32[]{:S(2)}, u32[]{:S(2)}) collective-permute-start(bf16[256,2048]{1,0:T(8,128)(2,1)} %get-tuple-element.176), channel_id=1, source_target_pairs={{0,2},{1,3},{2,0},{3,1},{4,6},{5,7},{6,4},{7,5},{8,10},{9,11},{10,... | collective-permute-start | bytes 3145736 | tf_op jit(solution)/shard_map/ppermute | solution.py:162
  189.7 24.2 %collective-permute-start.28 = (bf16[256,2048]{1,0:T(8,128)(2,1)}, bf16[256,2048]{1,0:T(8,128)(2,1)S(1)}, u32[]{:S(2)}, u32[]{:S(2)}) collective-permute-start(bf16[256,2048]{1,0:T(8,128)(2,1)} %get-tuple-element.176), channel_id=1, source_target_pairs={{0,4},{1,5},{2,6},{3,7},{4,0},{5,1},{6,2},{7,3},{8,12},{9,13},{10,... | collective-permute-start | bytes 3145736 | tf_op jit(solution)/shard_map/ppermute | solution.py:162
  190.4 27.0 %collective-permute-start.22 = (bf16[256,2048]{1,0:T(8,128)(2,1)}, bf16[256,2048]{1,0:T(8,128)(2,1)}, u32[]{:S(2)}, u32[]{:S(2)}) collective-permute-start(bf16[256,2048]{1,0:T(8,128)(2,1)} %get-tuple-element.176), channel_id=1, source_target_pairs={{0,1},{1,0},{2,3},{3,2},{4,5},{5,4},{6,7},{7,6},{8,9},{9,8},{10,11... | collective-permute-start | bytes 3145736 | tf_op jit(solution)/shard_map/ppermute | solution.py:162
  216.6 270.0 %reduce-scatter.4.cloned.1.call-start = ((), (), s32[]{:S(2)}) async-start(), calls=%async_computation.6 | async-start | bytes 3522560 | tf_op jit(solution)/shard_map/reduce_scatter | solution.py:356
  216.8 24.8 %collective-permute-start.25 = (bf16[256,2048]{1,0:T(8,128)(2,1)}, bf16[256,2048]{1,0:T(8,128)(2,1)}, u32[]{:S(2)}, u32[]{:S(2)}) collective-permute-start(bf16[256,2048]{1,0:T(8,128)(2,1)} %copy-done.22), channel_id=1, source_target_pairs={{0,1},{1,0},{2,3},{3,2},{4,5},{5,4},{6,7},{7,6},{8,9},{9,8},{10,11... | collective-permute-start | bytes 3145736 | tf_op jit(solution)/shard_map/ppermute | solution.py:162
  294.5 33.8 %collective-permute-start.23 = (bf16[256,2048]{1,0:T(8,128)(2,1)S(1)}, bf16[256,2048]{1,0:T(8,128)(2,1)S(1)}, u32[]{:S(2)}, u32[]{:S(2)}) collective-permute-start(bf16[256,2048]{1,0:T(8,128)(2,1)S(1)} %slice.353), channel_id=1, source_target_pairs={{0,1},{1,0},{2,3},{3,2},{4,5},{5,4},{6,7},{7,6},{8,9},{9,8},{10,11... | collective-permute-start | bytes 3145736 | tf_op jit(solution)/shard_map/ppermute | solution.py:162
  297.1 31.3 %collective-permute-start.35 = (bf16[128,2048]{1,0:T(8,128)(2,1)S(1)}, bf16[128,2048]{1,0:T(8,128)(2,1)S(1)}, u32[]{:S(2)}, u32[]{:S(2)}) collective-permute-start(bf16[128,2048]{1,0:T(8,128)(2,1)S(1)} %slice.560), channel_id=1, source_target_pairs={{0,2},{1,3},{2,0},{3,1},{4,6},{5,7},{6,4},{7,5},{8,10},{9,11},{10,... | collective-permute-start | bytes 1572872 | tf_op jit(solution)/shard_map/ppermute | solution.py:162
  298.6 24.6 %collective-permute-start.39 = (bf16[128,2048]{1,0:T(8,128)(2,1)S(1)}, bf16[128,2048]{1,0:T(8,128)(2,1)S(1)}, u32[]{:S(2)}, u32[]{:S(2)}) collective-permute-start(bf16[128,2048]{1,0:T(8,128)(2,1)S(1)} %get-tuple-element.204), channel_id=1, source_target_pairs={{0,2},{1,3},{2,0},{3,1},{4,6},{5,7},{6,4},{7,5},{8,10},{9,11},{10,... | collective-permute-start | bytes 1572872 | tf_op jit(solution)/shard_map/ppermute | solution.py:162
  299.6 28.7 %collective-permute-start.38 = (bf16[128,2048]{1,0:T(8,128)(2,1)S(1)}, bf16[128,2048]{1,0:T(8,128)(2,1)S(1)}, u32[]{:S(2)}, u32[]{:S(2)}) collective-permute-start(bf16[128,2048]{1,0:T(8,128)(2,1)S(1)} %slice.559), channel_id=1, source_target_pairs={{0,4},{1,5},{2,6},{3,7},{4,0},{5,1},{6,2},{7,3},{8,12},{9,13},{10,... | collective-permute-start | bytes 1572872 | tf_op jit(solution)/shard_map/ppermute | solution.py:162
  310.1 23.6 %collective-permute-start.34 = (bf16[128,2048]{1,0:T(8,128)(2,1)S(1)}, bf16[128,2048]{1,0:T(8,128)(2,1)S(1)}, u32[]{:S(2)}, u32[]{:S(2)}) collective-permute-start(bf16[128,2048]{1,0:T(8,128)(2,1)S(1)} %fusion.198), channel_id=1, source_target_pairs={{0,2},{1,3},{2,0},{3,1},{4,6},{5,7},{6,4},{7,5},{8,10},{9,11},{10,... | collective-permute-start | bytes 1572872 | tf_op jit(solution)/shard_map/ppermute | solution.py:162
  342.5 28.4 %collective-permute-start.41 = (bf16[256,2048]{1,0:T(8,128)(2,1)S(1)}, bf16[256,2048]{1,0:T(8,128)(2,1)S(1)}, u32[]{:S(2)}, u32[]{:S(2)}) collective-permute-start(bf16[256,2048]{1,0:T(8,128)(2,1)S(1)} %get-tuple-element.181), channel_id=1, source_target_pairs={{0,1},{1,0},{2,3},{3,2},{4,5},{5,4},{6,7},{7,6},{8,9},{9,8},{10,11... | collective-permute-start | bytes 3145736 | tf_op jit(solution)/shard_map/ppermute | solution.py:162
  342.6 25.6 %collective-permute-start.43 = (bf16[256,2048]{1,0:T(8,128)(2,1)S(1)}, bf16[256,2048]{1,0:T(8,128)(2,1)S(1)}, u32[]{:S(2)}, u32[]{:S(2)}) collective-permute-start(bf16[256,2048]{1,0:T(8,128)(2,1)S(1)} %get-tuple-element.181), channel_id=1, source_target_pairs={{0,2},{1,3},{2,0},{3,1},{4,6},{5,7},{6,4},{7,5},{8,10},{9,11},{10,... | collective-permute-start | bytes 3145736 | tf_op jit(solution)/shard_map/ppermute | solution.py:162
  344.1 25.2 %collective-permute-start.47 = (bf16[256,2048]{1,0:T(8,128)(2,1)S(1)}, bf16[256,2048]{1,0:T(8,128)(2,1)S(1)}, u32[]{:S(2)}, u32[]{:S(2)}) collective-permute-start(bf16[256,2048]{1,0:T(8,128)(2,1)S(1)} %get-tuple-element.181), channel_id=1, source_target_pairs={{0,4},{1,5},{2,6},{3,7},{4,0},{5,1},{6,2},{7,3},{8,12},{9,13},{10,... | collective-permute-start | bytes 3145736 | tf_op jit(solution)/shard_map/ppermute | solution.py:162
  379.5 100.1 %collective-permute-start.42 = (bf16[256,2048]{1,0:T(8,128)(2,1)}, bf16[256,2048]{1,0:T(8,128)(2,1)}, u32[]{:S(2)}, u32[]{:S(2)}) collective-permute-start(bf16[256,2048]{1,0:T(8,128)(2,1)} %slice.375), channel_id=1, source_target_pairs={{0,1},{1,0},{2,3},{3,2},{4,5},{5,4},{6,7},{7,6},{8,9},{9,8},{10,11... | collective-permute-start | bytes 3145736 | tf_op jit(solution)/shard_map/ppermute | solution.py:162
  407.6 24.1 %collective-permute-start.45 = (bf16[256,2048]{1,0:T(8,128)(2,1)}, bf16[256,2048]{1,0:T(8,128)(2,1)}, u32[]{:S(2)}, u32[]{:S(2)}) collective-permute-start(bf16[256,2048]{1,0:T(8,128)(2,1)} %slice.377), channel_id=1, source_target_pairs={{0,1},{1,0},{2,3},{3,2},{4,5},{5,4},{6,7},{7,6},{8,9},{9,8},{10,11... | collective-permute-start | bytes 3145736 | tf_op jit(solution)/shard_map/ppermute | solution.py:162
  428.0 169.0 %reduce-scatter.6.cloned.1.call-start = ((), (), s32[]{:S(2)}) async-start(), calls=%async_computation.7 | async-start | bytes 7045120 | tf_op jit(solution)/shard_map/reduce_scatter | solution.py:386
  434.4 45.2 %collective-permute-start.55 = (bf16[128,2048]{1,0:T(8,128)(2,1)}, bf16[128,2048]{1,0:T(8,128)(2,1)}, u32[]{:S(2)}, u32[]{:S(2)}) collective-permute-start(bf16[128,2048]{1,0:T(8,128)(2,1)} %slice.558), channel_id=1, source_target_pairs={{0,2},{1,3},{2,0},{3,1},{4,6},{5,7},{6,4},{7,5},{8,10},{9,11},{10,... | collective-permute-start | bytes 1572872 | tf_op jit(solution)/shard_map/ppermute | solution.py:162
  435.7 24.9 %collective-permute-start.58 = (bf16[128,2048]{1,0:T(8,128)(2,1)S(1)}, bf16[128,2048]{1,0:T(8,128)(2,1)S(1)}, u32[]{:S(2)}, u32[]{:S(2)}) collective-permute-start(bf16[128,2048]{1,0:T(8,128)(2,1)S(1)} %get-tuple-element.202), channel_id=1, source_target_pairs={{0,2},{1,3},{2,0},{3,1},{4,6},{5,7},{6,4},{7,5},{8,10},{9,11},{10,... | collective-permute-start | bytes 1572872 | tf_op jit(solution)/shard_map/ppermute | solution.py:162
  438.9 40.6 %collective-permute-start.57 = (bf16[128,2048]{1,0:T(8,128)(2,1)}, bf16[128,2048]{1,0:T(8,128)(2,1)}, u32[]{:S(2)}, u32[]{:S(2)}) collective-permute-start(bf16[128,2048]{1,0:T(8,128)(2,1)} %slice.557), channel_id=1, source_target_pairs={{0,4},{1,5},{2,6},{3,7},{4,0},{5,1},{6,2},{7,3},{8,12},{9,13},{10,... | collective-permute-start | bytes 1572872 | tf_op jit(solution)/shard_map/ppermute | solution.py:162
  446.4 33.2 %collective-permute-start.54 = (bf16[128,2048]{1,0:T(8,128)(2,1)}, bf16[128,2048]{1,0:T(8,128)(2,1)}, u32[]{:S(2)}, u32[]{:S(2)}) collective-permute-start(bf16[128,2048]{1,0:T(8,128)(2,1)} %fusion.196), channel_id=1, source_target_pairs={{0,2},{1,3},{2,0},{3,1},{4,6},{5,7},{6,4},{7,5},{8,10},{9,11},{10,... | collective-permute-start | bytes 1572872 | tf_op jit(solution)/shard_map/ppermute | solution.py:162
  486.7 208.9 %reduce-scatter.8.cloned.1.call-start = ((), (), s32[]{:S(2)}) async-start(), calls=%async_computation.8 | async-start | bytes 5242880 | tf_op jit(solution)/shard_map/reduce_scatter | solution.py:405
  490.7 23.5 %collective-permute-start.61 = (bf16[256,2048]{1,0:T(8,128)(2,1)S(1)}, bf16[256,2048]{1,0:T(8,128)(2,1)}, u32[]{:S(2)}, u32[]{:S(2)}) collective-permute-start(bf16[256,2048]{1,0:T(8,128)(2,1)S(1)} %get-tuple-element.74), channel_id=1, source_target_pairs={{0,2},{1,3},{2,0},{3,1},{4,6},{5,7},{6,4},{7,5},{8,10},{9,11},{10,... | collective-permute-start | bytes 3145736 | tf_op jit(solution)/shard_map/ppermute | solution.py:162
  491.8 24.8 %collective-permute-start.63 = (bf16[256,2048]{1,0:T(8,128)(2,1)S(1)}, bf16[256,2048]{1,0:T(8,128)(2,1)S(1)}, u32[]{:S(2)}, u32[]{:S(2)}) collective-permute-start(bf16[256,2048]{1,0:T(8,128)(2,1)S(1)} %get-tuple-element.74), channel_id=1, source_target_pairs={{0,4},{1,5},{2,6},{3,7},{4,0},{5,1},{6,2},{7,3},{8,12},{9,13},{10,... | collective-permute-start | bytes 3145736 | tf_op jit(solution)/shard_map/ppermute | solution.py:162
  494.8 32.9 %collective-permute-start.60 = (bf16[256,2048]{1,0:T(8,128)(2,1)S(1)}, bf16[256,2048]{1,0:T(8,128)(2,1)S(1)}, u32[]{:S(2)}, u32[]{:S(2)}) collective-permute-start(bf16[256,2048]{1,0:T(8,128)(2,1)S(1)} %get-tuple-element.74), channel_id=1, source_target_pairs={{0,1},{1,0},{2,3},{3,2},{4,5},{5,4},{6,7},{7,6},{8,9},{9,8},{10,11... | collective-permute-start | bytes 3145736 | tf_op jit(solution)/shard_map/ppermute | solution.py:162
  521.4 32.2 %collective-permute-start.62 = (bf16[256,2048]{1,0:T(8,128)(2,1)}, bf16[256,2048]{1,0:T(8,128)(2,1)}, u32[]{:S(2)}, u32[]{:S(2)}) collective-permute-start(bf16[256,2048]{1,0:T(8,128)(2,1)} %collective-permute-done.61), channel_id=1, source_target_pairs={{0,1},{1,0},{2,3},{3,2},{4,5},{5,4},{6,7},{7,6},{8,9},{9,8},{10,11... | collective-permute-start | bytes 3145736 | tf_op jit(solution)/shard_map/ppermute | solution.py:162
  521.4 24.4 %collective-permute-start.64 = (bf16[256,2048]{1,0:T(8,128)(2,1)S(1)}, bf16[256,2048]{1,0:T(8,128)(2,1)}, u32[]{:S(2)}, u32[]{:S(2)}) collective-permute-start(bf16[256,2048]{1,0:T(8,128)(2,1)S(1)} %collective-permute-done.63), channel_id=1, source_target_pairs={{0,1},{1,0},{2,3},{3,2},{4,5},{5,4},{6,7},{7,6},{8,9},{9,8},{10,11... | collective-permute-start | bytes 3145736 | tf_op jit(solution)/shard_map/ppermute | solution.py:162
  607.3 29.5 %collective-permute-start.69 = (bf16[256,2048]{1,0:T(8,128)(2,1)S(1)}, bf16[256,2048]{1,0:T(8,128)(2,1)S(1)}, u32[]{:S(2)}, u32[]{:S(2)}) collective-permute-start(bf16[256,2048]{1,0:T(8,128)(2,1)S(1)} %slice.393), channel_id=1, source_target_pairs={{0,1},{1,0},{2,3},{3,2},{4,5},{5,4},{6,7},{7,6},{8,9},{9,8},{10,11... | collective-permute-start | bytes 3145736 | tf_op jit(solution)/shard_map/ppermute | solution.py:162
  609.9 26.9 %collective-permute-start.76 = (bf16[128,2048]{1,0:T(8,128)(2,1)S(1)}, bf16[128,2048]{1,0:T(8,128)(2,1)S(1)}, u32[]{:S(2)}, u32[]{:S(2)}) collective-permute-start(bf16[128,2048]{1,0:T(8,128)(2,1)S(1)} %slice.555), channel_id=1, source_target_pairs={{0,4},{1,5},{2,6},{3,7},{4,0},{5,1},{6,2},{7,3},{8,12},{9,13},{10,... | collective-permute-start | bytes 1572872 | tf_op jit(solution)/shard_map/ppermute | solution.py:162
  610.7 25.3 %collective-permute-start.72 = (bf16[128,2048]{1,0:T(8,128)(2,1)S(1)}, bf16[128,2048]{1,0:T(8,128)(2,1)S(1)}, u32[]{:S(2)}, u32[]{:S(2)}) collective-permute-start(bf16[128,2048]{1,0:T(8,128)(2,1)S(1)} %get-tuple-element.200), channel_id=1, source_target_pairs={{0,4},{1,5},{2,6},{3,7},{4,0},{5,1},{6,2},{7,3},{8,12},{9,13},{10,... | collective-permute-start | bytes 1572872 | tf_op jit(solution)/shard_map/ppermute | solution.py:162
  612.5 24.3 %collective-permute-start.74 = (bf16[128,2048]{1,0:T(8,128)(2,1)S(1)}, bf16[128,2048]{1,0:T(8,128)(2,1)S(1)}, u32[]{:S(2)}, u32[]{:S(2)}) collective-permute-start(bf16[128,2048]{1,0:T(8,128)(2,1)S(1)} %slice.556), channel_id=1, source_target_pairs={{0,2},{1,3},{2,0},{3,1},{4,6},{5,7},{6,4},{7,5},{8,10},{9,11},{10,... | collective-permute-start | bytes 1572872 | tf_op jit(solution)/shard_map/ppermute | solution.py:162
  622.9 23.5 %collective-permute-start.78 = (bf16[128,2048]{1,0:T(8,128)(2,1)S(1)}, bf16[128,2048]{1,0:T(8,128)(2,1)S(1)}, u32[]{:S(2)}, u32[]{:S(2)}) collective-permute-start(bf16[128,2048]{1,0:T(8,128)(2,1)S(1)} %fusion.193), channel_id=1, source_target_pairs={{0,4},{1,5},{2,6},{3,7},{4,0},{5,1},{6,2},{7,3},{8,12},{9,13},{10,... | collective-permute-start | bytes 1572872 | tf_op jit(solution)/shard_map/ppermute | solution.py:162
  (158 other events, 1493.3 us)
Sparse Core Ops, SparseCore 0:
  10.2 81.5 all-gather.3
  93.9 102.9 all-gather.5
  216.8 64.7 all-gather.7
  428.1 53.5 reduce-scatter.3
  486.8 98.2 reduce-scatter.5
  597.1 75.1 reduce-scatter.7

commit v3 on v2

v3 whole, which is shorter than its diff:
```python
import jax
import jax.numpy as jnp
from jax import lax
from jax.experimental import pallas as pl
from jax.experimental.layout import Layout, with_layout_constraint
from jax.experimental.pallas import tpu as pltpu
from jax.sharding import PartitionSpec as P

D = 2048
HD = 128
FF = 5461
FF_PAD = 5472
STEP = 5


deep_alpha = 48.0**0.5
norm_eps = 1e-05
masked_score = -1e30
rope_base = 10000.0
beta_one = 0.5
beta_two = 0.5
adam_eps = 1e-08
decay_rate = 0.1


def rope_tables(position, head_dim):
    freqs = rope_base ** (-jnp.arange(0, head_dim, 2, dtype=jnp.float32) / head_dim)
    angles = position.astype(jnp.float32)[:, None] * freqs[None, :]
    cosine, sine = jnp.cos(angles), jnp.sin(angles)
    return (jnp.concatenate([cosine, cosine], -1), jnp.concatenate([-sine, sine], -1))


def turn(values, cosine, sine):
    return values * cosine + pltpu.roll(values, HD // 2, 1) * sine


def dot_nt(left, right):
    return lax.dot_general(
        left, right, (((1,), (1,)), ((), ())), preferred_element_type=jnp.float32
    )


def dot_nn(left, right):
    return lax.dot_general(
        left, right, (((1,), (0,)), ((), ())), preferred_element_type=jnp.float32
    )


def dot_tn(left, right):
    return lax.dot_general(
        left, right, (((0,), (0,)), ((), ())), preferred_element_type=jnp.float32
    )


def soft_rows(objective_ref, prefix_ref, place_ref, query, key):
    seq_len = query.shape[0]
    seq, flip = pl.program_id(0) ^ place_ref[0], place_ref[1]
    row_at = lax.broadcasted_iota(jnp.int32, (seq_len, seq_len), 0) ^ flip
    col_at = lax.broadcasted_iota(jnp.int32, (seq_len, seq_len), 1) ^ flip
    bound = jnp.where(objective_ref[seq] > 0, seq_len, prefix_ref[seq])
    visible = (col_at < bound) | (col_at <= row_at)
    scores = jnp.where(visible, dot_nt(query, key) * HD ** (-0.5), masked_score)
    exp_scores = jnp.exp(scores - jnp.max(scores, -1, keepdims=True))
    return exp_scores / jnp.sum(exp_scores, -1, keepdims=True)


def attend_kernel(
    objective_ref,
    prefix_ref,
    place_ref,
    proj_ref,
    cos_ref,
    sin_ref,
    query_ref,
    key_ref,
    value_ref,
    out_ref,
):
    local_dim = out_ref.shape[1]
    cosine, sine = cos_ref[...], sin_ref[...]
    for start in range(0, local_dim, HD):
        cols = slice(start, start + HD)
        query = turn(proj_ref[:, start : start + HD], cosine, sine).astype(jnp.bfloat16)
        key_at = local_dim + start
        key = turn(proj_ref[:, key_at : key_at + HD], cosine, sine).astype(jnp.bfloat16)
        value_at = 2 * local_dim + start
        value = proj_ref[:, value_at : value_at + HD].astype(jnp.bfloat16)
        soft = soft_rows(objective_ref, prefix_ref, place_ref, query, key)
        query_ref[:, cols] = query
        key_ref[:, cols] = key
        value_ref[:, cols] = value
        out_ref[:, cols] = dot_nn(soft.astype(jnp.bfloat16), value).astype(jnp.bfloat16)


def attend_back_kernel(
    objective_ref,
    prefix_ref,
    place_ref,
    query_ref,
    key_ref,
    value_ref,
    grad_ref,
    cos_ref,
    sin_ref,
    out_ref,
):
    local_dim = grad_ref.shape[1]
    cosine, sine = cos_ref[...], sin_ref[...]
    scale = HD ** (-0.5)
    for start in range(0, local_dim, HD):
        cols = slice(start, start + HD)
        query, key, value = query_ref[:, cols], key_ref[:, cols], value_ref[:, cols]
        grad = grad_ref[:, cols]
        soft = soft_rows(objective_ref, prefix_ref, place_ref, query, key)
        grad_soft = dot_nt(grad, value)
        row_dot = jnp.sum(soft * grad_soft, -1, keepdims=True)
        grad_scores = (soft * (grad_soft - row_dot)).astype(jnp.bfloat16)
        value_grad = dot_tn(soft.astype(jnp.bfloat16), grad)
        query_grad = turn(dot_nn(grad_scores, key) * scale, cosine, -sine)
        key_grad = turn(dot_tn(grad_scores, query) * scale, cosine, -sine)
        for index, rows in enumerate((query_grad, key_grad, value_grad)):
            at = index * local_dim + start
            out_ref[:, at : at + HD] = rows.astype(jnp.bfloat16)


def seq_specs(seq_len, widths):
    scalars = pl.BlockSpec(memory_space=pltpu.SMEM)
    table = pl.BlockSpec((seq_len, HD), lambda seq: (0, 0))
    rows = [pl.BlockSpec((seq_len, width), lambda seq: (seq, 0)) for width in widths]
    return [scalars] * 3 + rows + [table] * 2


def attend_forward(seq_info, proj, cosine, sine):
    seq_len, (rows, width) = cosine.shape[0], proj.shape
    local_dim = width // 3
    low = jax.ShapeDtypeStruct((rows, local_dim), jnp.bfloat16)
    block = pl.BlockSpec((seq_len, local_dim), lambda seq: (seq, 0))
    return pl.pallas_call(
        attend_kernel,
        grid=(rows // seq_len,),
        out_shape=(low,) * 4,
        in_specs=seq_specs(seq_len, (width,)),
        out_specs=(block,) * 4,
        name="attend_forward",
    )(*seq_info, proj, cosine, sine)


def attend_backward(seq_info, query, key, value, grad, cosine, sine):
    seq_len, (rows, local_dim) = cosine.shape[0], query.shape
    return pl.pallas_call(
        attend_back_kernel,
        grid=(rows // seq_len,),
        out_shape=jax.ShapeDtypeStruct((rows, 3 * local_dim), jnp.bfloat16),
        in_specs=seq_specs(seq_len, (local_dim,) * 4),
        out_specs=pl.BlockSpec((seq_len, 3 * local_dim), lambda seq: (seq, 0)),
        name="attend_backward",
    )(*seq_info, query, key, value, grad, cosine, sine)


def norm_forward(hidden, norm_gain, norm_bias):
    row_mean = jnp.mean(hidden, -1, keepdims=True)
    centred = hidden - row_mean
    variance = jnp.mean(centred * centred, -1, keepdims=True)
    inv_std = lax.rsqrt(variance + norm_eps)
    normed = centred * inv_std
    return (normed * norm_gain + norm_bias, normed, inv_std)


def norm_backward(grad_rows, normed, inv_std, norm_gain):
    grad_normed = grad_rows * norm_gain
    mean_grad = jnp.mean(grad_normed, -1, keepdims=True)
    mean_proj = jnp.mean(grad_normed * normed, -1, keepdims=True)
    grad_in = inv_std * (grad_normed - mean_grad - normed * mean_proj)
    return (grad_in, jnp.sum(grad_rows * normed, 0), jnp.sum(grad_rows, 0))


def adamw(weight, gradient, first_moment, second, step_rate):
    first_new = beta_one * first_moment + (1.0 - beta_one) * gradient
    second_new = beta_two * second + (1.0 - beta_two) * gradient * gradient
    first_hat = first_new / (1.0 - beta_one**STEP)
    second_hat = second_new / (1.0 - beta_two**STEP)
    weight_new = weight - step_rate * (
        first_hat / (jnp.sqrt(second_hat) + adam_eps) + decay_rate * weight
    )
    return (weight_new, first_new, second_new)


def swap(values, axis, bit):
    size = lax.axis_size(axis)
    return lax.ppermute(values, axis, [(at, at ^ bit) for at in range(size)])


def sum_everywhere(values):
    for axis in ("mp", "dp"):
        bit = 1
        while bit < lax.axis_size(axis):
            values = values + swap(values, axis, bit)
            bit *= 2
    return values


def gather_near(rows):
    half = rows.shape[0] // 2
    near_x, near_y = swap(rows, "mp", 2), swap(rows, "mp", 4)
    far_low, far_high = swap(near_x[:half], "mp", 4), swap(near_y[half:], "mp", 2)
    mates = [swap(part, "mp", 1) for part in (rows, near_x, near_y, far_low, far_high)]
    return jnp.concatenate(
        [rows, mates[0], near_x, mates[1], near_y, mates[2], far_low, far_high, mates[3], mates[4]],
        0,
    )


def scatter_near(whole):
    own_rows = whole.shape[0] // 8
    half = own_rows // 2
    blocks = [whole[at * own_rows : (at + 1) * own_rows] for at in range(8)]
    sums = [
        blocks[at].astype(jnp.float32) + swap(blocks[at + 1], "mp", 1).astype(jnp.float32)
        for at in range(0, 8, 2)
    ]
    far = sums[3].astype(jnp.bfloat16)
    far_low, far_high = swap(far[:half], "mp", 4), swap(far[half:], "mp", 2)
    x_low = (sums[1][:half] + far_low.astype(jnp.float32)).astype(jnp.bfloat16)
    y_high = (sums[2][half:] + far_high.astype(jnp.float32)).astype(jnp.bfloat16)
    x_high, y_low = sums[1][half:].astype(jnp.bfloat16), sums[2][:half].astype(jnp.bfloat16)
    x_low, x_high = swap(x_low, "mp", 2), swap(x_high, "mp", 2)
    y_low, y_high = swap(y_low, "mp", 4), swap(y_high, "mp", 4)
    across_x = jnp.concatenate([x_low, x_high], 0).astype(jnp.float32)
    across_y = jnp.concatenate([y_low, y_high], 0).astype(jnp.float32)
    return sums[0] + across_x + across_y


def gather_all(rows):
    return lax.all_gather(rows, "mp", axis=0, tiled=True)


def scatter_all(whole):
    return lax.psum_scatter(whole, "mp", scatter_dimension=0, tiled=True).astype(jnp.float32)


def adamw_as(order, weight, gradient, first_moment, second, step_rate, scale):
    turned = [jnp.transpose(rows, order) for rows in (weight, first_moment, second)]
    rank = len(order)
    gradient = with_layout_constraint(gradient, Layout(major_to_minor=tuple(range(rank))))
    gradient = gradient.astype(jnp.float32) * scale
    news = adamw(turned[0], gradient, turned[1], turned[2], step_rate)
    back = tuple(order.index(dim) for dim in range(rank))
    stored = Layout(major_to_minor=order)
    return tuple(with_layout_constraint(jnp.transpose(rows, back), stored) for rows in news)


def local(
    block_input,
    out_cotangent,
    objective,
    prefix_len,
    target_mask,
    qkv_weight,
    out_weight,
    gateup_weight,
    down_weight,
    norm_params,
    qkv_first,
    out_first,
    gateup_first,
    down_first,
    norm_first,
    qkv_second,
    out_second,
    gateup_second,
    down_second,
    norm_second,
):
    mp_index = lax.axis_index("mp")
    own_rows = block_input.shape[0]
    seq_count = objective.shape[0]
    seq_len = own_rows * lax.axis_size("mp") // seq_count
    shard_rows, _, local_dim = qkv_weight.shape
    local_units = gateup_weight.shape[2]
    near = lax.axis_size("mp") == 8 and seq_count == 4 and own_rows % 32 == 0
    if near:
        gather_rows, scatter_rows = gather_near, scatter_near
        place = jnp.stack([mp_index // 2, (mp_index % 2) * own_rows]).astype(jnp.int32)
    else:
        gather_rows, scatter_rows = gather_all, scatter_all
        place = jnp.zeros((2,), jnp.int32)
    seq_info = (objective, prefix_len, place)
    cosine, sine = rope_tables(jnp.arange(seq_len, dtype=jnp.int32) ^ place[1], HD)

    qkv_low = qkv_weight.astype(jnp.bfloat16).reshape(shard_rows, 3 * local_dim)
    qkv_full = lax.all_gather(qkv_low, "dp", axis=0, tiled=True)
    out_full = lax.all_gather(out_weight.astype(jnp.bfloat16), "dp", axis=1, tiled=True)
    gateup_low = jnp.transpose(gateup_weight, (1, 2, 0)).astype(jnp.bfloat16)
    gateup_full = lax.all_gather(gateup_low, "dp", axis=2, tiled=True)
    down_full = lax.all_gather(down_weight.astype(jnp.bfloat16), "dp", axis=1, tiled=True)

    mask_f32 = target_mask.astype(jnp.float32)
    target_count = sum_everywhere(jnp.full((8, 128), jnp.sum(mask_f32)))[0, 0]

    inputs = gather_rows(block_input)
    proj = jnp.dot(inputs, qkv_full, preferred_element_type=jnp.float32)
    *kept, attended = attend_forward(seq_info, proj, cosine, sine)
    attn_own = scatter_rows(jnp.dot(attended, out_full, preferred_element_type=jnp.bfloat16))
    hidden_one = deep_alpha * block_input.astype(jnp.float32) + attn_own
    middle, normed_one, inv_one = norm_forward(hidden_one, norm_params[0], norm_params[1])
    middle_low = gather_rows(middle.astype(jnp.bfloat16))

    live_units = (mp_index * local_units + jnp.arange(local_units) < FF).astype(jnp.float32)
    gate_up = jnp.einsum(
        "td,cfd->ctf", middle_low, gateup_full, preferred_element_type=jnp.float32
    )
    hidden_low = (jax.nn.gelu(gate_up[0]) * gate_up[1] * live_units).astype(jnp.bfloat16)
    ffn_own = scatter_rows(jnp.dot(hidden_low, down_full, preferred_element_type=jnp.bfloat16))
    hidden_two = deep_alpha * middle + ffn_own
    output_rows, normed_two, inv_two = norm_forward(hidden_two, norm_params[2], norm_params[3])
    grad_rows = out_cotangent.astype(jnp.float32) * mask_f32[:, None]
    grad_two, gain_two, bias_two = norm_backward(grad_rows, normed_two, inv_two, norm_params[2])

    ffn_back = gather_rows(grad_two.astype(jnp.bfloat16))
    down_grad = jnp.einsum("tf,td->fd", hidden_low, ffn_back, preferred_element_type=jnp.bfloat16)
    ffn_back, down_grad = lax.optimization_barrier((ffn_back, down_grad))
    down_grad = lax.psum_scatter(down_grad, "dp", scatter_dimension=1, tiled=True)
    gate_act, gelu_pull = jax.vjp(jax.nn.gelu, gate_up[0])
    grad_hidden = (
        jnp.einsum("td,fd->tf", ffn_back, down_full, preferred_element_type=jnp.float32)
        * live_units
    )
    grad_gate = gelu_pull(grad_hidden * gate_up[1])[0]
    grad_up = grad_hidden * gate_act
    grad_gateup = jnp.stack([grad_gate, grad_up], 0).astype(jnp.bfloat16)
    middle_part = jnp.einsum(
        "ctf,cfd->td", grad_gateup, gateup_full, preferred_element_type=jnp.bfloat16
    )
    middle_low, down_grad = lax.optimization_barrier((middle_low, down_grad))
    gateup_grad = jnp.einsum(
        "ctf,td->cfd", grad_gateup, middle_low, preferred_element_type=jnp.bfloat16
    )
    grad_middle = scatter_rows(middle_part) + deep_alpha * grad_two
    grad_one, gain_one, bias_one = norm_backward(grad_middle, normed_one, inv_one, norm_params[0])

    grad_one_low, gateup_grad = lax.optimization_barrier(
        (grad_one.astype(jnp.bfloat16), gateup_grad)
    )
    gateup_grad = with_layout_constraint(
        lax.psum_scatter(gateup_grad, "dp", scatter_dimension=2, tiled=True),
        Layout(major_to_minor=(0, 1, 2)),
    )
    attn_back = gather_rows(grad_one_low)
    grad_attended = jnp.einsum(
        "td,ed->te", attn_back, out_full, preferred_element_type=jnp.bfloat16
    )
    grad_proj = attend_backward(seq_info, *kept, grad_attended, cosine, sine)
    attended, grad_proj = lax.optimization_barrier((attended, grad_proj))
    attend_grad = jnp.concatenate(
        [
            jnp.einsum("te,td->ed", left, right, preferred_element_type=jnp.bfloat16)
            for left, right in ((attended, attn_back), (grad_proj, inputs))
        ],
        0,
    )
    grad_proj, attend_grad = lax.optimization_barrier((grad_proj, attend_grad))
    attend_grad, gateup_grad = lax.optimization_barrier((attend_grad, gateup_grad))
    attend_grad = lax.psum_scatter(attend_grad, "dp", scatter_dimension=1, tiled=True)
    input_raw = (
        scatter_rows(
            jnp.einsum("te,de->td", grad_proj, qkv_full, preferred_element_type=jnp.bfloat16)
        )
        + deep_alpha * grad_one
    )
    norm_grad = jnp.stack([gain_one, bias_one, gain_two, bias_two], 0)
    norm_grad, input_raw = lax.optimization_barrier((norm_grad, input_raw))
    norm_grad = sum_everywhere(norm_grad)
    rate_list = (D ** (-0.5), 0.5, D ** (-0.5), (FF_PAD // 64) ** (-0.5), 0.4)
    scale = 1.0 / target_count
    gateup_res = adamw_as(
        (2, 1, 0),
        gateup_weight,
        gateup_grad.transpose(1, 0, 2),
        gateup_first,
        gateup_second,
        rate_list[2],
        scale,
    )
    down_res = adamw_as(
        (0, 1), down_weight, down_grad, down_first, down_second, rate_list[3], scale
    )
    attend_grad, gateup_res, down_res = lax.optimization_barrier(
        (attend_grad, gateup_res, down_res)
    )
    out_grad = attend_grad[:local_dim]
    qkv_grad = attend_grad[local_dim:].reshape(3, local_dim, shard_rows)
    qkv_res = adamw_as(
        (1, 0, 2), qkv_weight, qkv_grad.transpose(0, 2, 1), qkv_first, qkv_second, rate_list[0], scale
    )
    out_res = adamw_as((0, 1), out_weight, out_grad, out_first, out_second, rate_list[1], scale)
    norm_res = adamw(norm_params, norm_grad * scale, norm_first, norm_second, rate_list[4])
    return (
        output_rows.astype(jnp.bfloat16),
        input_raw * scale,
        qkv_res[0],
        qkv_res[1],
        qkv_res[2],
        out_res[0],
        out_res[1],
        out_res[2],
        gateup_res[0],
        gateup_res[1],
        gateup_res[2],
        down_res[0],
        down_res[1],
        down_res[2],
        norm_res[0],
        norm_res[1],
        norm_res[2],
    )


def solution(mesh):
    return jax.shard_map(
        local,
        mesh=mesh,
        in_specs=(
            P(("dp", "mp"), None),
            P(("dp", "mp"), None),
            P("dp"),
            P("dp"),
            P(("dp", "mp")),
            P("dp", None, "mp"),
            P("mp", "dp"),
            P("dp", None, "mp"),
            P("mp", "dp"),
            P(),
            P("dp", None, "mp"),
            P("mp", "dp"),
            P("dp", None, "mp"),
            P("mp", "dp"),
            P(),
            P("dp", None, "mp"),
            P("mp", "dp"),
            P("dp", None, "mp"),
            P("mp", "dp"),
            P(),
        ),
        out_specs=(
            P(("dp", "mp"), None),
            P(("dp", "mp"), None),
            P("dp", None, "mp"),
            P("dp", None, "mp"),
            P("dp", None, "mp"),
            P("mp", "dp"),
            P("mp", "dp"),
            P("mp", "dp"),
            P("dp", None, "mp"),
            P("dp", None, "mp"),
            P("dp", None, "mp"),
            P("mp", "dp"),
            P("mp", "dp"),
            P("mp", "dp"),
            P(),
            P(),
            P(),
        ),
        check_vma=False,
    )
```

time: 719 us -> 733 us (1.019)
  waiting for transfers between devices: 248 us -> 326 us
  Pallas kernels: 71.1 us -> 24.3 us
  local copies, waits for them, and re-layouts: 93.4 us -> 68.1 us
  other arithmetic: 68.4 us -> 80.9 us
  matrix products: 153 us -> 143 us
    ppermute x86, waiting for transfers between devices: 216 us -> 268 us  [swap(): return lax.ppermute(values, axis, [(at, at ^ bit) for at in range(size)])]
    pallas_call x9 -> x2, Pallas kernels: 71.1 us -> 24.3 us  [the longest x1 14.3 us: attend_backward(): pl.pallas_call(attend_back_kernel, grid=(rows // seq_len,), out_shape=jax...]
    transpose x0 -> x2, other arithmetic: none -> 21.4 us  [adamw_as(): jnp.transpose(rows, back)]
    unnamed x260 -> x105, local copies, waits for them, and re-layouts: 69.4 us -> 48.1 us
    dot_general x32 -> x11, matrix products: 134 us -> 114 us  [the longest x1 18.3 us: local(): jnp.einsum('td,cfd->ctf', middle_low, gateup_full, preferred_element_type...]
    ppermute x86, starting transfers between devices: 54 us -> 64.6 us  [swap(): return lax.ppermute(values, axis, [(at, at ^ bit) for at in range(size)])]
    all_gather x1, waiting for transfers between devices: 0.02 us -> 10.5 us  [local(): qkv_full = lax.all_gather(qkv_low, 'dp', axis=0, tiled=True)]
    all_gather x1, waiting for transfers between devices: 21.8 us -> 31.7 us  [local(): lax.all_gather(down_weight.astype(jnp.bfloat16), 'dp', axis=1, tiled=True)]
  transfers between devices with their start and end apart: 95 -> 93, of which waited for: 37 -> 48; matrix products, arithmetic and copies ran while one was open for 39% -> 24% of each run, Pallas kernels for 10% -> 3%
where the time goes in v3:
time: 733 us; the launch traced here: 723 us
  waiting for transfers between devices  326 us (44%)
  matrix products  143 us (20%)
  other arithmetic  80.9 us (11%)
  local copies, waits for them, and re-layouts  68.1 us (9%)
  starting transfers between devices  64.9 us (9%)
  Pallas kernels  24.3 us (3%)
  between operations  16.2 us (2%)
    ppermute x86, waiting for transfers between devices, swap(): return lax.ppermute(values, axis, [(at, at ^ bit) for at in range(size)])  268 us
    ppermute x86, starting transfers between devices, swap(): return lax.ppermute(values, axis, [(at, at ^ bit) for at in range(size)])  64.6 us
    unnamed x105, local copies, waits for them, and re-layouts  48.1 us
    all_gather x1, waiting for transfers between devices, local(): lax.all_gather(down_weight.astype(jnp.bfloat16), 'dp', axis=1, tiled=True)  31.7 us
    dot_general x1, matrix products, local(): jnp.einsum('ctf,cfd->td', grad_gateup, gateup_full, preferred_element_typ...  28.5 us
    transpose x2, other arithmetic, adamw_as(): jnp.transpose(rows, back)  21.4 us
    dot_general x1, matrix products, local(): jnp.einsum('td,cfd->ctf', middle_low, gateup_full, preferred_element_type...  18.3 us
    dot_general x1, matrix products, local(): jnp.einsum('td,fd->tf', ffn_back, down_full, preferred_element_type=jnp.f...  17.6 us
  transfers between devices with their start and end apart: 93, of which 48 were waited for; matrix products, arithmetic and copies ran while one was open for 24% of the time, Pallas kernels for 3%

profile of v3, /device:TPU:0, one launch (start us, length us, event | category | flops | bytes accessed | tf_op | source)
XLA Modules:
  0.0 723.0 jit_solution(17171148046327506585)
XLA Ops:
  15.4 3.8 convert_bitcast_fusion
  19.3 17.7 %collective-permute-done.1 = bf16[256,2048]{1,0:T(8,128)(2,1)S(1)} collective-permute-done((bf16[256,2048]{1,0:T(8,128)(2,1)S(1)}, bf16[256,2048]{1,0:T(8,128)(2,1)S(1)}, u32[]{:S(2)}, u32[]{:S(2)}) %collective-permute-start.1) | collective-permute-done | bytes 1048608 | tf_op jit(solution)/shard_map/ppermute | solution.py:190
  49.5 7.0 collective-permute-done.5
  65.9 10.5 %all-gather.5.cloned.1.call-done = bf16[2048,768]{0,1:T(8,128)(2,1)} async-done(((bf16[512,768]{0,1:T(8,128)(2,1)}), bf16[2048,768]{0,1:T(8,128)(2,1)}) %all-gather.5.cloned.1.call-update) | async-done | bytes 3145744 | tf_op jit(solution)/shard_map/all_gather | solution.py:291
  76.4 11.7 %fusion.67.proj_ref = f32[2048,768]{1,0:T(8,128)} fusion(bf16[2048,2048]{1,0:T(8,128)(2,1)} %constant_dynamic-update-slice_fusion, bf16[2048,768]{0,1:T(8,128)(2,1)} %all-gather.5.cloned.1.call-done), kind=kOutput, calls=%fused_computation.199 | convolution fusion | flops 6442450944 | bytes 17825792 | tf_op jit(solution)/shard_map/dot_general | solution.py:301
  88.1 10.0 %attend_forward.1 = (bf16[2048,256]{1,0:T(8,128)(2,1)}, bf16[2048,256]{1,0:T(8,128)(2,1)}, bf16[2048,256]{1,0:T(8,128)(2,1)}, bf16[2048,256]{1,0:T(8,128)(2,1)}) custom-call(s32[4]{0:T(128)} %objective_ref.3, s32[4]{0:T(128)} %prefix_ref.3, s32[2]{0:T(128)} %pad_add_fusion.place_ref, f32[2048,768]{1,0:T(8,128)} %fusion.67.proj_ref, ...), custom_call_target="tpu_custom_call" | custom-call | tf_op jit(solution)/shard_map/attend_forward/pallas_call | solution.py:138
  98.0 7.1 all-gather.7.cloned.1.call-done
  105.2 3.9 fusion.68
  123.2 9.0 %collective-permute-done.17 = bf16[128,2048]{0,1:T(8,128)(2,1)S(1)} collective-permute-done((bf16[128,2048]{0,1:T(8,128)(2,1)S(1)}, bf16[128,2048]{0,1:T(8,128)(2,1)S(1)}, u32[]{:S(2)}, u32[]{:S(2)}) %collective-permute-start.17) | collective-permute-done | bytes 524320 | tf_op jit(solution)/shard_map/ppermute | solution.py:190
  138.6 6.4 collective-permute-done.16
  145.0 10.1 %collective-permute-done.18 = bf16[128,2048]{0,1:T(8,128)(2,1)} collective-permute-done((bf16[128,2048]{0,1:T(8,128)(2,1)}, bf16[128,2048]{0,1:T(8,128)(2,1)}, u32[]{:S(2)}, u32[]{:S(2)}) %collective-permute-start.18) | collective-permute-done | bytes 524320 | tf_op jit(solution)/shard_map/ppermute | solution.py:190
  162.5 22.3 %collective-permute-done.20 = bf16[256,2048]{0,1:T(8,128)(2,1)} collective-permute-done((bf16[256,2048]{0,1:T(8,128)(2,1)}, bf16[256,2048]{0,1:T(8,128)(2,1)}, u32[]{:S(2)}, u32[]{:S(2)}) %collective-permute-start.20) | collective-permute-done | bytes 1048608 | tf_op jit(solution)/shard_map/ppermute | solution.py:190
  193.8 7.5 %collective-permute-done.24 = bf16[128,2048]{0,1:T(8,128)(2,1)S(1)} collective-permute-done((bf16[128,2048]{0,1:T(8,128)(2,1)S(1)}, bf16[128,2048]{0,1:T(8,128)(2,1)S(1)}, u32[]{:S(2)}, u32[]{:S(2)}) %collective-permute-start.24) | collective-permute-done | bytes 524320 | tf_op jit(solution)/shard_map/ppermute | solution.py:190
  210.8 18.3 %fusion.11 = f32[2,2048,684]{1,2,0:T(8,128)S(1)} fusion(bf16[2048,2048]{0,1:T(8,128)(2,1)} %constant_dynamic-update-slice_fusion.10, bf16[2,684,2048]{2,0,1:T(2,128)(2,1)} %all-gather.9.cloned.1.call-done), kind=kOutput, calls=%fused_computation.20 | convolution fusion | flops 11475615744 | bytes 25198592 | tf_op jit(solution)/shard_map/td,cfd->ctf/dot_general | solution.py:309
  229.1 4.1 copy-done.5
  233.2 3.6 multiply_convert_fusion.1
  236.8 31.7 %all-gather.11.cloned.1.call-done = bf16[684,2048]{1,0:T(8,128)(2,1)} async-done(((bf16[684,512]{1,0:T(8,128)(2,1)}), bf16[684,2048]{1,0:T(8,128)(2,1)}) %all-gather.11.cloned.1.call-update) | async-done | bytes 2801680 | tf_op jit(solution)/shard_map/all_gather | solution.py:295
  268.5 9.4 %fusion.69 = bf16[2048,2048]{0,1:T(8,128)(2,1)S(1)} fusion(bf16[2048,684]{0,1:T(8,128)(2,1)} %multiply_convert_fusion.1, bf16[684,2048]{1,0:T(8,128)(2,1)} %all-gather.11.cloned.1.call-done), kind=kOutput, calls=%fused_computation.201 | convolution fusion | flops 5737807872 | bytes 13991936 | tf_op jit(solution)/shard_map/dot_general | solution.py:313
  291.9 9.0 %collective-permute-done.36 = bf16[128,2048]{0,1:T(8,128)(2,1)S(1)} collective-permute-done((bf16[128,2048]{0,1:T(8,128)(2,1)S(1)}, bf16[128,2048]{0,1:T(8,128)(2,1)S(1)}, u32[]{:S(2)}, u32[]{:S(2)}) %collective-permute-start.36) | collective-permute-done | bytes 524320 | tf_op jit(solution)/shard_map/ppermute | solution.py:190
  307.2 6.5 collective-permute-done.35
  313.7 10.1 %collective-permute-done.37 = bf16[128,2048]{0,1:T(8,128)(2,1)} collective-permute-done((bf16[128,2048]{0,1:T(8,128)(2,1)}, bf16[128,2048]{0,1:T(8,128)(2,1)}, u32[]{:S(2)}, u32[]{:S(2)}) %collective-permute-start.37) | collective-permute-done | bytes 524320 | tf_op jit(solution)/shard_map/ppermute | solution.py:190
  332.5 22.0 %collective-permute-done.39 = bf16[256,2048]{0,1:T(8,128)(2,1)S(1)} collective-permute-done((bf16[256,2048]{0,1:T(8,128)(2,1)S(1)}, bf16[256,2048]{0,1:T(8,128)(2,1)S(1)}, u32[]{:S(2)}, u32[]{:S(2)}) %collective-permute-start.39) | collective-permute-done | bytes 1048608 | tf_op jit(solution)/shard_map/ppermute | solution.py:190
  358.3 11.0 %collective-permute-done.43 = bf16[128,2048]{0,1:T(8,128)(2,1)S(1)} collective-permute-done((bf16[128,2048]{0,1:T(8,128)(2,1)S(1)}, bf16[128,2048]{0,1:T(8,128)(2,1)S(1)}, u32[]{:S(2)}, u32[]{:S(2)}) %collective-permute-start.43) | collective-permute-done | bytes 524320 | tf_op jit(solution)/shard_map/ppermute | solution.py:190
  375.9 7.4 %fusion.70 = bf16[684,2048]{1,0:T(8,128)(2,1)} fusion(bf16[2048,684]{0,1:T(8,128)(2,1)S(1)} %copy-done.16, bf16[2048,2048]{0,1:T(8,128)(2,1)S(1)} %constant_dynamic-update-slice_fusion.20), kind=kOutput, calls=%fused_computation.202 | convolution fusion | flops 5737807872 | bytes 13991936 | tf_op jit(solution)/shard_map/tf,td->fd/dot_general | solution.py:320
  383.3 17.6 %fusion.17 = (bf16[1,2048,684]{1,2,0:T(8,128)(2,1)}, bf16[1,2048,684]{1,2,0:T(8,128)(2,1)}) fusion(f32[2,2048,684]{1,2,0:T(8,128)} %copy-done.5, f32[684]{0:T(1024)S(1)} %fusion.45, bf16[2048,2048]{0,1:T(8,128)(2,1)} %copy-done.26, bf16[684,2048]{1,0:T(8,128)(2,1)} %all-gather.11.cloned.1.call-done), kind=kOutput, calls=%fused_computation.27 | convolution fusion | flops 5772828672 | bytes 28002992 | tf_op jit(solution)/shard_map/td,fd->tf/dot_general | solution.py:325
  400.9 28.5 %convolution_bitcast_fusion = bf16[2048,2048]{0,1:T(8,128)(2,1)S(1)} fusion(bf16[2,684,2048]{2,0,1:T(2,128)(2,1)} %all-gather.9.cloned.1.call-done, bf16[1,2048,684]{1,2,0:T(8,128)(2,1)} %get-tuple-element.145, bf16[1,2048,684]{1,2,0:T(8,128)(2,1)} %get-tuple-element.144), kind=kOutput, calls=%fused_computation.6 | convolution fusion | flops 11478417408 | bytes 19595264 | tf_op jit(solution)/shard_map/ctf,cfd->td/dot_general | solution.py:331
  440.0 3.5 convert_add_fusion.3
  448.0 10.4 %collective-permute-done.55 = bf16[128,2048]{0,1:T(8,128)(2,1)S(1)} collective-permute-done((bf16[128,2048]{0,1:T(8,128)(2,1)S(1)}, bf16[128,2048]{0,1:T(8,128)(2,1)S(1)}, u32[]{:S(2)}, u32[]{:S(2)}) %collective-permute-start.55) | collective-permute-done | bytes 524320 | tf_op jit(solution)/shard_map/ppermute | solution.py:190
  461.3 9.9 %collective-permute-done.54 = bf16[128,2048]{0,1:T(8,128)(2,1)S(1)} collective-permute-done((bf16[128,2048]{0,1:T(8,128)(2,1)S(1)}, bf16[128,2048]{0,1:T(8,128)(2,1)S(1)}, u32[]{:S(2)}, u32[]{:S(2)}) %collective-permute-start.54) | collective-permute-done | bytes 524320 | tf_op jit(solution)/shard_map/ppermute | solution.py:190
  471.2 10.1 %collective-permute-done.56 = bf16[128,2048]{0,1:T(8,128)(2,1)S(1)} collective-permute-done((bf16[128,2048]{0,1:T(8,128)(2,1)S(1)}, bf16[128,2048]{0,1:T(8,128)(2,1)S(1)}, u32[]{:S(2)}, u32[]{:S(2)}) %collective-permute-start.56) | collective-permute-done | bytes 524320 | tf_op jit(solution)/shard_map/ppermute | solution.py:190
  481.3 3.6 multiply_reduce_fusion
  488.3 17.6 %fusion = bf16[2,684,2048]{2,1,0:T(8,128)(2,1)} fusion(bf16[2048,2048]{0,1:T(8,128)(2,1)} %constant_dynamic-update-slice_fusion.10, bf16[1,2048,684]{1,2,0:T(8,128)(2,1)} %get-tuple-element.145, bf16[1,2048,684]{1,2,0:T(8,128)(2,1)} %get-tuple-element.144), kind=kOutput, calls=%fused_computation | convolution fusion | flops 11478417408 | bytes 19595264 | tf_op jit(solution)/shard_map/ctf,td->cfd/dot_general | solution.py:335
  509.0 21.5 %collective-permute-done.58 = bf16[256,2048]{0,1:T(8,128)(2,1)S(1)} collective-permute-done((bf16[256,2048]{0,1:T(8,128)(2,1)S(1)}, bf16[256,2048]{0,1:T(8,128)(2,1)S(1)}, u32[]{:S(2)}, u32[]{:S(2)}) %collective-permute-start.58) | collective-permute-done | bytes 1048608 | tf_op jit(solution)/shard_map/ppermute | solution.py:190
  534.1 10.8 %collective-permute-done.62 = bf16[128,2048]{0,1:T(8,128)(2,1)S(1)} collective-permute-done((bf16[128,2048]{0,1:T(8,128)(2,1)S(1)}, bf16[128,2048]{0,1:T(8,128)(2,1)S(1)}, u32[]{:S(2)}, u32[]{:S(2)}) %collective-permute-start.62) | collective-permute-done | bytes 524320 | tf_op jit(solution)/shard_map/ppermute | solution.py:190
  548.4 3.7 fusion.71.grad_ref
  552.1 14.3 %attend_backward.1 = bf16[2048,768]{1,0:T(8,128)(2,1)} custom-call(s32[4]{0:T(128)} %objective_ref.3, s32[4]{0:T(128)} %prefix_ref.3, s32[2]{0:T(128)} %pad_add_fusion.place_ref, bf16[2048,256]{1,0:T(8,128)(2,1)} %get-tuple-element.44.query_ref, bf16[2048,256]{1,0:T(8,128)(2,1)} %get-tuple-element.45.key_ref, bf16[2048,256]{1,0:T(8,128)(2,1)} %get-tuple-element.46.value_ref, ...), custom_call_target="tpu_custom_call" | custom-call | tf_op jit(solution)/shard_map/attend_backward/pallas_call | solution.py:150
  566.4 5.9 fusion.72
  572.4 9.3 %fusion.73 = bf16[768,2048]{1,0:T(8,128)(2,1)S(1)} fusion(bf16[2048,768]{1,0:T(8,128)(2,1)S(1)} %copy-done.15, bf16[2048,2048]{1,0:T(8,128)(2,1)} %constant_dynamic-update-slice_fusion), kind=kOutput, calls=%fused_computation.205 | convolution fusion | flops 6442450944 | bytes 14680064 | tf_op jit(solution)/shard_map/te,td->ed/dot_general | solution.py:356
  584.2 9.5 %fusion.74 = bf16[2048,2048]{0,1:T(8,128)(2,1)S(1)} fusion(bf16[2048,768]{1,0:T(8,128)(2,1)} %attend_backward.1, bf16[2048,768]{0,1:T(8,128)(2,1)} %all-gather.5.cloned.1.call-done), kind=kOutput, calls=%fused_computation.206 | convolution fusion | flops 6442450944 | bytes 14680064 | tf_op jit(solution)/shard_map/te,de->td/dot_general | solution.py:366
  599.0 6.9 reduce-scatter.6.cloned.1.call-done
  613.7 10.4 %collective-permute-done.69 = bf16[128,2048]{0,1:T(8,128)(2,1)S(1)} collective-permute-done((bf16[128,2048]{0,1:T(8,128)(2,1)S(1)}, bf16[128,2048]{0,1:T(8,128)(2,1)S(1)}, u32[]{:S(2)}, u32[]{:S(2)}) %collective-permute-start.69) | collective-permute-done | bytes 524320 | tf_op jit(solution)/shard_map/ppermute | solution.py:190
  627.5 9.3 %collective-permute-done.71 = bf16[128,2048]{0,1:T(8,128)(2,1)S(1)} collective-permute-done((bf16[128,2048]{0,1:T(8,128)(2,1)S(1)}, bf16[128,2048]{0,1:T(8,128)(2,1)S(1)}, u32[]{:S(2)}, u32[]{:S(2)}) %collective-permute-start.71) | collective-permute-done | bytes 524320 | tf_op jit(solution)/shard_map/ppermute | solution.py:190
  636.8 9.8 %collective-permute-done.70 = bf16[128,2048]{0,1:T(8,128)(2,1)S(1)} collective-permute-done((bf16[128,2048]{0,1:T(8,128)(2,1)S(1)}, bf16[128,2048]{0,1:T(8,128)(2,1)S(1)}, u32[]{:S(2)}, u32[]{:S(2)}) %collective-permute-start.70) | collective-permute-done | bytes 524320 | tf_op jit(solution)/shard_map/ppermute | solution.py:190
  663.3 3.6 collective-permute-done.79
  668.5 4.3 collective-permute-done.80
  675.6 5.0 multiply_subtract_fusion
  680.6 3.7 collective-permute-start.85
  687.9 18.0 %fusion.50 = (f32[512,2,684]{0,1,2:T(2,128)}, f32[512,2,684]{0,1,2:T(2,128)}, f32[512,2,684]{0,1,2:T(2,128)}) fusion(f32[]{:T(128)} %bitcast.28, bf16[2,684,512]{2,1,0:T(8,128)(2,1)S(1)} %copy-done.22, f32[512,2,684]{0,1,2:T(2,128)} %param.37, f32[512,2,684]{0,1,2:T(2,128)} %param.32, f32[512,2,684]{0,1,2:T(2,128)} %param.27), kind=kLoop, calls=%fused_computation.187 | loop fusion | flops 11206656 | bytes 18210820 | tf_op jit(solution)/shard_map/transpose | solution.py:249
  (356 shorter events, 199.1 us)
Async XLA Ops:
  7.2 69.1 %all-gather.5.cloned.1.call-start = ((), (), s32[]{:S(2)}) async-start(), calls=%async_computation.3 | async-start | bytes 3932160 | tf_op jit(solution)/shard_map/all_gather | solution.py:291
  9.9 95.2 %all-gather.7.cloned.1.call-start = ((), (), s32[]{:S(2)}) async-start(), calls=%async_computation.4 | async-start | bytes 1310720 | tf_op jit(solution)/shard_map/all_gather | solution.py:292
  10.8 200.0 %all-gather.9.cloned.1.call-start = ((), (), s32[]{:S(2)}) async-start(), calls=%async_computation.5 | async-start | bytes 7004160 | tf_op jit(solution)/shard_map/all_gather | solution.py:294
  10.8 26.2 %collective-permute-start.1 = (bf16[256,2048]{1,0:T(8,128)(2,1)S(1)}, bf16[256,2048]{1,0:T(8,128)(2,1)S(1)}, u32[]{:S(2)}, u32[]{:S(2)}) collective-permute-start(bf16[256,2048]{1,0:T(8,128)(2,1)S(1)} %copy-done.13), channel_id=1, source_target_pairs={{0,2},{1,3},{2,0},{3,1},{4,6},{5,7},{6,4},{7,5},{8,10},{9,11},{10,... | collective-permute-start | bytes 3145736 | tf_op jit(solution)/shard_map/ppermute | solution.py:190
  13.9 32.2 %collective-permute-start = (bf16[256,2048]{1,0:T(8,128)(2,1)S(1)}, bf16[256,2048]{1,0:T(8,128)(2,1)}, u32[]{:S(2)}, u32[]{:S(2)}) collective-permute-start(bf16[256,2048]{1,0:T(8,128)(2,1)S(1)} %copy-done.13), channel_id=1, source_target_pairs={{0,1},{1,0},{2,3},{3,2},{4,5},{5,4},{6,7},{7,6},{8,9},{9,8},{10,11... | collective-permute-start | bytes 3145736 | tf_op jit(solution)/shard_map/ppermute | solution.py:190
  13.9 30.0 %collective-permute-start.3 = (bf16[256,2048]{1,0:T(8,128)(2,1)S(1)}, bf16[256,2048]{1,0:T(8,128)(2,1)S(1)}, u32[]{:S(2)}, u32[]{:S(2)}) collective-permute-start(bf16[256,2048]{1,0:T(8,128)(2,1)S(1)} %copy-done.13), channel_id=1, source_target_pairs={{0,4},{1,5},{2,6},{3,7},{4,0},{5,1},{6,2},{7,3},{8,12},{9,13},{10,... | collective-permute-start | bytes 3145736 | tf_op jit(solution)/shard_map/ppermute | solution.py:190
  19.2 249.3 %all-gather.11.cloned.1.call-start = ((), (), s32[]{:S(2)}) async-start(), calls=%async_computation.6 | async-start | bytes 3522560 | tf_op jit(solution)/shard_map/all_gather | solution.py:295
  37.0 21.0 %collective-permute-start.2 = (bf16[256,2048]{1,0:T(8,128)(2,1)S(1)}, bf16[256,2048]{1,0:T(8,128)(2,1)}, u32[]{:S(2)}, u32[]{:S(2)}) collective-permute-start(bf16[256,2048]{1,0:T(8,128)(2,1)S(1)} %collective-permute-done.1), channel_id=1, source_target_pairs={{0,1},{1,0},{2,3},{3,2},{4,5},{5,4},{6,7},{7,6},{8,9},{9,8},{10,11... | collective-permute-start | bytes 3145736 | tf_op jit(solution)/shard_map/ppermute | solution.py:190
  45.5 16.0 %collective-permute-start.4 = (bf16[256,2048]{1,0:T(8,128)(2,1)S(1)}, bf16[256,2048]{1,0:T(8,128)(2,1)S(1)}, u32[]{:S(2)}, u32[]{:S(2)}) collective-permute-start(bf16[256,2048]{1,0:T(8,128)(2,1)S(1)} %collective-permute-done.3), channel_id=1, source_target_pairs={{0,1},{1,0},{2,3},{3,2},{4,5},{5,4},{6,7},{7,6},{8,9},{9,8},{10,11... | collective-permute-start | bytes 3145736 | tf_op jit(solution)/shard_map/ppermute | solution.py:190
  118.8 15.7 %collective-permute-start.12 = (bf16[128,2048]{0,1:T(8,128)(2,1)S(1)}, bf16[128,2048]{0,1:T(8,128)(2,1)S(1)}, u32[]{:S(2)}, u32[]{:S(2)}) collective-permute-start(bf16[128,2048]{0,1:T(8,128)(2,1)S(1)} %get-tuple-element.187), channel_id=1, source_target_pairs={{0,4},{1,5},{2,6},{3,7},{4,0},{5,1},{6,2},{7,3},{8,12},{9,13},{10,... | collective-permute-start | bytes 1572872 | tf_op jit(solution)/shard_map/ppermute | solution.py:190
  120.3 18.3 %collective-permute-start.9 = (bf16[256,2048]{0,1:T(8,128)(2,1)}, bf16[256,2048]{0,1:T(8,128)(2,1)}, u32[]{:S(2)}, u32[]{:S(2)}) collective-permute-start(bf16[256,2048]{0,1:T(8,128)(2,1)} %get-tuple-element.167), channel_id=1, source_target_pairs={{0,1},{1,0},{2,3},{3,2},{4,5},{5,4},{6,7},{7,6},{8,9},{9,8},{10,11... | collective-permute-start | bytes 3145736 | tf_op jit(solution)/shard_map/ppermute | solution.py:190
  121.2 23.8 %collective-permute-start.16 = (bf16[128,2048]{0,1:T(8,128)(2,1)}, bf16[128,2048]{0,1:T(8,128)(2,1)}, u32[]{:S(2)}, u32[]{:S(2)}) collective-permute-start(bf16[128,2048]{0,1:T(8,128)(2,1)} %slice.450), channel_id=1, source_target_pairs={{0,4},{1,5},{2,6},{3,7},{4,0},{5,1},{6,2},{7,3},{8,12},{9,13},{10,... | collective-permute-start | bytes 1572872 | tf_op jit(solution)/shard_map/ppermute | solution.py:190
  122.6 22.4 %collective-permute-start.14 = (bf16[128,2048]{0,1:T(8,128)(2,1)}, bf16[128,2048]{0,1:T(8,128)(2,1)}, u32[]{:S(2)}, u32[]{:S(2)}) collective-permute-start(bf16[128,2048]{0,1:T(8,128)(2,1)} %slice.451), channel_id=1, source_target_pairs={{0,2},{1,3},{2,0},{3,1},{4,6},{5,7},{6,4},{7,5},{8,10},{9,11},{10,... | collective-permute-start | bytes 1572872 | tf_op jit(solution)/shard_map/ppermute | solution.py:190
  133.1 22.0 %collective-permute-start.18 = (bf16[128,2048]{0,1:T(8,128)(2,1)}, bf16[128,2048]{0,1:T(8,128)(2,1)}, u32[]{:S(2)}, u32[]{:S(2)}) collective-permute-start(bf16[128,2048]{0,1:T(8,128)(2,1)} %fusion.37), channel_id=1, source_target_pairs={{0,4},{1,5},{2,6},{3,7},{4,0},{5,1},{6,2},{7,3},{8,12},{9,13},{10,... | collective-permute-start | bytes 1572872 | tf_op jit(solution)/shard_map/ppermute | solution.py:190
  135.4 19.7 %collective-permute-start.13 = (bf16[128,2048]{0,1:T(8,128)(2,1)}, bf16[128,2048]{0,1:T(8,128)(2,1)}, u32[]{:S(2)}, u32[]{:S(2)}) collective-permute-start(bf16[128,2048]{0,1:T(8,128)(2,1)} %fusion.38), channel_id=1, source_target_pairs={{0,2},{1,3},{2,0},{3,1},{4,6},{5,7},{6,4},{7,5},{8,10},{9,11},{10,... | collective-permute-start | bytes 1572872 | tf_op jit(solution)/shard_map/ppermute | solution.py:190
  160.5 24.4 %collective-permute-start.20 = (bf16[256,2048]{0,1:T(8,128)(2,1)}, bf16[256,2048]{0,1:T(8,128)(2,1)}, u32[]{:S(2)}, u32[]{:S(2)}) collective-permute-start(bf16[256,2048]{0,1:T(8,128)(2,1)} %get-tuple-element.141), channel_id=1, source_target_pairs={{0,2},{1,3},{2,0},{3,1},{4,6},{5,7},{6,4},{7,5},{8,10},{9,11},{10,... | collective-permute-start | bytes 3145736 | tf_op jit(solution)/shard_map/ppermute | solution.py:190
  161.0 27.5 %collective-permute-start.22 = (bf16[256,2048]{0,1:T(8,128)(2,1)}, bf16[256,2048]{0,1:T(8,128)(2,1)S(1)}, u32[]{:S(2)}, u32[]{:S(2)}) collective-permute-start(bf16[256,2048]{0,1:T(8,128)(2,1)} %get-tuple-element.141), channel_id=1, source_target_pairs={{0,4},{1,5},{2,6},{3,7},{4,0},{5,1},{6,2},{7,3},{8,12},{9,13},{10,... | collective-permute-start | bytes 3145736 | tf_op jit(solution)/shard_map/ppermute | solution.py:190
  162.5 26.7 %collective-permute-start.19 = (bf16[256,2048]{0,1:T(8,128)(2,1)}, bf16[256,2048]{0,1:T(8,128)(2,1)}, u32[]{:S(2)}, u32[]{:S(2)}) collective-permute-start(bf16[256,2048]{0,1:T(8,128)(2,1)} %get-tuple-element.141), channel_id=1, source_target_pairs={{0,1},{1,0},{2,3},{3,2},{4,5},{5,4},{6,7},{7,6},{8,9},{9,8},{10,11... | collective-permute-start | bytes 3145736 | tf_op jit(solution)/shard_map/ppermute | solution.py:190
  184.9 17.8 %collective-permute-start.21 = (bf16[256,2048]{0,1:T(8,128)(2,1)}, bf16[256,2048]{0,1:T(8,128)(2,1)}, u32[]{:S(2)}, u32[]{:S(2)}) collective-permute-start(bf16[256,2048]{0,1:T(8,128)(2,1)} %collective-permute-done.20), channel_id=1, source_target_pairs={{0,1},{1,0},{2,3},{3,2},{4,5},{5,4},{6,7},{7,6},{8,9},{9,8},{10,11... | collective-permute-start | bytes 3145736 | tf_op jit(solution)/shard_map/ppermute | solution.py:190
  185.8 302.5 %reduce-scatter.4.cloned.1.call-start = ((), (), s32[]{:S(2)}) async-start(), calls=%async_computation.7 | async-start | bytes 3522560 | tf_op jit(solution)/shard_map/reduce_scatter | solution.py:322
  189.2 16.9 %collective-permute-start.23 = (bf16[256,2048]{0,1:T(8,128)(2,1)S(1)}, bf16[256,2048]{0,1:T(8,128)(2,1)S(1)}, u32[]{:S(2)}, u32[]{:S(2)}) collective-permute-start(bf16[256,2048]{0,1:T(8,128)(2,1)S(1)} %collective-permute-done.22), channel_id=1, source_target_pairs={{0,1},{1,0},{2,3},{3,2},{4,5},{5,4},{6,7},{7,6},{8,9},{9,8},{10,11... | collective-permute-start | bytes 3145736 | tf_op jit(solution)/shard_map/ppermute | solution.py:190
  287.6 15.7 %collective-permute-start.31 = (bf16[128,2048]{0,1:T(8,128)(2,1)S(1)}, bf16[128,2048]{0,1:T(8,128)(2,1)S(1)}, u32[]{:S(2)}, u32[]{:S(2)}) collective-permute-start(bf16[128,2048]{0,1:T(8,128)(2,1)S(1)} %get-tuple-element.185), channel_id=1, source_target_pairs={{0,4},{1,5},{2,6},{3,7},{4,0},{5,1},{6,2},{7,3},{8,12},{9,13},{10,... | collective-permute-start | bytes 1572872 | tf_op jit(solution)/shard_map/ppermute | solution.py:190
  289.0 18.1 %collective-permute-start.28 = (bf16[256,2048]{0,1:T(8,128)(2,1)}, bf16[256,2048]{0,1:T(8,128)(2,1)}, u32[]{:S(2)}, u32[]{:S(2)}) collective-permute-start(bf16[256,2048]{0,1:T(8,128)(2,1)} %get-tuple-element.160), channel_id=1, source_target_pairs={{0,1},{1,0},{2,3},{3,2},{4,5},{5,4},{6,7},{7,6},{8,9},{9,8},{10,11... | collective-permute-start | bytes 3145736 | tf_op jit(solution)/shard_map/ppermute | solution.py:190
  289.9 23.8 %collective-permute-start.35 = (bf16[128,2048]{0,1:T(8,128)(2,1)}, bf16[128,2048]{0,1:T(8,128)(2,1)}, u32[]{:S(2)}, u32[]{:S(2)}) collective-permute-start(bf16[128,2048]{0,1:T(8,128)(2,1)} %slice.448), channel_id=1, source_target_pairs={{0,4},{1,5},{2,6},{3,7},{4,0},{5,1},{6,2},{7,3},{8,12},{9,13},{10,... | collective-permute-start | bytes 1572872 | tf_op jit(solution)/shard_map/ppermute | solution.py:190
  291.3 22.4 %collective-permute-start.33 = (bf16[128,2048]{0,1:T(8,128)(2,1)}, bf16[128,2048]{0,1:T(8,128)(2,1)}, u32[]{:S(2)}, u32[]{:S(2)}) collective-permute-start(bf16[128,2048]{0,1:T(8,128)(2,1)} %slice.449), channel_id=1, source_target_pairs={{0,2},{1,3},{2,0},{3,1},{4,6},{5,7},{6,4},{7,5},{8,10},{9,11},{10,... | collective-permute-start | bytes 1572872 | tf_op jit(solution)/shard_map/ppermute | solution.py:190
  301.8 22.0 %collective-permute-start.37 = (bf16[128,2048]{0,1:T(8,128)(2,1)}, bf16[128,2048]{0,1:T(8,128)(2,1)}, u32[]{:S(2)}, u32[]{:S(2)}) collective-permute-start(bf16[128,2048]{0,1:T(8,128)(2,1)} %fusion.35), channel_id=1, source_target_pairs={{0,4},{1,5},{2,6},{3,7},{4,0},{5,1},{6,2},{7,3},{8,12},{9,13},{10,... | collective-permute-start | bytes 1572872 | tf_op jit(solution)/shard_map/ppermute | solution.py:190
  304.2 19.6 %collective-permute-start.32 = (bf16[128,2048]{0,1:T(8,128)(2,1)}, bf16[128,2048]{0,1:T(8,128)(2,1)}, u32[]{:S(2)}, u32[]{:S(2)}) collective-permute-start(bf16[128,2048]{0,1:T(8,128)(2,1)} %fusion.36), channel_id=1, source_target_pairs={{0,2},{1,3},{2,0},{3,1},{4,6},{5,7},{6,4},{7,5},{8,10},{9,11},{10,... | collective-permute-start | bytes 1572872 | tf_op jit(solution)/shard_map/ppermute | solution.py:190
  330.4 24.1 %collective-permute-start.39 = (bf16[256,2048]{0,1:T(8,128)(2,1)S(1)}, bf16[256,2048]{0,1:T(8,128)(2,1)S(1)}, u32[]{:S(2)}, u32[]{:S(2)}) collective-permute-start(bf16[256,2048]{0,1:T(8,128)(2,1)S(1)} %get-tuple-element.137), channel_id=1, source_target_pairs={{0,2},{1,3},{2,0},{3,1},{4,6},{5,7},{6,4},{7,5},{8,10},{9,11},{10,... | collective-permute-start | bytes 3145736 | tf_op jit(solution)/shard_map/ppermute | solution.py:190
  331.1 23.8 %collective-permute-start.41 = (bf16[256,2048]{0,1:T(8,128)(2,1)S(1)}, bf16[256,2048]{0,1:T(8,128)(2,1)S(1)}, u32[]{:S(2)}, u32[]{:S(2)}) collective-permute-start(bf16[256,2048]{0,1:T(8,128)(2,1)S(1)} %get-tuple-element.137), channel_id=1, source_target_pairs={{0,4},{1,5},{2,6},{3,7},{4,0},{5,1},{6,2},{7,3},{8,12},{9,13},{10,... | collective-permute-start | bytes 3145736 | tf_op jit(solution)/shard_map/ppermute | solution.py:190
  332.5 25.5 %collective-permute-start.38 = (bf16[256,2048]{0,1:T(8,128)(2,1)S(1)}, bf16[256,2048]{0,1:T(8,128)(2,1)S(1)}, u32[]{:S(2)}, u32[]{:S(2)}) collective-permute-start(bf16[256,2048]{0,1:T(8,128)(2,1)S(1)} %get-tuple-element.137), channel_id=1, source_target_pairs={{0,1},{1,0},{2,3},{3,2},{4,5},{5,4},{6,7},{7,6},{8,9},{9,8},{10,11... | collective-permute-start | bytes 3145736 | tf_op jit(solution)/shard_map/ppermute | solution.py:190
  354.6 16.0 %collective-permute-start.40 = (bf16[256,2048]{0,1:T(8,128)(2,1)S(1)}, bf16[256,2048]{0,1:T(8,128)(2,1)S(1)}, u32[]{:S(2)}, u32[]{:S(2)}) collective-permute-start(bf16[256,2048]{0,1:T(8,128)(2,1)S(1)} %collective-permute-done.39), channel_id=1, source_target_pairs={{0,1},{1,0},{2,3},{3,2},{4,5},{5,4},{6,7},{7,6},{8,9},{9,8},{10,11... | collective-permute-start | bytes 3145736 | tf_op jit(solution)/shard_map/ppermute | solution.py:190
  354.8 16.1 %collective-permute-start.42 = (bf16[256,2048]{0,1:T(8,128)(2,1)S(1)}, bf16[256,2048]{0,1:T(8,128)(2,1)S(1)}, u32[]{:S(2)}, u32[]{:S(2)}) collective-permute-start(bf16[256,2048]{0,1:T(8,128)(2,1)S(1)} %collective-permute-done.41), channel_id=1, source_target_pairs={{0,1},{1,0},{2,3},{3,2},{4,5},{5,4},{6,7},{7,6},{8,9},{9,8},{10,11... | collective-permute-start | bytes 3145736 | tf_op jit(solution)/shard_map/ppermute | solution.py:190
  434.7 171.2 %reduce-scatter.6.cloned.1.call-start = ((), (), s32[]{:S(2)}) async-start(), calls=%async_computation.8 | async-start | bytes 7045120 | tf_op jit(solution)/shard_map/reduce_scatter | solution.py:345
  446.2 25.0 %collective-permute-start.54 = (bf16[128,2048]{0,1:T(8,128)(2,1)S(1)}, bf16[128,2048]{0,1:T(8,128)(2,1)S(1)}, u32[]{:S(2)}, u32[]{:S(2)}) collective-permute-start(bf16[128,2048]{0,1:T(8,128)(2,1)S(1)} %slice.446), channel_id=1, source_target_pairs={{0,4},{1,5},{2,6},{3,7},{4,0},{5,1},{6,2},{7,3},{8,12},{9,13},{10,... | collective-permute-start | bytes 1572872 | tf_op jit(solution)/shard_map/ppermute | solution.py:190
  447.4 23.8 %collective-permute-start.52 = (bf16[128,2048]{0,1:T(8,128)(2,1)S(1)}, bf16[128,2048]{0,1:T(8,128)(2,1)S(1)}, u32[]{:S(2)}, u32[]{:S(2)}) collective-permute-start(bf16[128,2048]{0,1:T(8,128)(2,1)S(1)} %slice.447), channel_id=1, source_target_pairs={{0,2},{1,3},{2,0},{3,1},{4,6},{5,7},{6,4},{7,5},{8,10},{9,11},{10,... | collective-permute-start | bytes 1572872 | tf_op jit(solution)/shard_map/ppermute | solution.py:190
  458.6 22.7 %collective-permute-start.56 = (bf16[128,2048]{0,1:T(8,128)(2,1)S(1)}, bf16[128,2048]{0,1:T(8,128)(2,1)S(1)}, u32[]{:S(2)}, u32[]{:S(2)}) collective-permute-start(bf16[128,2048]{0,1:T(8,128)(2,1)S(1)} %fusion.33), channel_id=1, source_target_pairs={{0,4},{1,5},{2,6},{3,7},{4,0},{5,1},{6,2},{7,3},{8,12},{9,13},{10,... | collective-permute-start | bytes 1572872 | tf_op jit(solution)/shard_map/ppermute | solution.py:190
  460.0 21.3 %collective-permute-start.51 = (bf16[128,2048]{0,1:T(8,128)(2,1)S(1)}, bf16[128,2048]{0,1:T(8,128)(2,1)S(1)}, u32[]{:S(2)}, u32[]{:S(2)}) collective-permute-start(bf16[128,2048]{0,1:T(8,128)(2,1)S(1)} %fusion.34), channel_id=1, source_target_pairs={{0,2},{1,3},{2,0},{3,1},{4,6},{5,7},{6,4},{7,5},{8,10},{9,11},{10,... | collective-permute-start | bytes 1572872 | tf_op jit(solution)/shard_map/ppermute | solution.py:190
  505.9 200.0 %reduce-scatter.8.cloned.1.call-start = ((), (), s32[]{:S(2)}) async-start(), calls=%async_computation.9 | async-start | bytes 5242880 | tf_op jit(solution)/shard_map/reduce_scatter | solution.py:363
  506.0 24.6 %collective-permute-start.58 = (bf16[256,2048]{0,1:T(8,128)(2,1)S(1)}, bf16[256,2048]{0,1:T(8,128)(2,1)S(1)}, u32[]{:S(2)}, u32[]{:S(2)}) collective-permute-start(bf16[256,2048]{0,1:T(8,128)(2,1)S(1)} %fusion.48), channel_id=1, source_target_pairs={{0,2},{1,3},{2,0},{3,1},{4,6},{5,7},{6,4},{7,5},{8,10},{9,11},{10,... | collective-permute-start | bytes 3145736 | tf_op jit(solution)/shard_map/ppermute | solution.py:190
  507.5 24.6 %collective-permute-start.60 = (bf16[256,2048]{0,1:T(8,128)(2,1)S(1)}, bf16[256,2048]{0,1:T(8,128)(2,1)S(1)}, u32[]{:S(2)}, u32[]{:S(2)}) collective-permute-start(bf16[256,2048]{0,1:T(8,128)(2,1)S(1)} %fusion.48), channel_id=1, source_target_pairs={{0,4},{1,5},{2,6},{3,7},{4,0},{5,1},{6,2},{7,3},{8,12},{9,13},{10,... | collective-permute-start | bytes 3145736 | tf_op jit(solution)/shard_map/ppermute | solution.py:190
  509.0 24.9 %collective-permute-start.57 = (bf16[256,2048]{0,1:T(8,128)(2,1)S(1)}, bf16[256,2048]{0,1:T(8,128)(2,1)S(1)}, u32[]{:S(2)}, u32[]{:S(2)}) collective-permute-start(bf16[256,2048]{0,1:T(8,128)(2,1)S(1)} %fusion.48), channel_id=1, source_target_pairs={{0,1},{1,0},{2,3},{3,2},{4,5},{5,4},{6,7},{7,6},{8,9},{9,8},{10,11... | collective-permute-start | bytes 3145736 | tf_op jit(solution)/shard_map/ppermute | solution.py:190
  530.5 15.7 %collective-permute-start.59 = (bf16[256,2048]{0,1:T(8,128)(2,1)S(1)}, bf16[256,2048]{0,1:T(8,128)(2,1)S(1)}, u32[]{:S(2)}, u32[]{:S(2)}) collective-permute-start(bf16[256,2048]{0,1:T(8,128)(2,1)S(1)} %collective-permute-done.58), channel_id=1, source_target_pairs={{0,1},{1,0},{2,3},{3,2},{4,5},{5,4},{6,7},{7,6},{8,9},{9,8},{10,11... | collective-permute-start | bytes 3145736 | tf_op jit(solution)/shard_map/ppermute | solution.py:190
  612.2 15.3 %collective-permute-start.66 = (bf16[256,2048]{0,1:T(8,128)(2,1)}, bf16[256,2048]{0,1:T(8,128)(2,1)S(1)}, u32[]{:S(2)}, u32[]{:S(2)}) collective-permute-start(bf16[256,2048]{0,1:T(8,128)(2,1)} %get-tuple-element.152), channel_id=1, source_target_pairs={{0,1},{1,0},{2,3},{3,2},{4,5},{5,4},{6,7},{7,6},{8,9},{9,8},{10,11... | collective-permute-start | bytes 3145736 | tf_op jit(solution)/shard_map/ppermute | solution.py:190
  612.4 24.5 %collective-permute-start.71 = (bf16[128,2048]{0,1:T(8,128)(2,1)S(1)}, bf16[128,2048]{0,1:T(8,128)(2,1)S(1)}, u32[]{:S(2)}, u32[]{:S(2)}) collective-permute-start(bf16[128,2048]{0,1:T(8,128)(2,1)S(1)} %slice.445), channel_id=1, source_target_pairs={{0,2},{1,3},{2,0},{3,1},{4,6},{5,7},{6,4},{7,5},{8,10},{9,11},{10,... | collective-permute-start | bytes 1572872 | tf_op jit(solution)/shard_map/ppermute | solution.py:190
  613.1 23.8 %collective-permute-start.73 = (bf16[128,2048]{0,1:T(8,128)(2,1)S(1)}, bf16[128,2048]{0,1:T(8,128)(2,1)S(1)}, u32[]{:S(2)}, u32[]{:S(2)}) collective-permute-start(bf16[128,2048]{0,1:T(8,128)(2,1)S(1)} %slice.444), channel_id=1, source_target_pairs={{0,4},{1,5},{2,6},{3,7},{4,0},{5,1},{6,2},{7,3},{8,12},{9,13},{10,... | collective-permute-start | bytes 1572872 | tf_op jit(solution)/shard_map/ppermute | solution.py:190
  624.2 22.3 %collective-permute-start.70 = (bf16[128,2048]{0,1:T(8,128)(2,1)S(1)}, bf16[128,2048]{0,1:T(8,128)(2,1)S(1)}, u32[]{:S(2)}, u32[]{:S(2)}) collective-permute-start(bf16[128,2048]{0,1:T(8,128)(2,1)S(1)} %fusion.32), channel_id=1, source_target_pairs={{0,2},{1,3},{2,0},{3,1},{4,6},{5,7},{6,4},{7,5},{8,10},{9,11},{10,... | collective-permute-start | bytes 1572872 | tf_op jit(solution)/shard_map/ppermute | solution.py:190
  625.9 20.7 %collective-permute-start.75 = (bf16[128,2048]{0,1:T(8,128)(2,1)S(1)}, bf16[128,2048]{0,1:T(8,128)(2,1)S(1)}, u32[]{:S(2)}, u32[]{:S(2)}) collective-permute-start(bf16[128,2048]{0,1:T(8,128)(2,1)S(1)} %fusion.31), channel_id=1, source_target_pairs={{0,4},{1,5},{2,6},{3,7},{4,0},{5,1},{6,2},{7,3},{8,12},{9,13},{10,... | collective-permute-start | bytes 1572872 | tf_op jit(solution)/shard_map/ppermute | solution.py:190
  655.6 19.8 %collective-permute-start.83 = (f32[4,2048]{1,0:T(4,128)S(1)}, f32[4,2048]{1,0:T(4,128)S(1)}, u32[]{:S(2)}, u32[]{:S(2)}) collective-permute-start(f32[4,2048]{1,0:T(4,128)S(1)} %add.354), channel_id=1, source_target_pairs={{0,4},{1,5},{2,6},{3,7},{4,0},{5,1},{6,2},{7,3},{8,12},{9,13},{10,... | collective-permute-start | bytes 98312 | tf_op jit(solution)/shard_map/ppermute | solution.py:190
  (78 other events, 730.3 us)
Sparse Core Ops, SparseCore 0:
  10.2 66.1 all-gather.4
  78.5 26.6 all-gather.6
  107.3 102.9 all-gather.8
  212.3 56.2 all-gather.10
  434.8 53.4 reduce-scatter.3
  506.0 99.8 reduce-scatter.5
  608.2 78.5 reduce-scatter.7

commit v4 on v3

--- a/solution.py
+++ b/solution.py
@@ -210,10 +210,24 @@
     )
 
 
-def scatter_near(whole):
-    own_rows = whole.shape[0] // 8
+def far_first(rows, product, quarters):
+    size = rows.shape[0] // 4
+    pieces = []
+    for first, last in quarters:
+        if pieces:
+            rows, pieces[0] = lax.optimization_barrier((rows, pieces[0]))
+        pieces.insert(0, product(rows[first * size : last * size]))
+    return pieces
+
+
+def scatter_near(pieces):
+    blocks = []
+    own_rows = sum(piece.shape[0] for piece in pieces) // 8
     half = own_rows // 2
-    blocks = [whole[at * own_rows : (at + 1) * own_rows] for at in range(8)]
+    for piece in pieces:
+        blocks += [
+            piece[at : at + own_rows] for at in range(0, piece.shape[0], own_rows)
+        ]
     sums = [
         blocks[at].astype(jnp.float32) + swap(blocks[at + 1], "mp", 1).astype(jnp.float32)
         for at in range(0, 8, 2)
@@ -234,7 +248,8 @@
     return lax.all_gather(rows, "mp", axis=0, tiled=True)
 
 
-def scatter_all(whole):
+def scatter_all(pieces):
+    whole = jnp.concatenate(pieces, 0)
     return lax.psum_scatter(whole, "mp", scatter_dimension=0, tiled=True).astype(jnp.float32)
 
 
@@ -284,23 +299,35 @@
     else:
         gather_rows, scatter_rows = gather_all, scatter_all
         place = jnp.zeros((2,), jnp.int32)
+    two_pieces, four_pieces = ((3, 4), (0, 3)), ((3, 4), (2, 3), (1, 2), (0, 1))
     seq_info = (objective, prefix_len, place)
     cosine, sine = rope_tables(jnp.arange(seq_len, dtype=jnp.int32) ^ place[1], HD)
 
     qkv_low = qkv_weight.astype(jnp.bfloat16).reshape(shard_rows, 3 * local_dim)
     qkv_full = lax.all_gather(qkv_low, "dp", axis=0, tiled=True)
     out_full = lax.all_gather(out_weight.astype(jnp.bfloat16), "dp", axis=1, tiled=True)
-    gateup_low = jnp.transpose(gateup_weight, (1, 2, 0)).astype(jnp.bfloat16)
+    gateup_low = with_layout_constraint(
+        jnp.transpose(gateup_weight, (1, 2, 0)).astype(jnp.bfloat16),
+        Layout(major_to_minor=(0, 1, 2)),
+    )
     gateup_full = lax.all_gather(gateup_low, "dp", axis=2, tiled=True)
     down_full = lax.all_gather(down_weight.astype(jnp.bfloat16), "dp", axis=1, tiled=True)
 
     mask_f32 = target_mask.astype(jnp.float32)
     target_count = sum_everywhere(jnp.full((8, 128), jnp.sum(mask_f32)))[0, 0]
+
+    cosine, target_count = lax.optimization_barrier((cosine, target_count))
 
     inputs = gather_rows(block_input)
     proj = jnp.dot(inputs, qkv_full, preferred_element_type=jnp.float32)
     *kept, attended = attend_forward(seq_info, proj, cosine, sine)
-    attn_own = scatter_rows(jnp.dot(attended, out_full, preferred_element_type=jnp.bfloat16))
+    attn_own = scatter_rows(
+        far_first(
+            attended,
+            lambda rows: jnp.dot(rows, out_full, preferred_element_type=jnp.bfloat16),
+            two_pieces,
+        )
+    )
     hidden_one = deep_alpha * block_input.astype(jnp.float32) + attn_own
     middle, normed_one, inv_one = norm_forward(hidden_one, norm_params[0], norm_params[1])
     middle_low = gather_rows(middle.astype(jnp.bfloat16))
@@ -310,7 +337,13 @@
         "td,cfd->ctf", middle_low, gateup_full, preferred_element_type=jnp.float32
     )
     hidden_low = (jax.nn.gelu(gate_up[0]) * gate_up[1] * live_units).astype(jnp.bfloat16)
-    ffn_own = scatter_rows(jnp.dot(hidden_low, down_full, preferred_element_type=jnp.bfloat16))
+    ffn_own = scatter_rows(
+        far_first(
+            hidden_low,
+            lambda rows: jnp.dot(rows, down_full, preferred_element_type=jnp.bfloat16),
+            two_pieces,
+        )
+    )
     hidden_two = deep_alpha * middle + ffn_own
     output_rows, normed_two, inv_two = norm_forward(hidden_two, norm_params[2], norm_params[3])
     grad_rows = out_cotangent.astype(jnp.float32) * mask_f32[:, None]
@@ -320,22 +353,34 @@
     down_grad = jnp.einsum("tf,td->fd", hidden_low, ffn_back, preferred_element_type=jnp.bfloat16)
     ffn_back, down_grad = lax.optimization_barrier((ffn_back, down_grad))
     down_grad = lax.psum_scatter(down_grad, "dp", scatter_dimension=1, tiled=True)
-    gate_act, gelu_pull = jax.vjp(jax.nn.gelu, gate_up[0])
-    grad_hidden = (
-        jnp.einsum("td,fd->tf", ffn_back, down_full, preferred_element_type=jnp.float32)
-        * live_units
-    )
-    grad_gate = gelu_pull(grad_hidden * gate_up[1])[0]
-    grad_up = grad_hidden * gate_act
-    grad_gateup = jnp.stack([grad_gate, grad_up], 0).astype(jnp.bfloat16)
-    middle_part = jnp.einsum(
-        "ctf,cfd->td", grad_gateup, gateup_full, preferred_element_type=jnp.bfloat16
-    )
-    middle_low, down_grad = lax.optimization_barrier((middle_low, down_grad))
+    quarter = ffn_back.shape[0] // 4
+    middle_parts, grad_gateups = [], []
+    for first, last in four_pieces:
+        at = slice(first * quarter, last * quarter)
+        if middle_parts:
+            ffn_back, middle_parts[0] = lax.optimization_barrier((ffn_back, middle_parts[0]))
+        gate_act, gelu_pull = jax.vjp(jax.nn.gelu, gate_up[0, at])
+        grad_hidden = (
+            jnp.einsum("td,fd->tf", ffn_back[at], down_full, preferred_element_type=jnp.float32)
+            * live_units
+        )
+        grad_gate = gelu_pull(grad_hidden * gate_up[1, at])[0]
+        grad_gateup = jnp.stack([grad_gate, grad_hidden * gate_act], 0).astype(jnp.bfloat16)
+        grad_gateups.insert(0, grad_gateup)
+        middle_parts.insert(
+            0,
+            jnp.einsum(
+                "ctf,cfd->td", grad_gateup, gateup_full, preferred_element_type=jnp.bfloat16
+            ),
+        )
     gateup_grad = jnp.einsum(
-        "ctf,td->cfd", grad_gateup, middle_low, preferred_element_type=jnp.bfloat16
-    )
-    grad_middle = scatter_rows(middle_part) + deep_alpha * grad_two
+        "ctf,td->cfd",
+        jnp.concatenate(grad_gateups, 1),
+        middle_low,
+        preferred_element_type=jnp.bfloat16,
+    )
+    gateup_grad, down_grad = lax.optimization_barrier((gateup_grad, down_grad))
+    grad_middle = scatter_rows(middle_parts) + deep_alpha * grad_two
     grad_one, gain_one, bias_one = norm_backward(grad_middle, normed_one, inv_one, norm_params[0])
 
     grad_one_low, gateup_grad = lax.optimization_barrier(
@@ -363,7 +408,13 @@
     attend_grad = lax.psum_scatter(attend_grad, "dp", scatter_dimension=1, tiled=True)
     input_raw = (
         scatter_rows(
-            jnp.einsum("te,de->td", grad_proj, qkv_full, preferred_element_type=jnp.bfloat16)
+            far_first(
+                grad_proj,
+                lambda rows: jnp.einsum(
+                    "te,de->td", rows, qkv_full, preferred_element_type=jnp.bfloat16
+                ),
+                two_pieces,
+            )
         )
         + deep_alpha * grad_one
     )

time: 733 us -> 688 us (0.939)
  waiting for transfers between devices: 326 us -> 300 us
  matrix products: 143 us -> 134 us
    ppermute x86, waiting for transfers between devices: 268 us -> 237 us  [swap(): return lax.ppermute(values, axis, [(at, at ^ bit) for at in range(size)])]
    dot_general x1 -> x4, matrix products: 28.5 us -> 18.1 us  [local(): jnp.einsum('ctf,cfd->td', grad_gateup, gateup_full, preferred_element_typ...]
    all_gather x1, waiting for transfers between devices: 0.01 us -> 9.09 us  [local(): gateup_full = lax.all_gather(gateup_low, 'dp', axis=2, tiled=True)]
    unnamed x105 -> x157, local copies, waits for them, and re-layouts: 48.1 us -> 42.6 us
    dot_general x5 -> x11, matrix products: 58.1 us -> 61.3 us  [the longest x4 19.6 us: local(): jnp.einsum('td,fd->tf', ffn_back[at], down_full, preferred_element_type=j...]
  transfers between devices with their start and end apart: 93 -> 93, of which waited for: 48 -> 40; matrix products, arithmetic and copies ran while one was open for 24% -> 31% of each run, Pallas kernels for 3% -> 4%
where the time goes in v4:
time: 688 us; the launch traced here: 683 us
  waiting for transfers between devices  300 us (44%)
  matrix products  134 us (19%)
  other arithmetic  77.2 us (11%)
  starting transfers between devices  68.1 us (10%)
  local copies, waits for them, and re-layouts  62.8 us (9%)
  Pallas kernels  24.5 us (4%)
  between operations  16.5 us (2%)
    ppermute x86, waiting for transfers between devices, swap(): return lax.ppermute(values, axis, [(at, at ^ bit) for at in range(size)])  237 us
    ppermute x86, starting transfers between devices, swap(): return lax.ppermute(values, axis, [(at, at ^ bit) for at in range(size)])  67.6 us
    unnamed x157, local copies, waits for them, and re-layouts  42.6 us
    all_gather x1, waiting for transfers between devices, local(): lax.all_gather(down_weight.astype(jnp.bfloat16), 'dp', axis=1, tiled=True)  34.6 us
    transpose x2, other arithmetic, adamw_as(): jnp.transpose(rows, back)  21.1 us
    dot_general x4, matrix products, local(): jnp.einsum('td,fd->tf', ffn_back[at], down_full, preferred_element_type=j...  19.6 us
    dot_general x4, matrix products, local(): jnp.einsum('ctf,cfd->td', grad_gateup, gateup_full, preferred_element_typ...  18.1 us
    dot_general x1, matrix products, local(): jnp.einsum('ctf,td->cfd', jnp.concatenate(grad_gateups, 1), middle_low, p...  17.1 us
  transfers between devices with their start and end apart: 93, of which 40 were waited for; matrix products, arithmetic and copies ran while one was open for 31% of the time, Pallas kernels for 4%

profile of v4, /device:TPU:0, one launch (start us, length us, event | category | flops | bytes accessed | tf_op | source)
XLA Modules:
  0.0 682.6 jit_solution(7529567607137480943)
XLA Ops:
  21.7 15.7 %collective-permute-done.10 = f32[8,128]{1,0:T(8,128)S(1)} collective-permute-done((f32[8,128]{1,0:T(8,128)S(1)}, f32[8,128]{1,0:T(8,128)S(1)}, u32[]{:S(2)}, u32[]{:S(2)}) %collective-permute-start.10) | collective-permute-done | bytes 4128 | tf_op jit(solution)/shard_map/ppermute | solution.py:190
  72.0 4.6 all-gather.5.cloned.1.call-done
  76.5 12.2 %fusion.175.proj_ref = f32[2048,768]{1,0:T(8,128)} fusion(bf16[2048,2048]{1,0:T(8,128)(2,1)} %constant_dynamic-update-slice_fusion, bf16[2048,768]{0,1:T(8,128)(2,1)} %all-gather.5.cloned.1.call-done), kind=kOutput, calls=%fused_computation.309 | convolution fusion | flops 6442450944 | bytes 17825792 | tf_op jit(solution)/shard_map/dot_general | solution.py:322
  88.8 10.0 %attend_forward.1 = (bf16[2048,256]{1,0:T(8,128)(2,1)}, bf16[2048,256]{1,0:T(8,128)(2,1)}, bf16[2048,256]{1,0:T(8,128)(2,1)}, bf16[2048,256]{1,0:T(8,128)(2,1)}) custom-call(s32[4]{0:T(128)} %objective_ref.3, s32[4]{0:T(128)} %prefix_ref.3, s32[2]{0:T(128)} %pad_add_fusion.place_ref, f32[2048,768]{1,0:T(8,128)} %fusion.175.proj_ref, ...), custom_call_target="tpu_custom_call" | custom-call | tf_op jit(solution)/shard_map/attend_forward/pallas_call | solution.py:138
  98.8 6.5 all-gather.7.cloned.1.call-done
  118.1 8.0 %collective-permute-done.22 = bf16[128,2048]{1,0:T(8,128)(2,1)S(1)} collective-permute-done((bf16[128,2048]{1,0:T(8,128)(2,1)S(1)}, bf16[128,2048]{1,0:T(8,128)(2,1)S(1)}, u32[]{:S(2)}, u32[]{:S(2)}) %collective-permute-start.22) | collective-permute-done | bytes 524320 | tf_op jit(solution)/shard_map/ppermute | solution.py:190
  129.6 9.3 %collective-permute-done.21 = bf16[128,2048]{1,0:T(8,128)(2,1)S(1)} collective-permute-done((bf16[128,2048]{1,0:T(8,128)(2,1)S(1)}, bf16[128,2048]{1,0:T(8,128)(2,1)S(1)}, u32[]{:S(2)}, u32[]{:S(2)}) %collective-permute-start.21) | collective-permute-done | bytes 524320 | tf_op jit(solution)/shard_map/ppermute | solution.py:190
  138.9 10.1 %collective-permute-done.23 = bf16[128,2048]{1,0:T(8,128)(2,1)S(1)} collective-permute-done((bf16[128,2048]{1,0:T(8,128)(2,1)S(1)}, bf16[128,2048]{1,0:T(8,128)(2,1)S(1)}, u32[]{:S(2)}, u32[]{:S(2)}) %collective-permute-start.23) | collective-permute-done | bytes 524320 | tf_op jit(solution)/shard_map/ppermute | solution.py:190
  154.1 22.4 %collective-permute-done.25 = bf16[256,2048]{1,0:T(8,128)(2,1)} collective-permute-done((bf16[256,2048]{1,0:T(8,128)(2,1)}, bf16[256,2048]{1,0:T(8,128)(2,1)}, u32[]{:S(2)}, u32[]{:S(2)}) %collective-permute-start.25) | collective-permute-done | bytes 1048608 | tf_op jit(solution)/shard_map/ppermute | solution.py:190
  185.6 7.5 %collective-permute-done.29 = bf16[128,2048]{1,0:T(8,128)(2,1)S(1)} collective-permute-done((bf16[128,2048]{1,0:T(8,128)(2,1)S(1)}, bf16[128,2048]{1,0:T(8,128)(2,1)S(1)}, u32[]{:S(2)}, u32[]{:S(2)}) %collective-permute-start.29) | collective-permute-done | bytes 524320 | tf_op jit(solution)/shard_map/ppermute | solution.py:190
  202.3 9.1 %all-gather.9.cloned.1.call-done = bf16[2,684,2048]{2,1,0:T(8,128)(2,1)} async-done(((bf16[2,684,512]{2,1,0:T(8,128)(2,1)}), bf16[2,684,2048]{2,1,0:T(8,128)(2,1)}) %all-gather.9.cloned.1.call-update) | async-done | bytes 5603344 | tf_op jit(solution)/shard_map/all_gather | solution.py:313
  211.4 16.0 %fusion.29 = f32[2,2048,684]{1,2,0:T(8,128)S(1)} fusion(bf16[2,684,2048]{2,1,0:T(8,128)(2,1)} %all-gather.9.cloned.1.call-done, bf16[2048,2048]{1,0:T(8,128)(2,1)} %constant_dynamic-update-slice_fusion.10), kind=kOutput, calls=%fused_computation.32 | convolution fusion | flops 11475615744 | bytes 25198592 | tf_op jit(solution)/shard_map/td,cfd->ctf/dot_general | solution.py:336
  227.4 4.2 copy-done.2
  235.1 34.6 %all-gather.11.cloned.1.call-done = bf16[684,2048]{1,0:T(8,128)(2,1)} async-done(((bf16[684,512]{1,0:T(8,128)(2,1)}), bf16[684,2048]{1,0:T(8,128)(2,1)}) %all-gather.11.cloned.1.call-update) | async-done | bytes 2801680 | tf_op jit(solution)/shard_map/all_gather | solution.py:314
  269.7 4.0 fusion.127
  273.9 5.7 fusion.38
  288.2 8.1 %collective-permute-done.41 = bf16[128,2048]{1,0:T(8,128)(2,1)S(1)} collective-permute-done((bf16[128,2048]{1,0:T(8,128)(2,1)S(1)}, bf16[128,2048]{1,0:T(8,128)(2,1)S(1)}, u32[]{:S(2)}, u32[]{:S(2)}) %collective-permute-start.41) | collective-permute-done | bytes 524320 | tf_op jit(solution)/shard_map/ppermute | solution.py:190
  299.6 9.4 %collective-permute-done.40 = bf16[128,2048]{1,0:T(8,128)(2,1)S(1)} collective-permute-done((bf16[128,2048]{1,0:T(8,128)(2,1)S(1)}, bf16[128,2048]{1,0:T(8,128)(2,1)S(1)}, u32[]{:S(2)}, u32[]{:S(2)}) %collective-permute-start.40) | collective-permute-done | bytes 524320 | tf_op jit(solution)/shard_map/ppermute | solution.py:190
  309.0 10.1 %collective-permute-done.42 = bf16[128,2048]{1,0:T(8,128)(2,1)S(1)} collective-permute-done((bf16[128,2048]{1,0:T(8,128)(2,1)S(1)}, bf16[128,2048]{1,0:T(8,128)(2,1)S(1)}, u32[]{:S(2)}, u32[]{:S(2)}) %collective-permute-start.42) | collective-permute-done | bytes 524320 | tf_op jit(solution)/shard_map/ppermute | solution.py:190
  327.1 22.0 %collective-permute-done.44 = bf16[256,2048]{1,0:T(8,128)(2,1)S(1)} collective-permute-done((bf16[256,2048]{1,0:T(8,128)(2,1)S(1)}, bf16[256,2048]{1,0:T(8,128)(2,1)S(1)}, u32[]{:S(2)}, u32[]{:S(2)}) %collective-permute-start.44) | collective-permute-done | bytes 1048608 | tf_op jit(solution)/shard_map/ppermute | solution.py:190
  352.7 11.1 %collective-permute-done.48 = bf16[128,2048]{1,0:T(8,128)(2,1)S(1)} collective-permute-done((bf16[128,2048]{1,0:T(8,128)(2,1)S(1)}, bf16[128,2048]{1,0:T(8,128)(2,1)S(1)}, u32[]{:S(2)}, u32[]{:S(2)}) %collective-permute-start.48) | collective-permute-done | bytes 524320 | tf_op jit(solution)/shard_map/ppermute | solution.py:190
  370.4 7.4 %fusion.176 = bf16[684,2048]{1,0:T(8,128)(2,1)} fusion(bf16[2048,684]{0,1:T(8,128)(2,1)S(1)} %copy-done.18, bf16[2048,2048]{1,0:T(8,128)(2,1)S(1)} %constant_dynamic-update-slice_fusion.20), kind=kOutput, calls=%fused_computation.310 | convolution fusion | flops 5737807872 | bytes 13991936 | tf_op jit(solution)/shard_map/tf,td->fd/dot_general | solution.py:353
  377.8 5.8 fusion.136
  384.7 6.9 %convolution_bitcast_fusion.3 = bf16[512,2048]{1,0:T(8,128)(2,1)S(1)} fusion(bf16[2,684,2048]{2,1,0:T(8,128)(2,1)} %all-gather.9.cloned.1.call-done, bf16[1,512,684]{1,2,0:T(8,128)(2,1)S(1)} %get-tuple-element.130, bf16[1,512,684]{1,2,0:T(8,128)(2,1)S(1)} %get-tuple-element.129), kind=kOutput, calls=%fused_computation.46 | convolution fusion | flops 2869604352 | bytes 9101312 | tf_op jit(solution)/shard_map/ctf,cfd->td/dot_general | solution.py:372
  391.7 5.1 fusion.135
  403.2 4.3 fusion.134
  412.6 4.3 fusion.133
  417.0 3.8 convolution_bitcast_fusion
  435.1 5.7 collective-permute-done.60
  442.6 13.8 %collective-permute-done.55 = bf16[128,2048]{1,0:T(8,128)(2,1)S(1)} collective-permute-done((bf16[128,2048]{1,0:T(8,128)(2,1)S(1)}, bf16[128,2048]{1,0:T(8,128)(2,1)S(1)}, u32[]{:S(2)}, u32[]{:S(2)}) %collective-permute-start.55) | collective-permute-done | bytes 524320 | tf_op jit(solution)/shard_map/ppermute | solution.py:190
  457.7 17.1 %fusion = bf16[2,684,2048]{2,1,0:T(8,128)(2,1)} fusion(bf16[2048,2048]{1,0:T(8,128)(2,1)} %constant_dynamic-update-slice_fusion.10, bf16[1,512,684]{1,2,0:T(8,128)(2,1)S(1)} %copy-done.46, bf16[1,512,684]{1,2,0:T(8,128)(2,1)S(1)} %copy-done.44, bf16[1,512,684]{1,2,0:T(8,128)(2,1)S(1)} %copy-done.50, bf16[1,512,684]{1,2,0:T(8,128)(2,1)S(1)} %copy-done.48, ...), kind=kOutput, calls=%fused_computation.1 | convolution fusion | flops 11520442368 | bytes 19595264 | tf_op jit(solution)/shard_map/ctf,td->cfd/dot_general | solution.py:376
  474.8 4.9 multiply_reduce_fusion
  484.4 20.7 %collective-permute-done.63 = bf16[256,2048]{1,0:T(8,128)(2,1)S(1)} collective-permute-done((bf16[256,2048]{1,0:T(8,128)(2,1)S(1)}, bf16[256,2048]{1,0:T(8,128)(2,1)S(1)}, u32[]{:S(2)}, u32[]{:S(2)}) %collective-permute-start.63) | collective-permute-done | bytes 1048608 | tf_op jit(solution)/shard_map/ppermute | solution.py:190
  507.8 11.7 %collective-permute-done.67 = bf16[128,2048]{1,0:T(8,128)(2,1)S(1)} collective-permute-done((bf16[128,2048]{1,0:T(8,128)(2,1)S(1)}, bf16[128,2048]{1,0:T(8,128)(2,1)S(1)}, u32[]{:S(2)}, u32[]{:S(2)}) %collective-permute-start.67) | collective-permute-done | bytes 524320 | tf_op jit(solution)/shard_map/ppermute | solution.py:190
  522.3 3.7 fusion.177.grad_ref
  526.0 14.5 %attend_backward.1 = bf16[2048,768]{1,0:T(8,128)(2,1)} custom-call(s32[4]{0:T(128)} %objective_ref.3, s32[4]{0:T(128)} %prefix_ref.3, s32[2]{0:T(128)} %pad_add_fusion.place_ref, bf16[2048,256]{1,0:T(8,128)(2,1)} %get-tuple-element.69.query_ref, bf16[2048,256]{1,0:T(8,128)(2,1)} %get-tuple-element.70.key_ref, bf16[2048,256]{1,0:T(8,128)(2,1)} %get-tuple-element.71.value_ref, ...), custom_call_target="tpu_custom_call" | custom-call | tf_op jit(solution)/shard_map/attend_backward/pallas_call | solution.py:150
  540.6 5.9 fusion.178
  546.4 9.4 %fusion.179 = bf16[768,2048]{1,0:T(8,128)(2,1)S(1)} fusion(bf16[2048,768]{1,0:T(8,128)(2,1)S(1)} %copy-done.15, bf16[2048,2048]{1,0:T(8,128)(2,1)} %constant_dynamic-update-slice_fusion), kind=kOutput, calls=%fused_computation.313 | convolution fusion | flops 6442450944 | bytes 14680064 | tf_op jit(solution)/shard_map/te,td->ed/dot_general | solution.py:401
  559.2 3.8 fusion.123
  565.6 7.1 %fusion.36 = bf16[1536,2048]{1,0:T(8,128)(2,1)} fusion(bf16[2048,768]{0,1:T(8,128)(2,1)S(1)} %copy-done.40, bf16[2048,768]{1,0:T(8,128)(2,1)S(1)} %copy-done.16), kind=kOutput, calls=%fused_computation.47 | convolution fusion | flops 4831838208 | bytes 11796480 | tf_op jit(solution)/shard_map/te,de->td/dot_general | solution.py:413
  572.7 7.6 %reduce-scatter.6.cloned.1.call-done = bf16[2,684,512]{2,1,0:T(8,128)(2,1)} async-done(((bf16[2,684,2048]{2,1,0:T(8,128)(2,1)}), bf16[2,684,512]{2,1,0:T(8,128)(2,1)}) %reduce-scatter.6.cloned.1.call-update) | async-done | bytes 1400848 | tf_op jit(solution)/shard_map/reduce_scatter | solution.py:390
  592.6 7.4 %collective-permute-done.74 = bf16[128,2048]{1,0:T(8,128)(2,1)S(1)} collective-permute-done((bf16[128,2048]{1,0:T(8,128)(2,1)S(1)}, bf16[128,2048]{1,0:T(8,128)(2,1)S(1)}, u32[]{:S(2)}, u32[]{:S(2)}) %collective-permute-start.74) | collective-permute-done | bytes 524320 | tf_op jit(solution)/shard_map/ppermute | solution.py:190
  603.3 9.4 %collective-permute-done.76 = bf16[128,2048]{1,0:T(8,128)(2,1)S(1)} collective-permute-done((bf16[128,2048]{1,0:T(8,128)(2,1)S(1)}, bf16[128,2048]{1,0:T(8,128)(2,1)S(1)}, u32[]{:S(2)}, u32[]{:S(2)}) %collective-permute-start.76) | collective-permute-done | bytes 524320 | tf_op jit(solution)/shard_map/ppermute | solution.py:190
  612.7 10.4 %collective-permute-done.75 = bf16[128,2048]{1,0:T(8,128)(2,1)S(1)} collective-permute-done((bf16[128,2048]{1,0:T(8,128)(2,1)S(1)}, bf16[128,2048]{1,0:T(8,128)(2,1)S(1)}, u32[]{:S(2)}, u32[]{:S(2)}) %collective-permute-start.75) | collective-permute-done | bytes 524320 | tf_op jit(solution)/shard_map/ppermute | solution.py:190
  637.0 5.0 multiply_subtract_fusion
  645.5 3.8 collective-permute-done.85
  650.0 16.3 %fusion.149 = (f32[512,2,684]{0,1,2:T(2,128)}, f32[512,2,684]{0,1,2:T(2,128)}, f32[512,2,684]{0,1,2:T(2,128)}) fusion(f32[]{:T(128)S(6)} %div.99, bf16[2,684,512]{2,1,0:T(8,128)(2,1)S(1)} %copy-done.32, f32[512,2,684]{0,1,2:T(2,128)S(1)} %copy-done.19, f32[512,2,684]{0,1,2:T(2,128)S(1)} %copy-done.20, f32[512,2,684]{0,1,2:T(2,128)S(1)} %copy-done.4), kind=kLoop, calls=%fused_computation.296 | loop fusion | flops 11206656 | bytes 18210820 | tf_op jit(solution)/shard_map/transpose | solution.py:264
  670.8 4.8 fusion.122
  (431 shorter events, 204.9 us)
Async XLA Ops:
  7.2 69.3 %all-gather.5.cloned.1.call-start = ((), (), s32[]{:S(2)}) async-start(), calls=%async_computation.3 | async-start | bytes 3932160 | tf_op jit(solution)/shard_map/all_gather | solution.py:307
  10.0 95.3 %all-gather.7.cloned.1.call-start = ((), (), s32[]{:S(2)}) async-start(), calls=%async_computation.4 | async-start | bytes 1310720 | tf_op jit(solution)/shard_map/all_gather | solution.py:308
  10.8 200.6 %all-gather.9.cloned.1.call-start = ((), (), s32[]{:S(2)}) async-start(), calls=%async_computation.5 | async-start | bytes 7045120 | tf_op jit(solution)/shard_map/all_gather | solution.py:313
  10.9 29.0 %collective-permute-start.1 = (bf16[256,2048]{1,0:T(8,128)(2,1)}, bf16[256,2048]{1,0:T(8,128)(2,1)}, u32[]{:S(2)}, u32[]{:S(2)}) collective-permute-start(bf16[256,2048]{1,0:T(8,128)(2,1)} %param.20), channel_id=1, source_target_pairs={{0,2},{1,3},{2,0},{3,1},{4,6},{5,7},{6,4},{7,5},{8,10},{9,11},{10,... | collective-permute-start | bytes 3145736 | tf_op jit(solution)/shard_map/ppermute | solution.py:190
  13.9 41.8 %collective-permute-start = (bf16[256,2048]{1,0:T(8,128)(2,1)}, bf16[256,2048]{1,0:T(8,128)(2,1)}, u32[]{:S(2)}, u32[]{:S(2)}) collective-permute-start(bf16[256,2048]{1,0:T(8,128)(2,1)} %param.20), channel_id=1, source_target_pairs={{0,1},{1,0},{2,3},{3,2},{4,5},{5,4},{6,7},{7,6},{8,9},{9,8},{10,11... | collective-permute-start | bytes 3145736 | tf_op jit(solution)/shard_map/ppermute | solution.py:190
  13.9 38.0 %collective-permute-start.3 = (bf16[256,2048]{1,0:T(8,128)(2,1)}, bf16[256,2048]{1,0:T(8,128)(2,1)}, u32[]{:S(2)}, u32[]{:S(2)}) collective-permute-start(bf16[256,2048]{1,0:T(8,128)(2,1)} %param.20), channel_id=1, source_target_pairs={{0,4},{1,5},{2,6},{3,7},{4,0},{5,1},{6,2},{7,3},{8,12},{9,13},{10,... | collective-permute-start | bytes 3145736 | tf_op jit(solution)/shard_map/ppermute | solution.py:190
  19.3 250.4 %all-gather.11.cloned.1.call-start = ((), (), s32[]{:S(2)}) async-start(), calls=%async_computation.6 | async-start | bytes 3522560 | tf_op jit(solution)/shard_map/all_gather | solution.py:314
  21.1 16.3 %collective-permute-start.10 = (f32[8,128]{1,0:T(8,128)S(1)}, f32[8,128]{1,0:T(8,128)S(1)}, u32[]{:S(2)}, u32[]{:S(2)}) collective-permute-start(f32[8,128]{1,0:T(8,128)S(1)} %broadcast_add_fusion), channel_id=1, source_target_pairs={{0,2},{1,3},{2,0},{3,1},{4,6},{5,7},{6,4},{7,5},{8,10},{9,11},{10,... | collective-permute-start | bytes 12296 | tf_op jit(solution)/shard_map/ppermute | solution.py:190
  39.9 24.2 %collective-permute-start.2 = (bf16[256,2048]{1,0:T(8,128)(2,1)}, bf16[256,2048]{1,0:T(8,128)(2,1)S(1)}, u32[]{:S(2)}, u32[]{:S(2)}) collective-permute-start(bf16[256,2048]{1,0:T(8,128)(2,1)} %collective-permute-done.1), channel_id=1, source_target_pairs={{0,1},{1,0},{2,3},{3,2},{4,5},{5,4},{6,7},{7,6},{8,9},{9,8},{10,11... | collective-permute-start | bytes 3145736 | tf_op jit(solution)/shard_map/ppermute | solution.py:190
  110.4 19.1 %collective-permute-start.14 = (bf16[256,2048]{1,0:T(8,128)(2,1)S(1)}, bf16[256,2048]{1,0:T(8,128)(2,1)S(1)}, u32[]{:S(2)}, u32[]{:S(2)}) collective-permute-start(bf16[256,2048]{1,0:T(8,128)(2,1)S(1)} %get-tuple-element.141), channel_id=1, source_target_pairs={{0,1},{1,0},{2,3},{3,2},{4,5},{5,4},{6,7},{7,6},{8,9},{9,8},{10,11... | collective-permute-start | bytes 3145736 | tf_op jit(solution)/shard_map/ppermute | solution.py:190
  115.2 23.7 %collective-permute-start.21 = (bf16[128,2048]{1,0:T(8,128)(2,1)S(1)}, bf16[128,2048]{1,0:T(8,128)(2,1)S(1)}, u32[]{:S(2)}, u32[]{:S(2)}) collective-permute-start(bf16[128,2048]{1,0:T(8,128)(2,1)S(1)} %slice.615), channel_id=1, source_target_pairs={{0,4},{1,5},{2,6},{3,7},{4,0},{5,1},{6,2},{7,3},{8,12},{9,13},{10,... | collective-permute-start | bytes 1572872 | tf_op jit(solution)/shard_map/ppermute | solution.py:190
  116.6 22.3 %collective-permute-start.19 = (bf16[128,2048]{1,0:T(8,128)(2,1)S(1)}, bf16[128,2048]{1,0:T(8,128)(2,1)S(1)}, u32[]{:S(2)}, u32[]{:S(2)}) collective-permute-start(bf16[128,2048]{1,0:T(8,128)(2,1)S(1)} %slice.616), channel_id=1, source_target_pairs={{0,2},{1,3},{2,0},{3,1},{4,6},{5,7},{6,4},{7,5},{8,10},{9,11},{10,... | collective-permute-start | bytes 1572872 | tf_op jit(solution)/shard_map/ppermute | solution.py:190
  126.3 22.6 %collective-permute-start.23 = (bf16[128,2048]{1,0:T(8,128)(2,1)S(1)}, bf16[128,2048]{1,0:T(8,128)(2,1)S(1)}, u32[]{:S(2)}, u32[]{:S(2)}) collective-permute-start(bf16[128,2048]{1,0:T(8,128)(2,1)S(1)} %fusion.119), channel_id=1, source_target_pairs={{0,4},{1,5},{2,6},{3,7},{4,0},{5,1},{6,2},{7,3},{8,12},{9,13},{10,... | collective-permute-start | bytes 1572872 | tf_op jit(solution)/shard_map/ppermute | solution.py:190
  128.0 21.0 %collective-permute-start.18 = (bf16[128,2048]{1,0:T(8,128)(2,1)S(1)}, bf16[128,2048]{1,0:T(8,128)(2,1)S(1)}, u32[]{:S(2)}, u32[]{:S(2)}) collective-permute-start(bf16[128,2048]{1,0:T(8,128)(2,1)S(1)} %fusion.120), channel_id=1, source_target_pairs={{0,2},{1,3},{2,0},{3,1},{4,6},{5,7},{6,4},{7,5},{8,10},{9,11},{10,... | collective-permute-start | bytes 1572872 | tf_op jit(solution)/shard_map/ppermute | solution.py:190
  152.1 24.4 %collective-permute-start.25 = (bf16[256,2048]{1,0:T(8,128)(2,1)}, bf16[256,2048]{1,0:T(8,128)(2,1)}, u32[]{:S(2)}, u32[]{:S(2)}) collective-permute-start(bf16[256,2048]{1,0:T(8,128)(2,1)} %get-tuple-element.120), channel_id=1, source_target_pairs={{0,2},{1,3},{2,0},{3,1},{4,6},{5,7},{6,4},{7,5},{8,10},{9,11},{10,... | collective-permute-start | bytes 3145736 | tf_op jit(solution)/shard_map/ppermute | solution.py:190
  152.6 27.7 %collective-permute-start.27 = (bf16[256,2048]{1,0:T(8,128)(2,1)}, bf16[256,2048]{1,0:T(8,128)(2,1)S(1)}, u32[]{:S(2)}, u32[]{:S(2)}) collective-permute-start(bf16[256,2048]{1,0:T(8,128)(2,1)} %get-tuple-element.120), channel_id=1, source_target_pairs={{0,4},{1,5},{2,6},{3,7},{4,0},{5,1},{6,2},{7,3},{8,12},{9,13},{10,... | collective-permute-start | bytes 3145736 | tf_op jit(solution)/shard_map/ppermute | solution.py:190
  154.1 26.9 %collective-permute-start.24 = (bf16[256,2048]{1,0:T(8,128)(2,1)}, bf16[256,2048]{1,0:T(8,128)(2,1)}, u32[]{:S(2)}, u32[]{:S(2)}) collective-permute-start(bf16[256,2048]{1,0:T(8,128)(2,1)} %get-tuple-element.120), channel_id=1, source_target_pairs={{0,1},{1,0},{2,3},{3,2},{4,5},{5,4},{6,7},{7,6},{8,9},{9,8},{10,11... | collective-permute-start | bytes 3145736 | tf_op jit(solution)/shard_map/ppermute | solution.py:190
  176.5 18.0 %collective-permute-start.26 = (bf16[256,2048]{1,0:T(8,128)(2,1)}, bf16[256,2048]{1,0:T(8,128)(2,1)}, u32[]{:S(2)}, u32[]{:S(2)}) collective-permute-start(bf16[256,2048]{1,0:T(8,128)(2,1)} %collective-permute-done.25), channel_id=1, source_target_pairs={{0,1},{1,0},{2,3},{3,2},{4,5},{5,4},{6,7},{7,6},{8,9},{9,8},{10,11... | collective-permute-start | bytes 3145736 | tf_op jit(solution)/shard_map/ppermute | solution.py:190
  177.5 304.4 %reduce-scatter.4.cloned.1.call-start = ((), (), s32[]{:S(2)}) async-start(), calls=%async_computation.7 | async-start | bytes 3522560 | tf_op jit(solution)/shard_map/reduce_scatter | solution.py:355
  181.0 16.9 %collective-permute-start.28 = (bf16[256,2048]{1,0:T(8,128)(2,1)S(1)}, bf16[256,2048]{1,0:T(8,128)(2,1)S(1)}, u32[]{:S(2)}, u32[]{:S(2)}) collective-permute-start(bf16[256,2048]{1,0:T(8,128)(2,1)S(1)} %collective-permute-done.27), channel_id=1, source_target_pairs={{0,1},{1,0},{2,3},{3,2},{4,5},{5,4},{6,7},{7,6},{8,9},{9,8},{10,11... | collective-permute-start | bytes 3145736 | tf_op jit(solution)/shard_map/ppermute | solution.py:190
  280.5 19.2 %collective-permute-start.33 = (bf16[256,2048]{1,0:T(8,128)(2,1)S(1)}, bf16[256,2048]{1,0:T(8,128)(2,1)S(1)}, u32[]{:S(2)}, u32[]{:S(2)}) collective-permute-start(bf16[256,2048]{1,0:T(8,128)(2,1)S(1)} %get-tuple-element.136), channel_id=1, source_target_pairs={{0,1},{1,0},{2,3},{3,2},{4,5},{5,4},{6,7},{7,6},{8,9},{9,8},{10,11... | collective-permute-start | bytes 3145736 | tf_op jit(solution)/shard_map/ppermute | solution.py:190
  285.3 23.7 %collective-permute-start.40 = (bf16[128,2048]{1,0:T(8,128)(2,1)S(1)}, bf16[128,2048]{1,0:T(8,128)(2,1)S(1)}, u32[]{:S(2)}, u32[]{:S(2)}) collective-permute-start(bf16[128,2048]{1,0:T(8,128)(2,1)S(1)} %slice.613), channel_id=1, source_target_pairs={{0,4},{1,5},{2,6},{3,7},{4,0},{5,1},{6,2},{7,3},{8,12},{9,13},{10,... | collective-permute-start | bytes 1572872 | tf_op jit(solution)/shard_map/ppermute | solution.py:190
  286.7 22.3 %collective-permute-start.38 = (bf16[128,2048]{1,0:T(8,128)(2,1)S(1)}, bf16[128,2048]{1,0:T(8,128)(2,1)S(1)}, u32[]{:S(2)}, u32[]{:S(2)}) collective-permute-start(bf16[128,2048]{1,0:T(8,128)(2,1)S(1)} %slice.614), channel_id=1, source_target_pairs={{0,2},{1,3},{2,0},{3,1},{4,6},{5,7},{6,4},{7,5},{8,10},{9,11},{10,... | collective-permute-start | bytes 1572872 | tf_op jit(solution)/shard_map/ppermute | solution.py:190
  296.4 22.6 %collective-permute-start.42 = (bf16[128,2048]{1,0:T(8,128)(2,1)S(1)}, bf16[128,2048]{1,0:T(8,128)(2,1)S(1)}, u32[]{:S(2)}, u32[]{:S(2)}) collective-permute-start(bf16[128,2048]{1,0:T(8,128)(2,1)S(1)} %fusion.117), channel_id=1, source_target_pairs={{0,4},{1,5},{2,6},{3,7},{4,0},{5,1},{6,2},{7,3},{8,12},{9,13},{10,... | collective-permute-start | bytes 1572872 | tf_op jit(solution)/shard_map/ppermute | solution.py:190
  298.1 21.0 %collective-permute-start.37 = (bf16[128,2048]{1,0:T(8,128)(2,1)S(1)}, bf16[128,2048]{1,0:T(8,128)(2,1)S(1)}, u32[]{:S(2)}, u32[]{:S(2)}) collective-permute-start(bf16[128,2048]{1,0:T(8,128)(2,1)S(1)} %fusion.118), channel_id=1, source_target_pairs={{0,2},{1,3},{2,0},{3,1},{4,6},{5,7},{6,4},{7,5},{8,10},{9,11},{10,... | collective-permute-start | bytes 1572872 | tf_op jit(solution)/shard_map/ppermute | solution.py:190
  325.0 24.1 %collective-permute-start.44 = (bf16[256,2048]{1,0:T(8,128)(2,1)S(1)}, bf16[256,2048]{1,0:T(8,128)(2,1)S(1)}, u32[]{:S(2)}, u32[]{:S(2)}) collective-permute-start(bf16[256,2048]{1,0:T(8,128)(2,1)S(1)} %get-tuple-element.116), channel_id=1, source_target_pairs={{0,2},{1,3},{2,0},{3,1},{4,6},{5,7},{6,4},{7,5},{8,10},{9,11},{10,... | collective-permute-start | bytes 3145736 | tf_op jit(solution)/shard_map/ppermute | solution.py:190
  325.6 23.7 %collective-permute-start.46 = (bf16[256,2048]{1,0:T(8,128)(2,1)S(1)}, bf16[256,2048]{1,0:T(8,128)(2,1)S(1)}, u32[]{:S(2)}, u32[]{:S(2)}) collective-permute-start(bf16[256,2048]{1,0:T(8,128)(2,1)S(1)} %get-tuple-element.116), channel_id=1, source_target_pairs={{0,4},{1,5},{2,6},{3,7},{4,0},{5,1},{6,2},{7,3},{8,12},{9,13},{10,... | collective-permute-start | bytes 3145736 | tf_op jit(solution)/shard_map/ppermute | solution.py:190
  327.1 25.4 %collective-permute-start.43 = (bf16[256,2048]{1,0:T(8,128)(2,1)S(1)}, bf16[256,2048]{1,0:T(8,128)(2,1)S(1)}, u32[]{:S(2)}, u32[]{:S(2)}) collective-permute-start(bf16[256,2048]{1,0:T(8,128)(2,1)S(1)} %get-tuple-element.116), channel_id=1, source_target_pairs={{0,1},{1,0},{2,3},{3,2},{4,5},{5,4},{6,7},{7,6},{8,9},{9,8},{10,11... | collective-permute-start | bytes 3145736 | tf_op jit(solution)/shard_map/ppermute | solution.py:190
  401.7 25.8 %collective-permute-start.58 = (bf16[256,2048]{1,0:T(8,128)(2,1)}, bf16[256,2048]{1,0:T(8,128)(2,1)}, u32[]{:S(2)}, u32[]{:S(2)}) collective-permute-start(bf16[256,2048]{1,0:T(8,128)(2,1)} %slice.350), channel_id=1, source_target_pairs={{0,1},{1,0},{2,3},{3,2},{4,5},{5,4},{6,7},{7,6},{8,9},{9,8},{10,11... | collective-permute-start | bytes 3145736 | tf_op jit(solution)/shard_map/ppermute | solution.py:190
  402.9 20.8 %collective-permute-start.54 = (bf16[256,2048]{1,0:T(8,128)(2,1)}, bf16[256,2048]{1,0:T(8,128)(2,1)}, u32[]{:S(2)}, u32[]{:S(2)}) collective-permute-start(bf16[256,2048]{1,0:T(8,128)(2,1)} %slice.346), channel_id=1, source_target_pairs={{0,1},{1,0},{2,3},{3,2},{4,5},{5,4},{6,7},{7,6},{8,9},{9,8},{10,11... | collective-permute-start | bytes 3145736 | tf_op jit(solution)/shard_map/ppermute | solution.py:190
  412.4 19.7 %collective-permute-start.53 = (bf16[256,2048]{1,0:T(8,128)(2,1)}, bf16[256,2048]{1,0:T(8,128)(2,1)}, u32[]{:S(2)}, u32[]{:S(2)}) collective-permute-start(bf16[256,2048]{1,0:T(8,128)(2,1)} %slice.343), channel_id=1, source_target_pairs={{0,1},{1,0},{2,3},{3,2},{4,5},{5,4},{6,7},{7,6},{8,9},{9,8},{10,11... | collective-permute-start | bytes 3145736 | tf_op jit(solution)/shard_map/ppermute | solution.py:190
  423.2 51.6 %collective-permute-start.52 = (bf16[256,2048]{1,0:T(8,128)(2,1)}, bf16[256,2048]{1,0:T(8,128)(2,1)}, u32[]{:S(2)}, u32[]{:S(2)}) collective-permute-start(bf16[256,2048]{1,0:T(8,128)(2,1)} %slice.416), channel_id=1, source_target_pairs={{0,1},{1,0},{2,3},{3,2},{4,5},{5,4},{6,7},{7,6},{8,9},{9,8},{10,11... | collective-permute-start | bytes 3145736 | tf_op jit(solution)/shard_map/ppermute | solution.py:190
  423.6 156.7 %reduce-scatter.6.cloned.1.call-start = ((), (), s32[]{:S(2)}) async-start(), calls=%async_computation.8 | async-start | bytes 7045120 | tf_op jit(solution)/shard_map/reduce_scatter | solution.py:390
  430.1 44.7 %collective-permute-start.59 = (bf16[128,2048]{1,0:T(8,128)(2,1)}, bf16[128,2048]{1,0:T(8,128)(2,1)}, u32[]{:S(2)}, u32[]{:S(2)}) collective-permute-start(bf16[128,2048]{1,0:T(8,128)(2,1)} %slice.611), channel_id=1, source_target_pairs={{0,4},{1,5},{2,6},{3,7},{4,0},{5,1},{6,2},{7,3},{8,12},{9,13},{10,... | collective-permute-start | bytes 1572872 | tf_op jit(solution)/shard_map/ppermute | solution.py:190
  430.8 25.6 %collective-permute-start.55 = (bf16[128,2048]{1,0:T(8,128)(2,1)S(1)}, bf16[128,2048]{1,0:T(8,128)(2,1)S(1)}, u32[]{:S(2)}, u32[]{:S(2)}) collective-permute-start(bf16[128,2048]{1,0:T(8,128)(2,1)S(1)} %get-tuple-element.155), channel_id=1, source_target_pairs={{0,4},{1,5},{2,6},{3,7},{4,0},{5,1},{6,2},{7,3},{8,12},{9,13},{10,... | collective-permute-start | bytes 1572872 | tf_op jit(solution)/shard_map/ppermute | solution.py:190
  434.7 40.1 %collective-permute-start.57 = (bf16[128,2048]{1,0:T(8,128)(2,1)}, bf16[128,2048]{1,0:T(8,128)(2,1)}, u32[]{:S(2)}, u32[]{:S(2)}) collective-permute-start(bf16[128,2048]{1,0:T(8,128)(2,1)} %slice.612), channel_id=1, source_target_pairs={{0,2},{1,3},{2,0},{3,1},{4,6},{5,7},{6,4},{7,5},{8,10},{9,11},{10,... | collective-permute-start | bytes 1572872 | tf_op jit(solution)/shard_map/ppermute | solution.py:190
  441.7 33.1 %collective-permute-start.61 = (bf16[128,2048]{1,0:T(8,128)(2,1)}, bf16[128,2048]{1,0:T(8,128)(2,1)}, u32[]{:S(2)}, u32[]{:S(2)}) collective-permute-start(bf16[128,2048]{1,0:T(8,128)(2,1)} %fusion.115), channel_id=1, source_target_pairs={{0,4},{1,5},{2,6},{3,7},{4,0},{5,1},{6,2},{7,3},{8,12},{9,13},{10,... | collective-permute-start | bytes 1572872 | tf_op jit(solution)/shard_map/ppermute | solution.py:190
  457.3 17.6 %collective-permute-start.56 = (bf16[128,2048]{1,0:T(8,128)(2,1)}, bf16[128,2048]{1,0:T(8,128)(2,1)}, u32[]{:S(2)}, u32[]{:S(2)}) collective-permute-start(bf16[128,2048]{1,0:T(8,128)(2,1)} %fusion.116), channel_id=1, source_target_pairs={{0,2},{1,3},{2,0},{3,1},{4,6},{5,7},{6,4},{7,5},{8,10},{9,11},{10,... | collective-permute-start | bytes 1572872 | tf_op jit(solution)/shard_map/ppermute | solution.py:190
  481.9 184.4 %reduce-scatter.8.cloned.1.call-start = ((), (), s32[]{:S(2)}) async-start(), calls=%async_computation.9 | async-start | bytes 5242880 | tf_op jit(solution)/shard_map/reduce_scatter | solution.py:408
  482.0 23.1 %collective-permute-start.63 = (bf16[256,2048]{1,0:T(8,128)(2,1)S(1)}, bf16[256,2048]{1,0:T(8,128)(2,1)S(1)}, u32[]{:S(2)}, u32[]{:S(2)}) collective-permute-start(bf16[256,2048]{1,0:T(8,128)(2,1)S(1)} %get-tuple-element.74), channel_id=1, source_target_pairs={{0,2},{1,3},{2,0},{3,1},{4,6},{5,7},{6,4},{7,5},{8,10},{9,11},{10,... | collective-permute-start | bytes 3145736 | tf_op jit(solution)/shard_map/ppermute | solution.py:190
  483.7 22.4 %collective-permute-start.65 = (bf16[256,2048]{1,0:T(8,128)(2,1)S(1)}, bf16[256,2048]{1,0:T(8,128)(2,1)S(1)}, u32[]{:S(2)}, u32[]{:S(2)}) collective-permute-start(bf16[256,2048]{1,0:T(8,128)(2,1)S(1)} %get-tuple-element.74), channel_id=1, source_target_pairs={{0,4},{1,5},{2,6},{3,7},{4,0},{5,1},{6,2},{7,3},{8,12},{9,13},{10,... | collective-permute-start | bytes 3145736 | tf_op jit(solution)/shard_map/ppermute | solution.py:190
  484.4 23.2 %collective-permute-start.62 = (bf16[256,2048]{1,0:T(8,128)(2,1)S(1)}, bf16[256,2048]{1,0:T(8,128)(2,1)S(1)}, u32[]{:S(2)}, u32[]{:S(2)}) collective-permute-start(bf16[256,2048]{1,0:T(8,128)(2,1)S(1)} %get-tuple-element.74), channel_id=1, source_target_pairs={{0,1},{1,0},{2,3},{3,2},{4,5},{5,4},{6,7},{7,6},{8,9},{9,8},{10,11... | collective-permute-start | bytes 3145736 | tf_op jit(solution)/shard_map/ppermute | solution.py:190
  565.4 18.0 %collective-permute-start.73 = (bf16[256,2048]{1,0:T(8,128)(2,1)}, bf16[256,2048]{1,0:T(8,128)(2,1)}, u32[]{:S(2)}, u32[]{:S(2)}) collective-permute-start(bf16[256,2048]{1,0:T(8,128)(2,1)} %slice.364), channel_id=1, source_target_pairs={{0,1},{1,0},{2,3},{3,2},{4,5},{5,4},{6,7},{7,6},{8,9},{9,8},{10,11... | collective-permute-start | bytes 3145736 | tf_op jit(solution)/shard_map/ppermute | solution.py:190
  583.3 20.0 %collective-permute-start.71 = (bf16[256,2048]{1,0:T(8,128)(2,1)S(1)}, bf16[256,2048]{1,0:T(8,128)(2,1)S(1)}, u32[]{:S(2)}, u32[]{:S(2)}) collective-permute-start(bf16[256,2048]{1,0:T(8,128)(2,1)S(1)} %get-tuple-element.135), channel_id=1, source_target_pairs={{0,1},{1,0},{2,3},{3,2},{4,5},{5,4},{6,7},{7,6},{8,9},{9,8},{10,11... | collective-permute-start | bytes 3145736 | tf_op jit(solution)/shard_map/ppermute | solution.py:190
  591.1 21.6 %collective-permute-start.76 = (bf16[128,2048]{1,0:T(8,128)(2,1)S(1)}, bf16[128,2048]{1,0:T(8,128)(2,1)S(1)}, u32[]{:S(2)}, u32[]{:S(2)}) collective-permute-start(bf16[128,2048]{1,0:T(8,128)(2,1)S(1)} %slice.610), channel_id=1, source_target_pairs={{0,2},{1,3},{2,0},{3,1},{4,6},{5,7},{6,4},{7,5},{8,10},{9,11},{10,... | collective-permute-start | bytes 1572872 | tf_op jit(solution)/shard_map/ppermute | solution.py:190
  591.3 21.4 %collective-permute-start.78 = (bf16[128,2048]{1,0:T(8,128)(2,1)S(1)}, bf16[128,2048]{1,0:T(8,128)(2,1)S(1)}, u32[]{:S(2)}, u32[]{:S(2)}) collective-permute-start(bf16[128,2048]{1,0:T(8,128)(2,1)S(1)} %slice.609), channel_id=1, source_target_pairs={{0,4},{1,5},{2,6},{3,7},{4,0},{5,1},{6,2},{7,3},{8,12},{9,13},{10,... | collective-permute-start | bytes 1572872 | tf_op jit(solution)/shard_map/ppermute | solution.py:190
  600.1 23.0 %collective-permute-start.75 = (bf16[128,2048]{1,0:T(8,128)(2,1)S(1)}, bf16[128,2048]{1,0:T(8,128)(2,1)S(1)}, u32[]{:S(2)}, u32[]{:S(2)}) collective-permute-start(bf16[128,2048]{1,0:T(8,128)(2,1)S(1)} %fusion.114), channel_id=1, source_target_pairs={{0,2},{1,3},{2,0},{3,1},{4,6},{5,7},{6,4},{7,5},{8,10},{9,11},{10,... | collective-permute-start | bytes 1572872 | tf_op jit(solution)/shard_map/ppermute | solution.py:190
  601.7 21.4 %collective-permute-start.80 = (bf16[128,2048]{1,0:T(8,128)(2,1)S(1)}, bf16[128,2048]{1,0:T(8,128)(2,1)S(1)}, u32[]{:S(2)}, u32[]{:S(2)}) collective-permute-start(bf16[128,2048]{1,0:T(8,128)(2,1)S(1)} %fusion.113), channel_id=1, source_target_pairs={{0,4},{1,5},{2,6},{3,7},{4,0},{5,1},{6,2},{7,3},{8,12},{9,13},{10,... | collective-permute-start | bytes 1572872 | tf_op jit(solution)/shard_map/ppermute | solution.py:190
  (107 other events, 923.6 us)
Sparse Core Ops, SparseCore 0:
  10.2 66.3 all-gather.4
  78.7 26.5 all-gather.6
  107.5 103.8 all-gather.8
  213.4 56.2 all-gather.10
  423.7 53.4 reduce-scatter.3
  482.0 98.2 reduce-scatter.5
  582.6 78.6 reduce-scatter.7

commit v5 on v4

--- a/solution.py
+++ b/solution.py
@@ -199,15 +199,18 @@
     return values
 
 
-def gather_near(rows):
+def gather_near(rows, ahead=None):
     half = rows.shape[0] // 2
     near_x, near_y = swap(rows, "mp", 2), swap(rows, "mp", 4)
+    if ahead is not None:
+        near_x, near_y, ahead = lax.optimization_barrier((near_x, near_y, ahead))
     far_low, far_high = swap(near_x[:half], "mp", 4), swap(near_y[half:], "mp", 2)
     mates = [swap(part, "mp", 1) for part in (rows, near_x, near_y, far_low, far_high)]
-    return jnp.concatenate(
+    whole = jnp.concatenate(
         [rows, mates[0], near_x, mates[1], near_y, mates[2], far_low, far_high, mates[3], mates[4]],
         0,
     )
+    return whole if ahead is None else (whole, ahead)
 
 
 def far_first(rows, product, quarters):
@@ -244,8 +247,37 @@
     return sums[0] + across_x + across_y
 
 
-def gather_all(rows):
-    return lax.all_gather(rows, "mp", axis=0, tiled=True)
+def core_sum(piece):
+    half = piece.shape[0] // 2
+    mate = swap(piece[half:], "mp", 1)
+    return piece[:half].astype(jnp.float32) + mate.astype(jnp.float32)
+
+
+def scatter_beside(rows, product):
+    far = product(rows, 3)
+    rows, far = lax.optimization_barrier((rows, far))
+    near_x = product(rows, 1)
+    far = core_sum(far).astype(jnp.bfloat16)
+    rows, far, near_x = lax.optimization_barrier((rows, far, near_x))
+    half = far.shape[0] // 2
+    far_low, far_high = swap(far[:half], "mp", 4), swap(far[half:], "mp", 2)
+    near_y, far_low, far_high = lax.optimization_barrier((product(rows, 2), far_low, far_high))
+    near_x, near_y = core_sum(near_x), core_sum(near_y)
+    low, high = slice(0, half), slice(half, 2 * half)
+    x_low = (near_x[low] + far_low.astype(jnp.float32)).astype(jnp.bfloat16)
+    y_high = (near_y[high] + far_high.astype(jnp.float32)).astype(jnp.bfloat16)
+    rows, x_low, y_high = lax.optimization_barrier((rows, x_low, y_high))
+    x_high, y_low = near_x[high].astype(jnp.bfloat16), near_y[low].astype(jnp.bfloat16)
+    across_x = jnp.concatenate([swap(x_low, "mp", 2), swap(x_high, "mp", 2)], 0)
+    across_y = jnp.concatenate([swap(y_low, "mp", 4), swap(y_high, "mp", 4)], 0)
+    own, across_x, across_y = lax.optimization_barrier((product(rows, 0), across_x, across_y))
+    own = core_sum(own)
+    return own + across_x.astype(jnp.float32) + across_y.astype(jnp.float32)
+
+
+def gather_all(rows, ahead=None):
+    whole = lax.all_gather(rows, "mp", axis=0, tiled=True)
+    return whole if ahead is None else (whole, ahead)
 
 
 def scatter_all(pieces):
@@ -299,13 +331,14 @@
     else:
         gather_rows, scatter_rows = gather_all, scatter_all
         place = jnp.zeros((2,), jnp.int32)
-    two_pieces, four_pieces = ((3, 4), (0, 3)), ((3, 4), (2, 3), (1, 2), (0, 1))
+    two_pieces = ((3, 4), (0, 3))
     seq_info = (objective, prefix_len, place)
     cosine, sine = rope_tables(jnp.arange(seq_len, dtype=jnp.int32) ^ place[1], HD)
 
     qkv_low = qkv_weight.astype(jnp.bfloat16).reshape(shard_rows, 3 * local_dim)
-    qkv_full = lax.all_gather(qkv_low, "dp", axis=0, tiled=True)
-    out_full = lax.all_gather(out_weight.astype(jnp.bfloat16), "dp", axis=1, tiled=True)
+    attend_low = jnp.concatenate([qkv_low, out_weight.T.astype(jnp.bfloat16)], 1)
+    attend_full = lax.all_gather(attend_low, "dp", axis=0, tiled=True)
+    qkv_full, out_full = attend_full[:, : 3 * local_dim], attend_full[:, 3 * local_dim :]
     gateup_low = with_layout_constraint(
         jnp.transpose(gateup_weight, (1, 2, 0)).astype(jnp.bfloat16),
         Layout(major_to_minor=(0, 1, 2)),
@@ -324,7 +357,9 @@
     attn_own = scatter_rows(
         far_first(
             attended,
-            lambda rows: jnp.dot(rows, out_full, preferred_element_type=jnp.bfloat16),
+            lambda rows: jnp.einsum(
+                "te,de->td", rows, out_full, preferred_element_type=jnp.bfloat16
+            ),
             two_pieces,
         )
     )
@@ -354,45 +389,41 @@
     ffn_back, down_grad = lax.optimization_barrier((ffn_back, down_grad))
     down_grad = lax.psum_scatter(down_grad, "dp", scatter_dimension=1, tiled=True)
     quarter = ffn_back.shape[0] // 4
-    middle_parts, grad_gateups = [], []
-    for first, last in four_pieces:
-        at = slice(first * quarter, last * quarter)
-        if middle_parts:
-            ffn_back, middle_parts[0] = lax.optimization_barrier((ffn_back, middle_parts[0]))
+    grad_gateups = [None] * 4
+
+    def back_quarter(rows, index):
+        at = slice(index * quarter, (index + 1) * quarter)
         gate_act, gelu_pull = jax.vjp(jax.nn.gelu, gate_up[0, at])
         grad_hidden = (
-            jnp.einsum("td,fd->tf", ffn_back[at], down_full, preferred_element_type=jnp.float32)
+            jnp.einsum("td,fd->tf", rows[at], down_full, preferred_element_type=jnp.float32)
             * live_units
         )
         grad_gate = gelu_pull(grad_hidden * gate_up[1, at])[0]
-        grad_gateup = jnp.stack([grad_gate, grad_hidden * gate_act], 0).astype(jnp.bfloat16)
-        grad_gateups.insert(0, grad_gateup)
-        middle_parts.insert(
-            0,
-            jnp.einsum(
-                "ctf,cfd->td", grad_gateup, gateup_full, preferred_element_type=jnp.bfloat16
-            ),
-        )
+        grads = jnp.stack([grad_gate, grad_hidden * gate_act], 0).astype(jnp.bfloat16)
+        grad_gateups[index] = grads
+        return jnp.einsum("ctf,cfd->td", grads, gateup_full, preferred_element_type=jnp.bfloat16)
+
+    if near:
+        grad_middle = scatter_beside(ffn_back, back_quarter)
+    else:
+        grad_middle = scatter_all([back_quarter(ffn_back, index) for index in range(4)])
+    grad_middle = grad_middle + deep_alpha * grad_two
+    middle_low, down_grad = lax.optimization_barrier((middle_low, down_grad))
     gateup_grad = jnp.einsum(
         "ctf,td->cfd",
         jnp.concatenate(grad_gateups, 1),
         middle_low,
         preferred_element_type=jnp.bfloat16,
     )
-    gateup_grad, down_grad = lax.optimization_barrier((gateup_grad, down_grad))
-    grad_middle = scatter_rows(middle_parts) + deep_alpha * grad_two
     grad_one, gain_one, bias_one = norm_backward(grad_middle, normed_one, inv_one, norm_params[0])
 
-    grad_one_low, gateup_grad = lax.optimization_barrier(
-        (grad_one.astype(jnp.bfloat16), gateup_grad)
-    )
+    attn_back, gateup_grad = gather_rows(grad_one.astype(jnp.bfloat16), gateup_grad)
     gateup_grad = with_layout_constraint(
         lax.psum_scatter(gateup_grad, "dp", scatter_dimension=2, tiled=True),
         Layout(major_to_minor=(0, 1, 2)),
     )
-    attn_back = gather_rows(grad_one_low)
     grad_attended = jnp.einsum(
-        "td,ed->te", attn_back, out_full, preferred_element_type=jnp.bfloat16
+        "td,de->te", attn_back, out_full, preferred_element_type=jnp.bfloat16
     )
     grad_proj = attend_backward(seq_info, *kept, grad_attended, cosine, sine)
     attended, grad_proj = lax.optimization_barrier((attended, grad_proj))

time: 688 us -> 674 us (0.980)
  waiting for transfers between devices: 300 us -> 288 us
    ppermute x86, waiting for transfers between devices: 237 us -> 222 us  [swap(): return lax.ppermute(values, axis, [(at, at ^ bit) for at in range(size)])]
    reduce_scatter x1, waiting for transfers between devices: 7.61 us -> 22.1 us  [local(): lax.psum_scatter(gateup_grad, 'dp', scatter_dimension=2, tiled=True)]
    all_gather x1, waiting for transfers between devices: 34.6 us -> 20.5 us  [local(): lax.all_gather(down_weight.astype(jnp.bfloat16), 'dp', axis=1, tiled=True)]
    all_gather x2 -> x1, waiting for transfers between devices: 11.1 us -> 22.6 us  [local(): attend_full = lax.all_gather(attend_low, 'dp', axis=0, tiled=True)]
    all_gather x1, waiting for transfers between devices: 9.09 us -> 0.01 us  [local(): gateup_full = lax.all_gather(gateup_low, 'dp', axis=2, tiled=True)]
    unnamed x157 -> x126, local copies, waits for them, and re-layouts: 42.6 us -> 48.2 us
  transfers between devices with their start and end apart: 93 -> 92, of which waited for: 40 -> 42; matrix products, arithmetic and copies ran while one was open for 31% -> 35% of each run, Pallas kernels for 4% -> 4%
where the time goes in v5:
time: 674 us; the launch traced here: 669 us
  waiting for transfers between devices  288 us (43%)
  matrix products  139 us (21%)
  other arithmetic  70.7 us (10%)
  starting transfers between devices  67.8 us (10%)
  local copies, waits for them, and re-layouts  63.7 us (9%)
  Pallas kernels  24.2 us (4%)
  between operations  16.3 us (2%)
    ppermute x86, waiting for transfers between devices, swap(): return lax.ppermute(values, axis, [(at, at ^ bit) for at in range(size)])  222 us
    ppermute x86, starting transfers between devices, swap(): return lax.ppermute(values, axis, [(at, at ^ bit) for at in range(size)])  67.2 us
    unnamed x126, local copies, waits for them, and re-layouts  48.2 us
    all_gather x1, waiting for transfers between devices, local(): attend_full = lax.all_gather(attend_low, 'dp', axis=0, tiled=True)  22.6 us
    reduce_scatter x1, waiting for transfers between devices, local(): lax.psum_scatter(gateup_grad, 'dp', scatter_dimension=2, tiled=True)  22.1 us
    transpose x2, other arithmetic, adamw_as(): jnp.transpose(rows, back)  21.1 us
    all_gather x1, waiting for transfers between devices, local(): lax.all_gather(down_weight.astype(jnp.bfloat16), 'dp', axis=1, tiled=True)  20.5 us
    dot_general x4, matrix products, back_quarter(): jnp.einsum('td,fd->tf', rows[at], down_full, preferred_element_type=jnp.f...  19.3 us
  transfers between devices with their start and end apart: 92, of which 42 were waited for; matrix products, arithmetic and copies ran while one was open for 35% of the time, Pallas kernels for 4%

profile of v5, /device:TPU:0, one launch (start us, length us, event | category | flops | bytes accessed | tf_op | source)
XLA Modules:
  0.0 669.1 jit_solution(9503499653933916595)
XLA Ops:
  23.1 15.7 %collective-permute-done.10 = f32[8,128]{1,0:T(8,128)S(1)} collective-permute-done((f32[8,128]{1,0:T(8,128)S(1)}, f32[8,128]{1,0:T(8,128)S(1)}, u32[]{:S(2)}, u32[]{:S(2)}) %collective-permute-start.10) | collective-permute-done | bytes 4128 | tf_op jit(solution)/shard_map/ppermute | solution.py:190
  73.4 22.6 %all-gather.4.cloned.1.call-done = bf16[2048,1024]{0,1:T(8,128)(2,1)} async-done(((bf16[512,1024]{0,1:T(8,128)(2,1)}), bf16[2048,1024]{0,1:T(8,128)(2,1)}) %all-gather.4.cloned.1.call-update) | async-done | bytes 4194320 | tf_op jit(solution)/shard_map/all_gather | solution.py:340
  96.0 11.9 %fusion.40.proj_ref = f32[2048,768]{1,0:T(8,128)} fusion(bf16[2048,2048]{1,0:T(8,128)(2,1)} %constant_dynamic-update-slice_fusion, bf16[2048,1024]{0,1:T(8,128)(2,1)} %all-gather.4.cloned.1.call-done), kind=kOutput, calls=%fused_computation.51 | convolution fusion | flops 6442450944 | bytes 17825792 | tf_op jit(solution)/shard_map/dot_general | solution.py:355
  107.9 10.0 %attend_forward.1 = (bf16[2048,256]{1,0:T(8,128)(2,1)}, bf16[2048,256]{1,0:T(8,128)(2,1)}, bf16[2048,256]{1,0:T(8,128)(2,1)}, bf16[2048,256]{1,0:T(8,128)(2,1)}) custom-call(s32[4]{0:T(128)} %objective_ref.3, s32[4]{0:T(128)} %prefix_ref.3, s32[2]{0:T(128)} %pad_add_fusion.place_ref, f32[2048,768]{1,0:T(8,128)} %fusion.40.proj_ref, ...), custom_call_target="tpu_custom_call" | custom-call | tf_op jit(solution)/shard_map/attend_forward/pallas_call | solution.py:138
  132.0 8.0 %collective-permute-done.17 = bf16[128,2048]{1,0:T(8,128)(2,1)S(1)} collective-permute-done((bf16[128,2048]{1,0:T(8,128)(2,1)S(1)}, bf16[128,2048]{1,0:T(8,128)(2,1)S(1)}, u32[]{:S(2)}, u32[]{:S(2)}) %collective-permute-start.17) | collective-permute-done | bytes 524320 | tf_op jit(solution)/shard_map/ppermute | solution.py:190
  143.5 9.3 %collective-permute-done.19 = bf16[128,2048]{1,0:T(8,128)(2,1)S(1)} collective-permute-done((bf16[128,2048]{1,0:T(8,128)(2,1)S(1)}, bf16[128,2048]{1,0:T(8,128)(2,1)S(1)}, u32[]{:S(2)}, u32[]{:S(2)}) %collective-permute-start.19) | collective-permute-done | bytes 524320 | tf_op jit(solution)/shard_map/ppermute | solution.py:190
  152.8 10.1 %collective-permute-done.18 = bf16[128,2048]{1,0:T(8,128)(2,1)S(1)} collective-permute-done((bf16[128,2048]{1,0:T(8,128)(2,1)S(1)}, bf16[128,2048]{1,0:T(8,128)(2,1)S(1)}, u32[]{:S(2)}, u32[]{:S(2)}) %collective-permute-start.18) | collective-permute-done | bytes 524320 | tf_op jit(solution)/shard_map/ppermute | solution.py:190
  168.0 22.4 %collective-permute-done.25 = bf16[256,2048]{1,0:T(8,128)(2,1)} collective-permute-done((bf16[256,2048]{1,0:T(8,128)(2,1)}, bf16[256,2048]{1,0:T(8,128)(2,1)}, u32[]{:S(2)}, u32[]{:S(2)}) %collective-permute-start.25) | collective-permute-done | bytes 1048608 | tf_op jit(solution)/shard_map/ppermute | solution.py:190
  199.6 7.5 %collective-permute-done.29 = bf16[128,2048]{1,0:T(8,128)(2,1)S(1)} collective-permute-done((bf16[128,2048]{1,0:T(8,128)(2,1)S(1)}, bf16[128,2048]{1,0:T(8,128)(2,1)S(1)}, u32[]{:S(2)}, u32[]{:S(2)}) %collective-permute-start.29) | collective-permute-done | bytes 524320 | tf_op jit(solution)/shard_map/ppermute | solution.py:190
  215.5 16.0 %fusion.29 = f32[2,2048,684]{1,2,0:T(8,128)S(1)} fusion(bf16[2,684,2048]{2,1,0:T(8,128)(2,1)} %all-gather.6.cloned.1.call-done, bf16[2048,2048]{1,0:T(8,128)(2,1)} %constant_dynamic-update-slice_fusion.10), kind=kOutput, calls=%fused_computation.32 | convolution fusion | flops 11475615744 | bytes 25198592 | tf_op jit(solution)/shard_map/td,cfd->ctf/dot_general | solution.py:371
  231.5 4.2 copy-done.2
  239.3 20.5 %all-gather.8.cloned.1.call-done = bf16[684,2048]{1,0:T(8,128)(2,1)} async-done(((bf16[684,512]{1,0:T(8,128)(2,1)}), bf16[684,2048]{1,0:T(8,128)(2,1)}) %all-gather.8.cloned.1.call-update) | async-done | bytes 2801680 | tf_op jit(solution)/shard_map/all_gather | solution.py:347
  259.7 4.0 fusion.136
  263.9 5.8 fusion.43
  278.3 8.2 %collective-permute-done.36 = bf16[128,2048]{1,0:T(8,128)(2,1)S(1)} collective-permute-done((bf16[128,2048]{1,0:T(8,128)(2,1)S(1)}, bf16[128,2048]{1,0:T(8,128)(2,1)S(1)}, u32[]{:S(2)}, u32[]{:S(2)}) %collective-permute-start.36) | collective-permute-done | bytes 524320 | tf_op jit(solution)/shard_map/ppermute | solution.py:190
  289.8 9.4 %collective-permute-done.38 = bf16[128,2048]{1,0:T(8,128)(2,1)S(1)} collective-permute-done((bf16[128,2048]{1,0:T(8,128)(2,1)S(1)}, bf16[128,2048]{1,0:T(8,128)(2,1)S(1)}, u32[]{:S(2)}, u32[]{:S(2)}) %collective-permute-start.38) | collective-permute-done | bytes 524320 | tf_op jit(solution)/shard_map/ppermute | solution.py:190
  299.2 10.1 %collective-permute-done.37 = bf16[128,2048]{1,0:T(8,128)(2,1)S(1)} collective-permute-done((bf16[128,2048]{1,0:T(8,128)(2,1)S(1)}, bf16[128,2048]{1,0:T(8,128)(2,1)S(1)}, u32[]{:S(2)}, u32[]{:S(2)}) %collective-permute-start.37) | collective-permute-done | bytes 524320 | tf_op jit(solution)/shard_map/ppermute | solution.py:190
  316.3 22.0 %collective-permute-done.44 = bf16[256,2048]{1,0:T(8,128)(2,1)S(1)} collective-permute-done((bf16[256,2048]{1,0:T(8,128)(2,1)S(1)}, bf16[256,2048]{1,0:T(8,128)(2,1)S(1)}, u32[]{:S(2)}, u32[]{:S(2)}) %collective-permute-start.44) | collective-permute-done | bytes 1048608 | tf_op jit(solution)/shard_map/ppermute | solution.py:190
  341.3 12.7 %collective-permute-done.48 = bf16[128,2048]{1,0:T(8,128)(2,1)S(1)} collective-permute-done((bf16[128,2048]{1,0:T(8,128)(2,1)S(1)}, bf16[128,2048]{1,0:T(8,128)(2,1)S(1)}, u32[]{:S(2)}, u32[]{:S(2)}) %collective-permute-start.48) | collective-permute-done | bytes 524320 | tf_op jit(solution)/shard_map/ppermute | solution.py:190
  360.0 7.3 %fusion.182 = bf16[684,2048]{1,0:T(8,128)(2,1)} fusion(bf16[2048,684]{0,1:T(8,128)(2,1)S(1)} %copy-done.16, bf16[2048,2048]{1,0:T(8,128)(2,1)S(1)} %constant_dynamic-update-slice_fusion.20), kind=kOutput, calls=%fused_computation.320 | convolution fusion | flops 5737807872 | bytes 13991936 | tf_op jit(solution)/shard_map/tf,td->fd/dot_general | solution.py:388
  367.4 6.0 fusion.145
  374.5 6.6 convolution_bitcast_fusion.3
  381.4 4.6 fusion.144
  386.0 3.7 convolution_bitcast_fusion.2
  392.1 4.3 fusion.143
  396.5 4.1 convolution_bitcast_fusion.1
  400.6 4.1 collective-permute-done.54
  411.5 4.4 fusion.142
  416.0 3.7 convolution_bitcast_fusion
  419.7 4.0 collective-permute-done.60
  423.7 10.4 %collective-permute-done.59 = bf16[128,2048]{1,0:T(8,128)(2,1)S(1)} collective-permute-done((bf16[128,2048]{1,0:T(8,128)(2,1)S(1)}, bf16[128,2048]{1,0:T(8,128)(2,1)S(1)}, u32[]{:S(2)}, u32[]{:S(2)}) %collective-permute-start.59) | collective-permute-done | bytes 524320 | tf_op jit(solution)/shard_map/ppermute | solution.py:190
  444.4 17.8 %fusion = bf16[2,684,2048]{2,1,0:T(8,128)(2,1)} fusion(bf16[2048,2048]{1,0:T(8,128)(2,1)} %constant_dynamic-update-slice_fusion.10, bf16[1,512,684]{1,2,0:T(8,128)(2,1)} %copy-done.35, bf16[1,512,684]{1,2,0:T(8,128)(2,1)} %copy-done.34, bf16[1,512,684]{1,2,0:T(8,128)(2,1)} %copy-done.39, bf16[1,512,684]{1,2,0:T(8,128)(2,1)} %copy-done.38, ...), kind=kOutput, calls=%fused_computation.1 | convolution fusion | flops 11520442368 | bytes 19595264 | tf_op jit(solution)/shard_map/ctf,td->cfd/dot_general | solution.py:412
  462.2 5.9 collective-permute-done.63
  474.0 9.7 %collective-permute-done.67 = bf16[128,2048]{1,0:T(8,128)(2,1)S(1)} collective-permute-done((bf16[128,2048]{1,0:T(8,128)(2,1)S(1)}, bf16[128,2048]{1,0:T(8,128)(2,1)S(1)}, u32[]{:S(2)}, u32[]{:S(2)}) %collective-permute-start.67) | collective-permute-done | bytes 524320 | tf_op jit(solution)/shard_map/ppermute | solution.py:190
  491.1 7.1 %fusion.127.grad_ref = bf16[2048,256]{1,0:T(8,128)(2,1)} fusion(bf16[2048,2048]{1,0:T(8,128)(2,1)} %constant_dynamic-update-slice_fusion.30, bf16[2048,1024]{0,1:T(8,128)(2,1)} %all-gather.4.cloned.1.call-done), kind=kOutput, calls=%fused_computation.210 | convolution fusion | flops 2147483648 | bytes 10485760 | tf_op jit(solution)/shard_map/td,de->te/dot_general | solution.py:425
  498.2 14.2 %attend_backward.1 = bf16[2048,768]{1,0:T(8,128)(2,1)} custom-call(s32[4]{0:T(128)} %objective_ref.3, s32[4]{0:T(128)} %prefix_ref.3, s32[2]{0:T(128)} %pad_add_fusion.place_ref, bf16[2048,256]{1,0:T(8,128)(2,1)} %get-tuple-element.86.query_ref, bf16[2048,256]{1,0:T(8,128)(2,1)} %get-tuple-element.87.key_ref, bf16[2048,256]{1,0:T(8,128)(2,1)} %get-tuple-element.88.value_ref, ...), custom_call_target="tpu_custom_call" | custom-call | tf_op jit(solution)/shard_map/attend_backward/pallas_call | solution.py:150
  512.4 5.9 fusion.183
  518.3 9.4 %fusion.184 = bf16[768,2048]{1,0:T(8,128)(2,1)S(1)} fusion(bf16[2048,768]{1,0:T(8,128)(2,1)S(1)} %copy-done.13, bf16[2048,2048]{1,0:T(8,128)(2,1)} %constant_dynamic-update-slice_fusion), kind=kOutput, calls=%fused_computation.322 | convolution fusion | flops 6442450944 | bytes 14680064 | tf_op jit(solution)/shard_map/te,td->ed/dot_general | solution.py:432
  531.1 3.8 fusion.38
  537.7 7.2 %fusion.36 = bf16[1536,2048]{1,0:T(8,128)(2,1)} fusion(bf16[2048,1024]{0,1:T(8,128)(2,1)S(1)} %copy-done.25, bf16[2048,768]{1,0:T(8,128)(2,1)S(1)} %copy-done.14), kind=kOutput, calls=%fused_computation.47 | convolution fusion | flops 4831838208 | bytes 11796480 | tf_op jit(solution)/shard_map/te,de->td/dot_general | solution.py:444
  544.8 22.1 %reduce-scatter.6.cloned.1.call-done = bf16[2,684,512]{2,1,0:T(8,128)(2,1)} async-done(((bf16[2,684,2048]{2,1,0:T(8,128)(2,1)}), bf16[2,684,512]{2,1,0:T(8,128)(2,1)}) %reduce-scatter.6.cloned.1.call-update) | async-done | bytes 1400848 | tf_op jit(solution)/shard_map/reduce_scatter | solution.py:422
  579.1 7.4 %collective-permute-done.79 = bf16[128,2048]{1,0:T(8,128)(2,1)S(1)} collective-permute-done((bf16[128,2048]{1,0:T(8,128)(2,1)S(1)}, bf16[128,2048]{1,0:T(8,128)(2,1)S(1)}, u32[]{:S(2)}, u32[]{:S(2)}) %collective-permute-start.79) | collective-permute-done | bytes 524320 | tf_op jit(solution)/shard_map/ppermute | solution.py:190
  589.9 7.9 %collective-permute-done.76 = bf16[128,2048]{1,0:T(8,128)(2,1)S(1)} collective-permute-done((bf16[128,2048]{1,0:T(8,128)(2,1)S(1)}, bf16[128,2048]{1,0:T(8,128)(2,1)S(1)}, u32[]{:S(2)}, u32[]{:S(2)}) %collective-permute-start.76) | collective-permute-done | bytes 524320 | tf_op jit(solution)/shard_map/ppermute | solution.py:190
  599.2 10.4 %collective-permute-done.80 = bf16[128,2048]{1,0:T(8,128)(2,1)S(1)} collective-permute-done((bf16[128,2048]{1,0:T(8,128)(2,1)S(1)}, bf16[128,2048]{1,0:T(8,128)(2,1)S(1)}, u32[]{:S(2)}, u32[]{:S(2)}) %collective-permute-start.80) | collective-permute-done | bytes 524320 | tf_op jit(solution)/shard_map/ppermute | solution.py:190
  623.6 5.0 multiply_subtract_fusion
  632.0 3.7 collective-permute-done.85
  636.5 16.3 %fusion.157 = (f32[512,2,684]{0,1,2:T(2,128)}, f32[512,2,684]{0,1,2:T(2,128)}, f32[512,2,684]{0,1,2:T(2,128)}) fusion(f32[]{:T(128)S(6)} %div.99, bf16[2,684,512]{2,1,0:T(8,128)(2,1)S(1)} %copy-done.24, f32[512,2,684]{0,1,2:T(2,128)S(1)} %copy-done.17, f32[512,2,684]{0,1,2:T(2,128)S(1)} %copy-done.18, f32[512,2,684]{0,1,2:T(2,128)S(1)} %copy-done.4), kind=kLoop, calls=%fused_computation.308 | loop fusion | flops 11206656 | bytes 18210820 | tf_op jit(solution)/shard_map/transpose | solution.py:296
  657.2 4.8 fusion.133
  (401 shorter events, 200.8 us)
Async XLA Ops:
  7.2 88.8 %all-gather.4.cloned.1.call-start = ((), (), s32[]{:S(2)}) async-start(), calls=%async_computation.3 | async-start | bytes 5242880 | tf_op jit(solution)/shard_map/all_gather | solution.py:340
  12.2 203.3 %all-gather.6.cloned.1.call-start = ((), (), s32[]{:S(2)}) async-start(), calls=%async_computation.4 | async-start | bytes 7045120 | tf_op jit(solution)/shard_map/all_gather | solution.py:346
  12.3 29.0 %collective-permute-start.1 = (bf16[256,2048]{1,0:T(8,128)(2,1)}, bf16[256,2048]{1,0:T(8,128)(2,1)}, u32[]{:S(2)}, u32[]{:S(2)}) collective-permute-start(bf16[256,2048]{1,0:T(8,128)(2,1)} %param.20), channel_id=1, source_target_pairs={{0,2},{1,3},{2,0},{3,1},{4,6},{5,7},{6,4},{7,5},{8,10},{9,11},{10,... | collective-permute-start | bytes 3145736 | tf_op jit(solution)/shard_map/ppermute | solution.py:190
  15.3 41.8 %collective-permute-start = (bf16[256,2048]{1,0:T(8,128)(2,1)}, bf16[256,2048]{1,0:T(8,128)(2,1)}, u32[]{:S(2)}, u32[]{:S(2)}) collective-permute-start(bf16[256,2048]{1,0:T(8,128)(2,1)} %param.20), channel_id=1, source_target_pairs={{0,1},{1,0},{2,3},{3,2},{4,5},{5,4},{6,7},{7,6},{8,9},{9,8},{10,11... | collective-permute-start | bytes 3145736 | tf_op jit(solution)/shard_map/ppermute | solution.py:190
  15.3 38.0 %collective-permute-start.3 = (bf16[256,2048]{1,0:T(8,128)(2,1)}, bf16[256,2048]{1,0:T(8,128)(2,1)}, u32[]{:S(2)}, u32[]{:S(2)}) collective-permute-start(bf16[256,2048]{1,0:T(8,128)(2,1)} %param.20), channel_id=1, source_target_pairs={{0,4},{1,5},{2,6},{3,7},{4,0},{5,1},{6,2},{7,3},{8,12},{9,13},{10,... | collective-permute-start | bytes 3145736 | tf_op jit(solution)/shard_map/ppermute | solution.py:190
  20.7 239.0 %all-gather.8.cloned.1.call-start = ((), (), s32[]{:S(2)}) async-start(), calls=%async_computation.5 | async-start | bytes 3522560 | tf_op jit(solution)/shard_map/all_gather | solution.py:347
  22.5 16.3 %collective-permute-start.10 = (f32[8,128]{1,0:T(8,128)S(1)}, f32[8,128]{1,0:T(8,128)S(1)}, u32[]{:S(2)}, u32[]{:S(2)}) collective-permute-start(f32[8,128]{1,0:T(8,128)S(1)} %broadcast_add_fusion), channel_id=1, source_target_pairs={{0,2},{1,3},{2,0},{3,1},{4,6},{5,7},{6,4},{7,5},{8,10},{9,11},{10,... | collective-permute-start | bytes 12296 | tf_op jit(solution)/shard_map/ppermute | solution.py:190
  41.3 24.2 %collective-permute-start.2 = (bf16[256,2048]{1,0:T(8,128)(2,1)}, bf16[256,2048]{1,0:T(8,128)(2,1)S(1)}, u32[]{:S(2)}, u32[]{:S(2)}) collective-permute-start(bf16[256,2048]{1,0:T(8,128)(2,1)} %collective-permute-done.1), channel_id=1, source_target_pairs={{0,1},{1,0},{2,3},{3,2},{4,5},{5,4},{6,7},{7,6},{8,9},{9,8},{10,11... | collective-permute-start | bytes 3145736 | tf_op jit(solution)/shard_map/ppermute | solution.py:190
  124.1 19.4 %collective-permute-start.14 = (bf16[256,2048]{1,0:T(8,128)(2,1)S(1)}, bf16[256,2048]{1,0:T(8,128)(2,1)S(1)}, u32[]{:S(2)}, u32[]{:S(2)}) collective-permute-start(bf16[256,2048]{1,0:T(8,128)(2,1)S(1)} %get-tuple-element.160), channel_id=1, source_target_pairs={{0,1},{1,0},{2,3},{3,2},{4,5},{5,4},{6,7},{7,6},{8,9},{9,8},{10,11... | collective-permute-start | bytes 3145736 | tf_op jit(solution)/shard_map/ppermute | solution.py:190
  126.8 15.0 %collective-permute-start.22 = (bf16[128,2048]{1,0:T(8,128)(2,1)S(1)}, bf16[128,2048]{1,0:T(8,128)(2,1)S(1)}, u32[]{:S(2)}, u32[]{:S(2)}) collective-permute-start(bf16[128,2048]{1,0:T(8,128)(2,1)S(1)} %get-tuple-element.179), channel_id=1, source_target_pairs={{0,2},{1,3},{2,0},{3,1},{4,6},{5,7},{6,4},{7,5},{8,10},{9,11},{10,... | collective-permute-start | bytes 1572872 | tf_op jit(solution)/shard_map/ppermute | solution.py:190
  129.2 23.7 %collective-permute-start.19 = (bf16[128,2048]{1,0:T(8,128)(2,1)S(1)}, bf16[128,2048]{1,0:T(8,128)(2,1)S(1)}, u32[]{:S(2)}, u32[]{:S(2)}) collective-permute-start(bf16[128,2048]{1,0:T(8,128)(2,1)S(1)} %slice.632), channel_id=1, source_target_pairs={{0,2},{1,3},{2,0},{3,1},{4,6},{5,7},{6,4},{7,5},{8,10},{9,11},{10,... | collective-permute-start | bytes 1572872 | tf_op jit(solution)/shard_map/ppermute | solution.py:190
  130.4 22.4 %collective-permute-start.21 = (bf16[128,2048]{1,0:T(8,128)(2,1)S(1)}, bf16[128,2048]{1,0:T(8,128)(2,1)S(1)}, u32[]{:S(2)}, u32[]{:S(2)}) collective-permute-start(bf16[128,2048]{1,0:T(8,128)(2,1)S(1)} %slice.631), channel_id=1, source_target_pairs={{0,4},{1,5},{2,6},{3,7},{4,0},{5,1},{6,2},{7,3},{8,12},{9,13},{10,... | collective-permute-start | bytes 1572872 | tf_op jit(solution)/shard_map/ppermute | solution.py:190
  140.1 22.8 %collective-permute-start.18 = (bf16[128,2048]{1,0:T(8,128)(2,1)S(1)}, bf16[128,2048]{1,0:T(8,128)(2,1)S(1)}, u32[]{:S(2)}, u32[]{:S(2)}) collective-permute-start(bf16[128,2048]{1,0:T(8,128)(2,1)S(1)} %fusion.125), channel_id=1, source_target_pairs={{0,2},{1,3},{2,0},{3,1},{4,6},{5,7},{6,4},{7,5},{8,10},{9,11},{10,... | collective-permute-start | bytes 1572872 | tf_op jit(solution)/shard_map/ppermute | solution.py:190
  141.9 21.0 %collective-permute-start.23 = (bf16[128,2048]{1,0:T(8,128)(2,1)S(1)}, bf16[128,2048]{1,0:T(8,128)(2,1)S(1)}, u32[]{:S(2)}, u32[]{:S(2)}) collective-permute-start(bf16[128,2048]{1,0:T(8,128)(2,1)S(1)} %fusion.124), channel_id=1, source_target_pairs={{0,4},{1,5},{2,6},{3,7},{4,0},{5,1},{6,2},{7,3},{8,12},{9,13},{10,... | collective-permute-start | bytes 1572872 | tf_op jit(solution)/shard_map/ppermute | solution.py:190
  166.0 24.4 %collective-permute-start.25 = (bf16[256,2048]{1,0:T(8,128)(2,1)}, bf16[256,2048]{1,0:T(8,128)(2,1)}, u32[]{:S(2)}, u32[]{:S(2)}) collective-permute-start(bf16[256,2048]{1,0:T(8,128)(2,1)} %get-tuple-element.139), channel_id=1, source_target_pairs={{0,2},{1,3},{2,0},{3,1},{4,6},{5,7},{6,4},{7,5},{8,10},{9,11},{10,... | collective-permute-start | bytes 3145736 | tf_op jit(solution)/shard_map/ppermute | solution.py:190
  167.5 25.9 %collective-permute-start.27 = (bf16[256,2048]{1,0:T(8,128)(2,1)}, bf16[256,2048]{1,0:T(8,128)(2,1)S(1)}, u32[]{:S(2)}, u32[]{:S(2)}) collective-permute-start(bf16[256,2048]{1,0:T(8,128)(2,1)} %get-tuple-element.139), channel_id=1, source_target_pairs={{0,4},{1,5},{2,6},{3,7},{4,0},{5,1},{6,2},{7,3},{8,12},{9,13},{10,... | collective-permute-start | bytes 3145736 | tf_op jit(solution)/shard_map/ppermute | solution.py:190
  168.0 27.0 %collective-permute-start.24 = (bf16[256,2048]{1,0:T(8,128)(2,1)}, bf16[256,2048]{1,0:T(8,128)(2,1)}, u32[]{:S(2)}, u32[]{:S(2)}) collective-permute-start(bf16[256,2048]{1,0:T(8,128)(2,1)} %get-tuple-element.139), channel_id=1, source_target_pairs={{0,1},{1,0},{2,3},{3,2},{4,5},{5,4},{6,7},{7,6},{8,9},{9,8},{10,11... | collective-permute-start | bytes 3145736 | tf_op jit(solution)/shard_map/ppermute | solution.py:190
  190.4 17.2 %collective-permute-start.26 = (bf16[256,2048]{1,0:T(8,128)(2,1)}, bf16[256,2048]{1,0:T(8,128)(2,1)}, u32[]{:S(2)}, u32[]{:S(2)}) collective-permute-start(bf16[256,2048]{1,0:T(8,128)(2,1)} %collective-permute-done.25), channel_id=1, source_target_pairs={{0,1},{1,0},{2,3},{3,2},{4,5},{5,4},{6,7},{7,6},{8,9},{9,8},{10,11... | collective-permute-start | bytes 3145736 | tf_op jit(solution)/shard_map/ppermute | solution.py:190
  191.4 253.0 %reduce-scatter.4.cloned.1.call-start = ((), (), s32[]{:S(2)}) async-start(), calls=%async_computation.6 | async-start | bytes 3522560 | tf_op jit(solution)/shard_map/reduce_scatter | solution.py:390
  194.9 16.2 %collective-permute-start.28 = (bf16[256,2048]{1,0:T(8,128)(2,1)S(1)}, bf16[256,2048]{1,0:T(8,128)(2,1)S(1)}, u32[]{:S(2)}, u32[]{:S(2)}) collective-permute-start(bf16[256,2048]{1,0:T(8,128)(2,1)S(1)} %collective-permute-done.27), channel_id=1, source_target_pairs={{0,1},{1,0},{2,3},{3,2},{4,5},{5,4},{6,7},{7,6},{8,9},{9,8},{10,11... | collective-permute-start | bytes 3145736 | tf_op jit(solution)/shard_map/ppermute | solution.py:190
  270.7 19.1 %collective-permute-start.33 = (bf16[256,2048]{1,0:T(8,128)(2,1)S(1)}, bf16[256,2048]{1,0:T(8,128)(2,1)S(1)}, u32[]{:S(2)}, u32[]{:S(2)}) collective-permute-start(bf16[256,2048]{1,0:T(8,128)(2,1)S(1)} %get-tuple-element.155), channel_id=1, source_target_pairs={{0,1},{1,0},{2,3},{3,2},{4,5},{5,4},{6,7},{7,6},{8,9},{9,8},{10,11... | collective-permute-start | bytes 3145736 | tf_op jit(solution)/shard_map/ppermute | solution.py:190
  273.1 15.0 %collective-permute-start.41 = (bf16[128,2048]{1,0:T(8,128)(2,1)S(1)}, bf16[128,2048]{1,0:T(8,128)(2,1)S(1)}, u32[]{:S(2)}, u32[]{:S(2)}) collective-permute-start(bf16[128,2048]{1,0:T(8,128)(2,1)S(1)} %get-tuple-element.177), channel_id=1, source_target_pairs={{0,2},{1,3},{2,0},{3,1},{4,6},{5,7},{6,4},{7,5},{8,10},{9,11},{10,... | collective-permute-start | bytes 1572872 | tf_op jit(solution)/shard_map/ppermute | solution.py:190
  275.4 23.8 %collective-permute-start.38 = (bf16[128,2048]{1,0:T(8,128)(2,1)S(1)}, bf16[128,2048]{1,0:T(8,128)(2,1)S(1)}, u32[]{:S(2)}, u32[]{:S(2)}) collective-permute-start(bf16[128,2048]{1,0:T(8,128)(2,1)S(1)} %slice.630), channel_id=1, source_target_pairs={{0,2},{1,3},{2,0},{3,1},{4,6},{5,7},{6,4},{7,5},{8,10},{9,11},{10,... | collective-permute-start | bytes 1572872 | tf_op jit(solution)/shard_map/ppermute | solution.py:190
  276.8 22.4 %collective-permute-start.40 = (bf16[128,2048]{1,0:T(8,128)(2,1)S(1)}, bf16[128,2048]{1,0:T(8,128)(2,1)S(1)}, u32[]{:S(2)}, u32[]{:S(2)}) collective-permute-start(bf16[128,2048]{1,0:T(8,128)(2,1)S(1)} %slice.629), channel_id=1, source_target_pairs={{0,4},{1,5},{2,6},{3,7},{4,0},{5,1},{6,2},{7,3},{8,12},{9,13},{10,... | collective-permute-start | bytes 1572872 | tf_op jit(solution)/shard_map/ppermute | solution.py:190
  286.6 22.7 %collective-permute-start.37 = (bf16[128,2048]{1,0:T(8,128)(2,1)S(1)}, bf16[128,2048]{1,0:T(8,128)(2,1)S(1)}, u32[]{:S(2)}, u32[]{:S(2)}) collective-permute-start(bf16[128,2048]{1,0:T(8,128)(2,1)S(1)} %fusion.123), channel_id=1, source_target_pairs={{0,2},{1,3},{2,0},{3,1},{4,6},{5,7},{6,4},{7,5},{8,10},{9,11},{10,... | collective-permute-start | bytes 1572872 | tf_op jit(solution)/shard_map/ppermute | solution.py:190
  288.2 21.0 %collective-permute-start.42 = (bf16[128,2048]{1,0:T(8,128)(2,1)S(1)}, bf16[128,2048]{1,0:T(8,128)(2,1)S(1)}, u32[]{:S(2)}, u32[]{:S(2)}) collective-permute-start(bf16[128,2048]{1,0:T(8,128)(2,1)S(1)} %fusion.122), channel_id=1, source_target_pairs={{0,4},{1,5},{2,6},{3,7},{4,0},{5,1},{6,2},{7,3},{8,12},{9,13},{10,... | collective-permute-start | bytes 1572872 | tf_op jit(solution)/shard_map/ppermute | solution.py:190
  314.2 24.1 %collective-permute-start.44 = (bf16[256,2048]{1,0:T(8,128)(2,1)S(1)}, bf16[256,2048]{1,0:T(8,128)(2,1)S(1)}, u32[]{:S(2)}, u32[]{:S(2)}) collective-permute-start(bf16[256,2048]{1,0:T(8,128)(2,1)S(1)} %get-tuple-element.135), channel_id=1, source_target_pairs={{0,2},{1,3},{2,0},{3,1},{4,6},{5,7},{6,4},{7,5},{8,10},{9,11},{10,... | collective-permute-start | bytes 3145736 | tf_op jit(solution)/shard_map/ppermute | solution.py:190
  315.7 23.7 %collective-permute-start.46 = (bf16[256,2048]{1,0:T(8,128)(2,1)S(1)}, bf16[256,2048]{1,0:T(8,128)(2,1)S(1)}, u32[]{:S(2)}, u32[]{:S(2)}) collective-permute-start(bf16[256,2048]{1,0:T(8,128)(2,1)S(1)} %get-tuple-element.135), channel_id=1, source_target_pairs={{0,4},{1,5},{2,6},{3,7},{4,0},{5,1},{6,2},{7,3},{8,12},{9,13},{10,... | collective-permute-start | bytes 3145736 | tf_op jit(solution)/shard_map/ppermute | solution.py:190
  316.3 24.8 %collective-permute-start.43 = (bf16[256,2048]{1,0:T(8,128)(2,1)S(1)}, bf16[256,2048]{1,0:T(8,128)(2,1)S(1)}, u32[]{:S(2)}, u32[]{:S(2)}) collective-permute-start(bf16[256,2048]{1,0:T(8,128)(2,1)S(1)} %get-tuple-element.135), channel_id=1, source_target_pairs={{0,1},{1,0},{2,3},{3,2},{4,5},{5,4},{6,7},{7,6},{8,9},{9,8},{10,11... | collective-permute-start | bytes 3145736 | tf_op jit(solution)/shard_map/ppermute | solution.py:190
  338.3 16.2 %collective-permute-start.45 = (bf16[256,2048]{1,0:T(8,128)(2,1)S(1)}, bf16[256,2048]{1,0:T(8,128)(2,1)S(1)}, u32[]{:S(2)}, u32[]{:S(2)}) collective-permute-start(bf16[256,2048]{1,0:T(8,128)(2,1)S(1)} %collective-permute-done.44), channel_id=1, source_target_pairs={{0,1},{1,0},{2,3},{3,2},{4,5},{5,4},{6,7},{7,6},{8,9},{9,8},{10,11... | collective-permute-start | bytes 3145736 | tf_op jit(solution)/shard_map/ppermute | solution.py:190
  339.5 15.2 %collective-permute-start.47 = (bf16[256,2048]{1,0:T(8,128)(2,1)S(1)}, bf16[256,2048]{1,0:T(8,128)(2,1)S(1)}, u32[]{:S(2)}, u32[]{:S(2)}) collective-permute-start(bf16[256,2048]{1,0:T(8,128)(2,1)S(1)} %collective-permute-done.46), channel_id=1, source_target_pairs={{0,1},{1,0},{2,3},{3,2},{4,5},{5,4},{6,7},{7,6},{8,9},{9,8},{10,11... | collective-permute-start | bytes 3145736 | tf_op jit(solution)/shard_map/ppermute | solution.py:190
  367.4 199.5 %reduce-scatter.6.cloned.1.call-start = ((), (), s32[]{:S(2)}) async-start(), calls=%async_computation.7 | async-start | bytes 7045120 | tf_op jit(solution)/shard_map/reduce_scatter | solution.py:422
  406.1 28.1 %collective-permute-start.58 = (bf16[128,2048]{1,0:T(8,128)(2,1)S(1)}, bf16[128,2048]{1,0:T(8,128)(2,1)S(1)}, u32[]{:S(2)}, u32[]{:S(2)}) collective-permute-start(bf16[128,2048]{1,0:T(8,128)(2,1)S(1)} %slice.628), channel_id=1, source_target_pairs={{0,2},{1,3},{2,0},{3,1},{4,6},{5,7},{6,4},{7,5},{8,10},{9,11},{10,... | collective-permute-start | bytes 1572872 | tf_op jit(solution)/shard_map/ppermute | solution.py:190
  409.8 24.3 %collective-permute-start.59 = (bf16[128,2048]{1,0:T(8,128)(2,1)S(1)}, bf16[128,2048]{1,0:T(8,128)(2,1)S(1)}, u32[]{:S(2)}, u32[]{:S(2)}) collective-permute-start(bf16[128,2048]{1,0:T(8,128)(2,1)S(1)} %slice.627), channel_id=1, source_target_pairs={{0,4},{1,5},{2,6},{3,7},{4,0},{5,1},{6,2},{7,3},{8,12},{9,13},{10,... | collective-permute-start | bytes 1572872 | tf_op jit(solution)/shard_map/ppermute | solution.py:190
  410.9 23.3 %collective-permute-start.57 = (bf16[128,2048]{1,0:T(8,128)(2,1)S(1)}, bf16[128,2048]{1,0:T(8,128)(2,1)S(1)}, u32[]{:S(2)}, u32[]{:S(2)}) collective-permute-start(bf16[128,2048]{1,0:T(8,128)(2,1)S(1)} %fusion.121), channel_id=1, source_target_pairs={{0,2},{1,3},{2,0},{3,1},{4,6},{5,7},{6,4},{7,5},{8,10},{9,11},{10,... | collective-permute-start | bytes 1572872 | tf_op jit(solution)/shard_map/ppermute | solution.py:190
  442.9 25.2 %collective-permute-start.63 = (bf16[256,2048]{1,0:T(8,128)(2,1)S(1)}, bf16[256,2048]{1,0:T(8,128)(2,1)S(1)}, u32[]{:S(2)}, u32[]{:S(2)}) collective-permute-start(bf16[256,2048]{1,0:T(8,128)(2,1)S(1)} %get-tuple-element.131), channel_id=1, source_target_pairs={{0,2},{1,3},{2,0},{3,1},{4,6},{5,7},{6,4},{7,5},{8,10},{9,11},{10,... | collective-permute-start | bytes 3145736 | tf_op jit(solution)/shard_map/ppermute | solution.py:190
  443.5 24.9 %collective-permute-start.64 = (bf16[256,2048]{1,0:T(8,128)(2,1)S(1)}, bf16[256,2048]{1,0:T(8,128)(2,1)S(1)}, u32[]{:S(2)}, u32[]{:S(2)}) collective-permute-start(bf16[256,2048]{1,0:T(8,128)(2,1)S(1)} %get-tuple-element.131), channel_id=1, source_target_pairs={{0,4},{1,5},{2,6},{3,7},{4,0},{5,1},{6,2},{7,3},{8,12},{9,13},{10,... | collective-permute-start | bytes 3145736 | tf_op jit(solution)/shard_map/ppermute | solution.py:190
  468.4 184.3 %reduce-scatter.8.cloned.1.call-start = ((), (), s32[]{:S(2)}) async-start(), calls=%async_computation.8 | async-start | bytes 5242880 | tf_op jit(solution)/shard_map/reduce_scatter | solution.py:439
  468.7 15.7 %collective-permute-start.65 = (bf16[256,2048]{1,0:T(8,128)(2,1)S(1)}, bf16[256,2048]{1,0:T(8,128)(2,1)S(1)}, u32[]{:S(2)}, u32[]{:S(2)}) collective-permute-start(bf16[256,2048]{1,0:T(8,128)(2,1)S(1)} %collective-permute-done.63), channel_id=1, source_target_pairs={{0,1},{1,0},{2,3},{3,2},{4,5},{5,4},{6,7},{7,6},{8,9},{9,8},{10,11... | collective-permute-start | bytes 3145736 | tf_op jit(solution)/shard_map/ppermute | solution.py:190
  469.2 17.3 %collective-permute-start.66 = (bf16[256,2048]{1,0:T(8,128)(2,1)S(1)}, bf16[256,2048]{1,0:T(8,128)(2,1)S(1)}, u32[]{:S(2)}, u32[]{:S(2)}) collective-permute-start(bf16[256,2048]{1,0:T(8,128)(2,1)S(1)} %collective-permute-done.64), channel_id=1, source_target_pairs={{0,1},{1,0},{2,3},{3,2},{4,5},{5,4},{6,7},{7,6},{8,9},{9,8},{10,11... | collective-permute-start | bytes 3145736 | tf_op jit(solution)/shard_map/ppermute | solution.py:190
  537.3 32.7 %collective-permute-start.73 = (bf16[256,2048]{1,0:T(8,128)(2,1)}, bf16[256,2048]{1,0:T(8,128)(2,1)}, u32[]{:S(2)}, u32[]{:S(2)}) collective-permute-start(bf16[256,2048]{1,0:T(8,128)(2,1)} %slice.372), channel_id=1, source_target_pairs={{0,1},{1,0},{2,3},{3,2},{4,5},{5,4},{6,7},{7,6},{8,9},{9,8},{10,11... | collective-permute-start | bytes 3145736 | tf_op jit(solution)/shard_map/ppermute | solution.py:190
  569.9 20.0 %collective-permute-start.71 = (bf16[256,2048]{1,0:T(8,128)(2,1)S(1)}, bf16[256,2048]{1,0:T(8,128)(2,1)S(1)}, u32[]{:S(2)}, u32[]{:S(2)}) collective-permute-start(bf16[256,2048]{1,0:T(8,128)(2,1)S(1)} %get-tuple-element.154), channel_id=1, source_target_pairs={{0,1},{1,0},{2,3},{3,2},{4,5},{5,4},{6,7},{7,6},{8,9},{9,8},{10,11... | collective-permute-start | bytes 3145736 | tf_op jit(solution)/shard_map/ppermute | solution.py:190
  571.7 14.9 %collective-permute-start.79 = (bf16[128,2048]{1,0:T(8,128)(2,1)S(1)}, bf16[128,2048]{1,0:T(8,128)(2,1)S(1)}, u32[]{:S(2)}, u32[]{:S(2)}) collective-permute-start(bf16[128,2048]{1,0:T(8,128)(2,1)S(1)} %get-tuple-element.172), channel_id=1, source_target_pairs={{0,2},{1,3},{2,0},{3,1},{4,6},{5,7},{6,4},{7,5},{8,10},{9,11},{10,... | collective-permute-start | bytes 1572872 | tf_op jit(solution)/shard_map/ppermute | solution.py:190
  573.2 15.0 %collective-permute-start.74 = (bf16[128,2048]{1,0:T(8,128)(2,1)S(1)}, bf16[128,2048]{1,0:T(8,128)(2,1)S(1)}, u32[]{:S(2)}, u32[]{:S(2)}) collective-permute-start(bf16[128,2048]{1,0:T(8,128)(2,1)S(1)} %get-tuple-element.173), channel_id=1, source_target_pairs={{0,4},{1,5},{2,6},{3,7},{4,0},{5,1},{6,2},{7,3},{8,12},{9,13},{10,... | collective-permute-start | bytes 1572872 | tf_op jit(solution)/shard_map/ppermute | solution.py:190
  577.7 20.1 %collective-permute-start.76 = (bf16[128,2048]{1,0:T(8,128)(2,1)S(1)}, bf16[128,2048]{1,0:T(8,128)(2,1)S(1)}, u32[]{:S(2)}, u32[]{:S(2)}) collective-permute-start(bf16[128,2048]{1,0:T(8,128)(2,1)S(1)} %slice.626), channel_id=1, source_target_pairs={{0,2},{1,3},{2,0},{3,1},{4,6},{5,7},{6,4},{7,5},{8,10},{9,11},{10,... | collective-permute-start | bytes 1572872 | tf_op jit(solution)/shard_map/ppermute | solution.py:190
  577.9 21.4 %collective-permute-start.78 = (bf16[128,2048]{1,0:T(8,128)(2,1)S(1)}, bf16[128,2048]{1,0:T(8,128)(2,1)S(1)}, u32[]{:S(2)}, u32[]{:S(2)}) collective-permute-start(bf16[128,2048]{1,0:T(8,128)(2,1)S(1)} %slice.625), channel_id=1, source_target_pairs={{0,4},{1,5},{2,6},{3,7},{4,0},{5,1},{6,2},{7,3},{8,12},{9,13},{10,... | collective-permute-start | bytes 1572872 | tf_op jit(solution)/shard_map/ppermute | solution.py:190
  586.7 23.0 %collective-permute-start.80 = (bf16[128,2048]{1,0:T(8,128)(2,1)S(1)}, bf16[128,2048]{1,0:T(8,128)(2,1)S(1)}, u32[]{:S(2)}, u32[]{:S(2)}) collective-permute-start(bf16[128,2048]{1,0:T(8,128)(2,1)S(1)} %fusion.118), channel_id=1, source_target_pairs={{0,4},{1,5},{2,6},{3,7},{4,0},{5,1},{6,2},{7,3},{8,12},{9,13},{10,... | collective-permute-start | bytes 1572872 | tf_op jit(solution)/shard_map/ppermute | solution.py:190
  588.3 21.4 %collective-permute-start.75 = (bf16[128,2048]{1,0:T(8,128)(2,1)S(1)}, bf16[128,2048]{1,0:T(8,128)(2,1)S(1)}, u32[]{:S(2)}, u32[]{:S(2)}) collective-permute-start(bf16[128,2048]{1,0:T(8,128)(2,1)S(1)} %fusion.119), channel_id=1, source_target_pairs={{0,2},{1,3},{2,0},{3,1},{4,6},{5,7},{6,4},{7,5},{8,10},{9,11},{10,... | collective-permute-start | bytes 1572872 | tf_op jit(solution)/shard_map/ppermute | solution.py:190
  (91 other events, 653.4 us)
Sparse Core Ops, SparseCore 0:
  12.4 83.5 all-gather.3
  98.1 103.0 all-gather.5
  203.4 56.3 all-gather.7
  367.5 52.7 reduce-scatter.3
  468.6 98.2 reduce-scatter.5
  569.0 78.6 reduce-scatter.7

commit v6 on v5

--- a/solution.py
+++ b/solution.py
@@ -223,7 +223,7 @@
     return pieces
 
 
-def scatter_near(pieces):
+def scatter_near(pieces, ahead=None):
     blocks = []
     own_rows = sum(piece.shape[0] for piece in pieces) // 8
     half = own_rows // 2
@@ -237,6 +237,8 @@
     ]
     far = sums[3].astype(jnp.bfloat16)
     far_low, far_high = swap(far[:half], "mp", 4), swap(far[half:], "mp", 2)
+    if ahead is not None:
+        far_low, far_high, ahead = lax.optimization_barrier((far_low, far_high, ahead))
     x_low = (sums[1][:half] + far_low.astype(jnp.float32)).astype(jnp.bfloat16)
     y_high = (sums[2][half:] + far_high.astype(jnp.float32)).astype(jnp.bfloat16)
     x_high, y_low = sums[1][half:].astype(jnp.bfloat16), sums[2][:half].astype(jnp.bfloat16)
@@ -244,7 +246,8 @@
     y_low, y_high = swap(y_low, "mp", 4), swap(y_high, "mp", 4)
     across_x = jnp.concatenate([x_low, x_high], 0).astype(jnp.float32)
     across_y = jnp.concatenate([y_low, y_high], 0).astype(jnp.float32)
-    return sums[0] + across_x + across_y
+    total = sums[0] + across_x + across_y
+    return total if ahead is None else (total, ahead)
 
 
 def core_sum(piece):
@@ -253,7 +256,7 @@
     return piece[:half].astype(jnp.float32) + mate.astype(jnp.float32)
 
 
-def scatter_beside(rows, product):
+def scatter_beside(rows, product, last=None):
     far = product(rows, 3)
     rows, far = lax.optimization_barrier((rows, far))
     near_x = product(rows, 1)
@@ -268,11 +271,14 @@
     y_high = (near_y[high] + far_high.astype(jnp.float32)).astype(jnp.bfloat16)
     rows, x_low, y_high = lax.optimization_barrier((rows, x_low, y_high))
     x_high, y_low = near_x[high].astype(jnp.bfloat16), near_y[low].astype(jnp.bfloat16)
-    across_x = jnp.concatenate([swap(x_low, "mp", 2), swap(x_high, "mp", 2)], 0)
-    across_y = jnp.concatenate([swap(y_low, "mp", 4), swap(y_high, "mp", 4)], 0)
-    own, across_x, across_y = lax.optimization_barrier((product(rows, 0), across_x, across_y))
+    across = [swap(x_low, "mp", 2), swap(x_high, "mp", 2), swap(y_low, "mp", 4), swap(y_high, "mp", 4)]
+    own = product(rows, 0)
+    ahead = () if last is None else last()
+    own, across, ahead = lax.optimization_barrier((own, across, ahead))
+    across_x, across_y = jnp.concatenate(across[:2], 0), jnp.concatenate(across[2:], 0)
     own = core_sum(own)
-    return own + across_x.astype(jnp.float32) + across_y.astype(jnp.float32)
+    total = own + across_x.astype(jnp.float32) + across_y.astype(jnp.float32)
+    return total if last is None else (total, ahead)
 
 
 def gather_all(rows, ahead=None):
@@ -280,9 +286,10 @@
     return whole if ahead is None else (whole, ahead)
 
 
-def scatter_all(pieces):
+def scatter_all(pieces, ahead=None):
     whole = jnp.concatenate(pieces, 0)
-    return lax.psum_scatter(whole, "mp", scatter_dimension=0, tiled=True).astype(jnp.float32)
+    total = lax.psum_scatter(whole, "mp", scatter_dimension=0, tiled=True).astype(jnp.float32)
+    return total if ahead is None else (total, ahead)
 
 
 def adamw_as(order, weight, gradient, first_moment, second, step_rate, scale):
@@ -372,13 +379,16 @@
         "td,cfd->ctf", middle_low, gateup_full, preferred_element_type=jnp.float32
     )
     hidden_low = (jax.nn.gelu(gate_up[0]) * gate_up[1] * live_units).astype(jnp.bfloat16)
-    ffn_own = scatter_rows(
-        far_first(
-            hidden_low,
-            lambda rows: jnp.dot(rows, down_full, preferred_element_type=jnp.bfloat16),
-            two_pieces,
-        )
-    )
+    quarter = hidden_low.shape[0] // 4
+
+    def down_quarter(rows, index):
+        rows = rows[index * quarter : (index + 1) * quarter]
+        return jnp.dot(rows, down_full, preferred_element_type=jnp.bfloat16)
+
+    if near:
+        ffn_own = scatter_beside(hidden_low, down_quarter)
+    else:
+        ffn_own = scatter_all([down_quarter(hidden_low, index) for index in range(4)])
     hidden_two = deep_alpha * middle + ffn_own
     output_rows, normed_two, inv_two = norm_forward(hidden_two, norm_params[2], norm_params[3])
     grad_rows = out_cotangent.astype(jnp.float32) * mask_f32[:, None]
@@ -388,7 +398,6 @@
     down_grad = jnp.einsum("tf,td->fd", hidden_low, ffn_back, preferred_element_type=jnp.bfloat16)
     ffn_back, down_grad = lax.optimization_barrier((ffn_back, down_grad))
     down_grad = lax.psum_scatter(down_grad, "dp", scatter_dimension=1, tiled=True)
-    quarter = ffn_back.shape[0] // 4
     grad_gateups = [None] * 4
 
     def back_quarter(rows, index):
@@ -403,21 +412,30 @@
         grad_gateups[index] = grads
         return jnp.einsum("ctf,cfd->td", grads, gateup_full, preferred_element_type=jnp.bfloat16)
 
+    middle_low, down_grad = lax.optimization_barrier((middle_low, down_grad))
+
+    def gateup_product():
+        return jnp.einsum(
+            "ctf,td->cfd",
+            jnp.concatenate(grad_gateups, 1),
+            middle_low,
+            preferred_element_type=jnp.bfloat16,
+        )
+
     if near:
-        grad_middle = scatter_beside(ffn_back, back_quarter)
+        grad_middle, gateup_grad = scatter_beside(ffn_back, back_quarter, gateup_product)
     else:
         grad_middle = scatter_all([back_quarter(ffn_back, index) for index in range(4)])
+        gateup_grad = gateup_product()
     grad_middle = grad_middle + deep_alpha * grad_two
-    middle_low, down_grad = lax.optimization_barrier((middle_low, down_grad))
-    gateup_grad = jnp.einsum(
-        "ctf,td->cfd",
-        jnp.concatenate(grad_gateups, 1),
-        middle_low,
-        preferred_element_type=jnp.bfloat16,
-    )
     grad_one, gain_one, bias_one = norm_backward(grad_middle, normed_one, inv_one, norm_params[0])
 
-    attn_back, gateup_grad = gather_rows(grad_one.astype(jnp.bfloat16), gateup_grad)
+    rate_list = (D ** (-0.5), 0.5, D ** (-0.5), (FF_PAD // 64) ** (-0.5), 0.4)
+    scale = 1.0 / target_count
+    down_res = adamw_as(
+        (0, 1), down_weight, down_grad, down_first, down_second, rate_list[3], scale
+    )
+    attn_back, down_res = gather_rows(grad_one.astype(jnp.bfloat16), down_res)
     gateup_grad = with_layout_constraint(
         lax.psum_scatter(gateup_grad, "dp", scatter_dimension=2, tiled=True),
         Layout(major_to_minor=(0, 1, 2)),
@@ -437,23 +455,6 @@
     grad_proj, attend_grad = lax.optimization_barrier((grad_proj, attend_grad))
     attend_grad, gateup_grad = lax.optimization_barrier((attend_grad, gateup_grad))
     attend_grad = lax.psum_scatter(attend_grad, "dp", scatter_dimension=1, tiled=True)
-    input_raw = (
-        scatter_rows(
-            far_first(
-                grad_proj,
-                lambda rows: jnp.einsum(
-                    "te,de->td", rows, qkv_full, preferred_element_type=jnp.bfloat16
-                ),
-                two_pieces,
-            )
-        )
-        + deep_alpha * grad_one
-    )
-    norm_grad = jnp.stack([gain_one, bias_one, gain_two, bias_two], 0)
-    norm_grad, input_raw = lax.optimization_barrier((norm_grad, input_raw))
-    norm_grad = sum_everywhere(norm_grad)
-    rate_list = (D ** (-0.5), 0.5, D ** (-0.5), (FF_PAD // 64) ** (-0.5), 0.4)
-    scale = 1.0 / target_count
     gateup_res = adamw_as(
         (2, 1, 0),
         gateup_weight,
@@ -463,12 +464,20 @@
         rate_list[2],
         scale,
     )
-    down_res = adamw_as(
-        (0, 1), down_weight, down_grad, down_first, down_second, rate_list[3], scale
-    )
-    attend_grad, gateup_res, down_res = lax.optimization_barrier(
-        (attend_grad, gateup_res, down_res)
-    )
+    input_raw, gateup_res = scatter_rows(
+        far_first(
+            grad_proj,
+            lambda rows: jnp.einsum(
+                "te,de->td", rows, qkv_full, preferred_element_type=jnp.bfloat16
+            ),
+            two_pieces,
+        ),
+        gateup_res,
+    )
+    input_raw = input_raw + deep_alpha * grad_one
+    norm_grad = jnp.stack([gain_one, bias_one, gain_two, bias_two], 0)
+    norm_grad, input_raw = lax.optimization_barrier((norm_grad, input_raw))
+    norm_grad = sum_everywhere(norm_grad)
     out_grad = attend_grad[:local_dim]
     qkv_grad = attend_grad[local_dim:].reshape(3, local_dim, shard_rows)
     qkv_res = adamw_as(

time: 674 us -> 651 us (0.966)
  waiting for transfers between devices: 288 us -> 272 us
    reduce_scatter x1, waiting for transfers between devices: 22.1 us -> 0.01 us  [local(): lax.psum_scatter(gateup_grad, 'dp', scatter_dimension=2, tiled=True)]
    unnamed x126 -> x132, local copies, waits for them, and re-layouts: 48.2 us -> 44.4 us
    dot_general x3 -> x5, matrix products: 27.7 us -> 27.4 us  [the longest x1 17.8 us: gateup_product(): jnp.einsum('ctf,td->cfd', jnp.concatenate(grad_gateups, 1), middle_low, p...]
  transfers between devices with their start and end apart: 92 -> 92, of which waited for: 42 -> 45; matrix products, arithmetic and copies ran while one was open for 35% -> 35% of each run, Pallas kernels for 4% -> 4%
where the time goes in v6:
time: 651 us; the launch traced here: 646 us
  waiting for transfers between devices  272 us (42%)
  matrix products  138 us (21%)
  other arithmetic  72.6 us (11%)
  starting transfers between devices  63.5 us (10%)
  local copies, waits for them, and re-layouts  59.9 us (9%)
  Pallas kernels  24.1 us (4%)
  between operations  16.5 us (3%)
    ppermute x86, waiting for transfers between devices, swap(): return lax.ppermute(values, axis, [(at, at ^ bit) for at in range(size)])  224 us
    ppermute x86, starting transfers between devices, swap(): return lax.ppermute(values, axis, [(at, at ^ bit) for at in range(size)])  62.7 us
    unnamed x132, local copies, waits for them, and re-layouts  44.4 us
    all_gather x1, waiting for transfers between devices, local(): attend_full = lax.all_gather(attend_low, 'dp', axis=0, tiled=True)  22.7 us
    transpose x2, other arithmetic, adamw_as(): jnp.transpose(rows, back)  21.9 us
    all_gather x1, waiting for transfers between devices, local(): lax.all_gather(down_weight.astype(jnp.bfloat16), 'dp', axis=1, tiled=True)  19.8 us
    dot_general x4, matrix products, back_quarter(): jnp.einsum('td,fd->tf', rows[at], down_full, preferred_element_type=jnp.f...  19.2 us
    dot_general x4, matrix products, back_quarter(): jnp.einsum('ctf,cfd->td', grads, gateup_full, preferred_element_type=jnp....  18.5 us
  transfers between devices with their start and end apart: 92, of which 45 were waited for; matrix products, arithmetic and copies ran while one was open for 35% of the time, Pallas kernels for 4%

profile of v6, /device:TPU:0, one launch (start us, length us, event | category | flops | bytes accessed | tf_op | source)
XLA Modules:
  0.0 646.1 jit_solution(9941049581802421513)
XLA Ops:
  23.1 15.7 %collective-permute-done.10 = f32[8,128]{1,0:T(8,128)S(1)} collective-permute-done((f32[8,128]{1,0:T(8,128)S(1)}, f32[8,128]{1,0:T(8,128)S(1)}, u32[]{:S(2)}, u32[]{:S(2)}) %collective-permute-start.10) | collective-permute-done | bytes 4128 | tf_op jit(solution)/shard_map/ppermute | solution.py:190
  73.3 22.7 %all-gather.4.cloned.1.call-done = bf16[2048,1024]{0,1:T(8,128)(2,1)} async-done(((bf16[512,1024]{0,1:T(8,128)(2,1)}), bf16[2048,1024]{0,1:T(8,128)(2,1)}) %all-gather.4.cloned.1.call-update) | async-done | bytes 4194320 | tf_op jit(solution)/shard_map/all_gather | solution.py:347
  96.0 12.0 %fusion.40.proj_ref = f32[2048,768]{1,0:T(8,128)} fusion(bf16[2048,2048]{1,0:T(8,128)(2,1)} %constant_dynamic-update-slice_fusion, bf16[2048,1024]{0,1:T(8,128)(2,1)} %all-gather.4.cloned.1.call-done), kind=kOutput, calls=%fused_computation.51 | convolution fusion | flops 6442450944 | bytes 17825792 | tf_op jit(solution)/shard_map/dot_general | solution.py:362
  108.0 10.0 %attend_forward.1 = (bf16[2048,256]{1,0:T(8,128)(2,1)}, bf16[2048,256]{1,0:T(8,128)(2,1)}, bf16[2048,256]{1,0:T(8,128)(2,1)}, bf16[2048,256]{1,0:T(8,128)(2,1)}) custom-call(s32[4]{0:T(128)} %objective_ref.3, s32[4]{0:T(128)} %prefix_ref.3, s32[2]{0:T(128)} %pad_add_fusion.place_ref, f32[2048,768]{1,0:T(8,128)} %fusion.40.proj_ref, ...), custom_call_target="tpu_custom_call" | custom-call | tf_op jit(solution)/shard_map/attend_forward/pallas_call | solution.py:138
  132.1 8.0 %collective-permute-done.17 = bf16[128,2048]{1,0:T(8,128)(2,1)S(1)} collective-permute-done((bf16[128,2048]{1,0:T(8,128)(2,1)S(1)}, bf16[128,2048]{1,0:T(8,128)(2,1)S(1)}, u32[]{:S(2)}, u32[]{:S(2)}) %collective-permute-start.17) | collective-permute-done | bytes 524320 | tf_op jit(solution)/shard_map/ppermute | solution.py:190
  143.6 9.3 %collective-permute-done.19 = bf16[128,2048]{1,0:T(8,128)(2,1)S(1)} collective-permute-done((bf16[128,2048]{1,0:T(8,128)(2,1)S(1)}, bf16[128,2048]{1,0:T(8,128)(2,1)S(1)}, u32[]{:S(2)}, u32[]{:S(2)}) %collective-permute-start.19) | collective-permute-done | bytes 524320 | tf_op jit(solution)/shard_map/ppermute | solution.py:190
  152.9 10.1 %collective-permute-done.18 = bf16[128,2048]{1,0:T(8,128)(2,1)S(1)} collective-permute-done((bf16[128,2048]{1,0:T(8,128)(2,1)S(1)}, bf16[128,2048]{1,0:T(8,128)(2,1)S(1)}, u32[]{:S(2)}, u32[]{:S(2)}) %collective-permute-start.18) | collective-permute-done | bytes 524320 | tf_op jit(solution)/shard_map/ppermute | solution.py:190
  168.1 22.4 %collective-permute-done.25 = bf16[256,2048]{1,0:T(8,128)(2,1)} collective-permute-done((bf16[256,2048]{1,0:T(8,128)(2,1)}, bf16[256,2048]{1,0:T(8,128)(2,1)}, u32[]{:S(2)}, u32[]{:S(2)}) %collective-permute-start.25) | collective-permute-done | bytes 1048608 | tf_op jit(solution)/shard_map/ppermute | solution.py:190
  200.0 7.5 %collective-permute-done.29 = bf16[128,2048]{1,0:T(8,128)(2,1)S(1)} collective-permute-done((bf16[128,2048]{1,0:T(8,128)(2,1)S(1)}, bf16[128,2048]{1,0:T(8,128)(2,1)S(1)}, u32[]{:S(2)}, u32[]{:S(2)}) %collective-permute-start.29) | collective-permute-done | bytes 524320 | tf_op jit(solution)/shard_map/ppermute | solution.py:190
  216.0 16.0 %fusion.29 = f32[2,2048,684]{1,2,0:T(8,128)S(1)} fusion(bf16[2,684,2048]{2,1,0:T(8,128)(2,1)} %all-gather.6.cloned.1.call-done, bf16[2048,2048]{1,0:T(8,128)(2,1)} %constant_dynamic-update-slice_fusion.10), kind=kOutput, calls=%fused_computation.32 | convolution fusion | flops 11475615744 | bytes 25198592 | tf_op jit(solution)/shard_map/td,cfd->ctf/dot_general | solution.py:378
  232.1 4.2 copy-done.4
  236.2 3.7 fusion.13
  239.9 19.8 %all-gather.8.cloned.1.call-done = bf16[684,2048]{1,0:T(8,128)(2,1)} async-done(((bf16[684,512]{1,0:T(8,128)(2,1)}), bf16[684,2048]{1,0:T(8,128)(2,1)}) %all-gather.8.cloned.1.call-update) | async-done | bytes 2801680 | tf_op jit(solution)/shard_map/all_gather | solution.py:354
  259.7 4.0 fusion.134
  272.3 9.4 %collective-permute-done.35 = bf16[128,2048]{1,0:T(8,128)(2,1)S(1)} collective-permute-done((bf16[128,2048]{1,0:T(8,128)(2,1)S(1)}, bf16[128,2048]{1,0:T(8,128)(2,1)S(1)}, u32[]{:S(2)}, u32[]{:S(2)}) %collective-permute-start.35) | collective-permute-done | bytes 524320 | tf_op jit(solution)/shard_map/ppermute | solution.py:190
  291.7 6.7 %collective-permute-done.39 = bf16[128,2048]{1,0:T(8,128)(2,1)S(1)} collective-permute-done((bf16[128,2048]{1,0:T(8,128)(2,1)S(1)}, bf16[128,2048]{1,0:T(8,128)(2,1)S(1)}, u32[]{:S(2)}, u32[]{:S(2)}) %collective-permute-start.39) | collective-permute-done | bytes 524320 | tf_op jit(solution)/shard_map/ppermute | solution.py:190
  298.4 10.8 %collective-permute-done.38 = bf16[128,2048]{1,0:T(8,128)(2,1)S(1)} collective-permute-done((bf16[128,2048]{1,0:T(8,128)(2,1)S(1)}, bf16[128,2048]{1,0:T(8,128)(2,1)S(1)}, u32[]{:S(2)}, u32[]{:S(2)}) %collective-permute-start.38) | collective-permute-done | bytes 524320 | tf_op jit(solution)/shard_map/ppermute | solution.py:190
  309.2 3.6 collective-permute-done.40
  323.7 24.1 %collective-permute-done.44 = bf16[256,2048]{1,0:T(8,128)(2,1)S(1)} collective-permute-done((bf16[256,2048]{1,0:T(8,128)(2,1)S(1)}, bf16[256,2048]{1,0:T(8,128)(2,1)S(1)}, u32[]{:S(2)}, u32[]{:S(2)}) %collective-permute-start.44) | collective-permute-done | bytes 1048608 | tf_op jit(solution)/shard_map/ppermute | solution.py:190
  350.5 12.0 %collective-permute-done.48 = bf16[128,2048]{1,0:T(8,128)(2,1)S(1)} collective-permute-done((bf16[128,2048]{1,0:T(8,128)(2,1)S(1)}, bf16[128,2048]{1,0:T(8,128)(2,1)S(1)}, u32[]{:S(2)}, u32[]{:S(2)}) %collective-permute-start.48) | collective-permute-done | bytes 524320 | tf_op jit(solution)/shard_map/ppermute | solution.py:190
  365.2 3.4 copy-done.27
  368.6 7.4 %fusion.185 = bf16[684,2048]{1,0:T(8,128)(2,1)} fusion(bf16[2048,684]{0,1:T(8,128)(2,1)S(1)} %copy-done.17, bf16[2048,2048]{1,0:T(8,128)(2,1)S(1)} %constant_dynamic-update-slice_fusion.20), kind=kOutput, calls=%fused_computation.321 | convolution fusion | flops 5737807872 | bytes 13991936 | tf_op jit(solution)/shard_map/tf,td->fd/dot_general | solution.py:398
  376.0 6.0 fusion.149
  383.1 6.4 convolution_bitcast_fusion.3
  389.9 4.5 fusion.148
  394.4 3.7 convolution_bitcast_fusion.2
  401.5 4.3 fusion.147
  405.9 3.8 convolution_bitcast_fusion.1
  409.7 3.4 collective-permute-done.54
  422.5 4.3 fusion.146
  428.0 4.6 convolution_bitcast_fusion
  432.6 17.8 %fusion = bf16[2,684,2048]{2,1,0:T(8,128)(2,1)} fusion(bf16[2048,2048]{1,0:T(8,128)(2,1)} %constant_dynamic-update-slice_fusion.10, bf16[1,512,684]{1,2,0:T(8,128)(2,1)} %copy-done.38, bf16[1,512,684]{1,2,0:T(8,128)(2,1)} %copy-done.37, bf16[1,512,684]{1,2,0:T(8,128)(2,1)} %copy-done.42, bf16[1,512,684]{1,2,0:T(8,128)(2,1)} %copy-done.41, ...), kind=kOutput, calls=%fused_computation.1 | convolution fusion | flops 11520442368 | bytes 19595264 | tf_op jit(solution)/shard_map/ctf,td->cfd/dot_general | solution.py:418
  454.7 4.9 multiply_reduce_fusion
  465.6 5.1 multiply_subtract_fusion
  470.6 17.1 %collective-permute-done.63 = bf16[256,2048]{1,0:T(8,128)(2,1)S(1)} collective-permute-done((bf16[256,2048]{1,0:T(8,128)(2,1)}, bf16[256,2048]{1,0:T(8,128)(2,1)S(1)}, u32[]{:S(2)}, u32[]{:S(2)}) %collective-permute-start.63) | collective-permute-done | bytes 1048608 | tf_op jit(solution)/shard_map/ppermute | solution.py:190
  492.7 10.8 %collective-permute-done.67 = bf16[128,2048]{1,0:T(8,128)(2,1)S(1)} collective-permute-done((bf16[128,2048]{1,0:T(8,128)(2,1)S(1)}, bf16[128,2048]{1,0:T(8,128)(2,1)S(1)}, u32[]{:S(2)}, u32[]{:S(2)}) %collective-permute-start.67) | collective-permute-done | bytes 524320 | tf_op jit(solution)/shard_map/ppermute | solution.py:190
  506.2 5.4 fusion.125.grad_ref
  511.6 14.1 %attend_backward.1 = bf16[2048,768]{1,0:T(8,128)(2,1)} custom-call(s32[4]{0:T(128)} %objective_ref.3, s32[4]{0:T(128)} %prefix_ref.3, s32[2]{0:T(128)} %pad_add_fusion.place_ref, bf16[2048,256]{1,0:T(8,128)(2,1)} %get-tuple-element.121.query_ref, bf16[2048,256]{1,0:T(8,128)(2,1)} %get-tuple-element.122.key_ref, ...), custom_call_target="tpu_custom_call" | custom-call | tf_op jit(solution)/shard_map/attend_backward/pallas_call | solution.py:150
  525.7 5.9 fusion.186
  531.7 9.7 %fusion.187 = bf16[768,2048]{1,0:T(8,128)(2,1)S(1)} fusion(bf16[2048,768]{1,0:T(8,128)(2,1)S(1)} %copy-done.15, bf16[2048,2048]{1,0:T(8,128)(2,1)} %constant_dynamic-update-slice_fusion), kind=kOutput, calls=%fused_computation.323 | convolution fusion | flops 6442450944 | bytes 14680064 | tf_op jit(solution)/shard_map/te,td->ed/dot_general | solution.py:450
  544.8 3.7 fusion.38
  551.0 7.1 %fusion.36 = bf16[1536,2048]{1,0:T(8,128)(2,1)S(1)} fusion(bf16[2048,1024]{0,1:T(8,128)(2,1)} %all-gather.4.cloned.1.call-done, bf16[2048,768]{1,0:T(8,128)(2,1)S(1)} %copy-done.16), kind=kOutput, calls=%fused_computation.47 | convolution fusion | flops 4831838208 | bytes 11796480 | tf_op jit(solution)/shard_map/te,de->td/dot_general | solution.py:470
  567.8 16.5 %fusion.161 = (f32[512,2,684]{0,1,2:T(2,128)}, f32[512,2,684]{0,1,2:T(2,128)}, f32[512,2,684]{0,1,2:T(2,128)}) fusion(f32[]{:T(128)S(6)} %div.99, bf16[2,684,512]{2,1,0:T(8,128)(2,1)S(1)} %copy-done.24, f32[512,2,684]{0,1,2:T(2,128)S(1)} %copy-done.18, f32[512,2,684]{0,1,2:T(2,128)S(1)} %copy-done.19, f32[512,2,684]{0,1,2:T(2,128)S(1)} %copy-done.6), kind=kLoop, calls=%fused_computation.310 | loop fusion | flops 11206656 | bytes 18210820 | tf_op jit(solution)/shard_map/transpose | solution.py:303
  588.4 9.9 %collective-permute-done.80 = bf16[128,2048]{1,0:T(8,128)(2,1)S(1)} collective-permute-done((bf16[128,2048]{1,0:T(8,128)(2,1)S(1)}, bf16[128,2048]{1,0:T(8,128)(2,1)S(1)}, u32[]{:S(2)}, u32[]{:S(2)}) %collective-permute-start.80) | collective-permute-done | bytes 524320 | tf_op jit(solution)/shard_map/ppermute | solution.py:190
  609.5 7.3 %collective-permute-done.84 = f32[4,2048]{1,0:T(4,128)S(1)} collective-permute-done((f32[4,2048]{1,0:T(4,128)S(1)}, f32[4,2048]{1,0:T(4,128)S(1)}, u32[]{:S(2)}, u32[]{:S(2)}) %collective-permute-start.84) | collective-permute-done | bytes 32800 | tf_op jit(solution)/shard_map/ppermute | solution.py:190
  618.6 4.9 collective-permute-done.85
  624.1 5.7 reduce-scatter.8.cloned.1.call-done
  631.3 5.4 fusion.131
  (409 shorter events, 194.6 us)
Async XLA Ops:
  7.2 88.8 %all-gather.4.cloned.1.call-start = ((), (), s32[]{:S(2)}) async-start(), calls=%async_computation.3 | async-start | bytes 5242880 | tf_op jit(solution)/shard_map/all_gather | solution.py:347
  12.2 203.8 %all-gather.6.cloned.1.call-start = ((), (), s32[]{:S(2)}) async-start(), calls=%async_computation.4 | async-start | bytes 7045120 | tf_op jit(solution)/shard_map/all_gather | solution.py:353
  12.3 29.0 %collective-permute-start.1 = (bf16[256,2048]{1,0:T(8,128)(2,1)}, bf16[256,2048]{1,0:T(8,128)(2,1)}, u32[]{:S(2)}, u32[]{:S(2)}) collective-permute-start(bf16[256,2048]{1,0:T(8,128)(2,1)} %param.20), channel_id=1, source_target_pairs={{0,2},{1,3},{2,0},{3,1},{4,6},{5,7},{6,4},{7,5},{8,10},{9,11},{10,... | collective-permute-start | bytes 3145736 | tf_op jit(solution)/shard_map/ppermute | solution.py:190
  15.3 41.8 %collective-permute-start = (bf16[256,2048]{1,0:T(8,128)(2,1)}, bf16[256,2048]{1,0:T(8,128)(2,1)}, u32[]{:S(2)}, u32[]{:S(2)}) collective-permute-start(bf16[256,2048]{1,0:T(8,128)(2,1)} %param.20), channel_id=1, source_target_pairs={{0,1},{1,0},{2,3},{3,2},{4,5},{5,4},{6,7},{7,6},{8,9},{9,8},{10,11... | collective-permute-start | bytes 3145736 | tf_op jit(solution)/shard_map/ppermute | solution.py:190
  15.3 38.0 %collective-permute-start.3 = (bf16[256,2048]{1,0:T(8,128)(2,1)}, bf16[256,2048]{1,0:T(8,128)(2,1)}, u32[]{:S(2)}, u32[]{:S(2)}) collective-permute-start(bf16[256,2048]{1,0:T(8,128)(2,1)} %param.20), channel_id=1, source_target_pairs={{0,4},{1,5},{2,6},{3,7},{4,0},{5,1},{6,2},{7,3},{8,12},{9,13},{10,... | collective-permute-start | bytes 3145736 | tf_op jit(solution)/shard_map/ppermute | solution.py:190
  20.7 239.0 %all-gather.8.cloned.1.call-start = ((), (), s32[]{:S(2)}) async-start(), calls=%async_computation.5 | async-start | bytes 3522560 | tf_op jit(solution)/shard_map/all_gather | solution.py:354
  22.5 16.3 %collective-permute-start.10 = (f32[8,128]{1,0:T(8,128)S(1)}, f32[8,128]{1,0:T(8,128)S(1)}, u32[]{:S(2)}, u32[]{:S(2)}) collective-permute-start(f32[8,128]{1,0:T(8,128)S(1)} %broadcast_add_fusion), channel_id=1, source_target_pairs={{0,2},{1,3},{2,0},{3,1},{4,6},{5,7},{6,4},{7,5},{8,10},{9,11},{10,... | collective-permute-start | bytes 12296 | tf_op jit(solution)/shard_map/ppermute | solution.py:190
  41.3 24.2 %collective-permute-start.2 = (bf16[256,2048]{1,0:T(8,128)(2,1)}, bf16[256,2048]{1,0:T(8,128)(2,1)S(1)}, u32[]{:S(2)}, u32[]{:S(2)}) collective-permute-start(bf16[256,2048]{1,0:T(8,128)(2,1)} %collective-permute-done.1), channel_id=1, source_target_pairs={{0,1},{1,0},{2,3},{3,2},{4,5},{5,4},{6,7},{7,6},{8,9},{9,8},{10,11... | collective-permute-start | bytes 3145736 | tf_op jit(solution)/shard_map/ppermute | solution.py:190
  124.2 19.4 %collective-permute-start.14 = (bf16[256,2048]{1,0:T(8,128)(2,1)S(1)}, bf16[256,2048]{1,0:T(8,128)(2,1)S(1)}, u32[]{:S(2)}, u32[]{:S(2)}) collective-permute-start(bf16[256,2048]{1,0:T(8,128)(2,1)S(1)} %get-tuple-element.189), channel_id=1, source_target_pairs={{0,1},{1,0},{2,3},{3,2},{4,5},{5,4},{6,7},{7,6},{8,9},{9,8},{10,11... | collective-permute-start | bytes 3145736 | tf_op jit(solution)/shard_map/ppermute | solution.py:190
  125.2 14.9 %collective-permute-start.17 = (bf16[128,2048]{1,0:T(8,128)(2,1)S(1)}, bf16[128,2048]{1,0:T(8,128)(2,1)S(1)}, u32[]{:S(2)}, u32[]{:S(2)}) collective-permute-start(bf16[128,2048]{1,0:T(8,128)(2,1)S(1)} %get-tuple-element.207), channel_id=1, source_target_pairs={{0,4},{1,5},{2,6},{3,7},{4,0},{5,1},{6,2},{7,3},{8,12},{9,13},{10,... | collective-permute-start | bytes 1572872 | tf_op jit(solution)/shard_map/ppermute | solution.py:190
  126.9 15.0 %collective-permute-start.22 = (bf16[128,2048]{1,0:T(8,128)(2,1)S(1)}, bf16[128,2048]{1,0:T(8,128)(2,1)S(1)}, u32[]{:S(2)}, u32[]{:S(2)}) collective-permute-start(bf16[128,2048]{1,0:T(8,128)(2,1)S(1)} %get-tuple-element.208), channel_id=1, source_target_pairs={{0,2},{1,3},{2,0},{3,1},{4,6},{5,7},{6,4},{7,5},{8,10},{9,11},{10,... | collective-permute-start | bytes 1572872 | tf_op jit(solution)/shard_map/ppermute | solution.py:190
  129.3 23.7 %collective-permute-start.19 = (bf16[128,2048]{1,0:T(8,128)(2,1)S(1)}, bf16[128,2048]{1,0:T(8,128)(2,1)S(1)}, u32[]{:S(2)}, u32[]{:S(2)}) collective-permute-start(bf16[128,2048]{1,0:T(8,128)(2,1)S(1)} %slice.638), channel_id=1, source_target_pairs={{0,2},{1,3},{2,0},{3,1},{4,6},{5,7},{6,4},{7,5},{8,10},{9,11},{10,... | collective-permute-start | bytes 1572872 | tf_op jit(solution)/shard_map/ppermute | solution.py:190
  130.5 22.4 %collective-permute-start.21 = (bf16[128,2048]{1,0:T(8,128)(2,1)S(1)}, bf16[128,2048]{1,0:T(8,128)(2,1)S(1)}, u32[]{:S(2)}, u32[]{:S(2)}) collective-permute-start(bf16[128,2048]{1,0:T(8,128)(2,1)S(1)} %slice.637), channel_id=1, source_target_pairs={{0,4},{1,5},{2,6},{3,7},{4,0},{5,1},{6,2},{7,3},{8,12},{9,13},{10,... | collective-permute-start | bytes 1572872 | tf_op jit(solution)/shard_map/ppermute | solution.py:190
  140.3 22.7 %collective-permute-start.18 = (bf16[128,2048]{1,0:T(8,128)(2,1)S(1)}, bf16[128,2048]{1,0:T(8,128)(2,1)S(1)}, u32[]{:S(2)}, u32[]{:S(2)}) collective-permute-start(bf16[128,2048]{1,0:T(8,128)(2,1)S(1)} %fusion.123), channel_id=1, source_target_pairs={{0,2},{1,3},{2,0},{3,1},{4,6},{5,7},{6,4},{7,5},{8,10},{9,11},{10,... | collective-permute-start | bytes 1572872 | tf_op jit(solution)/shard_map/ppermute | solution.py:190
  142.0 21.0 %collective-permute-start.23 = (bf16[128,2048]{1,0:T(8,128)(2,1)S(1)}, bf16[128,2048]{1,0:T(8,128)(2,1)S(1)}, u32[]{:S(2)}, u32[]{:S(2)}) collective-permute-start(bf16[128,2048]{1,0:T(8,128)(2,1)S(1)} %fusion.122), channel_id=1, source_target_pairs={{0,4},{1,5},{2,6},{3,7},{4,0},{5,1},{6,2},{7,3},{8,12},{9,13},{10,... | collective-permute-start | bytes 1572872 | tf_op jit(solution)/shard_map/ppermute | solution.py:190
  166.1 24.4 %collective-permute-start.25 = (bf16[256,2048]{1,0:T(8,128)(2,1)}, bf16[256,2048]{1,0:T(8,128)(2,1)}, u32[]{:S(2)}, u32[]{:S(2)}) collective-permute-start(bf16[256,2048]{1,0:T(8,128)(2,1)} %get-tuple-element.173), channel_id=1, source_target_pairs={{0,2},{1,3},{2,0},{3,1},{4,6},{5,7},{6,4},{7,5},{8,10},{9,11},{10,... | collective-permute-start | bytes 3145736 | tf_op jit(solution)/shard_map/ppermute | solution.py:190
  167.6 26.2 %collective-permute-start.27 = (bf16[256,2048]{1,0:T(8,128)(2,1)}, bf16[256,2048]{1,0:T(8,128)(2,1)S(1)}, u32[]{:S(2)}, u32[]{:S(2)}) collective-permute-start(bf16[256,2048]{1,0:T(8,128)(2,1)} %get-tuple-element.173), channel_id=1, source_target_pairs={{0,4},{1,5},{2,6},{3,7},{4,0},{5,1},{6,2},{7,3},{8,12},{9,13},{10,... | collective-permute-start | bytes 3145736 | tf_op jit(solution)/shard_map/ppermute | solution.py:190
  168.1 27.3 %collective-permute-start.24 = (bf16[256,2048]{1,0:T(8,128)(2,1)}, bf16[256,2048]{1,0:T(8,128)(2,1)}, u32[]{:S(2)}, u32[]{:S(2)}) collective-permute-start(bf16[256,2048]{1,0:T(8,128)(2,1)} %get-tuple-element.173), channel_id=1, source_target_pairs={{0,1},{1,0},{2,3},{3,2},{4,5},{5,4},{6,7},{7,6},{8,9},{9,8},{10,11... | collective-permute-start | bytes 3145736 | tf_op jit(solution)/shard_map/ppermute | solution.py:190
  190.5 17.5 %collective-permute-start.26 = (bf16[256,2048]{1,0:T(8,128)(2,1)}, bf16[256,2048]{1,0:T(8,128)(2,1)}, u32[]{:S(2)}, u32[]{:S(2)}) collective-permute-start(bf16[256,2048]{1,0:T(8,128)(2,1)} %collective-permute-done.25), channel_id=1, source_target_pairs={{0,1},{1,0},{2,3},{3,2},{4,5},{5,4},{6,7},{7,6},{8,9},{9,8},{10,11... | collective-permute-start | bytes 3145736 | tf_op jit(solution)/shard_map/ppermute | solution.py:190
  191.5 241.1 %reduce-scatter.4.cloned.1.call-start = ((), (), s32[]{:S(2)}) async-start(), calls=%async_computation.6 | async-start | bytes 3522560 | tf_op jit(solution)/shard_map/reduce_scatter | solution.py:400
  195.4 16.2 %collective-permute-start.28 = (bf16[256,2048]{1,0:T(8,128)(2,1)S(1)}, bf16[256,2048]{1,0:T(8,128)(2,1)S(1)}, u32[]{:S(2)}, u32[]{:S(2)}) collective-permute-start(bf16[256,2048]{1,0:T(8,128)(2,1)S(1)} %collective-permute-done.27), channel_id=1, source_target_pairs={{0,1},{1,0},{2,3},{3,2},{4,5},{5,4},{6,7},{7,6},{8,9},{9,8},{10,11... | collective-permute-start | bytes 3145736 | tf_op jit(solution)/shard_map/ppermute | solution.py:190
  267.1 16.0 %collective-permute-start.34 = (bf16[256,2048]{1,0:T(8,128)(2,1)S(1)}, bf16[256,2048]{1,0:T(8,128)(2,1)S(1)}, u32[]{:S(2)}, u32[]{:S(2)}) collective-permute-start(bf16[256,2048]{1,0:T(8,128)(2,1)S(1)} %slice.327), channel_id=1, source_target_pairs={{0,1},{1,0},{2,3},{3,2},{4,5},{5,4},{6,7},{7,6},{8,9},{9,8},{10,11... | collective-permute-start | bytes 3145736 | tf_op jit(solution)/shard_map/ppermute | solution.py:190
  283.5 14.9 %collective-permute-start.39 = (bf16[128,2048]{1,0:T(8,128)(2,1)S(1)}, bf16[128,2048]{1,0:T(8,128)(2,1)S(1)}, u32[]{:S(2)}, u32[]{:S(2)}) collective-permute-start(bf16[128,2048]{1,0:T(8,128)(2,1)S(1)} %slice.636), channel_id=1, source_target_pairs={{0,2},{1,3},{2,0},{3,1},{4,6},{5,7},{6,4},{7,5},{8,10},{9,11},{10,... | collective-permute-start | bytes 1572872 | tf_op jit(solution)/shard_map/ppermute | solution.py:190
  286.3 22.9 %collective-permute-start.38 = (bf16[128,2048]{1,0:T(8,128)(2,1)S(1)}, bf16[128,2048]{1,0:T(8,128)(2,1)S(1)}, u32[]{:S(2)}, u32[]{:S(2)}) collective-permute-start(bf16[128,2048]{1,0:T(8,128)(2,1)S(1)} %fusion.121), channel_id=1, source_target_pairs={{0,2},{1,3},{2,0},{3,1},{4,6},{5,7},{6,4},{7,5},{8,10},{9,11},{10,... | collective-permute-start | bytes 1572872 | tf_op jit(solution)/shard_map/ppermute | solution.py:190
  287.8 21.3 %collective-permute-start.41 = (bf16[128,2048]{1,0:T(8,128)(2,1)S(1)}, bf16[128,2048]{1,0:T(8,128)(2,1)S(1)}, u32[]{:S(2)}, u32[]{:S(2)}) collective-permute-start(bf16[128,2048]{1,0:T(8,128)(2,1)S(1)} %fusion.120), channel_id=1, source_target_pairs={{0,4},{1,5},{2,6},{3,7},{4,0},{5,1},{6,2},{7,3},{8,12},{9,13},{10,... | collective-permute-start | bytes 1572872 | tf_op jit(solution)/shard_map/ppermute | solution.py:190
  288.4 24.4 %collective-permute-start.40 = (bf16[128,2048]{1,0:T(8,128)(2,1)S(1)}, bf16[128,2048]{1,0:T(8,128)(2,1)S(1)}, u32[]{:S(2)}, u32[]{:S(2)}) collective-permute-start(bf16[128,2048]{1,0:T(8,128)(2,1)S(1)} %slice.635), channel_id=1, source_target_pairs={{0,4},{1,5},{2,6},{3,7},{4,0},{5,1},{6,2},{7,3},{8,12},{9,13},{10,... | collective-permute-start | bytes 1572872 | tf_op jit(solution)/shard_map/ppermute | solution.py:190
  322.5 25.3 %collective-permute-start.44 = (bf16[256,2048]{1,0:T(8,128)(2,1)S(1)}, bf16[256,2048]{1,0:T(8,128)(2,1)S(1)}, u32[]{:S(2)}, u32[]{:S(2)}) collective-permute-start(bf16[256,2048]{1,0:T(8,128)(2,1)S(1)} %get-tuple-element.169), channel_id=1, source_target_pairs={{0,2},{1,3},{2,0},{3,1},{4,6},{5,7},{6,4},{7,5},{8,10},{9,11},{10,... | collective-permute-start | bytes 3145736 | tf_op jit(solution)/shard_map/ppermute | solution.py:190
  323.1 24.9 %collective-permute-start.46 = (bf16[256,2048]{1,0:T(8,128)(2,1)S(1)}, bf16[256,2048]{1,0:T(8,128)(2,1)S(1)}, u32[]{:S(2)}, u32[]{:S(2)}) collective-permute-start(bf16[256,2048]{1,0:T(8,128)(2,1)S(1)} %get-tuple-element.169), channel_id=1, source_target_pairs={{0,4},{1,5},{2,6},{3,7},{4,0},{5,1},{6,2},{7,3},{8,12},{9,13},{10,... | collective-permute-start | bytes 3145736 | tf_op jit(solution)/shard_map/ppermute | solution.py:190
  323.7 26.6 %collective-permute-start.43 = (bf16[256,2048]{1,0:T(8,128)(2,1)S(1)}, bf16[256,2048]{1,0:T(8,128)(2,1)S(1)}, u32[]{:S(2)}, u32[]{:S(2)}) collective-permute-start(bf16[256,2048]{1,0:T(8,128)(2,1)S(1)} %get-tuple-element.169), channel_id=1, source_target_pairs={{0,1},{1,0},{2,3},{3,2},{4,5},{5,4},{6,7},{7,6},{8,9},{9,8},{10,11... | collective-permute-start | bytes 3145736 | tf_op jit(solution)/shard_map/ppermute | solution.py:190
  347.8 15.2 %collective-permute-start.45 = (bf16[256,2048]{1,0:T(8,128)(2,1)S(1)}, bf16[256,2048]{1,0:T(8,128)(2,1)S(1)}, u32[]{:S(2)}, u32[]{:S(2)}) collective-permute-start(bf16[256,2048]{1,0:T(8,128)(2,1)S(1)} %collective-permute-done.44), channel_id=1, source_target_pairs={{0,1},{1,0},{2,3},{3,2},{4,5},{5,4},{6,7},{7,6},{8,9},{9,8},{10,11... | collective-permute-start | bytes 3145736 | tf_op jit(solution)/shard_map/ppermute | solution.py:190
  348.0 15.2 %collective-permute-start.47 = (bf16[256,2048]{1,0:T(8,128)(2,1)S(1)}, bf16[256,2048]{1,0:T(8,128)(2,1)S(1)}, u32[]{:S(2)}, u32[]{:S(2)}) collective-permute-start(bf16[256,2048]{1,0:T(8,128)(2,1)S(1)} %collective-permute-done.46), channel_id=1, source_target_pairs={{0,1},{1,0},{2,3},{3,2},{4,5},{5,4},{6,7},{7,6},{8,9},{9,8},{10,11... | collective-permute-start | bytes 3145736 | tf_op jit(solution)/shard_map/ppermute | solution.py:190
  376.0 175.0 %reduce-scatter.6.cloned.1.call-start = ((), (), s32[]{:S(2)}) async-start(), calls=%async_computation.7 | async-start | bytes 7045120 | tf_op jit(solution)/shard_map/reduce_scatter | solution.py:440
  398.7 14.4 %collective-permute-start.54 = (bf16[128,2048]{1,0:T(8,128)(2,1)S(1)}, bf16[128,2048]{1,0:T(8,128)(2,1)S(1)}, u32[]{:S(2)}, u32[]{:S(2)}) collective-permute-start(bf16[128,2048]{1,0:T(8,128)(2,1)S(1)} %get-tuple-element.204), channel_id=1, source_target_pairs={{0,4},{1,5},{2,6},{3,7},{4,0},{5,1},{6,2},{7,3},{8,12},{9,13},{10,... | collective-permute-start | bytes 1572872 | tf_op jit(solution)/shard_map/ppermute | solution.py:190
  415.3 35.1 %collective-permute-start.58 = (bf16[128,2048]{1,0:T(8,128)(2,1)}, bf16[128,2048]{1,0:T(8,128)(2,1)}, u32[]{:S(2)}, u32[]{:S(2)}) collective-permute-start(bf16[128,2048]{1,0:T(8,128)(2,1)} %slice.634), channel_id=1, source_target_pairs={{0,2},{1,3},{2,0},{3,1},{4,6},{5,7},{6,4},{7,5},{8,10},{9,11},{10,... | collective-permute-start | bytes 1572872 | tf_op jit(solution)/shard_map/ppermute | solution.py:190
  419.9 30.5 %collective-permute-start.57 = (bf16[128,2048]{1,0:T(8,128)(2,1)}, bf16[128,2048]{1,0:T(8,128)(2,1)}, u32[]{:S(2)}, u32[]{:S(2)}) collective-permute-start(bf16[128,2048]{1,0:T(8,128)(2,1)} %fusion.119), channel_id=1, source_target_pairs={{0,2},{1,3},{2,0},{3,1},{4,6},{5,7},{6,4},{7,5},{8,10},{9,11},{10,... | collective-permute-start | bytes 1572872 | tf_op jit(solution)/shard_map/ppermute | solution.py:190
  420.4 30.0 %collective-permute-start.60 = (bf16[128,2048]{1,0:T(8,128)(2,1)}, bf16[128,2048]{1,0:T(8,128)(2,1)}, u32[]{:S(2)}, u32[]{:S(2)}) collective-permute-start(bf16[128,2048]{1,0:T(8,128)(2,1)} %fusion.118), channel_id=1, source_target_pairs={{0,4},{1,5},{2,6},{3,7},{4,0},{5,1},{6,2},{7,3},{8,12},{9,13},{10,... | collective-permute-start | bytes 1572872 | tf_op jit(solution)/shard_map/ppermute | solution.py:190
  421.4 29.1 %collective-permute-start.59 = (bf16[128,2048]{1,0:T(8,128)(2,1)}, bf16[128,2048]{1,0:T(8,128)(2,1)}, u32[]{:S(2)}, u32[]{:S(2)}) collective-permute-start(bf16[128,2048]{1,0:T(8,128)(2,1)} %slice.633), channel_id=1, source_target_pairs={{0,4},{1,5},{2,6},{3,7},{4,0},{5,1},{6,2},{7,3},{8,12},{9,13},{10,... | collective-permute-start | bytes 1572872 | tf_op jit(solution)/shard_map/ppermute | solution.py:190
  450.5 179.3 %reduce-scatter.8.cloned.1.call-start = ((), (), s32[]{:S(2)}) async-start(), calls=%async_computation.8 | async-start | bytes 5242880 | tf_op jit(solution)/shard_map/reduce_scatter | solution.py:457
  462.3 25.4 %collective-permute-start.63 = (bf16[256,2048]{1,0:T(8,128)(2,1)}, bf16[256,2048]{1,0:T(8,128)(2,1)S(1)}, u32[]{:S(2)}, u32[]{:S(2)}) collective-permute-start(bf16[256,2048]{1,0:T(8,128)(2,1)} %get-tuple-element.165), channel_id=1, source_target_pairs={{0,2},{1,3},{2,0},{3,1},{4,6},{5,7},{6,4},{7,5},{8,10},{9,11},{10,... | collective-permute-start | bytes 3145736 | tf_op jit(solution)/shard_map/ppermute | solution.py:190
  463.9 25.1 %collective-permute-start.64 = (bf16[256,2048]{1,0:T(8,128)(2,1)}, bf16[256,2048]{1,0:T(8,128)(2,1)S(1)}, u32[]{:S(2)}, u32[]{:S(2)}) collective-permute-start(bf16[256,2048]{1,0:T(8,128)(2,1)} %get-tuple-element.165), channel_id=1, source_target_pairs={{0,4},{1,5},{2,6},{3,7},{4,0},{5,1},{6,2},{7,3},{8,12},{9,13},{10,... | collective-permute-start | bytes 3145736 | tf_op jit(solution)/shard_map/ppermute | solution.py:190
  464.9 26.4 %collective-permute-start.62 = (bf16[256,2048]{1,0:T(8,128)(2,1)}, bf16[256,2048]{1,0:T(8,128)(2,1)}, u32[]{:S(2)}, u32[]{:S(2)}) collective-permute-start(bf16[256,2048]{1,0:T(8,128)(2,1)} %get-tuple-element.165), channel_id=1, source_target_pairs={{0,1},{1,0},{2,3},{3,2},{4,5},{5,4},{6,7},{7,6},{8,9},{9,8},{10,11... | collective-permute-start | bytes 3145736 | tf_op jit(solution)/shard_map/ppermute | solution.py:190
  489.0 15.3 %collective-permute-start.65 = (bf16[256,2048]{1,0:T(8,128)(2,1)S(1)}, bf16[256,2048]{1,0:T(8,128)(2,1)S(1)}, u32[]{:S(2)}, u32[]{:S(2)}) collective-permute-start(bf16[256,2048]{1,0:T(8,128)(2,1)S(1)} %collective-permute-done.63), channel_id=1, source_target_pairs={{0,1},{1,0},{2,3},{3,2},{4,5},{5,4},{6,7},{7,6},{8,9},{9,8},{10,11... | collective-permute-start | bytes 3145736 | tf_op jit(solution)/shard_map/ppermute | solution.py:190
  489.0 15.4 %collective-permute-start.66 = (bf16[256,2048]{1,0:T(8,128)(2,1)S(1)}, bf16[256,2048]{1,0:T(8,128)(2,1)S(1)}, u32[]{:S(2)}, u32[]{:S(2)}) collective-permute-start(bf16[256,2048]{1,0:T(8,128)(2,1)S(1)} %collective-permute-done.64), channel_id=1, source_target_pairs={{0,1},{1,0},{2,3},{3,2},{4,5},{5,4},{6,7},{7,6},{8,9},{9,8},{10,11... | collective-permute-start | bytes 3145736 | tf_op jit(solution)/shard_map/ppermute | solution.py:190
  559.1 27.5 %collective-permute-start.71 = (bf16[256,2048]{1,0:T(8,128)(2,1)S(1)}, bf16[256,2048]{1,0:T(8,128)(2,1)S(1)}, u32[]{:S(2)}, u32[]{:S(2)}) collective-permute-start(bf16[256,2048]{1,0:T(8,128)(2,1)S(1)} %get-tuple-element.188), channel_id=1, source_target_pairs={{0,1},{1,0},{2,3},{3,2},{4,5},{5,4},{6,7},{7,6},{8,9},{9,8},{10,11... | collective-permute-start | bytes 3145736 | tf_op jit(solution)/shard_map/ppermute | solution.py:190
  561.5 22.8 %collective-permute-start.74 = (bf16[128,2048]{1,0:T(8,128)(2,1)S(1)}, bf16[128,2048]{1,0:T(8,128)(2,1)S(1)}, u32[]{:S(2)}, u32[]{:S(2)}) collective-permute-start(bf16[128,2048]{1,0:T(8,128)(2,1)S(1)} %get-tuple-element.202), channel_id=1, source_target_pairs={{0,4},{1,5},{2,6},{3,7},{4,0},{5,1},{6,2},{7,3},{8,12},{9,13},{10,... | collective-permute-start | bytes 1572872 | tf_op jit(solution)/shard_map/ppermute | solution.py:190
  563.0 21.3 %collective-permute-start.75 = (bf16[128,2048]{1,0:T(8,128)(2,1)S(1)}, bf16[128,2048]{1,0:T(8,128)(2,1)S(1)}, u32[]{:S(2)}, u32[]{:S(2)}) collective-permute-start(bf16[128,2048]{1,0:T(8,128)(2,1)S(1)} %get-tuple-element.201), channel_id=1, source_target_pairs={{0,2},{1,3},{2,0},{3,1},{4,6},{5,7},{6,4},{7,5},{8,10},{9,11},{10,... | collective-permute-start | bytes 1572872 | tf_op jit(solution)/shard_map/ppermute | solution.py:190
  564.6 23.8 %collective-permute-start.77 = (bf16[128,2048]{1,0:T(8,128)(2,1)S(1)}, bf16[128,2048]{1,0:T(8,128)(2,1)S(1)}, u32[]{:S(2)}, u32[]{:S(2)}) collective-permute-start(bf16[128,2048]{1,0:T(8,128)(2,1)S(1)} %slice.632), channel_id=1, source_target_pairs={{0,2},{1,3},{2,0},{3,1},{4,6},{5,7},{6,4},{7,5},{8,10},{9,11},{10,... | collective-permute-start | bytes 1572872 | tf_op jit(solution)/shard_map/ppermute | solution.py:190
  566.0 22.4 %collective-permute-start.79 = (bf16[128,2048]{1,0:T(8,128)(2,1)S(1)}, bf16[128,2048]{1,0:T(8,128)(2,1)S(1)}, u32[]{:S(2)}, u32[]{:S(2)}) collective-permute-start(bf16[128,2048]{1,0:T(8,128)(2,1)S(1)} %slice.631), channel_id=1, source_target_pairs={{0,4},{1,5},{2,6},{3,7},{4,0},{5,1},{6,2},{7,3},{8,12},{9,13},{10,... | collective-permute-start | bytes 1572872 | tf_op jit(solution)/shard_map/ppermute | solution.py:190
  (93 other events, 626.3 us)
Sparse Core Ops, SparseCore 0:
  12.4 83.5 all-gather.3
  98.1 103.0 all-gather.5
  203.4 56.2 all-gather.7
  376.1 53.6 reduce-scatter.3
  450.6 98.2 reduce-scatter.5
  551.2 78.5 reduce-scatter.7

commit v7 on v6

--- a/solution.py
+++ b/solution.py
@@ -256,12 +256,12 @@
     return piece[:half].astype(jnp.float32) + mate.astype(jnp.float32)
 
 
-def scatter_beside(rows, product, last=None):
+def scatter_beside(own, rows, product, last):
     far = product(rows, 3)
     rows, far = lax.optimization_barrier((rows, far))
     near_x = product(rows, 1)
-    far = core_sum(far).astype(jnp.bfloat16)
-    rows, far, near_x = lax.optimization_barrier((rows, far, near_x))
+    far, own = core_sum(far).astype(jnp.bfloat16), core_sum(own)
+    rows, far, own, near_x = lax.optimization_barrier((rows, far, own, near_x))
     half = far.shape[0] // 2
     far_low, far_high = swap(far[:half], "mp", 4), swap(far[half:], "mp", 2)
     near_y, far_low, far_high = lax.optimization_barrier((product(rows, 2), far_low, far_high))
@@ -269,16 +269,24 @@
     low, high = slice(0, half), slice(half, 2 * half)
     x_low = (near_x[low] + far_low.astype(jnp.float32)).astype(jnp.bfloat16)
     y_high = (near_y[high] + far_high.astype(jnp.float32)).astype(jnp.bfloat16)
-    rows, x_low, y_high = lax.optimization_barrier((rows, x_low, y_high))
     x_high, y_low = near_x[high].astype(jnp.bfloat16), near_y[low].astype(jnp.bfloat16)
     across = [swap(x_low, "mp", 2), swap(x_high, "mp", 2), swap(y_low, "mp", 4), swap(y_high, "mp", 4)]
-    own = product(rows, 0)
-    ahead = () if last is None else last()
-    own, across, ahead = lax.optimization_barrier((own, across, ahead))
+    across, ahead = lax.optimization_barrier((across, last()))
     across_x, across_y = jnp.concatenate(across[:2], 0), jnp.concatenate(across[2:], 0)
-    own = core_sum(own)
-    total = own + across_x.astype(jnp.float32) + across_y.astype(jnp.float32)
-    return total if last is None else (total, ahead)
+    return own + across_x.astype(jnp.float32) + across_y.astype(jnp.float32), ahead
+
+
+def gather_beside(rows, product):
+    half = rows.shape[0] // 2
+    near_x, near_y, mate = swap(rows, "mp", 2), swap(rows, "mp", 4), swap(rows, "mp", 1)
+    own = product(jnp.concatenate([rows, mate], 0), 0)
+    near_x, near_y, own = lax.optimization_barrier((near_x, near_y, own))
+    far_low, far_high = swap(near_x[:half], "mp", 4), swap(near_y[half:], "mp", 2)
+    mates = [swap(part, "mp", 1) for part in (near_x, near_y, far_low, far_high)]
+    whole = jnp.concatenate(
+        [rows, mate, near_x, mates[0], near_y, mates[1], far_low, far_high, *mates[2:]], 0
+    )
+    return whole, own
 
 
 def gather_all(rows, ahead=None):
@@ -379,32 +387,26 @@
         "td,cfd->ctf", middle_low, gateup_full, preferred_element_type=jnp.float32
     )
     hidden_low = (jax.nn.gelu(gate_up[0]) * gate_up[1] * live_units).astype(jnp.bfloat16)
+    ffn_own = scatter_rows(
+        far_first(
+            hidden_low,
+            lambda rows: jnp.dot(rows, down_full, preferred_element_type=jnp.bfloat16),
+            two_pieces,
+        )
+    )
     quarter = hidden_low.shape[0] // 4
-
-    def down_quarter(rows, index):
-        rows = rows[index * quarter : (index + 1) * quarter]
-        return jnp.dot(rows, down_full, preferred_element_type=jnp.bfloat16)
-
-    if near:
-        ffn_own = scatter_beside(hidden_low, down_quarter)
-    else:
-        ffn_own = scatter_all([down_quarter(hidden_low, index) for index in range(4)])
     hidden_two = deep_alpha * middle + ffn_own
     output_rows, normed_two, inv_two = norm_forward(hidden_two, norm_params[2], norm_params[3])
     grad_rows = out_cotangent.astype(jnp.float32) * mask_f32[:, None]
     grad_two, gain_two, bias_two = norm_backward(grad_rows, normed_two, inv_two, norm_params[2])
 
-    ffn_back = gather_rows(grad_two.astype(jnp.bfloat16))
-    down_grad = jnp.einsum("tf,td->fd", hidden_low, ffn_back, preferred_element_type=jnp.bfloat16)
-    ffn_back, down_grad = lax.optimization_barrier((ffn_back, down_grad))
-    down_grad = lax.psum_scatter(down_grad, "dp", scatter_dimension=1, tiled=True)
     grad_gateups = [None] * 4
 
-    def back_quarter(rows, index):
+    def back_quarter(chunk, index):
         at = slice(index * quarter, (index + 1) * quarter)
         gate_act, gelu_pull = jax.vjp(jax.nn.gelu, gate_up[0, at])
         grad_hidden = (
-            jnp.einsum("td,fd->tf", rows[at], down_full, preferred_element_type=jnp.float32)
+            jnp.einsum("td,fd->tf", chunk, down_full, preferred_element_type=jnp.float32)
             * live_units
         )
         grad_gate = gelu_pull(grad_hidden * gate_up[1, at])[0]
@@ -412,7 +414,17 @@
         grad_gateups[index] = grads
         return jnp.einsum("ctf,cfd->td", grads, gateup_full, preferred_element_type=jnp.bfloat16)
 
-    middle_low, down_grad = lax.optimization_barrier((middle_low, down_grad))
+    def back_rows(rows, index):
+        return back_quarter(rows[index * quarter : (index + 1) * quarter], index)
+
+    back_low = grad_two.astype(jnp.bfloat16)
+    if near:
+        ffn_back, own_part = gather_beside(back_low, back_quarter)
+    else:
+        ffn_back = gather_rows(back_low)
+    down_grad = jnp.einsum("tf,td->fd", hidden_low, ffn_back, preferred_element_type=jnp.bfloat16)
+    ffn_back, down_grad = lax.optimization_barrier((ffn_back, down_grad))
+    down_grad = lax.psum_scatter(down_grad, "dp", scatter_dimension=1, tiled=True)
 
     def gateup_product():
         return jnp.einsum(
@@ -423,9 +435,11 @@
         )
 
     if near:
-        grad_middle, gateup_grad = scatter_beside(ffn_back, back_quarter, gateup_product)
+        grad_middle, gateup_grad = scatter_beside(
+            own_part, ffn_back, back_rows, gateup_product
+        )
     else:
-        grad_middle = scatter_all([back_quarter(ffn_back, index) for index in range(4)])
+        grad_middle = scatter_all([back_rows(ffn_back, index) for index in range(4)])
         gateup_grad = gateup_product()
     grad_middle = grad_middle + deep_alpha * grad_two
     grad_one, gain_one, bias_one = norm_backward(grad_middle, normed_one, inv_one, norm_params[0])
@@ -436,6 +450,7 @@
         (0, 1), down_weight, down_grad, down_first, down_second, rate_list[3], scale
     )
     attn_back, down_res = gather_rows(grad_one.astype(jnp.bfloat16), down_res)
+    gateup_grad, down_grad = lax.optimization_barrier((gateup_grad, down_grad))
     gateup_grad = with_layout_constraint(
         lax.psum_scatter(gateup_grad, "dp", scatter_dimension=2, tiled=True),
         Layout(major_to_minor=(0, 1, 2)),

time: 651 us -> 649 us (level)
  waiting for transfers between devices: 272 us -> 259 us
    ppermute x86, waiting for transfers between devices: 224 us -> 202 us  [swap(): return lax.ppermute(values, axis, [(at, at ^ bit) for at in range(size)])]
    dot_general x8 -> x6, matrix products: 28.8 us -> 31.2 us  [the longest x4 21.6 us: back_quarter(): jnp.einsum('td,fd->tf', chunk, down_full, preferred_element_type=jnp.floa...]
    unnamed x132 -> x144, local copies, waits for them, and re-layouts: 44.4 us -> 44.6 us
  transfers between devices with their start and end apart: 92 -> 92, of which waited for: 45 -> 43; matrix products, arithmetic and copies ran while one was open for 35% -> 37% of each run, Pallas kernels for 4% -> 4%
where the time goes in v7:
time: 649 us; the launch traced here: 644 us
  waiting for transfers between devices  259 us (40%)
  matrix products  139 us (21%)
  other arithmetic  76 us (12%)
  starting transfers between devices  68.4 us (11%)
  local copies, waits for them, and re-layouts  61.3 us (9%)
  Pallas kernels  24.1 us (4%)
  between operations  16.4 us (3%)
    ppermute x86, waiting for transfers between devices, swap(): return lax.ppermute(values, axis, [(at, at ^ bit) for at in range(size)])  202 us
    ppermute x86, starting transfers between devices, swap(): return lax.ppermute(values, axis, [(at, at ^ bit) for at in range(size)])  68 us
    unnamed x144, local copies, waits for them, and re-layouts  44.6 us
    all_gather x1, waiting for transfers between devices, local(): attend_full = lax.all_gather(attend_low, 'dp', axis=0, tiled=True)  22.6 us
    transpose x2, other arithmetic, adamw_as(): jnp.transpose(rows, back)  21.8 us
    dot_general x4, matrix products, back_quarter(): jnp.einsum('td,fd->tf', chunk, down_full, preferred_element_type=jnp.floa...  21.6 us
    dot_general x4, matrix products, back_quarter(): jnp.einsum('ctf,cfd->td', grads, gateup_full, preferred_element_type=jnp....  20.8 us
    all_gather x1, waiting for transfers between devices, local(): lax.all_gather(down_weight.astype(jnp.bfloat16), 'dp', axis=1, tiled=True)  20.2 us
  transfers between devices with their start and end apart: 92, of which 43 were waited for; matrix products, arithmetic and copies ran while one was open for 37% of the time, Pallas kernels for 4%

profile of v7, /device:TPU:0, one launch (start us, length us, event | category | flops | bytes accessed | tf_op | source)
XLA Modules:
  0.0 643.9 jit_solution(10227926321187612602)
XLA Ops:
  23.1 15.7 %collective-permute-done.10 = f32[8,128]{1,0:T(8,128)S(1)} collective-permute-done((f32[8,128]{1,0:T(8,128)S(1)}, f32[8,128]{1,0:T(8,128)S(1)}, u32[]{:S(2)}, u32[]{:S(2)}) %collective-permute-start.10) | collective-permute-done | bytes 4128 | tf_op jit(solution)/shard_map/ppermute | solution.py:190
  73.4 22.6 %all-gather.4.cloned.1.call-done = bf16[2048,1024]{0,1:T(8,128)(2,1)} async-done(((bf16[512,1024]{0,1:T(8,128)(2,1)}), bf16[2048,1024]{0,1:T(8,128)(2,1)}) %all-gather.4.cloned.1.call-update) | async-done | bytes 4194320 | tf_op jit(solution)/shard_map/all_gather | solution.py:355
  96.0 12.3 %fusion.40.proj_ref = f32[2048,768]{1,0:T(8,128)} fusion(bf16[2048,2048]{1,0:T(8,128)(2,1)} %constant_dynamic-update-slice_fusion, bf16[2048,1024]{0,1:T(8,128)(2,1)} %all-gather.4.cloned.1.call-done), kind=kOutput, calls=%fused_computation.51 | convolution fusion | flops 6442450944 | bytes 17825792 | tf_op jit(solution)/shard_map/dot_general | solution.py:370
  108.3 10.0 %attend_forward.1 = (bf16[2048,256]{1,0:T(8,128)(2,1)}, bf16[2048,256]{1,0:T(8,128)(2,1)}, bf16[2048,256]{1,0:T(8,128)(2,1)}, bf16[2048,256]{1,0:T(8,128)(2,1)}) custom-call(s32[4]{0:T(128)} %objective_ref.3, s32[4]{0:T(128)} %prefix_ref.3, s32[2]{0:T(128)} %pad_add_fusion.place_ref, f32[2048,768]{1,0:T(8,128)} %fusion.40.proj_ref, ...), custom_call_target="tpu_custom_call" | custom-call | tf_op jit(solution)/shard_map/attend_forward/pallas_call | solution.py:138
  132.3 8.0 %collective-permute-done.17 = bf16[128,2048]{1,0:T(8,128)(2,1)S(1)} collective-permute-done((bf16[128,2048]{1,0:T(8,128)(2,1)S(1)}, bf16[128,2048]{1,0:T(8,128)(2,1)S(1)}, u32[]{:S(2)}, u32[]{:S(2)}) %collective-permute-start.17) | collective-permute-done | bytes 524320 | tf_op jit(solution)/shard_map/ppermute | solution.py:190
  144.4 8.7 %collective-permute-done.19 = bf16[128,2048]{1,0:T(8,128)(2,1)S(1)} collective-permute-done((bf16[128,2048]{1,0:T(8,128)(2,1)S(1)}, bf16[128,2048]{1,0:T(8,128)(2,1)S(1)}, u32[]{:S(2)}, u32[]{:S(2)}) %collective-permute-start.19) | collective-permute-done | bytes 524320 | tf_op jit(solution)/shard_map/ppermute | solution.py:190
  153.1 10.1 %collective-permute-done.18 = bf16[128,2048]{1,0:T(8,128)(2,1)S(1)} collective-permute-done((bf16[128,2048]{1,0:T(8,128)(2,1)S(1)}, bf16[128,2048]{1,0:T(8,128)(2,1)S(1)}, u32[]{:S(2)}, u32[]{:S(2)}) %collective-permute-start.18) | collective-permute-done | bytes 524320 | tf_op jit(solution)/shard_map/ppermute | solution.py:190
  168.2 22.4 %collective-permute-done.25 = bf16[256,2048]{1,0:T(8,128)(2,1)} collective-permute-done((bf16[256,2048]{1,0:T(8,128)(2,1)}, bf16[256,2048]{1,0:T(8,128)(2,1)}, u32[]{:S(2)}, u32[]{:S(2)}) %collective-permute-start.25) | collective-permute-done | bytes 1048608 | tf_op jit(solution)/shard_map/ppermute | solution.py:190
  199.9 7.5 %collective-permute-done.29 = bf16[128,2048]{1,0:T(8,128)(2,1)S(1)} collective-permute-done((bf16[128,2048]{1,0:T(8,128)(2,1)S(1)}, bf16[128,2048]{1,0:T(8,128)(2,1)S(1)}, u32[]{:S(2)}, u32[]{:S(2)}) %collective-permute-start.29) | collective-permute-done | bytes 524320 | tf_op jit(solution)/shard_map/ppermute | solution.py:190
  215.8 16.0 %fusion.29 = f32[2,2048,684]{1,2,0:T(8,128)S(1)} fusion(bf16[2,684,2048]{2,1,0:T(8,128)(2,1)} %all-gather.6.cloned.1.call-done, bf16[2048,2048]{1,0:T(8,128)(2,1)} %constant_dynamic-update-slice_fusion.10), kind=kOutput, calls=%fused_computation.32 | convolution fusion | flops 11475615744 | bytes 25198592 | tf_op jit(solution)/shard_map/td,cfd->ctf/dot_general | solution.py:386
  231.8 4.2 copy-done.3
  236.0 3.6 fusion.13
  239.5 20.2 %all-gather.8.cloned.1.call-done = bf16[684,2048]{1,0:T(8,128)(2,1)} async-done(((bf16[684,512]{1,0:T(8,128)(2,1)}), bf16[684,2048]{1,0:T(8,128)(2,1)}) %all-gather.8.cloned.1.call-update) | async-done | bytes 2801680 | tf_op jit(solution)/shard_map/all_gather | solution.py:362
  259.7 4.0 fusion.138
  263.9 5.7 fusion.43
  278.2 8.1 %collective-permute-done.36 = bf16[128,2048]{1,0:T(8,128)(2,1)S(1)} collective-permute-done((bf16[128,2048]{1,0:T(8,128)(2,1)S(1)}, bf16[128,2048]{1,0:T(8,128)(2,1)S(1)}, u32[]{:S(2)}, u32[]{:S(2)}) %collective-permute-start.36) | collective-permute-done | bytes 524320 | tf_op jit(solution)/shard_map/ppermute | solution.py:190
  289.6 9.4 %collective-permute-done.38 = bf16[128,2048]{1,0:T(8,128)(2,1)S(1)} collective-permute-done((bf16[128,2048]{1,0:T(8,128)(2,1)S(1)}, bf16[128,2048]{1,0:T(8,128)(2,1)S(1)}, u32[]{:S(2)}, u32[]{:S(2)}) %collective-permute-start.38) | collective-permute-done | bytes 524320 | tf_op jit(solution)/shard_map/ppermute | solution.py:190
  299.0 10.1 %collective-permute-done.37 = bf16[128,2048]{1,0:T(8,128)(2,1)S(1)} collective-permute-done((bf16[128,2048]{1,0:T(8,128)(2,1)S(1)}, bf16[128,2048]{1,0:T(8,128)(2,1)S(1)}, u32[]{:S(2)}, u32[]{:S(2)}) %collective-permute-start.37) | collective-permute-done | bytes 524320 | tf_op jit(solution)/shard_map/ppermute | solution.py:190
  317.3 4.6 fusion.147
  321.9 3.7 convolution_bitcast_fusion.3
  325.7 14.5 %collective-permute-done.44 = bf16[256,2048]{1,0:T(8,128)(2,1)S(1)} collective-permute-done((bf16[256,2048]{1,0:T(8,128)(2,1)S(1)}, bf16[256,2048]{1,0:T(8,128)(2,1)S(1)}, u32[]{:S(2)}, u32[]{:S(2)}) %collective-permute-start.44) | collective-permute-done | bytes 1048608 | tf_op jit(solution)/shard_map/ppermute | solution.py:190
  344.5 11.3 %collective-permute-done.48 = bf16[128,2048]{1,0:T(8,128)(2,1)S(1)} collective-permute-done((bf16[128,2048]{1,0:T(8,128)(2,1)S(1)}, bf16[128,2048]{1,0:T(8,128)(2,1)S(1)}, u32[]{:S(2)}, u32[]{:S(2)}) %collective-permute-start.48) | collective-permute-done | bytes 524320 | tf_op jit(solution)/shard_map/ppermute | solution.py:190
  361.8 7.8 %fusion.185 = bf16[684,2048]{1,0:T(8,128)(2,1)} fusion(bf16[2048,684]{0,1:T(8,128)(2,1)S(1)} %copy-done.16, bf16[2048,2048]{1,0:T(8,128)(2,1)S(1)} %constant_dynamic-update-slice_fusion.20), kind=kOutput, calls=%fused_computation.322 | convolution fusion | flops 5737807872 | bytes 13991936 | tf_op jit(solution)/shard_map/tf,td->fd/dot_general | solution.py:425
  369.6 5.8 fusion.146
  375.4 6.8 %convolution_bitcast_fusion.2 = bf16[512,2048]{1,0:T(8,128)(2,1)S(1)} fusion(bf16[2,684,2048]{2,1,0:T(8,128)(2,1)} %all-gather.6.cloned.1.call-done, bf16[1,512,684]{1,2,0:T(8,128)(2,1)S(1)} %get-tuple-element.151, bf16[1,512,684]{1,2,0:T(8,128)(2,1)S(1)} %get-tuple-element.150), kind=kOutput, calls=%fused_computation.45 | convolution fusion | flops 2869604352 | bytes 9101312 | tf_op jit(solution)/shard_map/ctf,cfd->td/dot_general | solution.py:415
  384.8 6.0 fusion.145
  393.7 6.6 %convolution_bitcast_fusion.1 = bf16[512,2048]{1,0:T(8,128)(2,1)S(1)} fusion(bf16[2,684,2048]{2,1,0:T(8,128)(2,1)} %all-gather.6.cloned.1.call-done, bf16[1,512,684]{1,2,0:T(8,128)(2,1)S(1)} %get-tuple-element.149, bf16[1,512,684]{1,2,0:T(8,128)(2,1)S(1)} %get-tuple-element.148), kind=kOutput, calls=%fused_computation.44 | convolution fusion | flops 2869604352 | bytes 9101312 | tf_op jit(solution)/shard_map/ctf,cfd->td/dot_general | solution.py:415
  403.9 5.2 fusion.144
  409.2 3.7 convolution_bitcast_fusion
  412.9 3.4 collective-permute-done.55
  425.8 14.0 %fusion = bf16[2,684,2048]{2,1,0:T(8,128)(2,1)} fusion(bf16[2048,2048]{1,0:T(8,128)(2,1)S(1)} %bitcast.262, bf16[1,512,684]{1,2,0:T(8,128)(2,1)S(1)} %copy-done.48, bf16[1,512,684]{1,2,0:T(8,128)(2,1)S(1)} %copy-done.46, bf16[1,512,684]{1,2,0:T(8,128)(2,1)S(1)} %get-tuple-element.147, bf16[1,512,684]{1,2,0:T(8,128)(2,1)S(1)} %get-tuple-element.146, ...), kind=kOutput, calls=%fused_computation.1 | convolution fusion | flops 11520442368 | bytes 19595264 | tf_op jit(solution)/shard_map/ctf,td->cfd/dot_general | solution.py:430
  439.8 5.6 collective-permute-done.58
  445.4 3.6 collective-permute-done.60
  449.1 5.8 multiply_reduce_fusion
  459.7 5.0 multiply_subtract_fusion
  464.7 17.2 %collective-permute-done.63 = bf16[256,2048]{1,0:T(8,128)(2,1)S(1)} collective-permute-done((bf16[256,2048]{1,0:T(8,128)(2,1)}, bf16[256,2048]{1,0:T(8,128)(2,1)S(1)}, u32[]{:S(2)}, u32[]{:S(2)}) %collective-permute-start.63) | collective-permute-done | bytes 1048608 | tf_op jit(solution)/shard_map/ppermute | solution.py:190
  486.7 9.9 %collective-permute-done.67 = bf16[128,2048]{1,0:T(8,128)(2,1)S(1)} collective-permute-done((bf16[128,2048]{1,0:T(8,128)(2,1)S(1)}, bf16[128,2048]{1,0:T(8,128)(2,1)S(1)}, u32[]{:S(2)}, u32[]{:S(2)}) %collective-permute-start.67) | collective-permute-done | bytes 524320 | tf_op jit(solution)/shard_map/ppermute | solution.py:190
  499.3 5.4 fusion.129.grad_ref
  504.7 14.2 %attend_backward.1 = bf16[2048,768]{1,0:T(8,128)(2,1)} custom-call(s32[4]{0:T(128)} %objective_ref.3, s32[4]{0:T(128)} %prefix_ref.3, s32[2]{0:T(128)} %pad_add_fusion.place_ref, bf16[2048,256]{1,0:T(8,128)(2,1)} %get-tuple-element.90.query_ref, bf16[2048,256]{1,0:T(8,128)(2,1)} %get-tuple-element.91.key_ref, bf16[2048,256]{1,0:T(8,128)(2,1)} %get-tuple-element.92.value_ref, ...), custom_call_target="tpu_custom_call" | custom-call | tf_op jit(solution)/shard_map/attend_backward/pallas_call | solution.py:150
  518.9 5.9 fusion.186
  524.8 9.6 %fusion.187 = bf16[768,2048]{1,0:T(8,128)(2,1)S(1)} fusion(bf16[2048,768]{1,0:T(8,128)(2,1)S(1)} %copy-done.14, bf16[2048,2048]{1,0:T(8,128)(2,1)} %constant_dynamic-update-slice_fusion), kind=kOutput, calls=%fused_computation.324 | convolution fusion | flops 6442450944 | bytes 14680064 | tf_op jit(solution)/shard_map/te,td->ed/dot_general | solution.py:465
  537.8 3.8 fusion.38
  546.7 7.1 %fusion.36 = bf16[1536,2048]{1,0:T(8,128)(2,1)S(1)} fusion(bf16[2048,1024]{0,1:T(8,128)(2,1)} %all-gather.4.cloned.1.call-done, bf16[2048,768]{1,0:T(8,128)(2,1)S(1)} %copy-done.15), kind=kOutput, calls=%fused_computation.47 | convolution fusion | flops 4831838208 | bytes 11796480 | tf_op jit(solution)/shard_map/te,de->td/dot_general | solution.py:485
  564.4 16.4 %fusion.160 = (f32[512,2,684]{0,1,2:T(2,128)}, f32[512,2,684]{0,1,2:T(2,128)}, f32[512,2,684]{0,1,2:T(2,128)}) fusion(f32[]{:T(128)S(6)} %div.99, bf16[2,684,512]{2,1,0:T(8,128)(2,1)S(1)} %copy-done.27, f32[512,2,684]{0,1,2:T(2,128)S(1)} %copy-done.17, f32[512,2,684]{0,1,2:T(2,128)S(1)} %copy-done.18, f32[512,2,684]{0,1,2:T(2,128)S(1)} %copy-done.5), kind=kLoop, calls=%fused_computation.310 | loop fusion | flops 11206656 | bytes 18210820 | tf_op jit(solution)/shard_map/transpose | solution.py:311
  583.8 10.4 %collective-permute-done.80 = bf16[128,2048]{1,0:T(8,128)(2,1)S(1)} collective-permute-done((bf16[128,2048]{1,0:T(8,128)(2,1)S(1)}, bf16[128,2048]{1,0:T(8,128)(2,1)S(1)}, u32[]{:S(2)}, u32[]{:S(2)}) %collective-permute-start.80) | collective-permute-done | bytes 524320 | tf_op jit(solution)/shard_map/ppermute | solution.py:190
  606.6 3.3 collective-permute-done.84
  616.5 11.0 %reduce-scatter.8.cloned.1.call-done = bf16[1024,512]{1,0:T(8,128)(2,1)} async-done(((bf16[1024,2048]{1,0:T(8,128)(2,1)}), bf16[1024,512]{1,0:T(8,128)(2,1)}) %reduce-scatter.8.cloned.1.call-update) | async-done | bytes 1048592 | tf_op jit(solution)/shard_map/reduce_scatter | solution.py:472
  629.1 5.4 fusion.135
  (418 shorter events, 196.1 us)
Async XLA Ops:
  7.2 88.8 %all-gather.4.cloned.1.call-start = ((), (), s32[]{:S(2)}) async-start(), calls=%async_computation.3 | async-start | bytes 5242880 | tf_op jit(solution)/shard_map/all_gather | solution.py:355
  12.2 203.5 %all-gather.6.cloned.1.call-start = ((), (), s32[]{:S(2)}) async-start(), calls=%async_computation.4 | async-start | bytes 7045120 | tf_op jit(solution)/shard_map/all_gather | solution.py:361
  12.3 29.0 %collective-permute-start.1 = (bf16[256,2048]{1,0:T(8,128)(2,1)}, bf16[256,2048]{1,0:T(8,128)(2,1)}, u32[]{:S(2)}, u32[]{:S(2)}) collective-permute-start(bf16[256,2048]{1,0:T(8,128)(2,1)} %param.20), channel_id=1, source_target_pairs={{0,2},{1,3},{2,0},{3,1},{4,6},{5,7},{6,4},{7,5},{8,10},{9,11},{10,... | collective-permute-start | bytes 3145736 | tf_op jit(solution)/shard_map/ppermute | solution.py:190
  15.3 41.9 %collective-permute-start = (bf16[256,2048]{1,0:T(8,128)(2,1)}, bf16[256,2048]{1,0:T(8,128)(2,1)}, u32[]{:S(2)}, u32[]{:S(2)}) collective-permute-start(bf16[256,2048]{1,0:T(8,128)(2,1)} %param.20), channel_id=1, source_target_pairs={{0,1},{1,0},{2,3},{3,2},{4,5},{5,4},{6,7},{7,6},{8,9},{9,8},{10,11... | collective-permute-start | bytes 3145736 | tf_op jit(solution)/shard_map/ppermute | solution.py:190
  15.3 38.0 %collective-permute-start.3 = (bf16[256,2048]{1,0:T(8,128)(2,1)}, bf16[256,2048]{1,0:T(8,128)(2,1)}, u32[]{:S(2)}, u32[]{:S(2)}) collective-permute-start(bf16[256,2048]{1,0:T(8,128)(2,1)} %param.20), channel_id=1, source_target_pairs={{0,4},{1,5},{2,6},{3,7},{4,0},{5,1},{6,2},{7,3},{8,12},{9,13},{10,... | collective-permute-start | bytes 3145736 | tf_op jit(solution)/shard_map/ppermute | solution.py:190
  20.7 239.0 %all-gather.8.cloned.1.call-start = ((), (), s32[]{:S(2)}) async-start(), calls=%async_computation.5 | async-start | bytes 3522560 | tf_op jit(solution)/shard_map/all_gather | solution.py:362
  22.5 16.3 %collective-permute-start.10 = (f32[8,128]{1,0:T(8,128)S(1)}, f32[8,128]{1,0:T(8,128)S(1)}, u32[]{:S(2)}, u32[]{:S(2)}) collective-permute-start(f32[8,128]{1,0:T(8,128)S(1)} %broadcast_add_fusion), channel_id=1, source_target_pairs={{0,2},{1,3},{2,0},{3,1},{4,6},{5,7},{6,4},{7,5},{8,10},{9,11},{10,... | collective-permute-start | bytes 12296 | tf_op jit(solution)/shard_map/ppermute | solution.py:190
  41.3 24.2 %collective-permute-start.2 = (bf16[256,2048]{1,0:T(8,128)(2,1)}, bf16[256,2048]{1,0:T(8,128)(2,1)S(1)}, u32[]{:S(2)}, u32[]{:S(2)}) collective-permute-start(bf16[256,2048]{1,0:T(8,128)(2,1)} %collective-permute-done.1), channel_id=1, source_target_pairs={{0,1},{1,0},{2,3},{3,2},{4,5},{5,4},{6,7},{7,6},{8,9},{9,8},{10,11... | collective-permute-start | bytes 3145736 | tf_op jit(solution)/shard_map/ppermute | solution.py:190
  124.5 19.8 %collective-permute-start.14 = (bf16[256,2048]{1,0:T(8,128)(2,1)S(1)}, bf16[256,2048]{1,0:T(8,128)(2,1)S(1)}, u32[]{:S(2)}, u32[]{:S(2)}) collective-permute-start(bf16[256,2048]{1,0:T(8,128)(2,1)S(1)} %get-tuple-element.164), channel_id=1, source_target_pairs={{0,1},{1,0},{2,3},{3,2},{4,5},{5,4},{6,7},{7,6},{8,9},{9,8},{10,11... | collective-permute-start | bytes 3145736 | tf_op jit(solution)/shard_map/ppermute | solution.py:190
  127.1 15.0 %collective-permute-start.22 = (bf16[128,2048]{1,0:T(8,128)(2,1)S(1)}, bf16[128,2048]{1,0:T(8,128)(2,1)S(1)}, u32[]{:S(2)}, u32[]{:S(2)}) collective-permute-start(bf16[128,2048]{1,0:T(8,128)(2,1)S(1)} %get-tuple-element.183), channel_id=1, source_target_pairs={{0,2},{1,3},{2,0},{3,1},{4,6},{5,7},{6,4},{7,5},{8,10},{9,11},{10,... | collective-permute-start | bytes 1572872 | tf_op jit(solution)/shard_map/ppermute | solution.py:190
  129.4 23.7 %collective-permute-start.19 = (bf16[128,2048]{1,0:T(8,128)(2,1)S(1)}, bf16[128,2048]{1,0:T(8,128)(2,1)S(1)}, u32[]{:S(2)}, u32[]{:S(2)}) collective-permute-start(bf16[128,2048]{1,0:T(8,128)(2,1)S(1)} %slice.624), channel_id=1, source_target_pairs={{0,2},{1,3},{2,0},{3,1},{4,6},{5,7},{6,4},{7,5},{8,10},{9,11},{10,... | collective-permute-start | bytes 1572872 | tf_op jit(solution)/shard_map/ppermute | solution.py:190
  130.8 22.4 %collective-permute-start.21 = (bf16[128,2048]{1,0:T(8,128)(2,1)S(1)}, bf16[128,2048]{1,0:T(8,128)(2,1)S(1)}, u32[]{:S(2)}, u32[]{:S(2)}) collective-permute-start(bf16[128,2048]{1,0:T(8,128)(2,1)S(1)} %slice.623), channel_id=1, source_target_pairs={{0,4},{1,5},{2,6},{3,7},{4,0},{5,1},{6,2},{7,3},{8,12},{9,13},{10,... | collective-permute-start | bytes 1572872 | tf_op jit(solution)/shard_map/ppermute | solution.py:190
  140.5 22.7 %collective-permute-start.18 = (bf16[128,2048]{1,0:T(8,128)(2,1)S(1)}, bf16[128,2048]{1,0:T(8,128)(2,1)S(1)}, u32[]{:S(2)}, u32[]{:S(2)}) collective-permute-start(bf16[128,2048]{1,0:T(8,128)(2,1)S(1)} %fusion.127), channel_id=1, source_target_pairs={{0,2},{1,3},{2,0},{3,1},{4,6},{5,7},{6,4},{7,5},{8,10},{9,11},{10,... | collective-permute-start | bytes 1572872 | tf_op jit(solution)/shard_map/ppermute | solution.py:190
  142.2 21.0 %collective-permute-start.23 = (bf16[128,2048]{1,0:T(8,128)(2,1)S(1)}, bf16[128,2048]{1,0:T(8,128)(2,1)S(1)}, u32[]{:S(2)}, u32[]{:S(2)}) collective-permute-start(bf16[128,2048]{1,0:T(8,128)(2,1)S(1)} %fusion.126), channel_id=1, source_target_pairs={{0,4},{1,5},{2,6},{3,7},{4,0},{5,1},{6,2},{7,3},{8,12},{9,13},{10,... | collective-permute-start | bytes 1572872 | tf_op jit(solution)/shard_map/ppermute | solution.py:190
  166.3 24.4 %collective-permute-start.25 = (bf16[256,2048]{1,0:T(8,128)(2,1)}, bf16[256,2048]{1,0:T(8,128)(2,1)}, u32[]{:S(2)}, u32[]{:S(2)}) collective-permute-start(bf16[256,2048]{1,0:T(8,128)(2,1)} %get-tuple-element.143), channel_id=1, source_target_pairs={{0,2},{1,3},{2,0},{3,1},{4,6},{5,7},{6,4},{7,5},{8,10},{9,11},{10,... | collective-permute-start | bytes 3145736 | tf_op jit(solution)/shard_map/ppermute | solution.py:190
  167.7 25.9 %collective-permute-start.27 = (bf16[256,2048]{1,0:T(8,128)(2,1)}, bf16[256,2048]{1,0:T(8,128)(2,1)S(1)}, u32[]{:S(2)}, u32[]{:S(2)}) collective-permute-start(bf16[256,2048]{1,0:T(8,128)(2,1)} %get-tuple-element.143), channel_id=1, source_target_pairs={{0,4},{1,5},{2,6},{3,7},{4,0},{5,1},{6,2},{7,3},{8,12},{9,13},{10,... | collective-permute-start | bytes 3145736 | tf_op jit(solution)/shard_map/ppermute | solution.py:190
  168.2 26.9 %collective-permute-start.24 = (bf16[256,2048]{1,0:T(8,128)(2,1)}, bf16[256,2048]{1,0:T(8,128)(2,1)}, u32[]{:S(2)}, u32[]{:S(2)}) collective-permute-start(bf16[256,2048]{1,0:T(8,128)(2,1)} %get-tuple-element.143), channel_id=1, source_target_pairs={{0,1},{1,0},{2,3},{3,2},{4,5},{5,4},{6,7},{7,6},{8,9},{9,8},{10,11... | collective-permute-start | bytes 3145736 | tf_op jit(solution)/shard_map/ppermute | solution.py:190
  190.7 17.2 %collective-permute-start.26 = (bf16[256,2048]{1,0:T(8,128)(2,1)}, bf16[256,2048]{1,0:T(8,128)(2,1)}, u32[]{:S(2)}, u32[]{:S(2)}) collective-permute-start(bf16[256,2048]{1,0:T(8,128)(2,1)} %collective-permute-done.25), channel_id=1, source_target_pairs={{0,1},{1,0},{2,3},{3,2},{4,5},{5,4},{6,7},{7,6},{8,9},{9,8},{10,11... | collective-permute-start | bytes 3145736 | tf_op jit(solution)/shard_map/ppermute | solution.py:190
  191.7 257.3 %reduce-scatter.4.cloned.1.call-start = ((), (), s32[]{:S(2)}) async-start(), calls=%async_computation.6 | async-start | bytes 3522560 | tf_op jit(solution)/shard_map/reduce_scatter | solution.py:427
  195.2 16.2 %collective-permute-start.28 = (bf16[256,2048]{1,0:T(8,128)(2,1)S(1)}, bf16[256,2048]{1,0:T(8,128)(2,1)S(1)}, u32[]{:S(2)}, u32[]{:S(2)}) collective-permute-start(bf16[256,2048]{1,0:T(8,128)(2,1)S(1)} %collective-permute-done.27), channel_id=1, source_target_pairs={{0,1},{1,0},{2,3},{3,2},{4,5},{5,4},{6,7},{7,6},{8,9},{9,8},{10,11... | collective-permute-start | bytes 3145736 | tf_op jit(solution)/shard_map/ppermute | solution.py:190
  270.5 19.2 %collective-permute-start.33 = (bf16[256,2048]{1,0:T(8,128)(2,1)S(1)}, bf16[256,2048]{1,0:T(8,128)(2,1)S(1)}, u32[]{:S(2)}, u32[]{:S(2)}) collective-permute-start(bf16[256,2048]{1,0:T(8,128)(2,1)S(1)} %get-tuple-element.159), channel_id=1, source_target_pairs={{0,1},{1,0},{2,3},{3,2},{4,5},{5,4},{6,7},{7,6},{8,9},{9,8},{10,11... | collective-permute-start | bytes 3145736 | tf_op jit(solution)/shard_map/ppermute | solution.py:190
  273.0 15.0 %collective-permute-start.41 = (bf16[128,2048]{1,0:T(8,128)(2,1)S(1)}, bf16[128,2048]{1,0:T(8,128)(2,1)S(1)}, u32[]{:S(2)}, u32[]{:S(2)}) collective-permute-start(bf16[128,2048]{1,0:T(8,128)(2,1)S(1)} %get-tuple-element.181), channel_id=1, source_target_pairs={{0,2},{1,3},{2,0},{3,1},{4,6},{5,7},{6,4},{7,5},{8,10},{9,11},{10,... | collective-permute-start | bytes 1572872 | tf_op jit(solution)/shard_map/ppermute | solution.py:190
  275.3 23.7 %collective-permute-start.38 = (bf16[128,2048]{1,0:T(8,128)(2,1)S(1)}, bf16[128,2048]{1,0:T(8,128)(2,1)S(1)}, u32[]{:S(2)}, u32[]{:S(2)}) collective-permute-start(bf16[128,2048]{1,0:T(8,128)(2,1)S(1)} %slice.622), channel_id=1, source_target_pairs={{0,2},{1,3},{2,0},{3,1},{4,6},{5,7},{6,4},{7,5},{8,10},{9,11},{10,... | collective-permute-start | bytes 1572872 | tf_op jit(solution)/shard_map/ppermute | solution.py:190
  276.7 22.3 %collective-permute-start.40 = (bf16[128,2048]{1,0:T(8,128)(2,1)S(1)}, bf16[128,2048]{1,0:T(8,128)(2,1)S(1)}, u32[]{:S(2)}, u32[]{:S(2)}) collective-permute-start(bf16[128,2048]{1,0:T(8,128)(2,1)S(1)} %slice.621), channel_id=1, source_target_pairs={{0,4},{1,5},{2,6},{3,7},{4,0},{5,1},{6,2},{7,3},{8,12},{9,13},{10,... | collective-permute-start | bytes 1572872 | tf_op jit(solution)/shard_map/ppermute | solution.py:190
  286.4 22.6 %collective-permute-start.37 = (bf16[128,2048]{1,0:T(8,128)(2,1)S(1)}, bf16[128,2048]{1,0:T(8,128)(2,1)S(1)}, u32[]{:S(2)}, u32[]{:S(2)}) collective-permute-start(bf16[128,2048]{1,0:T(8,128)(2,1)S(1)} %fusion.125), channel_id=1, source_target_pairs={{0,2},{1,3},{2,0},{3,1},{4,6},{5,7},{6,4},{7,5},{8,10},{9,11},{10,... | collective-permute-start | bytes 1572872 | tf_op jit(solution)/shard_map/ppermute | solution.py:190
  288.1 21.0 %collective-permute-start.42 = (bf16[128,2048]{1,0:T(8,128)(2,1)S(1)}, bf16[128,2048]{1,0:T(8,128)(2,1)S(1)}, u32[]{:S(2)}, u32[]{:S(2)}) collective-permute-start(bf16[128,2048]{1,0:T(8,128)(2,1)S(1)} %fusion.124), channel_id=1, source_target_pairs={{0,4},{1,5},{2,6},{3,7},{4,0},{5,1},{6,2},{7,3},{8,12},{9,13},{10,... | collective-permute-start | bytes 1572872 | tf_op jit(solution)/shard_map/ppermute | solution.py:190
  314.6 25.6 %collective-permute-start.44 = (bf16[256,2048]{1,0:T(8,128)(2,1)S(1)}, bf16[256,2048]{1,0:T(8,128)(2,1)S(1)}, u32[]{:S(2)}, u32[]{:S(2)}) collective-permute-start(bf16[256,2048]{1,0:T(8,128)(2,1)S(1)} %get-tuple-element.139), channel_id=1, source_target_pairs={{0,2},{1,3},{2,0},{3,1},{4,6},{5,7},{6,4},{7,5},{8,10},{9,11},{10,... | collective-permute-start | bytes 3145736 | tf_op jit(solution)/shard_map/ppermute | solution.py:190
  316.2 25.2 %collective-permute-start.45 = (bf16[256,2048]{1,0:T(8,128)(2,1)S(1)}, bf16[256,2048]{1,0:T(8,128)(2,1)S(1)}, u32[]{:S(2)}, u32[]{:S(2)}) collective-permute-start(bf16[256,2048]{1,0:T(8,128)(2,1)S(1)} %get-tuple-element.139), channel_id=1, source_target_pairs={{0,4},{1,5},{2,6},{3,7},{4,0},{5,1},{6,2},{7,3},{8,12},{9,13},{10,... | collective-permute-start | bytes 3145736 | tf_op jit(solution)/shard_map/ppermute | solution.py:190
  341.4 15.0 %collective-permute-start.46 = (bf16[256,2048]{1,0:T(8,128)(2,1)S(1)}, bf16[256,2048]{1,0:T(8,128)(2,1)S(1)}, u32[]{:S(2)}, u32[]{:S(2)}) collective-permute-start(bf16[256,2048]{1,0:T(8,128)(2,1)S(1)} %collective-permute-done.44), channel_id=1, source_target_pairs={{0,1},{1,0},{2,3},{3,2},{4,5},{5,4},{6,7},{7,6},{8,9},{9,8},{10,11... | collective-permute-start | bytes 3145736 | tf_op jit(solution)/shard_map/ppermute | solution.py:190
  341.4 15.2 %collective-permute-start.47 = (bf16[256,2048]{1,0:T(8,128)(2,1)S(1)}, bf16[256,2048]{1,0:T(8,128)(2,1)S(1)}, u32[]{:S(2)}, u32[]{:S(2)}) collective-permute-start(bf16[256,2048]{1,0:T(8,128)(2,1)S(1)} %collective-permute-done.45), channel_id=1, source_target_pairs={{0,1},{1,0},{2,3},{3,2},{4,5},{5,4},{6,7},{7,6},{8,9},{9,8},{10,11... | collective-permute-start | bytes 3145736 | tf_op jit(solution)/shard_map/ppermute | solution.py:190
  344.3 46.5 %collective-permute-start.53 = (bf16[256,2048]{1,0:T(8,128)(2,1)}, bf16[256,2048]{1,0:T(8,128)(2,1)}, u32[]{:S(2)}, u32[]{:S(2)}) collective-permute-start(bf16[256,2048]{1,0:T(8,128)(2,1)} %slice.341), channel_id=1, source_target_pairs={{0,1},{1,0},{2,3},{3,2},{4,5},{5,4},{6,7},{7,6},{8,9},{9,8},{10,11... | collective-permute-start | bytes 3145736 | tf_op jit(solution)/shard_map/ppermute | solution.py:190
  384.5 15.8 %collective-permute-start.52 = (bf16[256,2048]{1,0:T(8,128)(2,1)}, bf16[256,2048]{1,0:T(8,128)(2,1)}, u32[]{:S(2)}, u32[]{:S(2)}) collective-permute-start(bf16[256,2048]{1,0:T(8,128)(2,1)} %slice.339), channel_id=1, source_target_pairs={{0,1},{1,0},{2,3},{3,2},{4,5},{5,4},{6,7},{7,6},{8,9},{9,8},{10,11... | collective-permute-start | bytes 3145736 | tf_op jit(solution)/shard_map/ppermute | solution.py:190
  384.7 161.9 %reduce-scatter.6.cloned.1.call-start = ((), (), s32[]{:S(2)}) async-start(), calls=%async_computation.7 | async-start | bytes 7045120 | tf_op jit(solution)/shard_map/reduce_scatter | solution.py:455
  419.5 20.3 %collective-permute-start.57 = (bf16[128,2048]{1,0:T(8,128)(2,1)}, bf16[128,2048]{1,0:T(8,128)(2,1)}, u32[]{:S(2)}, u32[]{:S(2)}) collective-permute-start(bf16[128,2048]{1,0:T(8,128)(2,1)} %fusion.123), channel_id=1, source_target_pairs={{0,2},{1,3},{2,0},{3,1},{4,6},{5,7},{6,4},{7,5},{8,10},{9,11},{10,... | collective-permute-start | bytes 1572872 | tf_op jit(solution)/shard_map/ppermute | solution.py:190
  420.0 25.3 %collective-permute-start.58 = (bf16[128,2048]{1,0:T(8,128)(2,1)}, bf16[128,2048]{1,0:T(8,128)(2,1)}, u32[]{:S(2)}, u32[]{:S(2)}) collective-permute-start(bf16[128,2048]{1,0:T(8,128)(2,1)} %slice.620), channel_id=1, source_target_pairs={{0,2},{1,3},{2,0},{3,1},{4,6},{5,7},{6,4},{7,5},{8,10},{9,11},{10,... | collective-permute-start | bytes 1572872 | tf_op jit(solution)/shard_map/ppermute | solution.py:190
  423.7 21.7 %collective-permute-start.61 = (bf16[128,2048]{1,0:T(8,128)(2,1)}, bf16[128,2048]{1,0:T(8,128)(2,1)}, u32[]{:S(2)}, u32[]{:S(2)}) collective-permute-start(bf16[128,2048]{1,0:T(8,128)(2,1)} %fusion.122), channel_id=1, source_target_pairs={{0,4},{1,5},{2,6},{3,7},{4,0},{5,1},{6,2},{7,3},{8,12},{9,13},{10,... | collective-permute-start | bytes 1572872 | tf_op jit(solution)/shard_map/ppermute | solution.py:190
  424.6 24.4 %collective-permute-start.60 = (bf16[128,2048]{1,0:T(8,128)(2,1)}, bf16[128,2048]{1,0:T(8,128)(2,1)}, u32[]{:S(2)}, u32[]{:S(2)}) collective-permute-start(bf16[128,2048]{1,0:T(8,128)(2,1)} %slice.619), channel_id=1, source_target_pairs={{0,4},{1,5},{2,6},{3,7},{4,0},{5,1},{6,2},{7,3},{8,12},{9,13},{10,... | collective-permute-start | bytes 1572872 | tf_op jit(solution)/shard_map/ppermute | solution.py:190
  449.0 178.5 %reduce-scatter.8.cloned.1.call-start = ((), (), s32[]{:S(2)}) async-start(), calls=%async_computation.8 | async-start | bytes 5242880 | tf_op jit(solution)/shard_map/reduce_scatter | solution.py:472
  457.5 24.3 %collective-permute-start.63 = (bf16[256,2048]{1,0:T(8,128)(2,1)}, bf16[256,2048]{1,0:T(8,128)(2,1)S(1)}, u32[]{:S(2)}, u32[]{:S(2)}) collective-permute-start(bf16[256,2048]{1,0:T(8,128)(2,1)} %get-tuple-element.135), channel_id=1, source_target_pairs={{0,2},{1,3},{2,0},{3,1},{4,6},{5,7},{6,4},{7,5},{8,10},{9,11},{10,... | collective-permute-start | bytes 3145736 | tf_op jit(solution)/shard_map/ppermute | solution.py:190
  458.1 24.1 %collective-permute-start.64 = (bf16[256,2048]{1,0:T(8,128)(2,1)}, bf16[256,2048]{1,0:T(8,128)(2,1)S(1)}, u32[]{:S(2)}, u32[]{:S(2)}) collective-permute-start(bf16[256,2048]{1,0:T(8,128)(2,1)} %get-tuple-element.135), channel_id=1, source_target_pairs={{0,4},{1,5},{2,6},{3,7},{4,0},{5,1},{6,2},{7,3},{8,12},{9,13},{10,... | collective-permute-start | bytes 3145736 | tf_op jit(solution)/shard_map/ppermute | solution.py:190
  459.0 26.3 %collective-permute-start.62 = (bf16[256,2048]{1,0:T(8,128)(2,1)}, bf16[256,2048]{1,0:T(8,128)(2,1)}, u32[]{:S(2)}, u32[]{:S(2)}) collective-permute-start(bf16[256,2048]{1,0:T(8,128)(2,1)} %get-tuple-element.135), channel_id=1, source_target_pairs={{0,1},{1,0},{2,3},{3,2},{4,5},{5,4},{6,7},{7,6},{8,9},{9,8},{10,11... | collective-permute-start | bytes 3145736 | tf_op jit(solution)/shard_map/ppermute | solution.py:190
  482.1 15.2 %collective-permute-start.65 = (bf16[256,2048]{1,0:T(8,128)(2,1)S(1)}, bf16[256,2048]{1,0:T(8,128)(2,1)S(1)}, u32[]{:S(2)}, u32[]{:S(2)}) collective-permute-start(bf16[256,2048]{1,0:T(8,128)(2,1)S(1)} %collective-permute-done.63), channel_id=1, source_target_pairs={{0,1},{1,0},{2,3},{3,2},{4,5},{5,4},{6,7},{7,6},{8,9},{9,8},{10,11... | collective-permute-start | bytes 3145736 | tf_op jit(solution)/shard_map/ppermute | solution.py:190
  482.1 15.4 %collective-permute-start.66 = (bf16[256,2048]{1,0:T(8,128)(2,1)S(1)}, bf16[256,2048]{1,0:T(8,128)(2,1)S(1)}, u32[]{:S(2)}, u32[]{:S(2)}) collective-permute-start(bf16[256,2048]{1,0:T(8,128)(2,1)S(1)} %collective-permute-done.64), channel_id=1, source_target_pairs={{0,1},{1,0},{2,3},{3,2},{4,5},{5,4},{6,7},{7,6},{8,9},{9,8},{10,11... | collective-permute-start | bytes 3145736 | tf_op jit(solution)/shard_map/ppermute | solution.py:190
  554.8 27.7 %collective-permute-start.71 = (bf16[256,2048]{1,0:T(8,128)(2,1)S(1)}, bf16[256,2048]{1,0:T(8,128)(2,1)S(1)}, u32[]{:S(2)}, u32[]{:S(2)}) collective-permute-start(bf16[256,2048]{1,0:T(8,128)(2,1)S(1)} %get-tuple-element.158), channel_id=1, source_target_pairs={{0,1},{1,0},{2,3},{3,2},{4,5},{5,4},{6,7},{7,6},{8,9},{9,8},{10,11... | collective-permute-start | bytes 3145736 | tf_op jit(solution)/shard_map/ppermute | solution.py:190
  557.4 23.5 %collective-permute-start.74 = (bf16[128,2048]{1,0:T(8,128)(2,1)S(1)}, bf16[128,2048]{1,0:T(8,128)(2,1)S(1)}, u32[]{:S(2)}, u32[]{:S(2)}) collective-permute-start(bf16[128,2048]{1,0:T(8,128)(2,1)S(1)} %get-tuple-element.177), channel_id=1, source_target_pairs={{0,4},{1,5},{2,6},{3,7},{4,0},{5,1},{6,2},{7,3},{8,12},{9,13},{10,... | collective-permute-start | bytes 1572872 | tf_op jit(solution)/shard_map/ppermute | solution.py:190
  558.9 21.9 %collective-permute-start.75 = (bf16[128,2048]{1,0:T(8,128)(2,1)S(1)}, bf16[128,2048]{1,0:T(8,128)(2,1)S(1)}, u32[]{:S(2)}, u32[]{:S(2)}) collective-permute-start(bf16[128,2048]{1,0:T(8,128)(2,1)S(1)} %get-tuple-element.176), channel_id=1, source_target_pairs={{0,2},{1,3},{2,0},{3,1},{4,6},{5,7},{6,4},{7,5},{8,10},{9,11},{10,... | collective-permute-start | bytes 1572872 | tf_op jit(solution)/shard_map/ppermute | solution.py:190
  561.3 22.5 %collective-permute-start.77 = (bf16[128,2048]{1,0:T(8,128)(2,1)S(1)}, bf16[128,2048]{1,0:T(8,128)(2,1)S(1)}, u32[]{:S(2)}, u32[]{:S(2)}) collective-permute-start(bf16[128,2048]{1,0:T(8,128)(2,1)S(1)} %slice.618), channel_id=1, source_target_pairs={{0,2},{1,3},{2,0},{3,1},{4,6},{5,7},{6,4},{7,5},{8,10},{9,11},{10,... | collective-permute-start | bytes 1572872 | tf_op jit(solution)/shard_map/ppermute | solution.py:190
  562.0 21.8 %collective-permute-start.79 = (bf16[128,2048]{1,0:T(8,128)(2,1)S(1)}, bf16[128,2048]{1,0:T(8,128)(2,1)S(1)}, u32[]{:S(2)}, u32[]{:S(2)}) collective-permute-start(bf16[128,2048]{1,0:T(8,128)(2,1)S(1)} %slice.617), channel_id=1, source_target_pairs={{0,4},{1,5},{2,6},{3,7},{4,0},{5,1},{6,2},{7,3},{8,12},{9,13},{10,... | collective-permute-start | bytes 1572872 | tf_op jit(solution)/shard_map/ppermute | solution.py:190
  (99 other events, 711.1 us)
Sparse Core Ops, SparseCore 0:
  12.4 83.5 all-gather.3
  98.1 103.0 all-gather.5
  203.4 56.2 all-gather.7
  384.8 52.7 reduce-scatter.3
  449.1 97.4 reduce-scatter.5
  548.8 78.7 reduce-scatter.7

commit v8 on v7

--- a/solution.py
+++ b/solution.py
@@ -256,16 +256,15 @@
     return piece[:half].astype(jnp.float32) + mate.astype(jnp.float32)
 
 
-def scatter_beside(own, rows, product, last):
-    far = product(rows, 3)
+def scatter_beside(own, near_x, rows, product, last):
+    own, near_x = core_sum(own), core_sum(near_x)
+    rows, own, near_x = lax.optimization_barrier((rows, own, near_x))
+    far = core_sum(product(rows, 3)).astype(jnp.bfloat16)
     rows, far = lax.optimization_barrier((rows, far))
-    near_x = product(rows, 1)
-    far, own = core_sum(far).astype(jnp.bfloat16), core_sum(own)
-    rows, far, own, near_x = lax.optimization_barrier((rows, far, own, near_x))
     half = far.shape[0] // 2
     far_low, far_high = swap(far[:half], "mp", 4), swap(far[half:], "mp", 2)
     near_y, far_low, far_high = lax.optimization_barrier((product(rows, 2), far_low, far_high))
-    near_x, near_y = core_sum(near_x), core_sum(near_y)
+    near_y = core_sum(near_y)
     low, high = slice(0, half), slice(half, 2 * half)
     x_low = (near_x[low] + far_low.astype(jnp.float32)).astype(jnp.bfloat16)
     y_high = (near_y[high] + far_high.astype(jnp.float32)).astype(jnp.bfloat16)
@@ -282,11 +281,14 @@
     own = product(jnp.concatenate([rows, mate], 0), 0)
     near_x, near_y, own = lax.optimization_barrier((near_x, near_y, own))
     far_low, far_high = swap(near_x[:half], "mp", 4), swap(near_y[half:], "mp", 2)
-    mates = [swap(part, "mp", 1) for part in (near_x, near_y, far_low, far_high)]
+    mate_x, mate_y = swap(near_x, "mp", 1), swap(near_y, "mp", 1)
+    across_x = product(jnp.concatenate([near_x, mate_x], 0), 1)
+    far_low, far_high, across_x = lax.optimization_barrier((far_low, far_high, across_x))
+    mates = [swap(far_low, "mp", 1), swap(far_high, "mp", 1)]
     whole = jnp.concatenate(
-        [rows, mate, near_x, mates[0], near_y, mates[1], far_low, far_high, *mates[2:]], 0
-    )
-    return whole, own
+        [rows, mate, near_x, mate_x, near_y, mate_y, far_low, far_high, *mates], 0
+    )
+    return whole, own, across_x
 
 
 def gather_all(rows, ahead=None):
@@ -419,7 +421,7 @@
 
     back_low = grad_two.astype(jnp.bfloat16)
     if near:
-        ffn_back, own_part = gather_beside(back_low, back_quarter)
+        ffn_back, own_part, x_part = gather_beside(back_low, back_quarter)
     else:
         ffn_back = gather_rows(back_low)
     down_grad = jnp.einsum("tf,td->fd", hidden_low, ffn_back, preferred_element_type=jnp.bfloat16)
@@ -436,7 +438,7 @@
 
     if near:
         grad_middle, gateup_grad = scatter_beside(
-            own_part, ffn_back, back_rows, gateup_product
+            own_part, x_part, ffn_back, back_rows, gateup_product
         )
     else:
         grad_middle = scatter_all([back_rows(ffn_back, index) for index in range(4)])

time: 649 us -> 645 us (level)
  matrix products: 139 us -> 130 us
    unnamed x144 -> x164, local copies, waits for them, and re-layouts: 44.6 us -> 43.6 us
  transfers between devices with their start and end apart: 92 -> 92, of which waited for: 43 -> 44; matrix products, arithmetic and copies ran while one was open for 37% -> 35% of each run, Pallas kernels for 4% -> 4%
where the time goes in v8:
time: 645 us; the launch traced here: 640 us
  waiting for transfers between devices  257 us (40%)
  matrix products  130 us (20%)
  other arithmetic  82.1 us (13%)
  starting transfers between devices  68.7 us (11%)
  local copies, waits for them, and re-layouts  60.9 us (9%)
  Pallas kernels  24.1 us (4%)
  between operations  16.8 us (3%)
    ppermute x86, waiting for transfers between devices, swap(): return lax.ppermute(values, axis, [(at, at ^ bit) for at in range(size)])  206 us
    ppermute x86, starting transfers between devices, swap(): return lax.ppermute(values, axis, [(at, at ^ bit) for at in range(size)])  68 us
    unnamed x164, local copies, waits for them, and re-layouts  43.6 us
    all_gather x1, waiting for transfers between devices, local(): attend_full = lax.all_gather(attend_low, 'dp', axis=0, tiled=True)  22.6 us
    transpose x2, other arithmetic, adamw_as(): jnp.transpose(rows, back)  21.9 us
    dot_general x4, matrix products, back_quarter(): jnp.einsum('td,fd->tf', chunk, down_full, preferred_element_type=jnp.floa...  19.6 us
    all_gather x1, waiting for transfers between devices, local(): lax.all_gather(down_weight.astype(jnp.bfloat16), 'dp', axis=1, tiled=True)  19.3 us
    dot_general x1, matrix products, local(): jnp.einsum('td,cfd->ctf', middle_low, gateup_full, preferred_element_type...  16 us
  transfers between devices with their start and end apart: 92, of which 44 were waited for; matrix products, arithmetic and copies ran while one was open for 35% of the time, Pallas kernels for 4%

profile of v8, /device:TPU:0, one launch (start us, length us, event | category | flops | bytes accessed | tf_op | source)
XLA Modules:
  0.0 639.6 jit_solution(16204613638343993956)
XLA Ops:
  24.1 15.7 %collective-permute-done.10 = f32[8,128]{1,0:T(8,128)S(1)} collective-permute-done((f32[8,128]{1,0:T(8,128)S(1)}, f32[8,128]{1,0:T(8,128)S(1)}, u32[]{:S(2)}, u32[]{:S(2)}) %collective-permute-start.10) | collective-permute-done | bytes 4128 | tf_op jit(solution)/shard_map/ppermute | solution.py:190
  74.4 22.6 %all-gather.4.cloned.1.call-done = bf16[2048,1024]{0,1:T(8,128)(2,1)} async-done(((bf16[512,1024]{0,1:T(8,128)(2,1)}), bf16[2048,1024]{0,1:T(8,128)(2,1)}) %all-gather.4.cloned.1.call-update) | async-done | bytes 4194320 | tf_op jit(solution)/shard_map/all_gather | solution.py:357
  97.0 12.0 %fusion.40.proj_ref = f32[2048,768]{1,0:T(8,128)} fusion(bf16[2048,2048]{1,0:T(8,128)(2,1)} %constant_dynamic-update-slice_fusion, bf16[2048,1024]{0,1:T(8,128)(2,1)} %all-gather.4.cloned.1.call-done), kind=kOutput, calls=%fused_computation.51 | convolution fusion | flops 6442450944 | bytes 17825792 | tf_op jit(solution)/shard_map/dot_general | solution.py:372
  108.9 10.0 %attend_forward.1 = (bf16[2048,256]{1,0:T(8,128)(2,1)}, bf16[2048,256]{1,0:T(8,128)(2,1)}, bf16[2048,256]{1,0:T(8,128)(2,1)}, bf16[2048,256]{1,0:T(8,128)(2,1)}) custom-call(s32[4]{0:T(128)} %objective_ref.3, s32[4]{0:T(128)} %prefix_ref.3, s32[2]{0:T(128)} %pad_add_fusion.place_ref, f32[2048,768]{1,0:T(8,128)} %fusion.40.proj_ref, ...), custom_call_target="tpu_custom_call" | custom-call | tf_op jit(solution)/shard_map/attend_forward/pallas_call | solution.py:138
  133.1 8.0 %collective-permute-done.22 = bf16[128,2048]{1,0:T(8,128)(2,1)S(1)} collective-permute-done((bf16[128,2048]{1,0:T(8,128)(2,1)S(1)}, bf16[128,2048]{1,0:T(8,128)(2,1)S(1)}, u32[]{:S(2)}, u32[]{:S(2)}) %collective-permute-start.22) | collective-permute-done | bytes 524320 | tf_op jit(solution)/shard_map/ppermute | solution.py:190
  145.2 8.7 %collective-permute-done.21 = bf16[128,2048]{1,0:T(8,128)(2,1)S(1)} collective-permute-done((bf16[128,2048]{1,0:T(8,128)(2,1)S(1)}, bf16[128,2048]{1,0:T(8,128)(2,1)S(1)}, u32[]{:S(2)}, u32[]{:S(2)}) %collective-permute-start.21) | collective-permute-done | bytes 524320 | tf_op jit(solution)/shard_map/ppermute | solution.py:190
  153.9 10.1 %collective-permute-done.23 = bf16[128,2048]{1,0:T(8,128)(2,1)S(1)} collective-permute-done((bf16[128,2048]{1,0:T(8,128)(2,1)S(1)}, bf16[128,2048]{1,0:T(8,128)(2,1)S(1)}, u32[]{:S(2)}, u32[]{:S(2)}) %collective-permute-start.23) | collective-permute-done | bytes 524320 | tf_op jit(solution)/shard_map/ppermute | solution.py:190
  169.1 22.3 %collective-permute-done.25 = bf16[256,2048]{1,0:T(8,128)(2,1)} collective-permute-done((bf16[256,2048]{1,0:T(8,128)(2,1)}, bf16[256,2048]{1,0:T(8,128)(2,1)}, u32[]{:S(2)}, u32[]{:S(2)}) %collective-permute-start.25) | collective-permute-done | bytes 1048608 | tf_op jit(solution)/shard_map/ppermute | solution.py:190
  200.8 7.5 %collective-permute-done.29 = bf16[128,2048]{1,0:T(8,128)(2,1)S(1)} collective-permute-done((bf16[128,2048]{1,0:T(8,128)(2,1)S(1)}, bf16[128,2048]{1,0:T(8,128)(2,1)S(1)}, u32[]{:S(2)}, u32[]{:S(2)}) %collective-permute-start.29) | collective-permute-done | bytes 524320 | tf_op jit(solution)/shard_map/ppermute | solution.py:190
  217.6 16.0 %fusion.29 = f32[2,2048,684]{1,2,0:T(8,128)S(1)} fusion(bf16[2,684,2048]{2,1,0:T(8,128)(2,1)} %all-gather.6.cloned.1.call-done, bf16[2048,2048]{1,0:T(8,128)(2,1)} %constant_dynamic-update-slice_fusion.10), kind=kOutput, calls=%fused_computation.32 | convolution fusion | flops 11475615744 | bytes 25198592 | tf_op jit(solution)/shard_map/td,cfd->ctf/dot_general | solution.py:388
  233.7 4.2 copy-done.3
  237.9 3.6 fusion.13
  241.4 19.3 %all-gather.8.cloned.1.call-done = bf16[684,2048]{1,0:T(8,128)(2,1)} async-done(((bf16[684,512]{1,0:T(8,128)(2,1)}), bf16[684,2048]{1,0:T(8,128)(2,1)}) %all-gather.8.cloned.1.call-update) | async-done | bytes 2801680 | tf_op jit(solution)/shard_map/all_gather | solution.py:364
  260.7 4.0 fusion.139
  264.9 5.6 fusion.43
  279.1 8.1 %collective-permute-done.41 = bf16[128,2048]{1,0:T(8,128)(2,1)S(1)} collective-permute-done((bf16[128,2048]{1,0:T(8,128)(2,1)S(1)}, bf16[128,2048]{1,0:T(8,128)(2,1)S(1)}, u32[]{:S(2)}, u32[]{:S(2)}) %collective-permute-start.41) | collective-permute-done | bytes 524320 | tf_op jit(solution)/shard_map/ppermute | solution.py:190
  290.6 9.4 %collective-permute-done.40 = bf16[128,2048]{1,0:T(8,128)(2,1)S(1)} collective-permute-done((bf16[128,2048]{1,0:T(8,128)(2,1)S(1)}, bf16[128,2048]{1,0:T(8,128)(2,1)S(1)}, u32[]{:S(2)}, u32[]{:S(2)}) %collective-permute-start.40) | collective-permute-done | bytes 524320 | tf_op jit(solution)/shard_map/ppermute | solution.py:190
  299.9 10.1 %collective-permute-done.42 = bf16[128,2048]{1,0:T(8,128)(2,1)S(1)} collective-permute-done((bf16[128,2048]{1,0:T(8,128)(2,1)S(1)}, bf16[128,2048]{1,0:T(8,128)(2,1)S(1)}, u32[]{:S(2)}, u32[]{:S(2)}) %collective-permute-start.42) | collective-permute-done | bytes 524320 | tf_op jit(solution)/shard_map/ppermute | solution.py:190
  318.2 4.6 fusion.148
  322.9 3.7 convolution_bitcast_fusion.3
  326.6 14.6 %collective-permute-done.44 = bf16[256,2048]{1,0:T(8,128)(2,1)S(1)} collective-permute-done((bf16[256,2048]{1,0:T(8,128)(2,1)S(1)}, bf16[256,2048]{1,0:T(8,128)(2,1)S(1)}, u32[]{:S(2)}, u32[]{:S(2)}) %collective-permute-start.44) | collective-permute-done | bytes 1048608 | tf_op jit(solution)/shard_map/ppermute | solution.py:190
  345.5 4.6 fusion.147
  350.1 4.1 convolution_bitcast_fusion.2
  364.2 7.4 %fusion.187 = bf16[684,2048]{1,0:T(8,128)(2,1)} fusion(bf16[2048,684]{0,1:T(8,128)(2,1)S(1)} %copy-done.18, bf16[2048,2048]{1,0:T(8,128)(2,1)S(1)} %constant_dynamic-update-slice_fusion.20), kind=kOutput, calls=%fused_computation.324 | convolution fusion | flops 5737807872 | bytes 13991936 | tf_op jit(solution)/shard_map/tf,td->fd/dot_general | solution.py:427
  375.0 5.2 fusion.146
  380.2 3.7 convolution_bitcast_fusion.1
  393.6 5.3 fusion.145
  398.9 3.9 convolution_bitcast_fusion
  414.4 14.0 %fusion = bf16[2,684,2048]{2,1,0:T(8,128)(2,1)} fusion(bf16[2048,2048]{1,0:T(8,128)(2,1)S(1)} %bitcast.262, bf16[1,512,684]{1,2,0:T(8,128)(2,1)S(1)} %copy-done.52, bf16[1,512,684]{1,2,0:T(8,128)(2,1)S(1)} %copy-done.50, bf16[1,512,684]{1,2,0:T(8,128)(2,1)S(1)} %copy-done.56, bf16[1,512,684]{1,2,0:T(8,128)(2,1)S(1)} %copy-done.54, ...), kind=kOutput, calls=%fused_computation.1 | convolution fusion | flops 11520442368 | bytes 19595264 | tf_op jit(solution)/shard_map/ctf,td->cfd/dot_general | solution.py:432
  428.4 4.6 collective-permute-done.57
  433.0 3.6 collective-permute-done.61
  440.2 5.6 multiply_reduce_fusion
  452.1 5.0 multiply_subtract_fusion
  457.1 16.1 %collective-permute-done.63 = bf16[256,2048]{1,0:T(8,128)(2,1)S(1)} collective-permute-done((bf16[256,2048]{1,0:T(8,128)(2,1)}, bf16[256,2048]{1,0:T(8,128)(2,1)S(1)}, u32[]{:S(2)}, u32[]{:S(2)}) %collective-permute-start.63) | collective-permute-done | bytes 1048608 | tf_op jit(solution)/shard_map/ppermute | solution.py:190
  478.5 10.3 %collective-permute-done.67 = bf16[128,2048]{1,0:T(8,128)(2,1)S(1)} collective-permute-done((bf16[128,2048]{1,0:T(8,128)(2,1)S(1)}, bf16[128,2048]{1,0:T(8,128)(2,1)S(1)}, u32[]{:S(2)}, u32[]{:S(2)}) %collective-permute-start.67) | collective-permute-done | bytes 524320 | tf_op jit(solution)/shard_map/ppermute | solution.py:190
  492.1 5.4 fusion.130.grad_ref
  497.4 14.2 %attend_backward.1 = bf16[2048,768]{1,0:T(8,128)(2,1)} custom-call(s32[4]{0:T(128)} %objective_ref.3, s32[4]{0:T(128)} %prefix_ref.3, s32[2]{0:T(128)} %pad_add_fusion.place_ref, bf16[2048,256]{1,0:T(8,128)(2,1)} %get-tuple-element.94.query_ref, bf16[2048,256]{1,0:T(8,128)(2,1)} %get-tuple-element.95.key_ref, bf16[2048,256]{1,0:T(8,128)(2,1)} %get-tuple-element.96.value_ref, ...), custom_call_target="tpu_custom_call" | custom-call | tf_op jit(solution)/shard_map/attend_backward/pallas_call | solution.py:150
  511.6 5.9 fusion.188
  517.5 9.5 %fusion.189 = bf16[768,2048]{1,0:T(8,128)(2,1)S(1)} fusion(bf16[2048,768]{1,0:T(8,128)(2,1)S(1)} %copy-done.16, bf16[2048,2048]{1,0:T(8,128)(2,1)} %constant_dynamic-update-slice_fusion), kind=kOutput, calls=%fused_computation.326 | convolution fusion | flops 6442450944 | bytes 14680064 | tf_op jit(solution)/shard_map/te,td->ed/dot_general | solution.py:467
  530.4 5.2 fusion.38
  535.6 5.3 fusion.36
  557.1 16.5 %fusion.162 = (f32[512,2,684]{0,1,2:T(2,128)}, f32[512,2,684]{0,1,2:T(2,128)}, f32[512,2,684]{0,1,2:T(2,128)}) fusion(f32[]{:T(128)S(6)} %div.99, bf16[2,684,512]{2,1,0:T(8,128)(2,1)S(1)} %copy-done.25, f32[512,2,684]{0,1,2:T(2,128)S(1)} %copy-done.19, f32[512,2,684]{0,1,2:T(2,128)S(1)} %copy-done.20, f32[512,2,684]{0,1,2:T(2,128)S(1)} %copy-done.5), kind=kLoop, calls=%fused_computation.312 | loop fusion | flops 11206656 | bytes 18210820 | tf_op jit(solution)/shard_map/transpose | solution.py:313
  573.6 3.9 collective-permute-done.75
  579.1 11.7 %collective-permute-done.76 = bf16[128,2048]{1,0:T(8,128)(2,1)S(1)} collective-permute-done((bf16[128,2048]{1,0:T(8,128)(2,1)S(1)}, bf16[128,2048]{1,0:T(8,128)(2,1)S(1)}, u32[]{:S(2)}, u32[]{:S(2)}) %collective-permute-start.76) | collective-permute-done | bytes 524320 | tf_op jit(solution)/shard_map/ppermute | solution.py:190
  603.2 6.6 %collective-permute-done.84 = f32[4,2048]{1,0:T(4,128)S(1)} collective-permute-done((f32[4,2048]{1,0:T(4,128)S(1)}, f32[4,2048]{1,0:T(4,128)S(1)}, u32[]{:S(2)}, u32[]{:S(2)}) %collective-permute-start.84) | collective-permute-done | bytes 32800 | tf_op jit(solution)/shard_map/ppermute | solution.py:190
  611.5 5.2 collective-permute-done.85
  617.4 5.6 reduce-scatter.8.cloned.1.call-done
  624.5 5.4 fusion.136
  (439 shorter events, 209.5 us)
Async XLA Ops:
  7.2 89.8 %all-gather.4.cloned.1.call-start = ((), (), s32[]{:S(2)}) async-start(), calls=%async_computation.3 | async-start | bytes 5242880 | tf_op jit(solution)/shard_map/all_gather | solution.py:357
  13.2 204.4 %all-gather.6.cloned.1.call-start = ((), (), s32[]{:S(2)}) async-start(), calls=%async_computation.4 | async-start | bytes 7045120 | tf_op jit(solution)/shard_map/all_gather | solution.py:363
  13.3 29.0 %collective-permute-start.1 = (bf16[256,2048]{1,0:T(8,128)(2,1)}, bf16[256,2048]{1,0:T(8,128)(2,1)}, u32[]{:S(2)}, u32[]{:S(2)}) collective-permute-start(bf16[256,2048]{1,0:T(8,128)(2,1)} %param.20), channel_id=1, source_target_pairs={{0,2},{1,3},{2,0},{3,1},{4,6},{5,7},{6,4},{7,5},{8,10},{9,11},{10,... | collective-permute-start | bytes 3145736 | tf_op jit(solution)/shard_map/ppermute | solution.py:190
  16.3 41.9 %collective-permute-start = (bf16[256,2048]{1,0:T(8,128)(2,1)}, bf16[256,2048]{1,0:T(8,128)(2,1)}, u32[]{:S(2)}, u32[]{:S(2)}) collective-permute-start(bf16[256,2048]{1,0:T(8,128)(2,1)} %param.20), channel_id=1, source_target_pairs={{0,1},{1,0},{2,3},{3,2},{4,5},{5,4},{6,7},{7,6},{8,9},{9,8},{10,11... | collective-permute-start | bytes 3145736 | tf_op jit(solution)/shard_map/ppermute | solution.py:190
  16.3 38.0 %collective-permute-start.3 = (bf16[256,2048]{1,0:T(8,128)(2,1)}, bf16[256,2048]{1,0:T(8,128)(2,1)}, u32[]{:S(2)}, u32[]{:S(2)}) collective-permute-start(bf16[256,2048]{1,0:T(8,128)(2,1)} %param.20), channel_id=1, source_target_pairs={{0,4},{1,5},{2,6},{3,7},{4,0},{5,1},{6,2},{7,3},{8,12},{9,13},{10,... | collective-permute-start | bytes 3145736 | tf_op jit(solution)/shard_map/ppermute | solution.py:190
  21.7 239.0 %all-gather.8.cloned.1.call-start = ((), (), s32[]{:S(2)}) async-start(), calls=%async_computation.5 | async-start | bytes 3522560 | tf_op jit(solution)/shard_map/all_gather | solution.py:364
  23.5 16.3 %collective-permute-start.10 = (f32[8,128]{1,0:T(8,128)S(1)}, f32[8,128]{1,0:T(8,128)S(1)}, u32[]{:S(2)}, u32[]{:S(2)}) collective-permute-start(f32[8,128]{1,0:T(8,128)S(1)} %broadcast_add_fusion), channel_id=1, source_target_pairs={{0,2},{1,3},{2,0},{3,1},{4,6},{5,7},{6,4},{7,5},{8,10},{9,11},{10,... | collective-permute-start | bytes 12296 | tf_op jit(solution)/shard_map/ppermute | solution.py:190
  42.3 24.2 %collective-permute-start.2 = (bf16[256,2048]{1,0:T(8,128)(2,1)}, bf16[256,2048]{1,0:T(8,128)(2,1)S(1)}, u32[]{:S(2)}, u32[]{:S(2)}) collective-permute-start(bf16[256,2048]{1,0:T(8,128)(2,1)} %collective-permute-done.1), channel_id=1, source_target_pairs={{0,1},{1,0},{2,3},{3,2},{4,5},{5,4},{6,7},{7,6},{8,9},{9,8},{10,11... | collective-permute-start | bytes 3145736 | tf_op jit(solution)/shard_map/ppermute | solution.py:190
  125.2 19.9 %collective-permute-start.14 = (bf16[256,2048]{1,0:T(8,128)(2,1)S(1)}, bf16[256,2048]{1,0:T(8,128)(2,1)S(1)}, u32[]{:S(2)}, u32[]{:S(2)}) collective-permute-start(bf16[256,2048]{1,0:T(8,128)(2,1)S(1)} %get-tuple-element.168), channel_id=1, source_target_pairs={{0,1},{1,0},{2,3},{3,2},{4,5},{5,4},{6,7},{7,6},{8,9},{9,8},{10,11... | collective-permute-start | bytes 3145736 | tf_op jit(solution)/shard_map/ppermute | solution.py:190
  126.2 14.9 %collective-permute-start.22 = (bf16[128,2048]{1,0:T(8,128)(2,1)S(1)}, bf16[128,2048]{1,0:T(8,128)(2,1)S(1)}, u32[]{:S(2)}, u32[]{:S(2)}) collective-permute-start(bf16[128,2048]{1,0:T(8,128)(2,1)S(1)} %get-tuple-element.187), channel_id=1, source_target_pairs={{0,2},{1,3},{2,0},{3,1},{4,6},{5,7},{6,4},{7,5},{8,10},{9,11},{10,... | collective-permute-start | bytes 1572872 | tf_op jit(solution)/shard_map/ppermute | solution.py:190
  127.8 15.0 %collective-permute-start.17 = (bf16[128,2048]{1,0:T(8,128)(2,1)S(1)}, bf16[128,2048]{1,0:T(8,128)(2,1)S(1)}, u32[]{:S(2)}, u32[]{:S(2)}) collective-permute-start(bf16[128,2048]{1,0:T(8,128)(2,1)S(1)} %get-tuple-element.186), channel_id=1, source_target_pairs={{0,4},{1,5},{2,6},{3,7},{4,0},{5,1},{6,2},{7,3},{8,12},{9,13},{10,... | collective-permute-start | bytes 1572872 | tf_op jit(solution)/shard_map/ppermute | solution.py:190
  130.2 23.6 %collective-permute-start.21 = (bf16[128,2048]{1,0:T(8,128)(2,1)S(1)}, bf16[128,2048]{1,0:T(8,128)(2,1)S(1)}, u32[]{:S(2)}, u32[]{:S(2)}) collective-permute-start(bf16[128,2048]{1,0:T(8,128)(2,1)S(1)} %slice.614), channel_id=1, source_target_pairs={{0,4},{1,5},{2,6},{3,7},{4,0},{5,1},{6,2},{7,3},{8,12},{9,13},{10,... | collective-permute-start | bytes 1572872 | tf_op jit(solution)/shard_map/ppermute | solution.py:190
  131.6 22.3 %collective-permute-start.19 = (bf16[128,2048]{1,0:T(8,128)(2,1)S(1)}, bf16[128,2048]{1,0:T(8,128)(2,1)S(1)}, u32[]{:S(2)}, u32[]{:S(2)}) collective-permute-start(bf16[128,2048]{1,0:T(8,128)(2,1)S(1)} %slice.615), channel_id=1, source_target_pairs={{0,2},{1,3},{2,0},{3,1},{4,6},{5,7},{6,4},{7,5},{8,10},{9,11},{10,... | collective-permute-start | bytes 1572872 | tf_op jit(solution)/shard_map/ppermute | solution.py:190
  141.2 22.7 %collective-permute-start.23 = (bf16[128,2048]{1,0:T(8,128)(2,1)S(1)}, bf16[128,2048]{1,0:T(8,128)(2,1)S(1)}, u32[]{:S(2)}, u32[]{:S(2)}) collective-permute-start(bf16[128,2048]{1,0:T(8,128)(2,1)S(1)} %fusion.127), channel_id=1, source_target_pairs={{0,4},{1,5},{2,6},{3,7},{4,0},{5,1},{6,2},{7,3},{8,12},{9,13},{10,... | collective-permute-start | bytes 1572872 | tf_op jit(solution)/shard_map/ppermute | solution.py:190
  143.0 20.9 %collective-permute-start.18 = (bf16[128,2048]{1,0:T(8,128)(2,1)S(1)}, bf16[128,2048]{1,0:T(8,128)(2,1)S(1)}, u32[]{:S(2)}, u32[]{:S(2)}) collective-permute-start(bf16[128,2048]{1,0:T(8,128)(2,1)S(1)} %fusion.128), channel_id=1, source_target_pairs={{0,2},{1,3},{2,0},{3,1},{4,6},{5,7},{6,4},{7,5},{8,10},{9,11},{10,... | collective-permute-start | bytes 1572872 | tf_op jit(solution)/shard_map/ppermute | solution.py:190
  167.0 24.4 %collective-permute-start.25 = (bf16[256,2048]{1,0:T(8,128)(2,1)}, bf16[256,2048]{1,0:T(8,128)(2,1)}, u32[]{:S(2)}, u32[]{:S(2)}) collective-permute-start(bf16[256,2048]{1,0:T(8,128)(2,1)} %get-tuple-element.147), channel_id=1, source_target_pairs={{0,2},{1,3},{2,0},{3,1},{4,6},{5,7},{6,4},{7,5},{8,10},{9,11},{10,... | collective-permute-start | bytes 3145736 | tf_op jit(solution)/shard_map/ppermute | solution.py:190
  167.5 28.0 %collective-permute-start.27 = (bf16[256,2048]{1,0:T(8,128)(2,1)}, bf16[256,2048]{1,0:T(8,128)(2,1)S(1)}, u32[]{:S(2)}, u32[]{:S(2)}) collective-permute-start(bf16[256,2048]{1,0:T(8,128)(2,1)} %get-tuple-element.147), channel_id=1, source_target_pairs={{0,4},{1,5},{2,6},{3,7},{4,0},{5,1},{6,2},{7,3},{8,12},{9,13},{10,... | collective-permute-start | bytes 3145736 | tf_op jit(solution)/shard_map/ppermute | solution.py:190
  169.1 27.1 %collective-permute-start.24 = (bf16[256,2048]{1,0:T(8,128)(2,1)}, bf16[256,2048]{1,0:T(8,128)(2,1)}, u32[]{:S(2)}, u32[]{:S(2)}) collective-permute-start(bf16[256,2048]{1,0:T(8,128)(2,1)} %get-tuple-element.147), channel_id=1, source_target_pairs={{0,1},{1,0},{2,3},{3,2},{4,5},{5,4},{6,7},{7,6},{8,9},{9,8},{10,11... | collective-permute-start | bytes 3145736 | tf_op jit(solution)/shard_map/ppermute | solution.py:190
  191.4 18.3 %collective-permute-start.26 = (bf16[256,2048]{1,0:T(8,128)(2,1)}, bf16[256,2048]{1,0:T(8,128)(2,1)}, u32[]{:S(2)}, u32[]{:S(2)}) collective-permute-start(bf16[256,2048]{1,0:T(8,128)(2,1)} %collective-permute-done.25), channel_id=1, source_target_pairs={{0,1},{1,0},{2,3},{3,2},{4,5},{5,4},{6,7},{7,6},{8,9},{9,8},{10,11... | collective-permute-start | bytes 3145736 | tf_op jit(solution)/shard_map/ppermute | solution.py:190
  192.4 247.7 %reduce-scatter.4.cloned.1.call-start = ((), (), s32[]{:S(2)}) async-start(), calls=%async_computation.6 | async-start | bytes 3522560 | tf_op jit(solution)/shard_map/reduce_scatter | solution.py:429
  193.9 14.4 %collective-permute-start.29 = (bf16[128,2048]{1,0:T(8,128)(2,1)S(1)}, bf16[128,2048]{1,0:T(8,128)(2,1)S(1)}, u32[]{:S(2)}, u32[]{:S(2)}) collective-permute-start(bf16[128,2048]{1,0:T(8,128)(2,1)S(1)} %slice.390), channel_id=1, source_target_pairs={{0,4},{1,5},{2,6},{3,7},{4,0},{5,1},{6,2},{7,3},{8,12},{9,13},{10,... | collective-permute-start | bytes 1572872 | tf_op jit(solution)/shard_map/ppermute | solution.py:190
  196.2 17.0 %collective-permute-start.28 = (bf16[256,2048]{1,0:T(8,128)(2,1)S(1)}, bf16[256,2048]{1,0:T(8,128)(2,1)S(1)}, u32[]{:S(2)}, u32[]{:S(2)}) collective-permute-start(bf16[256,2048]{1,0:T(8,128)(2,1)S(1)} %collective-permute-done.27), channel_id=1, source_target_pairs={{0,1},{1,0},{2,3},{3,2},{4,5},{5,4},{6,7},{7,6},{8,9},{9,8},{10,11... | collective-permute-start | bytes 3145736 | tf_op jit(solution)/shard_map/ppermute | solution.py:190
  271.4 19.1 %collective-permute-start.33 = (bf16[256,2048]{1,0:T(8,128)(2,1)S(1)}, bf16[256,2048]{1,0:T(8,128)(2,1)S(1)}, u32[]{:S(2)}, u32[]{:S(2)}) collective-permute-start(bf16[256,2048]{1,0:T(8,128)(2,1)S(1)} %get-tuple-element.163), channel_id=1, source_target_pairs={{0,1},{1,0},{2,3},{3,2},{4,5},{5,4},{6,7},{7,6},{8,9},{9,8},{10,11... | collective-permute-start | bytes 3145736 | tf_op jit(solution)/shard_map/ppermute | solution.py:190
  272.4 14.9 %collective-permute-start.41 = (bf16[128,2048]{1,0:T(8,128)(2,1)S(1)}, bf16[128,2048]{1,0:T(8,128)(2,1)S(1)}, u32[]{:S(2)}, u32[]{:S(2)}) collective-permute-start(bf16[128,2048]{1,0:T(8,128)(2,1)S(1)} %get-tuple-element.185), channel_id=1, source_target_pairs={{0,2},{1,3},{2,0},{3,1},{4,6},{5,7},{6,4},{7,5},{8,10},{9,11},{10,... | collective-permute-start | bytes 1572872 | tf_op jit(solution)/shard_map/ppermute | solution.py:190
  273.9 15.0 %collective-permute-start.36 = (bf16[128,2048]{1,0:T(8,128)(2,1)S(1)}, bf16[128,2048]{1,0:T(8,128)(2,1)S(1)}, u32[]{:S(2)}, u32[]{:S(2)}) collective-permute-start(bf16[128,2048]{1,0:T(8,128)(2,1)S(1)} %get-tuple-element.184), channel_id=1, source_target_pairs={{0,4},{1,5},{2,6},{3,7},{4,0},{5,1},{6,2},{7,3},{8,12},{9,13},{10,... | collective-permute-start | bytes 1572872 | tf_op jit(solution)/shard_map/ppermute | solution.py:190
  276.2 23.7 %collective-permute-start.40 = (bf16[128,2048]{1,0:T(8,128)(2,1)S(1)}, bf16[128,2048]{1,0:T(8,128)(2,1)S(1)}, u32[]{:S(2)}, u32[]{:S(2)}) collective-permute-start(bf16[128,2048]{1,0:T(8,128)(2,1)S(1)} %slice.612), channel_id=1, source_target_pairs={{0,4},{1,5},{2,6},{3,7},{4,0},{5,1},{6,2},{7,3},{8,12},{9,13},{10,... | collective-permute-start | bytes 1572872 | tf_op jit(solution)/shard_map/ppermute | solution.py:190
  277.6 22.3 %collective-permute-start.38 = (bf16[128,2048]{1,0:T(8,128)(2,1)S(1)}, bf16[128,2048]{1,0:T(8,128)(2,1)S(1)}, u32[]{:S(2)}, u32[]{:S(2)}) collective-permute-start(bf16[128,2048]{1,0:T(8,128)(2,1)S(1)} %slice.613), channel_id=1, source_target_pairs={{0,2},{1,3},{2,0},{3,1},{4,6},{5,7},{6,4},{7,5},{8,10},{9,11},{10,... | collective-permute-start | bytes 1572872 | tf_op jit(solution)/shard_map/ppermute | solution.py:190
  287.4 22.6 %collective-permute-start.42 = (bf16[128,2048]{1,0:T(8,128)(2,1)S(1)}, bf16[128,2048]{1,0:T(8,128)(2,1)S(1)}, u32[]{:S(2)}, u32[]{:S(2)}) collective-permute-start(bf16[128,2048]{1,0:T(8,128)(2,1)S(1)} %fusion.125), channel_id=1, source_target_pairs={{0,4},{1,5},{2,6},{3,7},{4,0},{5,1},{6,2},{7,3},{8,12},{9,13},{10,... | collective-permute-start | bytes 1572872 | tf_op jit(solution)/shard_map/ppermute | solution.py:190
  289.0 21.0 %collective-permute-start.37 = (bf16[128,2048]{1,0:T(8,128)(2,1)S(1)}, bf16[128,2048]{1,0:T(8,128)(2,1)S(1)}, u32[]{:S(2)}, u32[]{:S(2)}) collective-permute-start(bf16[128,2048]{1,0:T(8,128)(2,1)S(1)} %fusion.126), channel_id=1, source_target_pairs={{0,2},{1,3},{2,0},{3,1},{4,6},{5,7},{6,4},{7,5},{8,10},{9,11},{10,... | collective-permute-start | bytes 1572872 | tf_op jit(solution)/shard_map/ppermute | solution.py:190
  315.6 25.6 %collective-permute-start.44 = (bf16[256,2048]{1,0:T(8,128)(2,1)S(1)}, bf16[256,2048]{1,0:T(8,128)(2,1)S(1)}, u32[]{:S(2)}, u32[]{:S(2)}) collective-permute-start(bf16[256,2048]{1,0:T(8,128)(2,1)S(1)} %get-tuple-element.143), channel_id=1, source_target_pairs={{0,2},{1,3},{2,0},{3,1},{4,6},{5,7},{6,4},{7,5},{8,10},{9,11},{10,... | collective-permute-start | bytes 3145736 | tf_op jit(solution)/shard_map/ppermute | solution.py:190
  316.2 25.2 %collective-permute-start.45 = (bf16[256,2048]{1,0:T(8,128)(2,1)S(1)}, bf16[256,2048]{1,0:T(8,128)(2,1)S(1)}, u32[]{:S(2)}, u32[]{:S(2)}) collective-permute-start(bf16[256,2048]{1,0:T(8,128)(2,1)S(1)} %get-tuple-element.143), channel_id=1, source_target_pairs={{0,4},{1,5},{2,6},{3,7},{4,0},{5,1},{6,2},{7,3},{8,12},{9,13},{10,... | collective-permute-start | bytes 3145736 | tf_op jit(solution)/shard_map/ppermute | solution.py:190
  341.5 19.2 %collective-permute-start.47 = (bf16[256,2048]{1,0:T(8,128)(2,1)S(1)}, bf16[256,2048]{1,0:T(8,128)(2,1)S(1)}, u32[]{:S(2)}, u32[]{:S(2)}) collective-permute-start(bf16[256,2048]{1,0:T(8,128)(2,1)S(1)} %collective-permute-done.45), channel_id=1, source_target_pairs={{0,1},{1,0},{2,3},{3,2},{4,5},{5,4},{6,7},{7,6},{8,9},{9,8},{10,11... | collective-permute-start | bytes 3145736 | tf_op jit(solution)/shard_map/ppermute | solution.py:190
  386.8 157.9 %reduce-scatter.6.cloned.1.call-start = ((), (), s32[]{:S(2)}) async-start(), calls=%async_computation.7 | async-start | bytes 7045120 | tf_op jit(solution)/shard_map/reduce_scatter | solution.py:457
  407.2 21.3 %collective-permute-start.58 = (bf16[128,2048]{1,0:T(8,128)(2,1)}, bf16[128,2048]{1,0:T(8,128)(2,1)}, u32[]{:S(2)}, u32[]{:S(2)}) collective-permute-start(bf16[128,2048]{1,0:T(8,128)(2,1)} %slice.611), channel_id=1, source_target_pairs={{0,2},{1,3},{2,0},{3,1},{4,6},{5,7},{6,4},{7,5},{8,10},{9,11},{10,... | collective-permute-start | bytes 1572872 | tf_op jit(solution)/shard_map/ppermute | solution.py:190
  409.5 23.6 %collective-permute-start.57 = (bf16[128,2048]{1,0:T(8,128)(2,1)}, bf16[128,2048]{1,0:T(8,128)(2,1)}, u32[]{:S(2)}, u32[]{:S(2)}) collective-permute-start(bf16[128,2048]{1,0:T(8,128)(2,1)} %add_convert_fusion.5), channel_id=1, source_target_pairs={{0,2},{1,3},{2,0},{3,1},{4,6},{5,7},{6,4},{7,5},{8,10},{9,11},{10,... | collective-permute-start | bytes 1572872 | tf_op jit(solution)/shard_map/ppermute | solution.py:190
  411.4 21.7 %collective-permute-start.60 = (bf16[128,2048]{1,0:T(8,128)(2,1)}, bf16[128,2048]{1,0:T(8,128)(2,1)}, u32[]{:S(2)}, u32[]{:S(2)}) collective-permute-start(bf16[128,2048]{1,0:T(8,128)(2,1)} %slice.610), channel_id=1, source_target_pairs={{0,4},{1,5},{2,6},{3,7},{4,0},{5,1},{6,2},{7,3},{8,12},{9,13},{10,... | collective-permute-start | bytes 1572872 | tf_op jit(solution)/shard_map/ppermute | solution.py:190
  413.9 22.7 %collective-permute-start.61 = (bf16[128,2048]{1,0:T(8,128)(2,1)}, bf16[128,2048]{1,0:T(8,128)(2,1)}, u32[]{:S(2)}, u32[]{:S(2)}) collective-permute-start(bf16[128,2048]{1,0:T(8,128)(2,1)} %fusion.124), channel_id=1, source_target_pairs={{0,4},{1,5},{2,6},{3,7},{4,0},{5,1},{6,2},{7,3},{8,12},{9,13},{10,... | collective-permute-start | bytes 1572872 | tf_op jit(solution)/shard_map/ppermute | solution.py:190
  440.1 182.9 %reduce-scatter.8.cloned.1.call-start = ((), (), s32[]{:S(2)}) async-start(), calls=%async_computation.8 | async-start | bytes 5242880 | tf_op jit(solution)/shard_map/reduce_scatter | solution.py:474
  448.7 24.4 %collective-permute-start.63 = (bf16[256,2048]{1,0:T(8,128)(2,1)}, bf16[256,2048]{1,0:T(8,128)(2,1)S(1)}, u32[]{:S(2)}, u32[]{:S(2)}) collective-permute-start(bf16[256,2048]{1,0:T(8,128)(2,1)} %get-tuple-element.139), channel_id=1, source_target_pairs={{0,2},{1,3},{2,0},{3,1},{4,6},{5,7},{6,4},{7,5},{8,10},{9,11},{10,... | collective-permute-start | bytes 3145736 | tf_op jit(solution)/shard_map/ppermute | solution.py:190
  449.9 24.4 %collective-permute-start.64 = (bf16[256,2048]{1,0:T(8,128)(2,1)}, bf16[256,2048]{1,0:T(8,128)(2,1)S(1)}, u32[]{:S(2)}, u32[]{:S(2)}) collective-permute-start(bf16[256,2048]{1,0:T(8,128)(2,1)} %get-tuple-element.139), channel_id=1, source_target_pairs={{0,4},{1,5},{2,6},{3,7},{4,0},{5,1},{6,2},{7,3},{8,12},{9,13},{10,... | collective-permute-start | bytes 3145736 | tf_op jit(solution)/shard_map/ppermute | solution.py:190
  451.4 25.7 %collective-permute-start.62 = (bf16[256,2048]{1,0:T(8,128)(2,1)}, bf16[256,2048]{1,0:T(8,128)(2,1)}, u32[]{:S(2)}, u32[]{:S(2)}) collective-permute-start(bf16[256,2048]{1,0:T(8,128)(2,1)} %get-tuple-element.139), channel_id=1, source_target_pairs={{0,1},{1,0},{2,3},{3,2},{4,5},{5,4},{6,7},{7,6},{8,9},{9,8},{10,11... | collective-permute-start | bytes 3145736 | tf_op jit(solution)/shard_map/ppermute | solution.py:190
  474.3 15.8 %collective-permute-start.65 = (bf16[256,2048]{1,0:T(8,128)(2,1)S(1)}, bf16[256,2048]{1,0:T(8,128)(2,1)S(1)}, u32[]{:S(2)}, u32[]{:S(2)}) collective-permute-start(bf16[256,2048]{1,0:T(8,128)(2,1)S(1)} %collective-permute-done.63), channel_id=1, source_target_pairs={{0,1},{1,0},{2,3},{3,2},{4,5},{5,4},{6,7},{7,6},{8,9},{9,8},{10,11... | collective-permute-start | bytes 3145736 | tf_op jit(solution)/shard_map/ppermute | solution.py:190
  474.3 15.9 %collective-permute-start.66 = (bf16[256,2048]{1,0:T(8,128)(2,1)S(1)}, bf16[256,2048]{1,0:T(8,128)(2,1)S(1)}, u32[]{:S(2)}, u32[]{:S(2)}) collective-permute-start(bf16[256,2048]{1,0:T(8,128)(2,1)S(1)} %collective-permute-done.64), channel_id=1, source_target_pairs={{0,1},{1,0},{2,3},{3,2},{4,5},{5,4},{6,7},{7,6},{8,9},{9,8},{10,11... | collective-permute-start | bytes 3145736 | tf_op jit(solution)/shard_map/ppermute | solution.py:190
  546.5 32.6 %collective-permute-start.71 = (bf16[256,2048]{1,0:T(8,128)(2,1)S(1)}, bf16[256,2048]{1,0:T(8,128)(2,1)S(1)}, u32[]{:S(2)}, u32[]{:S(2)}) collective-permute-start(bf16[256,2048]{1,0:T(8,128)(2,1)S(1)} %get-tuple-element.162), channel_id=1, source_target_pairs={{0,1},{1,0},{2,3},{3,2},{4,5},{5,4},{6,7},{7,6},{8,9},{9,8},{10,11... | collective-permute-start | bytes 3145736 | tf_op jit(solution)/shard_map/ppermute | solution.py:190
  552.3 26.8 %collective-permute-start.77 = (bf16[128,2048]{1,0:T(8,128)(2,1)S(1)}, bf16[128,2048]{1,0:T(8,128)(2,1)S(1)}, u32[]{:S(2)}, u32[]{:S(2)}) collective-permute-start(bf16[128,2048]{1,0:T(8,128)(2,1)S(1)} %slice.609), channel_id=1, source_target_pairs={{0,2},{1,3},{2,0},{3,1},{4,6},{5,7},{6,4},{7,5},{8,10},{9,11},{10,... | collective-permute-start | bytes 1572872 | tf_op jit(solution)/shard_map/ppermute | solution.py:190
  553.0 20.6 %collective-permute-start.74 = (bf16[128,2048]{1,0:T(8,128)(2,1)S(1)}, bf16[128,2048]{1,0:T(8,128)(2,1)S(1)}, u32[]{:S(2)}, u32[]{:S(2)}) collective-permute-start(bf16[128,2048]{1,0:T(8,128)(2,1)S(1)} %get-tuple-element.181), channel_id=1, source_target_pairs={{0,4},{1,5},{2,6},{3,7},{4,0},{5,1},{6,2},{7,3},{8,12},{9,13},{10,... | collective-permute-start | bytes 1572872 | tf_op jit(solution)/shard_map/ppermute | solution.py:190
  554.0 23.5 %collective-permute-start.75 = (bf16[128,2048]{1,0:T(8,128)(2,1)S(1)}, bf16[128,2048]{1,0:T(8,128)(2,1)S(1)}, u32[]{:S(2)}, u32[]{:S(2)}) collective-permute-start(bf16[128,2048]{1,0:T(8,128)(2,1)S(1)} %get-tuple-element.180), channel_id=1, source_target_pairs={{0,2},{1,3},{2,0},{3,1},{4,6},{5,7},{6,4},{7,5},{8,10},{9,11},{10,... | collective-permute-start | bytes 1572872 | tf_op jit(solution)/shard_map/ppermute | solution.py:190
  555.6 23.5 %collective-permute-start.79 = (bf16[128,2048]{1,0:T(8,128)(2,1)S(1)}, bf16[128,2048]{1,0:T(8,128)(2,1)S(1)}, u32[]{:S(2)}, u32[]{:S(2)}) collective-permute-start(bf16[128,2048]{1,0:T(8,128)(2,1)S(1)} %slice.608), channel_id=1, source_target_pairs={{0,4},{1,5},{2,6},{3,7},{4,0},{5,1},{6,2},{7,3},{8,12},{9,13},{10,... | collective-permute-start | bytes 1572872 | tf_op jit(solution)/shard_map/ppermute | solution.py:190
  (109 other events, 738.9 us)
Sparse Core Ops, SparseCore 0:
  13.3 83.5 all-gather.3
  99.1 103.0 all-gather.5
  204.4 56.2 all-gather.7
  386.9 53.0 reduce-scatter.3
  442.2 99.8 reduce-scatter.5
  544.9 78.1 reduce-scatter.7

commit v9 on v8

--- a/solution.py
+++ b/solution.py
@@ -257,10 +257,11 @@
 
 
 def scatter_beside(own, near_x, rows, product, last):
+    far = product(rows, 3)
+    rows, far = lax.optimization_barrier((rows, far))
+    far = core_sum(far).astype(jnp.bfloat16)
     own, near_x = core_sum(own), core_sum(near_x)
-    rows, own, near_x = lax.optimization_barrier((rows, own, near_x))
-    far = core_sum(product(rows, 3)).astype(jnp.bfloat16)
-    rows, far = lax.optimization_barrier((rows, far))
+    rows, far, own, near_x = lax.optimization_barrier((rows, far, own, near_x))
     half = far.shape[0] // 2
     far_low, far_high = swap(far[:half], "mp", 4), swap(far[half:], "mp", 2)
     near_y, far_low, far_high = lax.optimization_barrier((product(rows, 2), far_low, far_high))

time: 645 us -> 647 us (level)
    unnamed x164 -> x162, local copies, waits for them, and re-layouts: 43.6 us -> 44.6 us
  transfers between devices with their start and end apart: 92 -> 92, of which waited for: 44 -> 44; matrix products, arithmetic and copies ran while one was open for 35% -> 37% of each run, Pallas kernels for 4% -> 4%
where the time goes in v9:
time: 647 us; the launch traced here: 642 us
  waiting for transfers between devices  254 us (39%)
  matrix products  134 us (21%)
  other arithmetic  81.5 us (13%)
  starting transfers between devices  68.5 us (11%)
  local copies, waits for them, and re-layouts  62.8 us (10%)
  Pallas kernels  24.1 us (4%)
  between operations  16.8 us (3%)
    ppermute x86, waiting for transfers between devices, swap(): return lax.ppermute(values, axis, [(at, at ^ bit) for at in range(size)])  203 us
    ppermute x86, starting transfers between devices, swap(): return lax.ppermute(values, axis, [(at, at ^ bit) for at in range(size)])  67.9 us
    unnamed x162, local copies, waits for them, and re-layouts  44.6 us
    all_gather x1, waiting for transfers between devices, local(): attend_full = lax.all_gather(attend_low, 'dp', axis=0, tiled=True)  22.6 us
    transpose x2, other arithmetic, adamw_as(): jnp.transpose(rows, back)  21.9 us
    dot_general x4, matrix products, back_quarter(): jnp.einsum('td,fd->tf', chunk, down_full, preferred_element_type=jnp.floa...  20.3 us
    all_gather x1, waiting for transfers between devices, local(): lax.all_gather(down_weight.astype(jnp.bfloat16), 'dp', axis=1, tiled=True)  19.2 us
    dot_general x4, matrix products, back_quarter(): jnp.einsum('ctf,cfd->td', grads, gateup_full, preferred_element_type=jnp....  18.5 us
  transfers between devices with their start and end apart: 92, of which 44 were waited for; matrix products, arithmetic and copies ran while one was open for 37% of the time, Pallas kernels for 4%

profile of v9, /device:TPU:0, one launch (start us, length us, event | category | flops | bytes accessed | tf_op | source)
XLA Modules:
  0.0 642.1 jit_solution(7666603370001244457)
XLA Ops:
  24.1 15.7 %collective-permute-done.10 = f32[8,128]{1,0:T(8,128)S(1)} collective-permute-done((f32[8,128]{1,0:T(8,128)S(1)}, f32[8,128]{1,0:T(8,128)S(1)}, u32[]{:S(2)}, u32[]{:S(2)}) %collective-permute-start.10) | collective-permute-done | bytes 4128 | tf_op jit(solution)/shard_map/ppermute | solution.py:190
  74.4 22.6 %all-gather.4.cloned.1.call-done = bf16[2048,1024]{0,1:T(8,128)(2,1)} async-done(((bf16[512,1024]{0,1:T(8,128)(2,1)}), bf16[2048,1024]{0,1:T(8,128)(2,1)}) %all-gather.4.cloned.1.call-update) | async-done | bytes 4194320 | tf_op jit(solution)/shard_map/all_gather | solution.py:358
  97.0 12.0 %fusion.40.proj_ref = f32[2048,768]{1,0:T(8,128)} fusion(bf16[2048,2048]{1,0:T(8,128)(2,1)} %constant_dynamic-update-slice_fusion, bf16[2048,1024]{0,1:T(8,128)(2,1)} %all-gather.4.cloned.1.call-done), kind=kOutput, calls=%fused_computation.51 | convolution fusion | flops 6442450944 | bytes 17825792 | tf_op jit(solution)/shard_map/dot_general | solution.py:373
  109.0 10.0 %attend_forward.1 = (bf16[2048,256]{1,0:T(8,128)(2,1)}, bf16[2048,256]{1,0:T(8,128)(2,1)}, bf16[2048,256]{1,0:T(8,128)(2,1)}, bf16[2048,256]{1,0:T(8,128)(2,1)}) custom-call(s32[4]{0:T(128)} %objective_ref.3, s32[4]{0:T(128)} %prefix_ref.3, s32[2]{0:T(128)} %pad_add_fusion.place_ref, f32[2048,768]{1,0:T(8,128)} %fusion.40.proj_ref, ...), custom_call_target="tpu_custom_call" | custom-call | tf_op jit(solution)/shard_map/attend_forward/pallas_call | solution.py:138
  133.1 8.0 %collective-permute-done.22 = bf16[128,2048]{1,0:T(8,128)(2,1)S(1)} collective-permute-done((bf16[128,2048]{1,0:T(8,128)(2,1)S(1)}, bf16[128,2048]{1,0:T(8,128)(2,1)S(1)}, u32[]{:S(2)}, u32[]{:S(2)}) %collective-permute-start.22) | collective-permute-done | bytes 524320 | tf_op jit(solution)/shard_map/ppermute | solution.py:190
  145.2 8.7 %collective-permute-done.21 = bf16[128,2048]{1,0:T(8,128)(2,1)S(1)} collective-permute-done((bf16[128,2048]{1,0:T(8,128)(2,1)S(1)}, bf16[128,2048]{1,0:T(8,128)(2,1)S(1)}, u32[]{:S(2)}, u32[]{:S(2)}) %collective-permute-start.21) | collective-permute-done | bytes 524320 | tf_op jit(solution)/shard_map/ppermute | solution.py:190
  153.9 10.1 %collective-permute-done.23 = bf16[128,2048]{1,0:T(8,128)(2,1)S(1)} collective-permute-done((bf16[128,2048]{1,0:T(8,128)(2,1)S(1)}, bf16[128,2048]{1,0:T(8,128)(2,1)S(1)}, u32[]{:S(2)}, u32[]{:S(2)}) %collective-permute-start.23) | collective-permute-done | bytes 524320 | tf_op jit(solution)/shard_map/ppermute | solution.py:190
  169.1 22.4 %collective-permute-done.25 = bf16[256,2048]{1,0:T(8,128)(2,1)} collective-permute-done((bf16[256,2048]{1,0:T(8,128)(2,1)}, bf16[256,2048]{1,0:T(8,128)(2,1)}, u32[]{:S(2)}, u32[]{:S(2)}) %collective-permute-start.25) | collective-permute-done | bytes 1048608 | tf_op jit(solution)/shard_map/ppermute | solution.py:190
  200.8 7.5 %collective-permute-done.29 = bf16[128,2048]{1,0:T(8,128)(2,1)S(1)} collective-permute-done((bf16[128,2048]{1,0:T(8,128)(2,1)S(1)}, bf16[128,2048]{1,0:T(8,128)(2,1)S(1)}, u32[]{:S(2)}, u32[]{:S(2)}) %collective-permute-start.29) | collective-permute-done | bytes 524320 | tf_op jit(solution)/shard_map/ppermute | solution.py:190
  217.7 16.0 %fusion.29 = f32[2,2048,684]{1,2,0:T(8,128)S(1)} fusion(bf16[2,684,2048]{2,1,0:T(8,128)(2,1)} %all-gather.6.cloned.1.call-done, bf16[2048,2048]{1,0:T(8,128)(2,1)} %constant_dynamic-update-slice_fusion.10), kind=kOutput, calls=%fused_computation.32 | convolution fusion | flops 11475615744 | bytes 25198592 | tf_op jit(solution)/shard_map/td,cfd->ctf/dot_general | solution.py:389
  233.7 4.2 copy-done.3
  241.5 19.2 %all-gather.8.cloned.1.call-done = bf16[684,2048]{1,0:T(8,128)(2,1)} async-done(((bf16[684,512]{1,0:T(8,128)(2,1)}), bf16[684,2048]{1,0:T(8,128)(2,1)}) %all-gather.8.cloned.1.call-update) | async-done | bytes 2801680 | tf_op jit(solution)/shard_map/all_gather | solution.py:365
  260.7 4.0 fusion.139
  264.9 5.6 fusion.43
  279.1 8.1 %collective-permute-done.41 = bf16[128,2048]{1,0:T(8,128)(2,1)S(1)} collective-permute-done((bf16[128,2048]{1,0:T(8,128)(2,1)S(1)}, bf16[128,2048]{1,0:T(8,128)(2,1)S(1)}, u32[]{:S(2)}, u32[]{:S(2)}) %collective-permute-start.41) | collective-permute-done | bytes 524320 | tf_op jit(solution)/shard_map/ppermute | solution.py:190
  290.6 9.4 %collective-permute-done.40 = bf16[128,2048]{1,0:T(8,128)(2,1)S(1)} collective-permute-done((bf16[128,2048]{1,0:T(8,128)(2,1)S(1)}, bf16[128,2048]{1,0:T(8,128)(2,1)S(1)}, u32[]{:S(2)}, u32[]{:S(2)}) %collective-permute-start.40) | collective-permute-done | bytes 524320 | tf_op jit(solution)/shard_map/ppermute | solution.py:190
  299.9 10.1 %collective-permute-done.42 = bf16[128,2048]{1,0:T(8,128)(2,1)S(1)} collective-permute-done((bf16[128,2048]{1,0:T(8,128)(2,1)S(1)}, bf16[128,2048]{1,0:T(8,128)(2,1)S(1)}, u32[]{:S(2)}, u32[]{:S(2)}) %collective-permute-start.42) | collective-permute-done | bytes 524320 | tf_op jit(solution)/shard_map/ppermute | solution.py:190
  318.2 4.6 fusion.148
  322.9 3.7 convolution_bitcast_fusion.3
  326.6 14.5 %collective-permute-done.44 = bf16[256,2048]{1,0:T(8,128)(2,1)S(1)} collective-permute-done((bf16[256,2048]{1,0:T(8,128)(2,1)S(1)}, bf16[256,2048]{1,0:T(8,128)(2,1)S(1)}, u32[]{:S(2)}, u32[]{:S(2)}) %collective-permute-start.44) | collective-permute-done | bytes 1048608 | tf_op jit(solution)/shard_map/ppermute | solution.py:190
  346.4 4.6 fusion.147
  351.0 4.1 convolution_bitcast_fusion.2
  363.1 7.4 %fusion.187 = bf16[684,2048]{1,0:T(8,128)(2,1)} fusion(bf16[2048,684]{0,1:T(8,128)(2,1)S(1)} %copy-done.17, bf16[2048,2048]{1,0:T(8,128)(2,1)S(1)} %constant_dynamic-update-slice_fusion.20), kind=kOutput, calls=%fused_computation.324 | convolution fusion | flops 5737807872 | bytes 13991936 | tf_op jit(solution)/shard_map/tf,td->fd/dot_general | solution.py:428
  370.5 5.8 fusion.146
  376.3 6.8 %convolution_bitcast_fusion.1 = bf16[512,2048]{1,0:T(8,128)(2,1)S(1)} fusion(bf16[2,684,2048]{2,1,0:T(8,128)(2,1)} %all-gather.6.cloned.1.call-done, bf16[1,512,684]{1,2,0:T(8,128)(2,1)S(1)} %get-tuple-element.155, bf16[1,512,684]{1,2,0:T(8,128)(2,1)S(1)} %get-tuple-element.154), kind=kOutput, calls=%fused_computation.44 | convolution fusion | flops 2869604352 | bytes 9101312 | tf_op jit(solution)/shard_map/ctf,cfd->td/dot_general | solution.py:418
  395.6 5.3 fusion.145
  400.9 3.9 convolution_bitcast_fusion
  416.1 14.0 %fusion = bf16[2,684,2048]{2,1,0:T(8,128)(2,1)} fusion(bf16[2048,2048]{1,0:T(8,128)(2,1)S(1)} %bitcast.262, bf16[1,512,684]{1,2,0:T(8,128)(2,1)S(1)} %copy-done.53, bf16[1,512,684]{1,2,0:T(8,128)(2,1)S(1)} %copy-done.51, bf16[1,512,684]{1,2,0:T(8,128)(2,1)S(1)} %copy-done.57, bf16[1,512,684]{1,2,0:T(8,128)(2,1)S(1)} %copy-done.55, ...), kind=kOutput, calls=%fused_computation.1 | convolution fusion | flops 11520442368 | bytes 19595264 | tf_op jit(solution)/shard_map/ctf,td->cfd/dot_general | solution.py:433
  430.1 4.6 collective-permute-done.57
  434.7 3.6 collective-permute-done.61
  438.4 4.2 reduce-scatter.4.cloned.1.call-done
  442.7 5.6 multiply_reduce_fusion
  454.6 5.0 multiply_subtract_fusion
  459.6 16.0 %collective-permute-done.63 = bf16[256,2048]{1,0:T(8,128)(2,1)S(1)} collective-permute-done((bf16[256,2048]{1,0:T(8,128)(2,1)}, bf16[256,2048]{1,0:T(8,128)(2,1)S(1)}, u32[]{:S(2)}, u32[]{:S(2)}) %collective-permute-start.63) | collective-permute-done | bytes 1048608 | tf_op jit(solution)/shard_map/ppermute | solution.py:190
  481.0 10.3 %collective-permute-done.67 = bf16[128,2048]{1,0:T(8,128)(2,1)S(1)} collective-permute-done((bf16[128,2048]{1,0:T(8,128)(2,1)S(1)}, bf16[128,2048]{1,0:T(8,128)(2,1)S(1)}, u32[]{:S(2)}, u32[]{:S(2)}) %collective-permute-start.67) | collective-permute-done | bytes 524320 | tf_op jit(solution)/shard_map/ppermute | solution.py:190
  494.6 5.4 fusion.130.grad_ref
  499.9 14.2 %attend_backward.1 = bf16[2048,768]{1,0:T(8,128)(2,1)} custom-call(s32[4]{0:T(128)} %objective_ref.3, s32[4]{0:T(128)} %prefix_ref.3, s32[2]{0:T(128)} %pad_add_fusion.place_ref, bf16[2048,256]{1,0:T(8,128)(2,1)} %get-tuple-element.96.query_ref, bf16[2048,256]{1,0:T(8,128)(2,1)} %get-tuple-element.97.key_ref, bf16[2048,256]{1,0:T(8,128)(2,1)} %get-tuple-element.98.value_ref, ...), custom_call_target="tpu_custom_call" | custom-call | tf_op jit(solution)/shard_map/attend_backward/pallas_call | solution.py:150
  514.1 5.9 fusion.188
  520.0 9.5 %fusion.189 = bf16[768,2048]{1,0:T(8,128)(2,1)S(1)} fusion(bf16[2048,768]{1,0:T(8,128)(2,1)S(1)} %copy-done.15, bf16[2048,2048]{1,0:T(8,128)(2,1)} %constant_dynamic-update-slice_fusion), kind=kOutput, calls=%fused_computation.326 | convolution fusion | flops 6442450944 | bytes 14680064 | tf_op jit(solution)/shard_map/te,td->ed/dot_general | solution.py:468
  532.9 5.2 fusion.38
  538.1 5.3 fusion.36
  559.5 16.5 %fusion.162 = (f32[512,2,684]{0,1,2:T(2,128)}, f32[512,2,684]{0,1,2:T(2,128)}, f32[512,2,684]{0,1,2:T(2,128)}) fusion(f32[]{:T(128)S(6)} %div.99, bf16[2,684,512]{2,1,0:T(8,128)(2,1)S(1)} %copy-done.27, f32[512,2,684]{0,1,2:T(2,128)S(1)} %copy-done.18, f32[512,2,684]{0,1,2:T(2,128)S(1)} %copy-done.19, f32[512,2,684]{0,1,2:T(2,128)S(1)} %copy-done.5), kind=kLoop, calls=%fused_computation.312 | loop fusion | flops 11206656 | bytes 18210820 | tf_op jit(solution)/shard_map/transpose | solution.py:314
  576.0 3.9 collective-permute-done.75
  581.6 11.7 %collective-permute-done.76 = bf16[128,2048]{1,0:T(8,128)(2,1)S(1)} collective-permute-done((bf16[128,2048]{1,0:T(8,128)(2,1)S(1)}, bf16[128,2048]{1,0:T(8,128)(2,1)S(1)}, u32[]{:S(2)}, u32[]{:S(2)}) %collective-permute-start.76) | collective-permute-done | bytes 524320 | tf_op jit(solution)/shard_map/ppermute | solution.py:190
  605.8 6.6 %collective-permute-done.84 = f32[4,2048]{1,0:T(4,128)S(1)} collective-permute-done((f32[4,2048]{1,0:T(4,128)S(1)}, f32[4,2048]{1,0:T(4,128)S(1)}, u32[]{:S(2)}, u32[]{:S(2)}) %collective-permute-start.84) | collective-permute-done | bytes 32800 | tf_op jit(solution)/shard_map/ppermute | solution.py:190
  614.0 5.2 collective-permute-done.85
  619.9 5.6 reduce-scatter.8.cloned.1.call-done
  627.0 5.4 fusion.136
  (436 shorter events, 207.8 us)
Async XLA Ops:
  7.2 89.8 %all-gather.4.cloned.1.call-start = ((), (), s32[]{:S(2)}) async-start(), calls=%async_computation.3 | async-start | bytes 5242880 | tf_op jit(solution)/shard_map/all_gather | solution.py:358
  13.2 204.5 %all-gather.6.cloned.1.call-start = ((), (), s32[]{:S(2)}) async-start(), calls=%async_computation.4 | async-start | bytes 7045120 | tf_op jit(solution)/shard_map/all_gather | solution.py:364
  13.3 29.0 %collective-permute-start.1 = (bf16[256,2048]{1,0:T(8,128)(2,1)}, bf16[256,2048]{1,0:T(8,128)(2,1)}, u32[]{:S(2)}, u32[]{:S(2)}) collective-permute-start(bf16[256,2048]{1,0:T(8,128)(2,1)} %param.20), channel_id=1, source_target_pairs={{0,2},{1,3},{2,0},{3,1},{4,6},{5,7},{6,4},{7,5},{8,10},{9,11},{10,... | collective-permute-start | bytes 3145736 | tf_op jit(solution)/shard_map/ppermute | solution.py:190
  16.3 41.8 %collective-permute-start = (bf16[256,2048]{1,0:T(8,128)(2,1)}, bf16[256,2048]{1,0:T(8,128)(2,1)}, u32[]{:S(2)}, u32[]{:S(2)}) collective-permute-start(bf16[256,2048]{1,0:T(8,128)(2,1)} %param.20), channel_id=1, source_target_pairs={{0,1},{1,0},{2,3},{3,2},{4,5},{5,4},{6,7},{7,6},{8,9},{9,8},{10,11... | collective-permute-start | bytes 3145736 | tf_op jit(solution)/shard_map/ppermute | solution.py:190
  16.3 38.0 %collective-permute-start.3 = (bf16[256,2048]{1,0:T(8,128)(2,1)}, bf16[256,2048]{1,0:T(8,128)(2,1)}, u32[]{:S(2)}, u32[]{:S(2)}) collective-permute-start(bf16[256,2048]{1,0:T(8,128)(2,1)} %param.20), channel_id=1, source_target_pairs={{0,4},{1,5},{2,6},{3,7},{4,0},{5,1},{6,2},{7,3},{8,12},{9,13},{10,... | collective-permute-start | bytes 3145736 | tf_op jit(solution)/shard_map/ppermute | solution.py:190
  21.7 239.0 %all-gather.8.cloned.1.call-start = ((), (), s32[]{:S(2)}) async-start(), calls=%async_computation.5 | async-start | bytes 3522560 | tf_op jit(solution)/shard_map/all_gather | solution.py:365
  23.5 16.3 %collective-permute-start.10 = (f32[8,128]{1,0:T(8,128)S(1)}, f32[8,128]{1,0:T(8,128)S(1)}, u32[]{:S(2)}, u32[]{:S(2)}) collective-permute-start(f32[8,128]{1,0:T(8,128)S(1)} %broadcast_add_fusion), channel_id=1, source_target_pairs={{0,2},{1,3},{2,0},{3,1},{4,6},{5,7},{6,4},{7,5},{8,10},{9,11},{10,... | collective-permute-start | bytes 12296 | tf_op jit(solution)/shard_map/ppermute | solution.py:190
  42.3 24.2 %collective-permute-start.2 = (bf16[256,2048]{1,0:T(8,128)(2,1)}, bf16[256,2048]{1,0:T(8,128)(2,1)S(1)}, u32[]{:S(2)}, u32[]{:S(2)}) collective-permute-start(bf16[256,2048]{1,0:T(8,128)(2,1)} %collective-permute-done.1), channel_id=1, source_target_pairs={{0,1},{1,0},{2,3},{3,2},{4,5},{5,4},{6,7},{7,6},{8,9},{9,8},{10,11... | collective-permute-start | bytes 3145736 | tf_op jit(solution)/shard_map/ppermute | solution.py:190
  125.3 19.9 %collective-permute-start.14 = (bf16[256,2048]{1,0:T(8,128)(2,1)S(1)}, bf16[256,2048]{1,0:T(8,128)(2,1)S(1)}, u32[]{:S(2)}, u32[]{:S(2)}) collective-permute-start(bf16[256,2048]{1,0:T(8,128)(2,1)S(1)} %get-tuple-element.170), channel_id=1, source_target_pairs={{0,1},{1,0},{2,3},{3,2},{4,5},{5,4},{6,7},{7,6},{8,9},{9,8},{10,11... | collective-permute-start | bytes 3145736 | tf_op jit(solution)/shard_map/ppermute | solution.py:190
  127.8 15.0 %collective-permute-start.17 = (bf16[128,2048]{1,0:T(8,128)(2,1)S(1)}, bf16[128,2048]{1,0:T(8,128)(2,1)S(1)}, u32[]{:S(2)}, u32[]{:S(2)}) collective-permute-start(bf16[128,2048]{1,0:T(8,128)(2,1)S(1)} %get-tuple-element.188), channel_id=1, source_target_pairs={{0,4},{1,5},{2,6},{3,7},{4,0},{5,1},{6,2},{7,3},{8,12},{9,13},{10,... | collective-permute-start | bytes 1572872 | tf_op jit(solution)/shard_map/ppermute | solution.py:190
  130.2 23.6 %collective-permute-start.21 = (bf16[128,2048]{1,0:T(8,128)(2,1)S(1)}, bf16[128,2048]{1,0:T(8,128)(2,1)S(1)}, u32[]{:S(2)}, u32[]{:S(2)}) collective-permute-start(bf16[128,2048]{1,0:T(8,128)(2,1)S(1)} %slice.612), channel_id=1, source_target_pairs={{0,4},{1,5},{2,6},{3,7},{4,0},{5,1},{6,2},{7,3},{8,12},{9,13},{10,... | collective-permute-start | bytes 1572872 | tf_op jit(solution)/shard_map/ppermute | solution.py:190
  131.6 22.3 %collective-permute-start.19 = (bf16[128,2048]{1,0:T(8,128)(2,1)S(1)}, bf16[128,2048]{1,0:T(8,128)(2,1)S(1)}, u32[]{:S(2)}, u32[]{:S(2)}) collective-permute-start(bf16[128,2048]{1,0:T(8,128)(2,1)S(1)} %slice.613), channel_id=1, source_target_pairs={{0,2},{1,3},{2,0},{3,1},{4,6},{5,7},{6,4},{7,5},{8,10},{9,11},{10,... | collective-permute-start | bytes 1572872 | tf_op jit(solution)/shard_map/ppermute | solution.py:190
  141.2 22.7 %collective-permute-start.23 = (bf16[128,2048]{1,0:T(8,128)(2,1)S(1)}, bf16[128,2048]{1,0:T(8,128)(2,1)S(1)}, u32[]{:S(2)}, u32[]{:S(2)}) collective-permute-start(bf16[128,2048]{1,0:T(8,128)(2,1)S(1)} %fusion.127), channel_id=1, source_target_pairs={{0,4},{1,5},{2,6},{3,7},{4,0},{5,1},{6,2},{7,3},{8,12},{9,13},{10,... | collective-permute-start | bytes 1572872 | tf_op jit(solution)/shard_map/ppermute | solution.py:190
  143.0 20.9 %collective-permute-start.18 = (bf16[128,2048]{1,0:T(8,128)(2,1)S(1)}, bf16[128,2048]{1,0:T(8,128)(2,1)S(1)}, u32[]{:S(2)}, u32[]{:S(2)}) collective-permute-start(bf16[128,2048]{1,0:T(8,128)(2,1)S(1)} %fusion.128), channel_id=1, source_target_pairs={{0,2},{1,3},{2,0},{3,1},{4,6},{5,7},{6,4},{7,5},{8,10},{9,11},{10,... | collective-permute-start | bytes 1572872 | tf_op jit(solution)/shard_map/ppermute | solution.py:190
  167.0 24.4 %collective-permute-start.25 = (bf16[256,2048]{1,0:T(8,128)(2,1)}, bf16[256,2048]{1,0:T(8,128)(2,1)}, u32[]{:S(2)}, u32[]{:S(2)}) collective-permute-start(bf16[256,2048]{1,0:T(8,128)(2,1)} %get-tuple-element.149), channel_id=1, source_target_pairs={{0,2},{1,3},{2,0},{3,1},{4,6},{5,7},{6,4},{7,5},{8,10},{9,11},{10,... | collective-permute-start | bytes 3145736 | tf_op jit(solution)/shard_map/ppermute | solution.py:190
  167.5 28.0 %collective-permute-start.27 = (bf16[256,2048]{1,0:T(8,128)(2,1)}, bf16[256,2048]{1,0:T(8,128)(2,1)S(1)}, u32[]{:S(2)}, u32[]{:S(2)}) collective-permute-start(bf16[256,2048]{1,0:T(8,128)(2,1)} %get-tuple-element.149), channel_id=1, source_target_pairs={{0,4},{1,5},{2,6},{3,7},{4,0},{5,1},{6,2},{7,3},{8,12},{9,13},{10,... | collective-permute-start | bytes 3145736 | tf_op jit(solution)/shard_map/ppermute | solution.py:190
  169.1 27.1 %collective-permute-start.24 = (bf16[256,2048]{1,0:T(8,128)(2,1)}, bf16[256,2048]{1,0:T(8,128)(2,1)}, u32[]{:S(2)}, u32[]{:S(2)}) collective-permute-start(bf16[256,2048]{1,0:T(8,128)(2,1)} %get-tuple-element.149), channel_id=1, source_target_pairs={{0,1},{1,0},{2,3},{3,2},{4,5},{5,4},{6,7},{7,6},{8,9},{9,8},{10,11... | collective-permute-start | bytes 3145736 | tf_op jit(solution)/shard_map/ppermute | solution.py:190
  191.4 18.3 %collective-permute-start.26 = (bf16[256,2048]{1,0:T(8,128)(2,1)}, bf16[256,2048]{1,0:T(8,128)(2,1)}, u32[]{:S(2)}, u32[]{:S(2)}) collective-permute-start(bf16[256,2048]{1,0:T(8,128)(2,1)} %collective-permute-done.25), channel_id=1, source_target_pairs={{0,1},{1,0},{2,3},{3,2},{4,5},{5,4},{6,7},{7,6},{8,9},{9,8},{10,11... | collective-permute-start | bytes 3145736 | tf_op jit(solution)/shard_map/ppermute | solution.py:190
  192.4 250.2 %reduce-scatter.4.cloned.1.call-start = ((), (), s32[]{:S(2)}) async-start(), calls=%async_computation.6 | async-start | bytes 3522560 | tf_op jit(solution)/shard_map/reduce_scatter | solution.py:430
  196.2 17.0 %collective-permute-start.28 = (bf16[256,2048]{1,0:T(8,128)(2,1)S(1)}, bf16[256,2048]{1,0:T(8,128)(2,1)S(1)}, u32[]{:S(2)}, u32[]{:S(2)}) collective-permute-start(bf16[256,2048]{1,0:T(8,128)(2,1)S(1)} %collective-permute-done.27), channel_id=1, source_target_pairs={{0,1},{1,0},{2,3},{3,2},{4,5},{5,4},{6,7},{7,6},{8,9},{9,8},{10,11... | collective-permute-start | bytes 3145736 | tf_op jit(solution)/shard_map/ppermute | solution.py:190
  271.4 19.2 %collective-permute-start.33 = (bf16[256,2048]{1,0:T(8,128)(2,1)S(1)}, bf16[256,2048]{1,0:T(8,128)(2,1)S(1)}, u32[]{:S(2)}, u32[]{:S(2)}) collective-permute-start(bf16[256,2048]{1,0:T(8,128)(2,1)S(1)} %get-tuple-element.165), channel_id=1, source_target_pairs={{0,1},{1,0},{2,3},{3,2},{4,5},{5,4},{6,7},{7,6},{8,9},{9,8},{10,11... | collective-permute-start | bytes 3145736 | tf_op jit(solution)/shard_map/ppermute | solution.py:190
  272.4 14.9 %collective-permute-start.41 = (bf16[128,2048]{1,0:T(8,128)(2,1)S(1)}, bf16[128,2048]{1,0:T(8,128)(2,1)S(1)}, u32[]{:S(2)}, u32[]{:S(2)}) collective-permute-start(bf16[128,2048]{1,0:T(8,128)(2,1)S(1)} %get-tuple-element.187), channel_id=1, source_target_pairs={{0,2},{1,3},{2,0},{3,1},{4,6},{5,7},{6,4},{7,5},{8,10},{9,11},{10,... | collective-permute-start | bytes 1572872 | tf_op jit(solution)/shard_map/ppermute | solution.py:190
  273.9 15.0 %collective-permute-start.36 = (bf16[128,2048]{1,0:T(8,128)(2,1)S(1)}, bf16[128,2048]{1,0:T(8,128)(2,1)S(1)}, u32[]{:S(2)}, u32[]{:S(2)}) collective-permute-start(bf16[128,2048]{1,0:T(8,128)(2,1)S(1)} %get-tuple-element.186), channel_id=1, source_target_pairs={{0,4},{1,5},{2,6},{3,7},{4,0},{5,1},{6,2},{7,3},{8,12},{9,13},{10,... | collective-permute-start | bytes 1572872 | tf_op jit(solution)/shard_map/ppermute | solution.py:190
  276.2 23.7 %collective-permute-start.40 = (bf16[128,2048]{1,0:T(8,128)(2,1)S(1)}, bf16[128,2048]{1,0:T(8,128)(2,1)S(1)}, u32[]{:S(2)}, u32[]{:S(2)}) collective-permute-start(bf16[128,2048]{1,0:T(8,128)(2,1)S(1)} %slice.610), channel_id=1, source_target_pairs={{0,4},{1,5},{2,6},{3,7},{4,0},{5,1},{6,2},{7,3},{8,12},{9,13},{10,... | collective-permute-start | bytes 1572872 | tf_op jit(solution)/shard_map/ppermute | solution.py:190
  277.6 22.3 %collective-permute-start.38 = (bf16[128,2048]{1,0:T(8,128)(2,1)S(1)}, bf16[128,2048]{1,0:T(8,128)(2,1)S(1)}, u32[]{:S(2)}, u32[]{:S(2)}) collective-permute-start(bf16[128,2048]{1,0:T(8,128)(2,1)S(1)} %slice.611), channel_id=1, source_target_pairs={{0,2},{1,3},{2,0},{3,1},{4,6},{5,7},{6,4},{7,5},{8,10},{9,11},{10,... | collective-permute-start | bytes 1572872 | tf_op jit(solution)/shard_map/ppermute | solution.py:190
  287.4 22.6 %collective-permute-start.42 = (bf16[128,2048]{1,0:T(8,128)(2,1)S(1)}, bf16[128,2048]{1,0:T(8,128)(2,1)S(1)}, u32[]{:S(2)}, u32[]{:S(2)}) collective-permute-start(bf16[128,2048]{1,0:T(8,128)(2,1)S(1)} %fusion.125), channel_id=1, source_target_pairs={{0,4},{1,5},{2,6},{3,7},{4,0},{5,1},{6,2},{7,3},{8,12},{9,13},{10,... | collective-permute-start | bytes 1572872 | tf_op jit(solution)/shard_map/ppermute | solution.py:190
  289.0 21.0 %collective-permute-start.37 = (bf16[128,2048]{1,0:T(8,128)(2,1)S(1)}, bf16[128,2048]{1,0:T(8,128)(2,1)S(1)}, u32[]{:S(2)}, u32[]{:S(2)}) collective-permute-start(bf16[128,2048]{1,0:T(8,128)(2,1)S(1)} %fusion.126), channel_id=1, source_target_pairs={{0,2},{1,3},{2,0},{3,1},{4,6},{5,7},{6,4},{7,5},{8,10},{9,11},{10,... | collective-permute-start | bytes 1572872 | tf_op jit(solution)/shard_map/ppermute | solution.py:190
  315.6 25.6 %collective-permute-start.44 = (bf16[256,2048]{1,0:T(8,128)(2,1)S(1)}, bf16[256,2048]{1,0:T(8,128)(2,1)S(1)}, u32[]{:S(2)}, u32[]{:S(2)}) collective-permute-start(bf16[256,2048]{1,0:T(8,128)(2,1)S(1)} %get-tuple-element.145), channel_id=1, source_target_pairs={{0,2},{1,3},{2,0},{3,1},{4,6},{5,7},{6,4},{7,5},{8,10},{9,11},{10,... | collective-permute-start | bytes 3145736 | tf_op jit(solution)/shard_map/ppermute | solution.py:190
  316.2 25.2 %collective-permute-start.45 = (bf16[256,2048]{1,0:T(8,128)(2,1)S(1)}, bf16[256,2048]{1,0:T(8,128)(2,1)S(1)}, u32[]{:S(2)}, u32[]{:S(2)}) collective-permute-start(bf16[256,2048]{1,0:T(8,128)(2,1)S(1)} %get-tuple-element.145), channel_id=1, source_target_pairs={{0,4},{1,5},{2,6},{3,7},{4,0},{5,1},{6,2},{7,3},{8,12},{9,13},{10,... | collective-permute-start | bytes 3145736 | tf_op jit(solution)/shard_map/ppermute | solution.py:190
  341.5 16.5 %collective-permute-start.47 = (bf16[256,2048]{1,0:T(8,128)(2,1)S(1)}, bf16[256,2048]{1,0:T(8,128)(2,1)S(1)}, u32[]{:S(2)}, u32[]{:S(2)}) collective-permute-start(bf16[256,2048]{1,0:T(8,128)(2,1)S(1)} %collective-permute-done.45), channel_id=1, source_target_pairs={{0,1},{1,0},{2,3},{3,2},{4,5},{5,4},{6,7},{7,6},{8,9},{9,8},{10,11... | collective-permute-start | bytes 3145736 | tf_op jit(solution)/shard_map/ppermute | solution.py:190
  346.1 39.5 %collective-permute-start.53 = (bf16[256,2048]{1,0:T(8,128)(2,1)}, bf16[256,2048]{1,0:T(8,128)(2,1)}, u32[]{:S(2)}, u32[]{:S(2)}) collective-permute-start(bf16[256,2048]{1,0:T(8,128)(2,1)} %slice.340), channel_id=1, source_target_pairs={{0,1},{1,0},{2,3},{3,2},{4,5},{5,4},{6,7},{7,6},{8,9},{9,8},{10,11... | collective-permute-start | bytes 3145736 | tf_op jit(solution)/shard_map/ppermute | solution.py:190
  359.1 30.3 %collective-permute-start.54 = (bf16[256,2048]{1,0:T(8,128)(2,1)}, bf16[256,2048]{1,0:T(8,128)(2,1)}, u32[]{:S(2)}, u32[]{:S(2)}) collective-permute-start(bf16[256,2048]{1,0:T(8,128)(2,1)} %slice.342), channel_id=1, source_target_pairs={{0,1},{1,0},{2,3},{3,2},{4,5},{5,4},{6,7},{7,6},{8,9},{9,8},{10,11... | collective-permute-start | bytes 3145736 | tf_op jit(solution)/shard_map/ppermute | solution.py:190
  389.3 157.9 %reduce-scatter.6.cloned.1.call-start = ((), (), s32[]{:S(2)}) async-start(), calls=%async_computation.7 | async-start | bytes 7045120 | tf_op jit(solution)/shard_map/reduce_scatter | solution.py:458
  408.8 21.3 %collective-permute-start.58 = (bf16[128,2048]{1,0:T(8,128)(2,1)}, bf16[128,2048]{1,0:T(8,128)(2,1)}, u32[]{:S(2)}, u32[]{:S(2)}) collective-permute-start(bf16[128,2048]{1,0:T(8,128)(2,1)} %slice.609), channel_id=1, source_target_pairs={{0,2},{1,3},{2,0},{3,1},{4,6},{5,7},{6,4},{7,5},{8,10},{9,11},{10,... | collective-permute-start | bytes 1572872 | tf_op jit(solution)/shard_map/ppermute | solution.py:190
  411.2 23.5 %collective-permute-start.57 = (bf16[128,2048]{1,0:T(8,128)(2,1)}, bf16[128,2048]{1,0:T(8,128)(2,1)}, u32[]{:S(2)}, u32[]{:S(2)}) collective-permute-start(bf16[128,2048]{1,0:T(8,128)(2,1)} %add_convert_fusion.5), channel_id=1, source_target_pairs={{0,2},{1,3},{2,0},{3,1},{4,6},{5,7},{6,4},{7,5},{8,10},{9,11},{10,... | collective-permute-start | bytes 1572872 | tf_op jit(solution)/shard_map/ppermute | solution.py:190
  413.0 21.7 %collective-permute-start.60 = (bf16[128,2048]{1,0:T(8,128)(2,1)}, bf16[128,2048]{1,0:T(8,128)(2,1)}, u32[]{:S(2)}, u32[]{:S(2)}) collective-permute-start(bf16[128,2048]{1,0:T(8,128)(2,1)} %slice.608), channel_id=1, source_target_pairs={{0,4},{1,5},{2,6},{3,7},{4,0},{5,1},{6,2},{7,3},{8,12},{9,13},{10,... | collective-permute-start | bytes 1572872 | tf_op jit(solution)/shard_map/ppermute | solution.py:190
  415.4 22.9 %collective-permute-start.61 = (bf16[128,2048]{1,0:T(8,128)(2,1)}, bf16[128,2048]{1,0:T(8,128)(2,1)}, u32[]{:S(2)}, u32[]{:S(2)}) collective-permute-start(bf16[128,2048]{1,0:T(8,128)(2,1)} %fusion.124), channel_id=1, source_target_pairs={{0,4},{1,5},{2,6},{3,7},{4,0},{5,1},{6,2},{7,3},{8,12},{9,13},{10,... | collective-permute-start | bytes 1572872 | tf_op jit(solution)/shard_map/ppermute | solution.py:190
  442.6 182.9 %reduce-scatter.8.cloned.1.call-start = ((), (), s32[]{:S(2)}) async-start(), calls=%async_computation.8 | async-start | bytes 5242880 | tf_op jit(solution)/shard_map/reduce_scatter | solution.py:475
  451.2 24.4 %collective-permute-start.63 = (bf16[256,2048]{1,0:T(8,128)(2,1)}, bf16[256,2048]{1,0:T(8,128)(2,1)S(1)}, u32[]{:S(2)}, u32[]{:S(2)}) collective-permute-start(bf16[256,2048]{1,0:T(8,128)(2,1)} %get-tuple-element.141), channel_id=1, source_target_pairs={{0,2},{1,3},{2,0},{3,1},{4,6},{5,7},{6,4},{7,5},{8,10},{9,11},{10,... | collective-permute-start | bytes 3145736 | tf_op jit(solution)/shard_map/ppermute | solution.py:190
  452.4 24.4 %collective-permute-start.64 = (bf16[256,2048]{1,0:T(8,128)(2,1)}, bf16[256,2048]{1,0:T(8,128)(2,1)S(1)}, u32[]{:S(2)}, u32[]{:S(2)}) collective-permute-start(bf16[256,2048]{1,0:T(8,128)(2,1)} %get-tuple-element.141), channel_id=1, source_target_pairs={{0,4},{1,5},{2,6},{3,7},{4,0},{5,1},{6,2},{7,3},{8,12},{9,13},{10,... | collective-permute-start | bytes 3145736 | tf_op jit(solution)/shard_map/ppermute | solution.py:190
  453.9 25.7 %collective-permute-start.62 = (bf16[256,2048]{1,0:T(8,128)(2,1)}, bf16[256,2048]{1,0:T(8,128)(2,1)}, u32[]{:S(2)}, u32[]{:S(2)}) collective-permute-start(bf16[256,2048]{1,0:T(8,128)(2,1)} %get-tuple-element.141), channel_id=1, source_target_pairs={{0,1},{1,0},{2,3},{3,2},{4,5},{5,4},{6,7},{7,6},{8,9},{9,8},{10,11... | collective-permute-start | bytes 3145736 | tf_op jit(solution)/shard_map/ppermute | solution.py:190
  476.8 15.8 %collective-permute-start.65 = (bf16[256,2048]{1,0:T(8,128)(2,1)S(1)}, bf16[256,2048]{1,0:T(8,128)(2,1)S(1)}, u32[]{:S(2)}, u32[]{:S(2)}) collective-permute-start(bf16[256,2048]{1,0:T(8,128)(2,1)S(1)} %collective-permute-done.63), channel_id=1, source_target_pairs={{0,1},{1,0},{2,3},{3,2},{4,5},{5,4},{6,7},{7,6},{8,9},{9,8},{10,11... | collective-permute-start | bytes 3145736 | tf_op jit(solution)/shard_map/ppermute | solution.py:190
  476.8 15.9 %collective-permute-start.66 = (bf16[256,2048]{1,0:T(8,128)(2,1)S(1)}, bf16[256,2048]{1,0:T(8,128)(2,1)S(1)}, u32[]{:S(2)}, u32[]{:S(2)}) collective-permute-start(bf16[256,2048]{1,0:T(8,128)(2,1)S(1)} %collective-permute-done.64), channel_id=1, source_target_pairs={{0,1},{1,0},{2,3},{3,2},{4,5},{5,4},{6,7},{7,6},{8,9},{9,8},{10,11... | collective-permute-start | bytes 3145736 | tf_op jit(solution)/shard_map/ppermute | solution.py:190
  549.0 32.6 %collective-permute-start.71 = (bf16[256,2048]{1,0:T(8,128)(2,1)S(1)}, bf16[256,2048]{1,0:T(8,128)(2,1)S(1)}, u32[]{:S(2)}, u32[]{:S(2)}) collective-permute-start(bf16[256,2048]{1,0:T(8,128)(2,1)S(1)} %get-tuple-element.164), channel_id=1, source_target_pairs={{0,1},{1,0},{2,3},{3,2},{4,5},{5,4},{6,7},{7,6},{8,9},{9,8},{10,11... | collective-permute-start | bytes 3145736 | tf_op jit(solution)/shard_map/ppermute | solution.py:190
  554.7 26.8 %collective-permute-start.77 = (bf16[128,2048]{1,0:T(8,128)(2,1)S(1)}, bf16[128,2048]{1,0:T(8,128)(2,1)S(1)}, u32[]{:S(2)}, u32[]{:S(2)}) collective-permute-start(bf16[128,2048]{1,0:T(8,128)(2,1)S(1)} %slice.607), channel_id=1, source_target_pairs={{0,2},{1,3},{2,0},{3,1},{4,6},{5,7},{6,4},{7,5},{8,10},{9,11},{10,... | collective-permute-start | bytes 1572872 | tf_op jit(solution)/shard_map/ppermute | solution.py:190
  555.5 20.6 %collective-permute-start.74 = (bf16[128,2048]{1,0:T(8,128)(2,1)S(1)}, bf16[128,2048]{1,0:T(8,128)(2,1)S(1)}, u32[]{:S(2)}, u32[]{:S(2)}) collective-permute-start(bf16[128,2048]{1,0:T(8,128)(2,1)S(1)} %get-tuple-element.183), channel_id=1, source_target_pairs={{0,4},{1,5},{2,6},{3,7},{4,0},{5,1},{6,2},{7,3},{8,12},{9,13},{10,... | collective-permute-start | bytes 1572872 | tf_op jit(solution)/shard_map/ppermute | solution.py:190
  556.5 23.4 %collective-permute-start.75 = (bf16[128,2048]{1,0:T(8,128)(2,1)S(1)}, bf16[128,2048]{1,0:T(8,128)(2,1)S(1)}, u32[]{:S(2)}, u32[]{:S(2)}) collective-permute-start(bf16[128,2048]{1,0:T(8,128)(2,1)S(1)} %get-tuple-element.182), channel_id=1, source_target_pairs={{0,2},{1,3},{2,0},{3,1},{4,6},{5,7},{6,4},{7,5},{8,10},{9,11},{10,... | collective-permute-start | bytes 1572872 | tf_op jit(solution)/shard_map/ppermute | solution.py:190
  558.0 23.5 %collective-permute-start.79 = (bf16[128,2048]{1,0:T(8,128)(2,1)S(1)}, bf16[128,2048]{1,0:T(8,128)(2,1)S(1)}, u32[]{:S(2)}, u32[]{:S(2)}) collective-permute-start(bf16[128,2048]{1,0:T(8,128)(2,1)S(1)} %slice.606), channel_id=1, source_target_pairs={{0,4},{1,5},{2,6},{3,7},{4,0},{5,1},{6,2},{7,3},{8,12},{9,13},{10,... | collective-permute-start | bytes 1572872 | tf_op jit(solution)/shard_map/ppermute | solution.py:190
  (108 other events, 747.1 us)
Sparse Core Ops, SparseCore 0:
  13.3 83.5 all-gather.3
  99.1 103.0 all-gather.5
  204.4 56.2 all-gather.7
  389.5 53.0 reduce-scatter.3
  444.7 99.8 reduce-scatter.5
  547.3 78.1 reduce-scatter.7

commit v10 on v8

--- a/solution.py
+++ b/solution.py
@@ -428,6 +428,8 @@
     ffn_back, down_grad = lax.optimization_barrier((ffn_back, down_grad))
     down_grad = lax.psum_scatter(down_grad, "dp", scatter_dimension=1, tiled=True)
 
+    middle_low, down_grad = lax.optimization_barrier((middle_low, down_grad))
+
     def gateup_product():
         return jnp.einsum(
             "ctf,td->cfd",

time: 645 us -> 662 us (1.026)
  waiting for transfers between devices: 257 us -> 268 us
    reduce_scatter x1, waiting for transfers between devices: 3.39 us -> 25.8 us  [local(): lax.psum_scatter(down_grad, 'dp', scatter_dimension=1, tiled=True)]
    ppermute x86, waiting for transfers between devices: 206 us -> 195 us  [swap(): return lax.ppermute(values, axis, [(at, at ^ bit) for at in range(size)])]
    unnamed x164 -> x144, local copies, waits for them, and re-layouts: 43.6 us -> 43.9 us
  transfers between devices with their start and end apart: 92 -> 92, of which waited for: 44 -> 42; matrix products, arithmetic and copies ran while one was open for 35% -> 35% of each run, Pallas kernels for 4% -> 4%
where the time goes in v10:
time: 662 us; the launch traced here: 657 us
  waiting for transfers between devices  268 us (40%)
  matrix products  135 us (20%)
  other arithmetic  82.2 us (12%)
  starting transfers between devices  70.1 us (11%)
  local copies, waits for them, and re-layouts  61.2 us (9%)
  Pallas kernels  24.1 us (4%)
  between operations  16.5 us (2%)
    ppermute x86, waiting for transfers between devices, swap(): return lax.ppermute(values, axis, [(at, at ^ bit) for at in range(size)])  195 us
    ppermute x86, starting transfers between devices, swap(): return lax.ppermute(values, axis, [(at, at ^ bit) for at in range(size)])  69.7 us
    unnamed x144, local copies, waits for them, and re-layouts  43.9 us
    reduce_scatter x1, waiting for transfers between devices, local(): lax.psum_scatter(down_grad, 'dp', scatter_dimension=1, tiled=True)  25.8 us
    all_gather x1, waiting for transfers between devices, local(): attend_full = lax.all_gather(attend_low, 'dp', axis=0, tiled=True)  22.6 us
    transpose x2, other arithmetic, adamw_as(): jnp.transpose(rows, back)  21.8 us
    dot_general x4, matrix products, back_quarter(): jnp.einsum('td,fd->tf', chunk, down_full, preferred_element_type=jnp.floa...  19.6 us
    all_gather x1, waiting for transfers between devices, local(): lax.all_gather(down_weight.astype(jnp.bfloat16), 'dp', axis=1, tiled=True)  19.4 us
  transfers between devices with their start and end apart: 92, of which 42 were waited for; matrix products, arithmetic and copies ran while one was open for 35% of the time, Pallas kernels for 4%

profile of v10, /device:TPU:0, one launch (start us, length us, event | category | flops | bytes accessed | tf_op | source)
XLA Modules:
  0.0 657.0 jit_solution(2133783071254491959)
XLA Ops:
  24.1 15.7 %collective-permute-done.10 = f32[8,128]{1,0:T(8,128)S(1)} collective-permute-done((f32[8,128]{1,0:T(8,128)S(1)}, f32[8,128]{1,0:T(8,128)S(1)}, u32[]{:S(2)}, u32[]{:S(2)}) %collective-permute-start.10) | collective-permute-done | bytes 4128 | tf_op jit(solution)/shard_map/ppermute | solution.py:190
  74.3 22.6 %all-gather.4.cloned.1.call-done = bf16[2048,1024]{0,1:T(8,128)(2,1)} async-done(((bf16[512,1024]{0,1:T(8,128)(2,1)}), bf16[2048,1024]{0,1:T(8,128)(2,1)}) %all-gather.4.cloned.1.call-update) | async-done | bytes 4194320 | tf_op jit(solution)/shard_map/all_gather | solution.py:357
  97.0 12.3 %fusion.40.proj_ref = f32[2048,768]{1,0:T(8,128)} fusion(bf16[2048,2048]{1,0:T(8,128)(2,1)} %constant_dynamic-update-slice_fusion, bf16[2048,1024]{0,1:T(8,128)(2,1)} %all-gather.4.cloned.1.call-done), kind=kOutput, calls=%fused_computation.51 | convolution fusion | flops 6442450944 | bytes 17825792 | tf_op jit(solution)/shard_map/dot_general | solution.py:372
  109.2 10.0 %attend_forward.1 = (bf16[2048,256]{1,0:T(8,128)(2,1)}, bf16[2048,256]{1,0:T(8,128)(2,1)}, bf16[2048,256]{1,0:T(8,128)(2,1)}, bf16[2048,256]{1,0:T(8,128)(2,1)}) custom-call(s32[4]{0:T(128)} %objective_ref.3, s32[4]{0:T(128)} %prefix_ref.3, s32[2]{0:T(128)} %pad_add_fusion.place_ref, f32[2048,768]{1,0:T(8,128)} %fusion.40.proj_ref, ...), custom_call_target="tpu_custom_call" | custom-call | tf_op jit(solution)/shard_map/attend_forward/pallas_call | solution.py:138
  133.3 8.0 %collective-permute-done.22 = bf16[128,2048]{1,0:T(8,128)(2,1)S(1)} collective-permute-done((bf16[128,2048]{1,0:T(8,128)(2,1)S(1)}, bf16[128,2048]{1,0:T(8,128)(2,1)S(1)}, u32[]{:S(2)}, u32[]{:S(2)}) %collective-permute-start.22) | collective-permute-done | bytes 524320 | tf_op jit(solution)/shard_map/ppermute | solution.py:190
  145.4 8.7 %collective-permute-done.21 = bf16[128,2048]{1,0:T(8,128)(2,1)S(1)} collective-permute-done((bf16[128,2048]{1,0:T(8,128)(2,1)S(1)}, bf16[128,2048]{1,0:T(8,128)(2,1)S(1)}, u32[]{:S(2)}, u32[]{:S(2)}) %collective-permute-start.21) | collective-permute-done | bytes 524320 | tf_op jit(solution)/shard_map/ppermute | solution.py:190
  154.0 10.1 %collective-permute-done.23 = bf16[128,2048]{1,0:T(8,128)(2,1)S(1)} collective-permute-done((bf16[128,2048]{1,0:T(8,128)(2,1)S(1)}, bf16[128,2048]{1,0:T(8,128)(2,1)S(1)}, u32[]{:S(2)}, u32[]{:S(2)}) %collective-permute-start.23) | collective-permute-done | bytes 524320 | tf_op jit(solution)/shard_map/ppermute | solution.py:190
  169.3 22.4 %collective-permute-done.25 = bf16[256,2048]{1,0:T(8,128)(2,1)} collective-permute-done((bf16[256,2048]{1,0:T(8,128)(2,1)}, bf16[256,2048]{1,0:T(8,128)(2,1)}, u32[]{:S(2)}, u32[]{:S(2)}) %collective-permute-start.25) | collective-permute-done | bytes 1048608 | tf_op jit(solution)/shard_map/ppermute | solution.py:190
  200.8 7.5 %collective-permute-done.29 = bf16[128,2048]{1,0:T(8,128)(2,1)S(1)} collective-permute-done((bf16[128,2048]{1,0:T(8,128)(2,1)S(1)}, bf16[128,2048]{1,0:T(8,128)(2,1)S(1)}, u32[]{:S(2)}, u32[]{:S(2)}) %collective-permute-start.29) | collective-permute-done | bytes 524320 | tf_op jit(solution)/shard_map/ppermute | solution.py:190
  217.5 16.0 %fusion.29 = f32[2,2048,684]{1,2,0:T(8,128)S(1)} fusion(bf16[2,684,2048]{2,1,0:T(8,128)(2,1)} %all-gather.6.cloned.1.call-done, bf16[2048,2048]{1,0:T(8,128)(2,1)} %constant_dynamic-update-slice_fusion.10), kind=kOutput, calls=%fused_computation.32 | convolution fusion | flops 11475615744 | bytes 25198592 | tf_op jit(solution)/shard_map/td,cfd->ctf/dot_general | solution.py:388
  233.6 4.2 copy-done.3
  237.8 3.6 fusion.13
  241.3 19.4 %all-gather.8.cloned.1.call-done = bf16[684,2048]{1,0:T(8,128)(2,1)} async-done(((bf16[684,512]{1,0:T(8,128)(2,1)}), bf16[684,2048]{1,0:T(8,128)(2,1)}) %all-gather.8.cloned.1.call-update) | async-done | bytes 2801680 | tf_op jit(solution)/shard_map/all_gather | solution.py:364
  260.7 4.0 fusion.139
  264.9 5.7 fusion.43
  279.2 8.1 %collective-permute-done.41 = bf16[128,2048]{1,0:T(8,128)(2,1)S(1)} collective-permute-done((bf16[128,2048]{1,0:T(8,128)(2,1)S(1)}, bf16[128,2048]{1,0:T(8,128)(2,1)S(1)}, u32[]{:S(2)}, u32[]{:S(2)}) %collective-permute-start.41) | collective-permute-done | bytes 524320 | tf_op jit(solution)/shard_map/ppermute | solution.py:190
  290.6 9.4 %collective-permute-done.40 = bf16[128,2048]{1,0:T(8,128)(2,1)S(1)} collective-permute-done((bf16[128,2048]{1,0:T(8,128)(2,1)S(1)}, bf16[128,2048]{1,0:T(8,128)(2,1)S(1)}, u32[]{:S(2)}, u32[]{:S(2)}) %collective-permute-start.40) | collective-permute-done | bytes 524320 | tf_op jit(solution)/shard_map/ppermute | solution.py:190
  300.0 10.1 %collective-permute-done.42 = bf16[128,2048]{1,0:T(8,128)(2,1)S(1)} collective-permute-done((bf16[128,2048]{1,0:T(8,128)(2,1)S(1)}, bf16[128,2048]{1,0:T(8,128)(2,1)S(1)}, u32[]{:S(2)}, u32[]{:S(2)}) %collective-permute-start.42) | collective-permute-done | bytes 524320 | tf_op jit(solution)/shard_map/ppermute | solution.py:190
  318.3 4.6 fusion.148
  322.9 3.7 convolution_bitcast_fusion.3
  326.6 14.6 %collective-permute-done.44 = bf16[256,2048]{1,0:T(8,128)(2,1)S(1)} collective-permute-done((bf16[256,2048]{1,0:T(8,128)(2,1)S(1)}, bf16[256,2048]{1,0:T(8,128)(2,1)S(1)}, u32[]{:S(2)}, u32[]{:S(2)}) %collective-permute-start.44) | collective-permute-done | bytes 1048608 | tf_op jit(solution)/shard_map/ppermute | solution.py:190
  345.5 4.6 fusion.147
  350.2 4.1 convolution_bitcast_fusion.2
  364.2 7.4 %fusion.187 = bf16[684,2048]{1,0:T(8,128)(2,1)} fusion(bf16[2048,684]{0,1:T(8,128)(2,1)S(1)} %copy-done.18, bf16[2048,2048]{1,0:T(8,128)(2,1)S(1)} %constant_dynamic-update-slice_fusion.20), kind=kOutput, calls=%fused_computation.324 | convolution fusion | flops 5737807872 | bytes 13991936 | tf_op jit(solution)/shard_map/tf,td->fd/dot_general | solution.py:427
  375.0 5.2 fusion.146
  380.3 3.7 convolution_bitcast_fusion.1
  393.6 5.3 fusion.145
  398.9 3.8 convolution_bitcast_fusion
  414.3 25.8 %reduce-scatter.4.cloned.1.call-done = bf16[684,512]{1,0:T(8,128)(2,1)} async-done(((bf16[684,2048]{1,0:T(8,128)(2,1)}), bf16[684,512]{1,0:T(8,128)(2,1)}) %reduce-scatter.4.cloned.1.call-update) | async-done | bytes 700432 | tf_op jit(solution)/shard_map/reduce_scatter | solution.py:429
  440.1 17.8 %fusion = bf16[2,684,2048]{2,1,0:T(8,128)(2,1)} fusion(bf16[2048,2048]{1,0:T(8,128)(2,1)} %constant_dynamic-update-slice_fusion.10, bf16[1,512,684]{1,2,0:T(8,128)(2,1)} %copy-done.46, bf16[1,512,684]{1,2,0:T(8,128)(2,1)} %copy-done.45, bf16[1,512,684]{1,2,0:T(8,128)(2,1)} %copy-done.48, bf16[1,512,684]{1,2,0:T(8,128)(2,1)} %copy-done.47, ...), kind=kOutput, calls=%fused_computation.1 | convolution fusion | flops 11520442368 | bytes 19595264 | tf_op jit(solution)/shard_map/ctf,td->cfd/dot_general | solution.py:434
  458.6 5.7 multiply_reduce_fusion
  470.7 5.0 multiply_subtract_fusion
  475.7 16.1 %collective-permute-done.63 = bf16[256,2048]{1,0:T(8,128)(2,1)S(1)} collective-permute-done((bf16[256,2048]{1,0:T(8,128)(2,1)}, bf16[256,2048]{1,0:T(8,128)(2,1)S(1)}, u32[]{:S(2)}, u32[]{:S(2)}) %collective-permute-start.63) | collective-permute-done | bytes 1048608 | tf_op jit(solution)/shard_map/ppermute | solution.py:190
  497.1 10.3 %collective-permute-done.67 = bf16[128,2048]{1,0:T(8,128)(2,1)S(1)} collective-permute-done((bf16[128,2048]{1,0:T(8,128)(2,1)S(1)}, bf16[128,2048]{1,0:T(8,128)(2,1)S(1)}, u32[]{:S(2)}, u32[]{:S(2)}) %collective-permute-start.67) | collective-permute-done | bytes 524320 | tf_op jit(solution)/shard_map/ppermute | solution.py:190
  510.7 5.4 fusion.130.grad_ref
  516.0 14.2 %attend_backward.1 = bf16[2048,768]{1,0:T(8,128)(2,1)} custom-call(s32[4]{0:T(128)} %objective_ref.3, s32[4]{0:T(128)} %prefix_ref.3, s32[2]{0:T(128)} %pad_add_fusion.place_ref, bf16[2048,256]{1,0:T(8,128)(2,1)} %get-tuple-element.98.query_ref, bf16[2048,256]{1,0:T(8,128)(2,1)} %get-tuple-element.99.key_ref, ...), custom_call_target="tpu_custom_call" | custom-call | tf_op jit(solution)/shard_map/attend_backward/pallas_call | solution.py:150
  530.2 5.9 fusion.188
  536.1 9.6 %fusion.189 = bf16[768,2048]{1,0:T(8,128)(2,1)S(1)} fusion(bf16[2048,768]{1,0:T(8,128)(2,1)S(1)} %copy-done.16, bf16[2048,2048]{1,0:T(8,128)(2,1)} %constant_dynamic-update-slice_fusion), kind=kOutput, calls=%fused_computation.326 | convolution fusion | flops 6442450944 | bytes 14680064 | tf_op jit(solution)/shard_map/te,td->ed/dot_general | solution.py:469
  549.2 5.3 fusion.38
  554.4 5.3 fusion.36
  567.5 3.8 convert_add_fusion
  576.2 16.4 %fusion.162 = (f32[512,2,684]{0,1,2:T(2,128)}, f32[512,2,684]{0,1,2:T(2,128)}, f32[512,2,684]{0,1,2:T(2,128)}) fusion(f32[]{:T(128)S(6)} %div.99, bf16[2,684,512]{2,1,0:T(8,128)(2,1)S(1)} %copy-done.25, f32[512,2,684]{0,1,2:T(2,128)S(1)} %copy-done.19, f32[512,2,684]{0,1,2:T(2,128)S(1)} %copy-done.20, f32[512,2,684]{0,1,2:T(2,128)S(1)} %copy-done.5), kind=kLoop, calls=%fused_computation.312 | loop fusion | flops 11206656 | bytes 18210820 | tf_op jit(solution)/shard_map/transpose | solution.py:313
  592.7 4.1 collective-permute-done.75
  598.2 12.0 %collective-permute-done.76 = bf16[128,2048]{1,0:T(8,128)(2,1)S(1)} collective-permute-done((bf16[128,2048]{1,0:T(8,128)(2,1)S(1)}, bf16[128,2048]{1,0:T(8,128)(2,1)S(1)}, u32[]{:S(2)}, u32[]{:S(2)}) %collective-permute-start.76) | collective-permute-done | bytes 524320 | tf_op jit(solution)/shard_map/ppermute | solution.py:190
  622.9 4.6 collective-permute-done.84
  631.1 3.6 collective-permute-done.85
  635.4 5.3 reduce-scatter.8.cloned.1.call-done
  642.2 5.4 fusion.136
  (418 shorter events, 204.9 us)
Async XLA Ops:
  7.2 89.8 %all-gather.4.cloned.1.call-start = ((), (), s32[]{:S(2)}) async-start(), calls=%async_computation.3 | async-start | bytes 5242880 | tf_op jit(solution)/shard_map/all_gather | solution.py:357
  13.2 204.3 %all-gather.6.cloned.1.call-start = ((), (), s32[]{:S(2)}) async-start(), calls=%async_computation.4 | async-start | bytes 7045120 | tf_op jit(solution)/shard_map/all_gather | solution.py:363
  13.3 29.0 %collective-permute-start.1 = (bf16[256,2048]{1,0:T(8,128)(2,1)}, bf16[256,2048]{1,0:T(8,128)(2,1)}, u32[]{:S(2)}, u32[]{:S(2)}) collective-permute-start(bf16[256,2048]{1,0:T(8,128)(2,1)} %param.20), channel_id=1, source_target_pairs={{0,2},{1,3},{2,0},{3,1},{4,6},{5,7},{6,4},{7,5},{8,10},{9,11},{10,... | collective-permute-start | bytes 3145736 | tf_op jit(solution)/shard_map/ppermute | solution.py:190
  16.3 41.8 %collective-permute-start = (bf16[256,2048]{1,0:T(8,128)(2,1)}, bf16[256,2048]{1,0:T(8,128)(2,1)}, u32[]{:S(2)}, u32[]{:S(2)}) collective-permute-start(bf16[256,2048]{1,0:T(8,128)(2,1)} %param.20), channel_id=1, source_target_pairs={{0,1},{1,0},{2,3},{3,2},{4,5},{5,4},{6,7},{7,6},{8,9},{9,8},{10,11... | collective-permute-start | bytes 3145736 | tf_op jit(solution)/shard_map/ppermute | solution.py:190
  16.3 38.0 %collective-permute-start.3 = (bf16[256,2048]{1,0:T(8,128)(2,1)}, bf16[256,2048]{1,0:T(8,128)(2,1)}, u32[]{:S(2)}, u32[]{:S(2)}) collective-permute-start(bf16[256,2048]{1,0:T(8,128)(2,1)} %param.20), channel_id=1, source_target_pairs={{0,4},{1,5},{2,6},{3,7},{4,0},{5,1},{6,2},{7,3},{8,12},{9,13},{10,... | collective-permute-start | bytes 3145736 | tf_op jit(solution)/shard_map/ppermute | solution.py:190
  21.7 239.0 %all-gather.8.cloned.1.call-start = ((), (), s32[]{:S(2)}) async-start(), calls=%async_computation.5 | async-start | bytes 3522560 | tf_op jit(solution)/shard_map/all_gather | solution.py:364
  23.5 16.3 %collective-permute-start.10 = (f32[8,128]{1,0:T(8,128)S(1)}, f32[8,128]{1,0:T(8,128)S(1)}, u32[]{:S(2)}, u32[]{:S(2)}) collective-permute-start(f32[8,128]{1,0:T(8,128)S(1)} %broadcast_add_fusion), channel_id=1, source_target_pairs={{0,2},{1,3},{2,0},{3,1},{4,6},{5,7},{6,4},{7,5},{8,10},{9,11},{10,... | collective-permute-start | bytes 12296 | tf_op jit(solution)/shard_map/ppermute | solution.py:190
  42.3 24.2 %collective-permute-start.2 = (bf16[256,2048]{1,0:T(8,128)(2,1)}, bf16[256,2048]{1,0:T(8,128)(2,1)S(1)}, u32[]{:S(2)}, u32[]{:S(2)}) collective-permute-start(bf16[256,2048]{1,0:T(8,128)(2,1)} %collective-permute-done.1), channel_id=1, source_target_pairs={{0,1},{1,0},{2,3},{3,2},{4,5},{5,4},{6,7},{7,6},{8,9},{9,8},{10,11... | collective-permute-start | bytes 3145736 | tf_op jit(solution)/shard_map/ppermute | solution.py:190
  125.5 19.9 %collective-permute-start.14 = (bf16[256,2048]{1,0:T(8,128)(2,1)S(1)}, bf16[256,2048]{1,0:T(8,128)(2,1)S(1)}, u32[]{:S(2)}, u32[]{:S(2)}) collective-permute-start(bf16[256,2048]{1,0:T(8,128)(2,1)S(1)} %get-tuple-element.172), channel_id=1, source_target_pairs={{0,1},{1,0},{2,3},{3,2},{4,5},{5,4},{6,7},{7,6},{8,9},{9,8},{10,11... | collective-permute-start | bytes 3145736 | tf_op jit(solution)/shard_map/ppermute | solution.py:190
  126.5 14.9 %collective-permute-start.22 = (bf16[128,2048]{1,0:T(8,128)(2,1)S(1)}, bf16[128,2048]{1,0:T(8,128)(2,1)S(1)}, u32[]{:S(2)}, u32[]{:S(2)}) collective-permute-start(bf16[128,2048]{1,0:T(8,128)(2,1)S(1)} %get-tuple-element.191), channel_id=1, source_target_pairs={{0,2},{1,3},{2,0},{3,1},{4,6},{5,7},{6,4},{7,5},{8,10},{9,11},{10,... | collective-permute-start | bytes 1572872 | tf_op jit(solution)/shard_map/ppermute | solution.py:190
  128.0 15.0 %collective-permute-start.17 = (bf16[128,2048]{1,0:T(8,128)(2,1)S(1)}, bf16[128,2048]{1,0:T(8,128)(2,1)S(1)}, u32[]{:S(2)}, u32[]{:S(2)}) collective-permute-start(bf16[128,2048]{1,0:T(8,128)(2,1)S(1)} %get-tuple-element.190), channel_id=1, source_target_pairs={{0,4},{1,5},{2,6},{3,7},{4,0},{5,1},{6,2},{7,3},{8,12},{9,13},{10,... | collective-permute-start | bytes 1572872 | tf_op jit(solution)/shard_map/ppermute | solution.py:190
  130.4 23.6 %collective-permute-start.21 = (bf16[128,2048]{1,0:T(8,128)(2,1)S(1)}, bf16[128,2048]{1,0:T(8,128)(2,1)S(1)}, u32[]{:S(2)}, u32[]{:S(2)}) collective-permute-start(bf16[128,2048]{1,0:T(8,128)(2,1)S(1)} %slice.614), channel_id=1, source_target_pairs={{0,4},{1,5},{2,6},{3,7},{4,0},{5,1},{6,2},{7,3},{8,12},{9,13},{10,... | collective-permute-start | bytes 1572872 | tf_op jit(solution)/shard_map/ppermute | solution.py:190
  131.8 22.3 %collective-permute-start.19 = (bf16[128,2048]{1,0:T(8,128)(2,1)S(1)}, bf16[128,2048]{1,0:T(8,128)(2,1)S(1)}, u32[]{:S(2)}, u32[]{:S(2)}) collective-permute-start(bf16[128,2048]{1,0:T(8,128)(2,1)S(1)} %slice.615), channel_id=1, source_target_pairs={{0,2},{1,3},{2,0},{3,1},{4,6},{5,7},{6,4},{7,5},{8,10},{9,11},{10,... | collective-permute-start | bytes 1572872 | tf_op jit(solution)/shard_map/ppermute | solution.py:190
  141.5 22.6 %collective-permute-start.23 = (bf16[128,2048]{1,0:T(8,128)(2,1)S(1)}, bf16[128,2048]{1,0:T(8,128)(2,1)S(1)}, u32[]{:S(2)}, u32[]{:S(2)}) collective-permute-start(bf16[128,2048]{1,0:T(8,128)(2,1)S(1)} %fusion.127), channel_id=1, source_target_pairs={{0,4},{1,5},{2,6},{3,7},{4,0},{5,1},{6,2},{7,3},{8,12},{9,13},{10,... | collective-permute-start | bytes 1572872 | tf_op jit(solution)/shard_map/ppermute | solution.py:190
  143.2 20.9 %collective-permute-start.18 = (bf16[128,2048]{1,0:T(8,128)(2,1)S(1)}, bf16[128,2048]{1,0:T(8,128)(2,1)S(1)}, u32[]{:S(2)}, u32[]{:S(2)}) collective-permute-start(bf16[128,2048]{1,0:T(8,128)(2,1)S(1)} %fusion.128), channel_id=1, source_target_pairs={{0,2},{1,3},{2,0},{3,1},{4,6},{5,7},{6,4},{7,5},{8,10},{9,11},{10,... | collective-permute-start | bytes 1572872 | tf_op jit(solution)/shard_map/ppermute | solution.py:190
  167.2 24.4 %collective-permute-start.25 = (bf16[256,2048]{1,0:T(8,128)(2,1)}, bf16[256,2048]{1,0:T(8,128)(2,1)}, u32[]{:S(2)}, u32[]{:S(2)}) collective-permute-start(bf16[256,2048]{1,0:T(8,128)(2,1)} %get-tuple-element.151), channel_id=1, source_target_pairs={{0,2},{1,3},{2,0},{3,1},{4,6},{5,7},{6,4},{7,5},{8,10},{9,11},{10,... | collective-permute-start | bytes 3145736 | tf_op jit(solution)/shard_map/ppermute | solution.py:190
  167.7 27.7 %collective-permute-start.27 = (bf16[256,2048]{1,0:T(8,128)(2,1)}, bf16[256,2048]{1,0:T(8,128)(2,1)S(1)}, u32[]{:S(2)}, u32[]{:S(2)}) collective-permute-start(bf16[256,2048]{1,0:T(8,128)(2,1)} %get-tuple-element.151), channel_id=1, source_target_pairs={{0,4},{1,5},{2,6},{3,7},{4,0},{5,1},{6,2},{7,3},{8,12},{9,13},{10,... | collective-permute-start | bytes 3145736 | tf_op jit(solution)/shard_map/ppermute | solution.py:190
  169.3 26.9 %collective-permute-start.24 = (bf16[256,2048]{1,0:T(8,128)(2,1)}, bf16[256,2048]{1,0:T(8,128)(2,1)}, u32[]{:S(2)}, u32[]{:S(2)}) collective-permute-start(bf16[256,2048]{1,0:T(8,128)(2,1)} %get-tuple-element.151), channel_id=1, source_target_pairs={{0,1},{1,0},{2,3},{3,2},{4,5},{5,4},{6,7},{7,6},{8,9},{9,8},{10,11... | collective-permute-start | bytes 3145736 | tf_op jit(solution)/shard_map/ppermute | solution.py:190
  191.6 18.0 %collective-permute-start.26 = (bf16[256,2048]{1,0:T(8,128)(2,1)}, bf16[256,2048]{1,0:T(8,128)(2,1)}, u32[]{:S(2)}, u32[]{:S(2)}) collective-permute-start(bf16[256,2048]{1,0:T(8,128)(2,1)} %collective-permute-done.25), channel_id=1, source_target_pairs={{0,1},{1,0},{2,3},{3,2},{4,5},{5,4},{6,7},{7,6},{8,9},{9,8},{10,11... | collective-permute-start | bytes 3145736 | tf_op jit(solution)/shard_map/ppermute | solution.py:190
  192.6 247.5 %reduce-scatter.4.cloned.1.call-start = ((), (), s32[]{:S(2)}) async-start(), calls=%async_computation.6 | async-start | bytes 3522560 | tf_op jit(solution)/shard_map/reduce_scatter | solution.py:429
  193.9 14.4 %collective-permute-start.29 = (bf16[128,2048]{1,0:T(8,128)(2,1)S(1)}, bf16[128,2048]{1,0:T(8,128)(2,1)S(1)}, u32[]{:S(2)}, u32[]{:S(2)}) collective-permute-start(bf16[128,2048]{1,0:T(8,128)(2,1)S(1)} %slice.390), channel_id=1, source_target_pairs={{0,4},{1,5},{2,6},{3,7},{4,0},{5,1},{6,2},{7,3},{8,12},{9,13},{10,... | collective-permute-start | bytes 1572872 | tf_op jit(solution)/shard_map/ppermute | solution.py:190
  196.1 17.0 %collective-permute-start.28 = (bf16[256,2048]{1,0:T(8,128)(2,1)S(1)}, bf16[256,2048]{1,0:T(8,128)(2,1)S(1)}, u32[]{:S(2)}, u32[]{:S(2)}) collective-permute-start(bf16[256,2048]{1,0:T(8,128)(2,1)S(1)} %collective-permute-done.27), channel_id=1, source_target_pairs={{0,1},{1,0},{2,3},{3,2},{4,5},{5,4},{6,7},{7,6},{8,9},{9,8},{10,11... | collective-permute-start | bytes 3145736 | tf_op jit(solution)/shard_map/ppermute | solution.py:190
  271.5 19.1 %collective-permute-start.33 = (bf16[256,2048]{1,0:T(8,128)(2,1)S(1)}, bf16[256,2048]{1,0:T(8,128)(2,1)S(1)}, u32[]{:S(2)}, u32[]{:S(2)}) collective-permute-start(bf16[256,2048]{1,0:T(8,128)(2,1)S(1)} %get-tuple-element.167), channel_id=1, source_target_pairs={{0,1},{1,0},{2,3},{3,2},{4,5},{5,4},{6,7},{7,6},{8,9},{9,8},{10,11... | collective-permute-start | bytes 3145736 | tf_op jit(solution)/shard_map/ppermute | solution.py:190
  272.4 14.9 %collective-permute-start.41 = (bf16[128,2048]{1,0:T(8,128)(2,1)S(1)}, bf16[128,2048]{1,0:T(8,128)(2,1)S(1)}, u32[]{:S(2)}, u32[]{:S(2)}) collective-permute-start(bf16[128,2048]{1,0:T(8,128)(2,1)S(1)} %get-tuple-element.189), channel_id=1, source_target_pairs={{0,2},{1,3},{2,0},{3,1},{4,6},{5,7},{6,4},{7,5},{8,10},{9,11},{10,... | collective-permute-start | bytes 1572872 | tf_op jit(solution)/shard_map/ppermute | solution.py:190
  273.9 15.0 %collective-permute-start.36 = (bf16[128,2048]{1,0:T(8,128)(2,1)S(1)}, bf16[128,2048]{1,0:T(8,128)(2,1)S(1)}, u32[]{:S(2)}, u32[]{:S(2)}) collective-permute-start(bf16[128,2048]{1,0:T(8,128)(2,1)S(1)} %get-tuple-element.188), channel_id=1, source_target_pairs={{0,4},{1,5},{2,6},{3,7},{4,0},{5,1},{6,2},{7,3},{8,12},{9,13},{10,... | collective-permute-start | bytes 1572872 | tf_op jit(solution)/shard_map/ppermute | solution.py:190
  276.3 23.7 %collective-permute-start.40 = (bf16[128,2048]{1,0:T(8,128)(2,1)S(1)}, bf16[128,2048]{1,0:T(8,128)(2,1)S(1)}, u32[]{:S(2)}, u32[]{:S(2)}) collective-permute-start(bf16[128,2048]{1,0:T(8,128)(2,1)S(1)} %slice.612), channel_id=1, source_target_pairs={{0,4},{1,5},{2,6},{3,7},{4,0},{5,1},{6,2},{7,3},{8,12},{9,13},{10,... | collective-permute-start | bytes 1572872 | tf_op jit(solution)/shard_map/ppermute | solution.py:190
  277.6 22.3 %collective-permute-start.38 = (bf16[128,2048]{1,0:T(8,128)(2,1)S(1)}, bf16[128,2048]{1,0:T(8,128)(2,1)S(1)}, u32[]{:S(2)}, u32[]{:S(2)}) collective-permute-start(bf16[128,2048]{1,0:T(8,128)(2,1)S(1)} %slice.613), channel_id=1, source_target_pairs={{0,2},{1,3},{2,0},{3,1},{4,6},{5,7},{6,4},{7,5},{8,10},{9,11},{10,... | collective-permute-start | bytes 1572872 | tf_op jit(solution)/shard_map/ppermute | solution.py:190
  287.4 22.6 %collective-permute-start.42 = (bf16[128,2048]{1,0:T(8,128)(2,1)S(1)}, bf16[128,2048]{1,0:T(8,128)(2,1)S(1)}, u32[]{:S(2)}, u32[]{:S(2)}) collective-permute-start(bf16[128,2048]{1,0:T(8,128)(2,1)S(1)} %fusion.125), channel_id=1, source_target_pairs={{0,4},{1,5},{2,6},{3,7},{4,0},{5,1},{6,2},{7,3},{8,12},{9,13},{10,... | collective-permute-start | bytes 1572872 | tf_op jit(solution)/shard_map/ppermute | solution.py:190
  289.1 21.0 %collective-permute-start.37 = (bf16[128,2048]{1,0:T(8,128)(2,1)S(1)}, bf16[128,2048]{1,0:T(8,128)(2,1)S(1)}, u32[]{:S(2)}, u32[]{:S(2)}) collective-permute-start(bf16[128,2048]{1,0:T(8,128)(2,1)S(1)} %fusion.126), channel_id=1, source_target_pairs={{0,2},{1,3},{2,0},{3,1},{4,6},{5,7},{6,4},{7,5},{8,10},{9,11},{10,... | collective-permute-start | bytes 1572872 | tf_op jit(solution)/shard_map/ppermute | solution.py:190
  315.6 25.6 %collective-permute-start.44 = (bf16[256,2048]{1,0:T(8,128)(2,1)S(1)}, bf16[256,2048]{1,0:T(8,128)(2,1)S(1)}, u32[]{:S(2)}, u32[]{:S(2)}) collective-permute-start(bf16[256,2048]{1,0:T(8,128)(2,1)S(1)} %get-tuple-element.147), channel_id=1, source_target_pairs={{0,2},{1,3},{2,0},{3,1},{4,6},{5,7},{6,4},{7,5},{8,10},{9,11},{10,... | collective-permute-start | bytes 3145736 | tf_op jit(solution)/shard_map/ppermute | solution.py:190
  316.2 25.2 %collective-permute-start.45 = (bf16[256,2048]{1,0:T(8,128)(2,1)S(1)}, bf16[256,2048]{1,0:T(8,128)(2,1)S(1)}, u32[]{:S(2)}, u32[]{:S(2)}) collective-permute-start(bf16[256,2048]{1,0:T(8,128)(2,1)S(1)} %get-tuple-element.147), channel_id=1, source_target_pairs={{0,4},{1,5},{2,6},{3,7},{4,0},{5,1},{6,2},{7,3},{8,12},{9,13},{10,... | collective-permute-start | bytes 3145736 | tf_op jit(solution)/shard_map/ppermute | solution.py:190
  341.5 19.2 %collective-permute-start.47 = (bf16[256,2048]{1,0:T(8,128)(2,1)S(1)}, bf16[256,2048]{1,0:T(8,128)(2,1)S(1)}, u32[]{:S(2)}, u32[]{:S(2)}) collective-permute-start(bf16[256,2048]{1,0:T(8,128)(2,1)S(1)} %collective-permute-done.45), channel_id=1, source_target_pairs={{0,1},{1,0},{2,3},{3,2},{4,5},{5,4},{6,7},{7,6},{8,9},{9,8},{10,11... | collective-permute-start | bytes 3145736 | tf_op jit(solution)/shard_map/ppermute | solution.py:190
  386.8 176.7 %reduce-scatter.6.cloned.1.call-start = ((), (), s32[]{:S(2)}) async-start(), calls=%async_computation.7 | async-start | bytes 7045120 | tf_op jit(solution)/shard_map/reduce_scatter | solution.py:459
  407.2 50.7 %collective-permute-start.58 = (bf16[128,2048]{1,0:T(8,128)(2,1)}, bf16[128,2048]{1,0:T(8,128)(2,1)}, u32[]{:S(2)}, u32[]{:S(2)}) collective-permute-start(bf16[128,2048]{1,0:T(8,128)(2,1)} %slice.611), channel_id=1, source_target_pairs={{0,2},{1,3},{2,0},{3,1},{4,6},{5,7},{6,4},{7,5},{8,10},{9,11},{10,... | collective-permute-start | bytes 1572872 | tf_op jit(solution)/shard_map/ppermute | solution.py:190
  409.5 48.5 %collective-permute-start.57 = (bf16[128,2048]{1,0:T(8,128)(2,1)}, bf16[128,2048]{1,0:T(8,128)(2,1)}, u32[]{:S(2)}, u32[]{:S(2)}) collective-permute-start(bf16[128,2048]{1,0:T(8,128)(2,1)} %add_convert_fusion.5), channel_id=1, source_target_pairs={{0,2},{1,3},{2,0},{3,1},{4,6},{5,7},{6,4},{7,5},{8,10},{9,11},{10,... | collective-permute-start | bytes 1572872 | tf_op jit(solution)/shard_map/ppermute | solution.py:190
  411.3 46.6 %collective-permute-start.60 = (bf16[128,2048]{1,0:T(8,128)(2,1)}, bf16[128,2048]{1,0:T(8,128)(2,1)}, u32[]{:S(2)}, u32[]{:S(2)}) collective-permute-start(bf16[128,2048]{1,0:T(8,128)(2,1)} %slice.610), channel_id=1, source_target_pairs={{0,4},{1,5},{2,6},{3,7},{4,0},{5,1},{6,2},{7,3},{8,12},{9,13},{10,... | collective-permute-start | bytes 1572872 | tf_op jit(solution)/shard_map/ppermute | solution.py:190
  413.9 44.0 %collective-permute-start.61 = (bf16[128,2048]{1,0:T(8,128)(2,1)}, bf16[128,2048]{1,0:T(8,128)(2,1)}, u32[]{:S(2)}, u32[]{:S(2)}) collective-permute-start(bf16[128,2048]{1,0:T(8,128)(2,1)} %fusion.124), channel_id=1, source_target_pairs={{0,4},{1,5},{2,6},{3,7},{4,0},{5,1},{6,2},{7,3},{8,12},{9,13},{10,... | collective-permute-start | bytes 1572872 | tf_op jit(solution)/shard_map/ppermute | solution.py:190
  458.0 182.7 %reduce-scatter.8.cloned.1.call-start = ((), (), s32[]{:S(2)}) async-start(), calls=%async_computation.8 | async-start | bytes 5242880 | tf_op jit(solution)/shard_map/reduce_scatter | solution.py:476
  467.0 24.7 %collective-permute-start.63 = (bf16[256,2048]{1,0:T(8,128)(2,1)}, bf16[256,2048]{1,0:T(8,128)(2,1)S(1)}, u32[]{:S(2)}, u32[]{:S(2)}) collective-permute-start(bf16[256,2048]{1,0:T(8,128)(2,1)} %get-tuple-element.143), channel_id=1, source_target_pairs={{0,2},{1,3},{2,0},{3,1},{4,6},{5,7},{6,4},{7,5},{8,10},{9,11},{10,... | collective-permute-start | bytes 3145736 | tf_op jit(solution)/shard_map/ppermute | solution.py:190
  468.5 24.5 %collective-permute-start.64 = (bf16[256,2048]{1,0:T(8,128)(2,1)}, bf16[256,2048]{1,0:T(8,128)(2,1)S(1)}, u32[]{:S(2)}, u32[]{:S(2)}) collective-permute-start(bf16[256,2048]{1,0:T(8,128)(2,1)} %get-tuple-element.143), channel_id=1, source_target_pairs={{0,4},{1,5},{2,6},{3,7},{4,0},{5,1},{6,2},{7,3},{8,12},{9,13},{10,... | collective-permute-start | bytes 3145736 | tf_op jit(solution)/shard_map/ppermute | solution.py:190
  470.0 25.7 %collective-permute-start.62 = (bf16[256,2048]{1,0:T(8,128)(2,1)}, bf16[256,2048]{1,0:T(8,128)(2,1)}, u32[]{:S(2)}, u32[]{:S(2)}) collective-permute-start(bf16[256,2048]{1,0:T(8,128)(2,1)} %get-tuple-element.143), channel_id=1, source_target_pairs={{0,1},{1,0},{2,3},{3,2},{4,5},{5,4},{6,7},{7,6},{8,9},{9,8},{10,11... | collective-permute-start | bytes 3145736 | tf_op jit(solution)/shard_map/ppermute | solution.py:190
  492.9 15.8 %collective-permute-start.65 = (bf16[256,2048]{1,0:T(8,128)(2,1)S(1)}, bf16[256,2048]{1,0:T(8,128)(2,1)S(1)}, u32[]{:S(2)}, u32[]{:S(2)}) collective-permute-start(bf16[256,2048]{1,0:T(8,128)(2,1)S(1)} %collective-permute-done.63), channel_id=1, source_target_pairs={{0,1},{1,0},{2,3},{3,2},{4,5},{5,4},{6,7},{7,6},{8,9},{9,8},{10,11... | collective-permute-start | bytes 3145736 | tf_op jit(solution)/shard_map/ppermute | solution.py:190
  492.9 15.9 %collective-permute-start.66 = (bf16[256,2048]{1,0:T(8,128)(2,1)S(1)}, bf16[256,2048]{1,0:T(8,128)(2,1)S(1)}, u32[]{:S(2)}, u32[]{:S(2)}) collective-permute-start(bf16[256,2048]{1,0:T(8,128)(2,1)S(1)} %collective-permute-done.64), channel_id=1, source_target_pairs={{0,1},{1,0},{2,3},{3,2},{4,5},{5,4},{6,7},{7,6},{8,9},{9,8},{10,11... | collective-permute-start | bytes 3145736 | tf_op jit(solution)/shard_map/ppermute | solution.py:190
  565.3 32.9 %collective-permute-start.71 = (bf16[256,2048]{1,0:T(8,128)(2,1)S(1)}, bf16[256,2048]{1,0:T(8,128)(2,1)S(1)}, u32[]{:S(2)}, u32[]{:S(2)}) collective-permute-start(bf16[256,2048]{1,0:T(8,128)(2,1)S(1)} %get-tuple-element.166), channel_id=1, source_target_pairs={{0,1},{1,0},{2,3},{3,2},{4,5},{5,4},{6,7},{7,6},{8,9},{9,8},{10,11... | collective-permute-start | bytes 3145736 | tf_op jit(solution)/shard_map/ppermute | solution.py:190
  571.4 26.8 %collective-permute-start.77 = (bf16[128,2048]{1,0:T(8,128)(2,1)S(1)}, bf16[128,2048]{1,0:T(8,128)(2,1)S(1)}, u32[]{:S(2)}, u32[]{:S(2)}) collective-permute-start(bf16[128,2048]{1,0:T(8,128)(2,1)S(1)} %slice.609), channel_id=1, source_target_pairs={{0,2},{1,3},{2,0},{3,1},{4,6},{5,7},{6,4},{7,5},{8,10},{9,11},{10,... | collective-permute-start | bytes 1572872 | tf_op jit(solution)/shard_map/ppermute | solution.py:190
  572.0 20.7 %collective-permute-start.74 = (bf16[128,2048]{1,0:T(8,128)(2,1)S(1)}, bf16[128,2048]{1,0:T(8,128)(2,1)S(1)}, u32[]{:S(2)}, u32[]{:S(2)}) collective-permute-start(bf16[128,2048]{1,0:T(8,128)(2,1)S(1)} %get-tuple-element.185), channel_id=1, source_target_pairs={{0,4},{1,5},{2,6},{3,7},{4,0},{5,1},{6,2},{7,3},{8,12},{9,13},{10,... | collective-permute-start | bytes 1572872 | tf_op jit(solution)/shard_map/ppermute | solution.py:190
  572.8 23.9 %collective-permute-start.75 = (bf16[128,2048]{1,0:T(8,128)(2,1)S(1)}, bf16[128,2048]{1,0:T(8,128)(2,1)S(1)}, u32[]{:S(2)}, u32[]{:S(2)}) collective-permute-start(bf16[128,2048]{1,0:T(8,128)(2,1)S(1)} %get-tuple-element.184), channel_id=1, source_target_pairs={{0,2},{1,3},{2,0},{3,1},{4,6},{5,7},{6,4},{7,5},{8,10},{9,11},{10,... | collective-permute-start | bytes 1572872 | tf_op jit(solution)/shard_map/ppermute | solution.py:190
  574.8 23.4 %collective-permute-start.79 = (bf16[128,2048]{1,0:T(8,128)(2,1)S(1)}, bf16[128,2048]{1,0:T(8,128)(2,1)S(1)}, u32[]{:S(2)}, u32[]{:S(2)}) collective-permute-start(bf16[128,2048]{1,0:T(8,128)(2,1)S(1)} %slice.608), channel_id=1, source_target_pairs={{0,4},{1,5},{2,6},{3,7},{4,0},{5,1},{6,2},{7,3},{8,12},{9,13},{10,... | collective-permute-start | bytes 1572872 | tf_op jit(solution)/shard_map/ppermute | solution.py:190
  (99 other events, 657.9 us)
Sparse Core Ops, SparseCore 0:
  13.3 83.5 all-gather.3
  99.1 103.0 all-gather.5
  204.4 56.2 all-gather.7
  387.0 53.0 reduce-scatter.3
  458.1 99.8 reduce-scatter.5
  563.7 76.9 reduce-scatter.7
